TPU v7x, 32 devices: a whole 2x2x4 slice. The times are simulated.
32 devices in a mesh: seq: 8 (over z, core), fsdp: 4 (over y, x).
Axes of the slice: x: 2, y: 2, z: 4, core: 2. Of those that a mesh axis runs over, the one named last changes fastest.
Arguments:
- signal: bfloat16 [4, 8192, 1024], P('fsdp', 'seq'), may hold values from -6 to 6
- cotangent: bfloat16 [4, 8192, 1024], P('fsdp', 'seq'), may hold values from -6 to 6
- w_in: bfloat16 [1024, 1024], P('fsdp'), may hold values from -0.1875 to 0.1875
- w_conv: bfloat16 [2, 1024, 128], P(None, 'seq'), may hold values from -0.5 to 0.5
- w_out: bfloat16 [1024, 1024], P('fsdp'), may hold values from -0.1875 to 0.1875
- dilation: int32 [16], P('seq'), may hold values from 512 to 4095
- lengths: int32 [4], P('fsdp'), may hold values from 2048 to 8192, as said below
Outputs:
- grad_signal: bfloat16 [4, 8192, 1024], P('fsdp', 'seq')
- grad_in: float32 [1024, 1024], P('fsdp')
- grad_out: float32 [1024, 1024], P('fsdp')
- grad_conv: float32 [2, 1024, 128], P(None, 'seq')
Inputs may be any that keep to these rules, and one draw needn't show every extreme that they name: `lengths`: some record in every draw holds all 8192 samples.
All inputs are finite; a program needn't handle non-finite values.
Results may differ from a plain program's by a relative error of at most 0.0068.
Values may be sent and summed in bfloat16 or wider, within the bound.
No kernel may reach another device: no remote copies, remote signals or barrier semaphores. Data moves between devices by JAX's collectives and lax.ppermute only.
A program may use at most 128 MiB of HBM per device.

v0:
```python
import functools
import math

import jax
import jax.numpy as jnp
from jax import lax
from jax.experimental import pallas as pl
from jax.experimental.pallas import tpu as pltpu
from jax.sharding import PartitionSpec as P


MAX_DILATION = 4095
LANES = 128
BF = jnp.bfloat16
F32 = jnp.float32
VM = pl.BlockSpec(memory_space=pltpu.VMEM)
SM = pl.BlockSpec(memory_space=pltpu.SMEM)


def dot(a, b, ca, cb):
    return lax.dot_general(a, b, (((ca,), (cb,)), ((), ())), preferred_element_type=F32)


def call(body, outs, ins, scratch=(), flops=0, scalars=1, small=0):
    moved = sum(math.prod(x.shape) * x.dtype.itemsize for x in list(ins) + list(outs))
    return pl.pallas_call(
        body,
        out_shape=tuple(outs),
        in_specs=[SM] * scalars + [VM] * (len(ins) - scalars),
        out_specs=tuple([SM] * small + [VM] * (len(outs) - small)),
        scratch_shapes=list(scratch),
        cost_estimate=pl.CostEstimate(flops=flops, bytes_accessed=moved, transcendentals=0),
        compiler_params=pltpu.CompilerParams(vmem_limit_bytes=60 * 1024 * 1024),
    )(*ins)


def shape(dims, kind):
    return jax.ShapeDtypeStruct(dims, kind)


def forward_body(parts, tile, meta, own, partner, *rest):
    weights, outs = rest[:parts], rest[parts:]
    me = meta[0]
    rows = weights[0].shape[0]
    panel = outs[-1]
    for k in range(parts):
        panel[pl.ds(pl.multiple_of((me ^ k) * rows, rows), rows), :] = weights[k][...]
    targets = outs[:-1]
    for source, slot in ((own, 0), (partner, 1)):

        def step(i, carry, source=source, slot=slot):
            at = pl.multiple_of(i * tile, tile)
            got = dot(source[pl.ds(at, tile), :], panel[...], 1, 0).astype(BF)
            for j, target in enumerate(targets):
                target[slot, pl.ds(at, tile), :] = got[:, j * LANES : (j + 1) * LANES]
            return carry

        lax.fori_loop(0, source.shape[0] // tile, step, 0)


def upstream_body(parts, tile, meta, own, partner, *rest):
    weights, outs = rest[:parts], rest[parts:]
    me = meta[0]
    rows = weights[0].shape[0]
    panel = outs[-1]
    targets = outs[:-1]
    for k in range(parts):
        panel[me ^ k] = weights[k][...]
    for source, slot in ((own, 0), (partner, 1)):

        def step(i, carry, source=source, slot=slot):
            at = pl.multiple_of(i * tile, tile)
            whole = panel[...].reshape(parts * rows, panel.shape[2])
            got = dot(source[pl.ds(at, tile), :], whole, 1, 1).astype(BF)
            for j, target in enumerate(targets):
                target[slot, pl.ds(at, tile), :] = got[:, j * LANES : (j + 1) * LANES]
            return carry

        lax.fori_loop(0, source.shape[0] // tile, step, 0)


def select_lanes(a, b):
    lane = lax.broadcasted_iota(jnp.int32, a.shape, 1)
    return jnp.where(lane < LANES // 2, a, b)


def conv_body(hops, tile, pair, meta, amounts, *rest):
    sources, rest = rest[: hops + 1], rest[hops + 1 :]
    upstream, kernel, gated, tap_zero, tap_one, grad_kernel, series, total = rest
    half = sources[0].shape[1]
    core, alive = meta[2], meta[3]
    late_a, late_b = amounts[2 * pair], amounts[2 * pair + 1]
    for n in range(hops + 1):
        for h in range(2):
            series[(2 * (hops - n) + h) * half : (2 * (hops - n) + h + 1) * half, :] = (
                sources[n][h ^ core].astype(F32)
            )
    total[...] = jnp.zeros_like(total)
    per_half = half // tile

    def step(i, carry):
        slot = (i // per_half) ^ core
        row = pl.multiple_of((i % per_half) * tile, tile)
        start = 2 * hops * half + i * tile
        late = select_lanes(
            series[pl.ds(start - late_a, tile), :], series[pl.ds(start - late_b, tile), :]
        ).astype(BF)
        stacked = jnp.concatenate([sources[0][slot, pl.ds(row, tile), :], late], axis=1)
        pre = dot(stacked, kernel[...], 1, 0)
        tanh_act = jnp.tanh(pre[:, :LANES])
        sig_act = jax.nn.sigmoid(pre[:, LANES:])
        moment = i * tile + lax.broadcasted_iota(jnp.int32, tanh_act.shape, 0)
        mask = (moment < alive).astype(F32)
        gated[slot, pl.ds(row, tile), :] = (tanh_act * sig_act * mask).astype(BF)
        masked = upstream[slot, pl.ds(row, tile), :].astype(F32) * mask
        grad_filter = masked * sig_act * (1.0 - tanh_act * tanh_act)
        grad_gate = masked * tanh_act * sig_act * (1.0 - sig_act)
        acts = jnp.concatenate([grad_filter.astype(BF), grad_gate.astype(BF)], axis=1)
        total[...] += dot(stacked, acts, 0, 0)
        back = dot(acts, kernel[...], 1, 1)
        tap_zero[slot, pl.ds(row, tile), :] = back[:, :LANES]
        tap_one[slot, pl.ds(row, tile), :] = back[:, LANES:].astype(BF)
        return carry

    lax.fori_loop(0, 2 * per_half, step, 0)
    width = LANES // 2
    for tap in range(2):
        for g in range(2):
            top = tap * LANES + g * width
            left = total[top : top + width, :LANES]
            right = total[top : top + width, LANES:]
            if g == 0:
                right = pltpu.roll(right, width, 1)
            else:
                left = pltpu.roll(left, width, 1)
            grad_kernel[tap, g * width : (g + 1) * width, :] = select_lanes(left, right).astype(BF)


def mixed_body(hops, tile, pair, meta, amounts, tap_zero, *rest):
    sources, (own, partner, series) = rest[: hops + 1], rest[hops + 1 :]
    half = tap_zero.shape[1]
    core = meta[2]
    early_a, early_b = amounts[2 * pair], amounts[2 * pair + 1]
    for n in range(hops + 1):
        for h in range(2):
            series[(2 * n + h) * half : (2 * n + h + 1) * half, :] = sources[n][h ^ core].astype(
                F32
            )
    for slot, target in ((0, own), (1, partner)):

        def step(i, carry, slot=slot, target=target):
            row = pl.multiple_of(i * tile, tile)
            start = (slot ^ core) * half + row
            early = select_lanes(
                series[pl.ds(start + early_a, tile), :], series[pl.ds(start + early_b, tile), :]
            )
            target[pl.ds(row, tile), :] = (tap_zero[slot, pl.ds(row, tile), :] + early).astype(BF)
            return carry

        lax.fori_loop(0, half // tile, step, 0)


def outer_body(chunks, parts, tile, by_rows, split, meta, *rest):
    count = chunks * (2 if split else 1)
    lefts, rest = rest[:count], rest[count:]
    rights, outs, total = rest[:2], rest[2:-1], rest[-1]
    me = meta[0]
    total[...] = jnp.zeros_like(total)
    for slot in range(2):

        def step(i, carry, slot=slot):
            at = pl.multiple_of(i * tile, tile)
            if split:
                left = [lefts[2 * j + slot][pl.ds(at, tile), :] for j in range(chunks)]
            else:
                left = [lefts[j][slot, pl.ds(at, tile), :] for j in range(chunks)]
            left = jnp.concatenate(left, axis=1)
            if split and slot == 1:
                outs[parts][pl.ds(at, tile), :] = left
            total[...] += dot(left, rights[slot][pl.ds(at, tile), :], 0, 0)
            return carry

        lax.fori_loop(0, rights[slot].shape[0] // tile, step, 0)
    rows, columns = outs[0].shape
    for k in range(parts):
        if by_rows:
            at = pl.multiple_of((me ^ k) * rows, rows)
            got = total[pl.ds(at, rows), :]
        else:
            at = pl.multiple_of((me ^ k) * columns, columns)
            got = total[:, pl.ds(at, columns)]
        outs[k][...] = got.astype(outs[k].dtype)


def tree(values):
    while len(values) > 1:
        values = [values[i] + values[i + 1] for i in range(0, len(values), 2)]
    return values[0]


def split_body(count, parts, meta, *rest):
    ins, outs, total = rest[:count], rest[count:-1], rest[-1]
    total[...] = tree([x[...].astype(F32) for x in ins])
    rows = outs[0].shape[0]
    for k in range(parts):
        at = pl.multiple_of((meta[1] ^ k) * rows, rows)
        outs[k][...] = total[pl.ds(at, rows), :].astype(outs[k].dtype)


def sum_body(count, factor, *rest):
    got = tree([x[...].astype(F32) for x in rest[:count]])
    rest[count][...] = (got if factor is None else got * factor).astype(rest[count].dtype)


def pack_body(count, meta, *rest):
    for k in range(count):
        rest[count][meta[1] ^ k] = rest[k][...]


def share_body(parts, meta, whole, *outs):
    piece = whole.shape[1] // (2 * parts)
    each = parts // len(outs)
    for n, out in enumerate(outs):
        got = []
        for f in range(n * each, (n + 1) * each):
            both = whole[:, 2 * f * piece : 2 * (f + 1) * piece]
            got.append(jnp.where(meta[2] == 0, both[:, :piece], both[:, piece:]))
        out[...] = jnp.concatenate(got, axis=1)


def taps_body(chips, groups, meta, *rest):
    delays, blocks = rest[:chips], rest[chips : 2 * chips]
    amounts, outs = rest[2 * chips], rest[2 * chips + 1 :]
    width = LANES // 2
    for out in outs:
        out[...] = jnp.zeros_like(out)
    for k in range(chips):
        at = meta[1] ^ k
        for n in range(groups):
            group = at * groups + n
            amounts[group] = delays[k][n]
            for spot in range(2 * len(outs)):

                @pl.when(group == spot)
                def _(k=k, n=n, spot=spot):
                    out, g = outs[spot // 2], spot % 2
                    for tap in range(2):
                        top = tap * LANES + g * width
                        block = blocks[k][tap, n * width : (n + 1) * width, :].astype(F32)
                        lane = lax.broadcasted_iota(jnp.int32, block.shape, 1)
                        here = (lane < width) == (g == 0)
                        other = pltpu.roll(block, width, 1)
                        left, right = (block, other) if g == 0 else (other, block)
                        zero = jnp.zeros_like(block)
                        out[top : top + width, :LANES] = jnp.where(here, left, zero).astype(BF)
                        out[top : top + width, LANES:] = jnp.where(here, right, zero).astype(BF)


def pick_body(chips, count, meta, *rest):
    ins, outs, held = rest[:count], rest[count:-1], rest[-1]
    rows = outs[0].shape[1]
    each = LANES // rows
    for j in range(count):
        for n in range(each):
            held[j * each + n] = ins[j][:, n * rows : (n + 1) * rows, :]
    for k in range(chips):
        outs[k][...] = held[meta[1] ^ k]


def local_step(signal, cotangent, w_in, w_conv, w_out, dilation, lengths):
    record, upstream = signal[0], cotangent[0]
    samples, channels = record.shape
    seq_size, fsdp_size = lax.axis_size("seq"), lax.axis_size("fsdp")
    chips = seq_size // 2
    seq_at, fsdp_at = lax.axis_index("seq"), lax.axis_index("fsdp")
    core, chip = seq_at % 2, seq_at // 2
    factor = 1.0 / math.sqrt(samples * seq_size * fsdp_size)
    block = 2 * samples
    hops = -(-MAX_DILATION // block)
    share = channels // 2
    piece = share // fsdp_size
    conv_chans = w_conv.shape[1]
    local_groups = dilation.shape[0]
    width = conv_chans // local_groups
    assert 2 * width == LANES and chips == fsdp_size and piece == conv_chans
    chunks = share // LANES
    per_half = max(chunks // 2, 1)

    def to_partner(x):
        return lax.ppermute(x, "seq", [(i, i ^ 1) for i in range(seq_size)])

    def from_fsdp(blocks):
        got = [blocks[0]]
        for k in range(1, fsdp_size):
            pairs = [(i, i ^ k) for i in range(fsdp_size)]
            got.append(lax.ppermute(blocks[k], "fsdp", pairs))
        return got

    def from_chips(blocks):
        got = [blocks[0]]
        for k in range(1, chips):
            pairs = [(i, i ^ (2 * k)) for i in range(seq_size)]
            got.append(lax.ppermute(blocks[k], "seq", pairs))
        return got

    def up(x, hop):
        return lax.ppermute(x, "seq", [(i, i + 2) for i in range(2 * (hop - 1), seq_size - 2)])

    def down(x, hop):
        return lax.ppermute(x, "seq", [(i + 2, i) for i in range(seq_size - 2 * hop)])

    where = jnp.stack([fsdp_at, chip, core, lengths[0] - chip * block]).astype(jnp.int32)
    wide = per_half * LANES
    halves = range(0, chunks, per_half)
    in_shares = call(
        functools.partial(share_body, fsdp_size),
        [shape((w_in.shape[0], wide), BF)] * len(halves),
        [where, w_in],
    )
    out_share = lax.dynamic_index_in_dim(
        w_out.reshape(2, piece, channels), core, 0, keepdims=False
    )
    record_far = to_partner(record)
    in_parts = [from_fsdp([x] * fsdp_size) for x in in_shares]
    upstream_far = to_partner(upstream)
    out_parts = from_fsdp([out_share] * fsdp_size)
    delays = from_chips([dilation] * chips)
    conv_parts = from_chips([w_conv] * chips)
    taps = call(
        functools.partial(taps_body, chips, local_groups),
        [shape((2 * chunks,), jnp.int32)] + [shape((2 * LANES, 2 * LANES), BF)] * chunks,
        [where] + delays + conv_parts,
        scalars=1 + chips,
        small=1,
    )
    amounts, kernels = taps[0], taps[1:]

    series = shape((2, samples, LANES), BF)
    tile = min(512, samples)
    projected, panels = [], []
    for n in range(len(halves)):
        got = call(
            functools.partial(forward_body, fsdp_size, tile),
            [series] * per_half + [shape((channels, wide), BF)],
            [where, record, record_far] + in_parts[n],
            flops=2 * block * channels * wide,
        )
        projected += got[:-1]
        panels.append(got[-1])
    grad_gated = call(
        functools.partial(upstream_body, fsdp_size, tile),
        [series] * chunks,
        [where, upstream, upstream_far] + out_parts,
        scratch=[pltpu.VMEM((fsdp_size, piece, channels), BF)],
        flops=2 * block * channels * share,
    )
    panels_far = [to_partner(x) for x in panels]

    tile = min(256, samples)
    gated, own_mixed, far_mixed, kernel_grads = [], [], [], []
    long = pltpu.VMEM((2 * (hops + 1) * samples, LANES), F32)
    for j in range(chunks):
        chain = [projected[j]]
        for hop in range(1, hops + 1):
            chain.append(up(chain[-1], hop))
        out, tap_zero, tap_one, grad_kernel = call(
            functools.partial(conv_body, hops, tile, j),
            [series, shape((2, samples, LANES), F32), series, shape((2, LANES, LANES), BF)],
            [where, amounts] + chain + [grad_gated[j], kernels[j]],
            scratch=[long, pltpu.VMEM((2 * LANES, 2 * LANES), F32)],
            flops=6 * block * 4 * LANES * LANES,
            scalars=2,
        )
        gated.append(out)
        kernel_grads.append(grad_kernel)
        back = [tap_one]
        for hop in range(1, hops + 1):
            back.append(down(back[-1], hop))
        own, far = call(
            functools.partial(mixed_body, hops, tile, j),
            [shape((samples, LANES), BF)] * 2,
            [where, amounts, tap_zero] + back,
            scratch=[long],
            scalars=2,
        )
        own_mixed.append(own)
        far_mixed.append(far)

    def over_all(blocks):
        got = from_fsdp(blocks)
        rows, columns = blocks[0].shape
        part = rows // chips
        cut = call(
            functools.partial(split_body, fsdp_size, chips),
            [shape((part, columns), F32)] + [shape((part, columns), BF)] * (chips - 1),
            [where] + got,
            scratch=[pltpu.VMEM((rows, columns), F32)],
        )
        got = from_chips(cut)
        (mine,) = call(
            functools.partial(sum_body, chips, None), [shape((part, columns), BF)], got, scalars=0
        )
        got = from_chips([mine] * chips)
        (packed,) = call(
            functools.partial(pack_body, chips), [shape((chips, part, columns), BF)], [where] + got
        )
        return [packed, to_partner(packed)]

    def outer(lefts, rights, by_rows, split, tile):
        count = len(lefts) // 2 if split else len(lefts)
        rows, columns = LANES * count, channels
        one = (piece, columns) if by_rows else (rows, columns // fsdp_size)
        return call(
            functools.partial(outer_body, count, fsdp_size, tile, by_rows, split),
            [shape(one, F32)]
            + [shape(one, BF)] * (fsdp_size - 1)
            + ([shape((samples, rows), BF)] if split else []),
            [where] + lefts + list(rights),
            scratch=[pltpu.VMEM((rows, columns), F32)],
            flops=2 * block * rows * columns,
        )

    tile = min(512, samples)
    finals = over_all(outer(gated, (upstream, upstream_far), True, False, tile))
    mixed_in = []
    for start in halves:
        sides = []
        for j in range(start, start + per_half):
            sides += [own_mixed[j], far_mixed[j]]
        got = outer(sides, (record, record_far), False, True, tile)
        mixed_in.append(to_partner(got[-1]))
        finals += over_all(got[:fsdp_size])

    cuts = call(
        functools.partial(pick_body, chips, chunks),
        [shape((2, conv_chans, LANES), BF)] * chips,
        [where] + kernel_grads,
        scratch=[pltpu.VMEM((chips, 2, conv_chans, LANES), BF)],
    )
    got = from_chips(cuts)
    (mine,) = call(
        functools.partial(sum_body, chips, None),
        [shape((2, conv_chans, LANES), BF)],
        got,
        scalars=0,
    )
    got = from_fsdp([mine] * fsdp_size)
    (grad_conv,) = call(
        functools.partial(sum_body, fsdp_size, factor),
        [shape((2, conv_chans, LANES), F32)],
        got,
        scalars=0,
    )

    tile = min(256, samples)

    def signal_body(base, *rest):
        target = rest[-1]
        mixes, others, sides = rest[:chunks], rest[chunks : chunks + len(halves)], rest[
            chunks + len(halves) : -1
        ]
        acc = base[...].astype(F32)
        for n in range(len(halves)):
            mix = jnp.concatenate(
                [mixes[n * per_half + j][...] for j in range(per_half)], axis=1
            )
            acc += dot(mix, sides[n][...], 1, 1)
            acc += dot(others[n][...], sides[len(halves) + n][...], 1, 1)
        target[...] = acc.astype(BF)

    sides = panels + panels_far
    grad_signal = pl.pallas_call(
        signal_body,
        grid=(samples // tile,),
        out_shape=shape((samples, channels), BF),
        in_specs=[pl.BlockSpec((tile, channels), lambda i: (i, 0))]
        + [pl.BlockSpec((tile, LANES), lambda i: (i, 0))] * chunks
        + [pl.BlockSpec((tile, wide), lambda i: (i, 0))] * len(halves)
        + [pl.BlockSpec(x.shape, lambda i: (0, 0)) for x in sides],
        out_specs=pl.BlockSpec((tile, channels), lambda i: (i, 0)),
        cost_estimate=pl.CostEstimate(
            flops=2 * samples * channels * channels,
            bytes_accessed=8 * samples * channels,
            transcendentals=0,
        ),
        compiler_params=pltpu.CompilerParams(vmem_limit_bytes=60 * 1024 * 1024),
        name="signal",
    )(upstream, *own_mixed, *mixed_in, *sides)

    def finish_body(meta, *rest):
        ins, (grad_in, grad_out, turned) = rest[:-3], rest[-3:]
        core_at = meta[2]
        for side in range(2):
            whole = ins[side][...].astype(F32) * factor
            at = pl.multiple_of((side ^ core_at) * piece, piece)
            grad_out[pl.ds(at, piece), :] = whole.reshape(piece, channels)
            for n in range(len(halves)):
                whole = ins[2 * (n + 1) + side][...].astype(F32) * factor
                turned[side ^ core_at, n * wide : (n + 1) * wide, :] = whole.reshape(
                    wide, turned.shape[2]
                )
        for f in range(fsdp_size):
            both = jnp.concatenate(
                [turned[c, f * piece : (f + 1) * piece, :] for c in range(2)], axis=0
            )
            grad_in[:, 2 * f * piece : 2 * (f + 1) * piece] = both.T

    own_rows = channels // fsdp_size
    grad_in, grad_out = call(
        finish_body,
        [shape((own_rows, channels), F32)] * 2,
        [where] + finals,
        scratch=[pltpu.VMEM((2, share, own_rows), F32)],
    )
    return (grad_signal[None], grad_in, grad_out, grad_conv)


def solution(mesh):
    placed = (
        P("fsdp", "seq", None),
        P("fsdp", "seq", None),
        P("fsdp", None),
        P(None, "seq", None),
        P("fsdp", None),
        P("seq"),
        P("fsdp"),
    )
    return jax.shard_map(
        local_step,
        mesh=mesh,
        in_specs=placed,
        out_specs=(P("fsdp", "seq", None), P("fsdp", None), P("fsdp", None), P(None, "seq", None)),
        check_vma=False,
    )
```

profile of v0, /device:TPU:0, one launch (start us, length us, event | category | flops | bytes accessed | tf_op | source)
XLA Modules:
  0.0 361.4 jit_solution(12624271647739353567)
XLA Ops:
  1.3 3.0 collective-permute-start.3
  4.3 2.6 collective-permute-start.4
  8.6 1.8 shard_map.103
  11.0 4.2 %collective-permute-done.1.rest_2_ = s32[2]{0:T(128)S(1)} collective-permute-done((s32[2]{0:T(128)}, s32[2]{0:T(128)S(1)}, u32[]{:S(2)}, u32[]{:S(2)}) %collective-permute-start.1) | collective-permute-done | bytes 40 | tf_op jit(solution)/shard_map/ppermute | solution.py:303
  16.4 4.4 %collective-permute-done.2.rest_3_ = s32[2]{0:T(128)S(1)} collective-permute-done((s32[2]{0:T(128)}, s32[2]{0:T(128)S(1)}, u32[]{:S(2)}, u32[]{:S(2)}) %collective-permute-start.2) | collective-permute-done | bytes 40 | tf_op jit(solution)/shard_map/ppermute | solution.py:303
  24.9 5.1 %collective-permute-done.5.rest_7_ = bf16[2,128,128]{2,1,0:T(8,128)(2,1)S(1)} collective-permute-done((bf16[2,128,128]{2,1,0:T(8,128)(2,1)}, bf16[2,128,128]{2,1,0:T(8,128)(2,1)S(1)}, u32[]{:S(2)}, u32[]{:S(2)}) %collective-permute-start.5) | collective-permute-done | bytes 65568 | tf_op jit(solution)/shard_map/ppermute | solution.py:303
  33.6 4.0 %collective-permute-done.9.rest_3_ = bf16[256,256]{1,0:T(8,128)(2,1)S(1)} collective-permute-done((bf16[256,256]{1,0:T(8,128)(2,1)}, bf16[256,256]{1,0:T(8,128)(2,1)S(1)}, u32[]{:S(2)}, u32[]{:S(2)}) %collective-permute-start.9) | collective-permute-done | bytes 131104 | tf_op jit(solution)/shard_map/ppermute | solution.py:296
  40.9 2.3 collective-permute-done.23.rest_2_
  45.3 5.2 %shard_map.104 = (bf16[2,1024,128]{2,1,0:T(8,128)(2,1)}, bf16[2,1024,128]{2,1,0:T(8,128)(2,1)}, bf16[1024,256]{1,0:T(8,128)(2,1)}) custom-call(s32[4]{0:T(128)} %pad_add_fusion.meta, bf16[1024,1024]{1,0:T(8,128)(2,1)} %bitcast.14, bf16[1024,1024]{1,0:T(8,128)(2,1)} %copy-done.1, bf16[256,256]{1,0:T(8,128)(2,1)} %get-tuple-element.78.rest_0_, ...), custom_call_target="tpu_custom_call" | custom-call | flops 1073741824 | bytes 6291472 | tf_op jit(solution)/shard_map/pallas_call | solution.py:26
  53.3 5.3 %shard_map.110 = (bf16[2,1024,128]{2,1,0:T(8,128)(2,1)}, bf16[2,1024,128]{2,1,0:T(8,128)(2,1)}, bf16[1024,256]{1,0:T(8,128)(2,1)}) custom-call(s32[4]{0:T(128)} %pad_add_fusion.meta, bf16[1024,1024]{1,0:T(8,128)(2,1)} %bitcast.15, bf16[1024,1024]{1,0:T(8,128)(2,1)} %copy-done.1, bf16[256,256]{1,0:T(8,128)(2,1)} %get-tuple-element.91.rest_0_, ...), custom_call_target="tpu_custom_call" | custom-call | flops 1073741824 | bytes 6291472 | tf_op jit(solution)/shard_map/pallas_call | solution.py:26
  58.6 5.3 %collective-permute-start.25 = (bf16[2,1024,128]{2,1,0:T(8,128)(2,1)}, bf16[2,1024,128]{2,1,0:T(8,128)(2,1)S(1)}, u32[]{:S(2)}, u32[]{:S(2)}) collective-permute-start(bf16[2,1024,128]{2,1,0:T(8,128)(2,1)} %get-tuple-element.92.rest_0_), channel_id=1, source_target_pairs={{0,8},{4,12},{8,16},{12,20},{16,24},{20,28},{1,9},{5,13},{9,17},{1... | collective-permute-start | bytes 1572872 | tf_op jit(solution)/shard_map/ppermute | solution.py:307
  63.9 1.9 collective-permute-start.29
  67.3 8.0 %collective-permute-done.18.rest_1_ = bf16[2,1024,128]{2,1,0:T(8,128)(2,1)S(1)} collective-permute-done((bf16[2,1024,128]{2,1,0:T(8,128)(2,1)}, bf16[2,1024,128]{2,1,0:T(8,128)(2,1)S(1)}, u32[]{:S(2)}, u32[]{:S(2)}) %collective-permute-start.18) | collective-permute-done | bytes 524320 | tf_op jit(solution)/shard_map/ppermute | solution.py:307
  76.7 4.1 %collective-permute-done.25.rest_1_ = bf16[2,1024,128]{2,1,0:T(8,128)(2,1)S(1)} collective-permute-done((bf16[2,1024,128]{2,1,0:T(8,128)(2,1)}, bf16[2,1024,128]{2,1,0:T(8,128)(2,1)S(1)}, u32[]{:S(2)}, u32[]{:S(2)}) %collective-permute-start.25) | collective-permute-done | bytes 524320 | tf_op jit(solution)/shard_map/ppermute | solution.py:307
  81.5 4.9 %collective-permute-done.29.rest_1_ = bf16[2,1024,128]{2,1,0:T(8,128)(2,1)S(1)} collective-permute-done((bf16[2,1024,128]{2,1,0:T(8,128)(2,1)}, bf16[2,1024,128]{2,1,0:T(8,128)(2,1)S(1)}, u32[]{:S(2)}, u32[]{:S(2)}) %collective-permute-start.29) | collective-permute-done | bytes 524320 | tf_op jit(solution)/shard_map/ppermute | solution.py:307
  87.2 2.6 shard_map.102
  89.8 6.9 %shard_map.105 = (bf16[2,1024,128]{2,1,0:T(8,128)(2,1)}, bf16[2,1024,128]{2,1,0:T(8,128)(2,1)}, bf16[2,1024,128]{2,1,0:T(8,128)(2,1)}, bf16[2,1024,128]{2,1,0:T(8,128)(2,1)}) custom-call(s32[4]{0:T(128)} %pad_add_fusion.meta, bf16[1024,1024]{1,0:T(8,128)(2,1)} %bitcast.19, bf16[1024,1024]{1,0:T(8,128)(2,1)} %collective-permute-done.12.partner.rest_5_, ...), custom_call_target="tpu_custom_call" | custom-call | flops 2147483648 | bytes 7340048 | tf_op jit(solution)/shard_map/pallas_call | solution.py:26
  96.7 6.6 %shard_map.106 = (bf16[2,1024,128]{2,1,0:T(8,128)(2,1)}, f32[2,1024,128]{2,1,0:T(8,128)}, bf16[2,1024,128]{2,1,0:T(8,128)(2,1)}, bf16[2,128,128]{2,1,0:T(8,128)(2,1)}) custom-call(s32[4]{0:T(128)} %pad_add_fusion.meta, s32[8]{0:T(128)} %get-tuple-element.77.amounts, bf16[2,1024,128]{2,1,0:T(8,128)(2,1)} %get-tuple-element.79.rest_0_, ...), custom_call_target="tpu_custom_call" | custom-call | flops 805306368 | bytes 4390960 | tf_op jit(solution)/shard_map/pallas_call | solution.py:26
  103.3 6.5 %shard_map.108 = (bf16[2,1024,128]{2,1,0:T(8,128)(2,1)}, f32[2,1024,128]{2,1,0:T(8,128)}, bf16[2,1024,128]{2,1,0:T(8,128)(2,1)}, bf16[2,128,128]{2,1,0:T(8,128)(2,1)}) custom-call(s32[4]{0:T(128)} %pad_add_fusion.meta, s32[8]{0:T(128)} %get-tuple-element.77.amounts, bf16[2,1024,128]{2,1,0:T(8,128)(2,1)} %get-tuple-element.85.rest_0_, ...), custom_call_target="tpu_custom_call" | custom-call | flops 805306368 | bytes 4390960 | tf_op jit(solution)/shard_map/pallas_call | solution.py:26
  110.7 6.7 %shard_map.111 = (bf16[2,1024,128]{2,1,0:T(8,128)(2,1)}, f32[2,1024,128]{2,1,0:T(8,128)}, bf16[2,1024,128]{2,1,0:T(8,128)(2,1)}, bf16[2,128,128]{2,1,0:T(8,128)(2,1)}) custom-call(s32[4]{0:T(128)} %pad_add_fusion.meta, s32[8]{0:T(128)} %get-tuple-element.77.amounts, bf16[2,1024,128]{2,1,0:T(8,128)(2,1)} %get-tuple-element.92.rest_0_, ...), custom_call_target="tpu_custom_call" | custom-call | flops 805306368 | bytes 4390960 | tf_op jit(solution)/shard_map/pallas_call | solution.py:26
  118.1 6.6 %shard_map.113 = (bf16[2,1024,128]{2,1,0:T(8,128)(2,1)}, f32[2,1024,128]{2,1,0:T(8,128)}, bf16[2,1024,128]{2,1,0:T(8,128)(2,1)}, bf16[2,128,128]{2,1,0:T(8,128)(2,1)}) custom-call(s32[4]{0:T(128)} %pad_add_fusion.meta, s32[8]{0:T(128)} %get-tuple-element.77.amounts, bf16[2,1024,128]{2,1,0:T(8,128)(2,1)} %get-tuple-element.98.rest_0_, ...), custom_call_target="tpu_custom_call" | custom-call | flops 805306368 | bytes 4390960 | tf_op jit(solution)/shard_map/pallas_call | solution.py:26
  124.8 7.3 %shard_map.117 = (f32[128,1024]{1,0:T(8,128)}, bf16[128,1024]{1,0:T(8,128)(2,1)}, bf16[128,1024]{1,0:T(8,128)(2,1)}, bf16[128,1024]{1,0:T(8,128)(2,1)}) custom-call(s32[4]{0:T(128)} %pad_add_fusion.meta, bf16[2,1024,128]{2,1,0:T(8,128)(2,1)} %get-tuple-element.112.rest_0_, bf16[2,1024,128]{2,1,0:T(8,128)(2,1)} %get-tuple-element.113.rest_1_, ...), custom_call_target="tpu_custom_call" | custom-call | flops 2147483648 | bytes 7602192 | tf_op jit(solution)/shard_map/pallas_call | solution.py:26
  138.0 3.3 collective-permute-done.37.rest_1_
  141.7 6.1 %collective-permute-done.38.rest_2_ = bf16[128,1024]{1,0:T(8,128)(2,1)S(1)} collective-permute-done((bf16[128,1024]{1,0:T(8,128)(2,1)}, bf16[128,1024]{1,0:T(8,128)(2,1)S(1)}, u32[]{:S(2)}, u32[]{:S(2)}) %collective-permute-start.38) | collective-permute-done | bytes 262176 | tf_op jit(solution)/shard_map/ppermute | solution.py:296
  149.2 14.9 %collective-permute-done.16.rest_1_ = bf16[2,1024,128]{2,1,0:T(8,128)(2,1)} collective-permute-done((bf16[2,1024,128]{2,1,0:T(8,128)(2,1)S(1)}, bf16[2,1024,128]{2,1,0:T(8,128)(2,1)}, u32[]{:S(2)}, u32[]{:S(2)}) %collective-permute-start.16) | collective-permute-done | bytes 524320 | tf_op jit(solution)/shard_map/ppermute | solution.py:310
  165.4 9.9 %collective-permute-done.20.rest_1_ = bf16[2,1024,128]{2,1,0:T(8,128)(2,1)} collective-permute-done((bf16[2,1024,128]{2,1,0:T(8,128)(2,1)S(1)}, bf16[2,1024,128]{2,1,0:T(8,128)(2,1)}, u32[]{:S(2)}, u32[]{:S(2)}) %collective-permute-start.20) | collective-permute-done | bytes 524320 | tf_op jit(solution)/shard_map/ppermute | solution.py:310
  176.7 9.8 %collective-permute-done.27.rest_1_ = bf16[2,1024,128]{2,1,0:T(8,128)(2,1)S(1)} collective-permute-done((bf16[2,1024,128]{2,1,0:T(8,128)(2,1)S(1)}, bf16[2,1024,128]{2,1,0:T(8,128)(2,1)S(1)}, u32[]{:S(2)}, u32[]{:S(2)}) %collective-permute-start.27) | collective-permute-done | bytes 524320 | tf_op jit(solution)/shard_map/ppermute | solution.py:310
  187.8 9.9 %collective-permute-done.31.rest_1_ = bf16[2,1024,128]{2,1,0:T(8,128)(2,1)S(1)} collective-permute-done((bf16[2,1024,128]{2,1,0:T(8,128)(2,1)S(1)}, bf16[2,1024,128]{2,1,0:T(8,128)(2,1)S(1)}, u32[]{:S(2)}, u32[]{:S(2)}) %collective-permute-start.31) | collective-permute-done | bytes 524320 | tf_op jit(solution)/shard_map/ppermute | solution.py:310
  199.2 2.2 shard_map.118
  201.4 3.4 collective-permute-start.40
  204.9 26.7 %collective-permute-done.40.rest_1_ = bf16[32,1024]{1,0:T(8,128)(2,1)S(1)} collective-permute-done((bf16[32,1024]{1,0:T(8,128)(2,1)}, bf16[32,1024]{1,0:T(8,128)(2,1)S(1)}, u32[]{:S(2)}, u32[]{:S(2)}) %collective-permute-start.40) | collective-permute-done | bytes 65568 | tf_op jit(solution)/shard_map/ppermute | solution.py:303
  231.6 5.4 %collective-permute-done.41.rest_2_ = bf16[32,1024]{1,0:T(8,128)(2,1)S(1)} collective-permute-done((bf16[32,1024]{1,0:T(8,128)(2,1)}, bf16[32,1024]{1,0:T(8,128)(2,1)S(1)}, u32[]{:S(2)}, u32[]{:S(2)}) %collective-permute-start.41) | collective-permute-done | bytes 65568 | tf_op jit(solution)/shard_map/ppermute | solution.py:303
  237.0 6.6 %collective-permute-done.42.rest_3_ = bf16[32,1024]{1,0:T(8,128)(2,1)S(1)} collective-permute-done((bf16[32,1024]{1,0:T(8,128)(2,1)}, bf16[32,1024]{1,0:T(8,128)(2,1)S(1)}, u32[]{:S(2)}, u32[]{:S(2)}) %collective-permute-start.42) | collective-permute-done | bytes 65568 | tf_op jit(solution)/shard_map/ppermute | solution.py:303
  244.2 1.6 shard_map.119.rest_0_
  245.8 1.7 shard_map.128
  247.5 2.0 collective-permute-start.67
  249.6 3.0 shard_map.107
  253.3 2.9 shard_map.109
  256.2 1.7 collective-permute-start.45
  258.0 5.6 %shard_map.115 = (f32[256,256]{1,0:T(8,128)}, bf16[256,256]{1,0:T(8,128)(2,1)}, bf16[256,256]{1,0:T(8,128)(2,1)}, bf16[256,256]{1,0:T(8,128)(2,1)}, bf16[1024,256]{1,0:T(8,128)(2,1)}) custom-call(s32[4]{0:T(128)} %pad_add_fusion.meta, bf16[1024,128]{1,0:T(8,128)(2,1)} %get-tuple-element.84.rest_0_, bf16[1024,128]{1,0:T(8,128)(2,1)} %get-tuple-element.104.rest_1_, ...), custom_call_target="tpu_custom_call" | custom-call | flops 1073741824 | bytes 6422544 | tf_op jit(solution)/shard_map/pallas_call | solution.py:26
  264.9 1.7 shard_map.120.rest_0_
  266.6 3.0 collective-permute-start.69
  269.6 3.0 shard_map.112
  273.4 3.0 shard_map.114
  276.4 1.8 collective-permute-start.48
  278.2 5.6 %shard_map.116 = (f32[256,256]{1,0:T(8,128)}, bf16[256,256]{1,0:T(8,128)(2,1)}, bf16[256,256]{1,0:T(8,128)(2,1)}, bf16[256,256]{1,0:T(8,128)(2,1)}, bf16[1024,256]{1,0:T(8,128)(2,1)}) custom-call(s32[4]{0:T(128)} %pad_add_fusion.meta, bf16[1024,128]{1,0:T(8,128)(2,1)} %get-tuple-element.97.rest_0_.rest_2_, bf16[1024,128]{1,0:T(8,128)(2,1)} %get-tuple-element.107.rest_1_, ...), custom_call_target="tpu_custom_call" | custom-call | flops 1073741824 | bytes 6422544 | tf_op jit(solution)/shard_map/pallas_call | solution.py:26
  285.7 1.7 collective-permute-start.58
  292.8 1.7 collective-permute-start.71
  295.7 1.9 shard_map.121
  298.3 1.9 shard_map.124
  301.1 2.9 collective-permute-start.52
  309.3 1.9 collective-permute-start.62
  312.7 2.6 collective-permute-done.62.rest_3_
  315.4 4.1 %collective-permute-done.53.rest_1_ = bf16[64,256]{1,0:T(8,128)(2,1)} collective-permute-done((bf16[64,256]{1,0:T(8,128)(2,1)}, bf16[64,256]{1,0:T(8,128)(2,1)}, u32[]{:S(2)}, u32[]{:S(2)}) %collective-permute-start.53) | collective-permute-done | bytes 32800 | tf_op jit(solution)/shard_map/ppermute | solution.py:303
  320.0 5.0 %collective-permute-done.54.rest_2_ = bf16[64,256]{1,0:T(8,128)(2,1)} collective-permute-done((bf16[64,256]{1,0:T(8,128)(2,1)}, bf16[64,256]{1,0:T(8,128)(2,1)}, u32[]{:S(2)}, u32[]{:S(2)}) %collective-permute-start.54) | collective-permute-done | bytes 32800 | tf_op jit(solution)/shard_map/ppermute | solution.py:303
  324.9 1.9 collective-permute-start.55
  328.3 2.6 collective-permute-done.55.rest_3_
  331.0 4.2 %collective-permute-done.63.rest_1_ = bf16[64,256]{1,0:T(8,128)(2,1)} collective-permute-done((bf16[64,256]{1,0:T(8,128)(2,1)}, bf16[64,256]{1,0:T(8,128)(2,1)}, u32[]{:S(2)}, u32[]{:S(2)}) %collective-permute-start.63) | collective-permute-done | bytes 32800 | tf_op jit(solution)/shard_map/ppermute | solution.py:303
  335.7 4.7 %collective-permute-done.64.rest_2_ = bf16[64,256]{1,0:T(8,128)(2,1)} collective-permute-done((bf16[64,256]{1,0:T(8,128)(2,1)}, bf16[64,256]{1,0:T(8,128)(2,1)}, u32[]{:S(2)}, u32[]{:S(2)}) %collective-permute-start.64) | collective-permute-done | bytes 32800 | tf_op jit(solution)/shard_map/ppermute | solution.py:303
  340.3 1.9 collective-permute-start.65
  343.7 2.6 collective-permute-done.65.rest_3_
  348.3 1.6 shard_map.130
  350.0 3.0 shard_map.127
  354.9 6.5 %signal.1 = bf16[1024,1024]{1,0:T(8,128)(2,1)} custom-call(bf16[1024,1024]{1,0:T(8,128)(2,1)} %bitcast.21, bf16[1024,128]{1,0:T(8,128)(2,1)} %get-tuple-element.84.rest_0_, bf16[1024,128]{1,0:T(8,128)(2,1)} %get-tuple-element.90.rest_2_.rest_1_, bf16[1024,128]{1,0:T(8,128)(2,1)} %get-tuple-element.97.rest_0_.rest_2_, ...), custom_call_target="tpu_custom_call" | custom-call | flops 2147483648 | bytes 8388608 | tf_op jit(solution)/shard_map/signal/pallas_call | solution.py:472
  (250 shorter events, 66.2 us)
Async XLA Ops:
  0.6 43.2 %collective-permute-start.6 = (bf16[1024,1024]{1,0:T(8,128)(2,1)}, bf16[1024,1024]{1,0:T(8,128)(2,1)S(1)}, u32[]{:S(2)}, u32[]{:S(2)}) collective-permute-start(bf16[1024,1024]{1,0:T(8,128)(2,1)} %bitcast.13), channel_id=1, source_target_pairs={{0,4},{4,0},{8,12},{12,8},{16,20},{20,16},{24,28},{28,24},{1,5},{5... | collective-permute-start | bytes 6291464 | tf_op jit(solution)/shard_map/ppermute | solution.py:290
  1.2 88.5 %collective-permute-start.12 = (bf16[1024,1024]{1,0:T(8,128)(2,1)}, bf16[1024,1024]{1,0:T(8,128)(2,1)}, u32[]{:S(2)}, u32[]{:S(2)}) collective-permute-start(bf16[1024,1024]{1,0:T(8,128)(2,1)} %bitcast.18), channel_id=1, source_target_pairs={{0,4},{4,0},{8,12},{12,8},{16,20},{20,16},{24,28},{28,24},{1,5},{5... | collective-permute-start | bytes 6291464 | tf_op jit(solution)/shard_map/ppermute | solution.py:290
  1.3 20.9 %collective-permute-start.3 = (bf16[2,128,128]{2,1,0:T(8,128)(2,1)}, bf16[2,128,128]{2,1,0:T(8,128)(2,1)S(1)}, u32[]{:S(2)}, u32[]{:S(2)}) collective-permute-start(bf16[2,128,128]{2,1,0:T(8,128)(2,1)} %rest_4_.1), channel_id=1, source_target_pairs={{0,8},{4,12},{8,0},{12,4},{16,24},{20,28},{24,16},{28,20},{1,9},{5... | collective-permute-start | bytes 196616 | tf_op jit(solution)/shard_map/ppermute | solution.py:303
  4.3 19.5 %collective-permute-start.4 = (bf16[2,128,128]{2,1,0:T(8,128)(2,1)}, bf16[2,128,128]{2,1,0:T(8,128)(2,1)S(1)}, u32[]{:S(2)}, u32[]{:S(2)}) collective-permute-start(bf16[2,128,128]{2,1,0:T(8,128)(2,1)} %rest_4_.1), channel_id=1, source_target_pairs={{0,16},{4,20},{8,24},{12,28},{16,0},{20,4},{24,8},{28,12},{1,17},{... | collective-permute-start | bytes 196616 | tf_op jit(solution)/shard_map/ppermute | solution.py:303
  15.2 5.5 %collective-permute-start.2 = (s32[2]{0:T(128)}, s32[2]{0:T(128)S(1)}, u32[]{:S(2)}, u32[]{:S(2)}) collective-permute-start(s32[2]{0:T(128)} %rest_0_.1), channel_id=1, source_target_pairs={{0,24},{4,28},{8,16},{12,20},{16,8},{20,12},{24,0},{28,4},{1,25},{... | collective-permute-start | bytes 32 | tf_op jit(solution)/shard_map/ppermute | solution.py:303
  20.7 9.8 %collective-permute-start.7 = (bf16[256,256]{1,0:T(8,128)(2,1)}, bf16[256,256]{1,0:T(8,128)(2,1)S(1)}, u32[]{:S(2)}, u32[]{:S(2)}) collective-permute-start(bf16[256,256]{1,0:T(8,128)(2,1)} %get-tuple-element.78.rest_0_), channel_id=1, source_target_pairs={{0,1},{1,0},{2,3},{3,2},{4,5},{5,4},{6,7},{7,6},{8,9},{9,8},{10,11... | collective-permute-start | bytes 393224 | tf_op jit(solution)/shard_map/ppermute | solution.py:296
  22.2 9.8 %collective-permute-start.8 = (bf16[256,256]{1,0:T(8,128)(2,1)}, bf16[256,256]{1,0:T(8,128)(2,1)S(1)}, u32[]{:S(2)}, u32[]{:S(2)}) collective-permute-start(bf16[256,256]{1,0:T(8,128)(2,1)} %get-tuple-element.78.rest_0_), channel_id=1, source_target_pairs={{0,2},{1,3},{2,0},{3,1},{4,6},{5,7},{6,4},{7,5},{8,10},{9,11},{10,... | collective-permute-start | bytes 393224 | tf_op jit(solution)/shard_map/ppermute | solution.py:296
  23.8 6.3 %collective-permute-start.5 = (bf16[2,128,128]{2,1,0:T(8,128)(2,1)}, bf16[2,128,128]{2,1,0:T(8,128)(2,1)S(1)}, u32[]{:S(2)}, u32[]{:S(2)}) collective-permute-start(bf16[2,128,128]{2,1,0:T(8,128)(2,1)} %rest_4_.1), channel_id=1, source_target_pairs={{0,24},{4,28},{8,16},{12,20},{16,8},{20,12},{24,0},{28,4},{1,25},{... | collective-permute-start | bytes 196616 | tf_op jit(solution)/shard_map/ppermute | solution.py:303
  30.0 7.6 %collective-permute-start.9 = (bf16[256,256]{1,0:T(8,128)(2,1)}, bf16[256,256]{1,0:T(8,128)(2,1)S(1)}, u32[]{:S(2)}, u32[]{:S(2)}) collective-permute-start(bf16[256,256]{1,0:T(8,128)(2,1)} %get-tuple-element.78.rest_0_), channel_id=1, source_target_pairs={{0,3},{1,2},{2,1},{3,0},{4,7},{5,6},{6,5},{7,4},{8,11},{9,10},{10,... | collective-permute-start | bytes 393224 | tf_op jit(solution)/shard_map/ppermute | solution.py:296
  30.5 8.8 %collective-permute-start.22 = (bf16[256,256]{1,0:T(8,128)(2,1)}, bf16[256,256]{1,0:T(8,128)(2,1)S(1)}, u32[]{:S(2)}, u32[]{:S(2)}) collective-permute-start(bf16[256,256]{1,0:T(8,128)(2,1)} %get-tuple-element.91.rest_0_), channel_id=1, source_target_pairs={{0,1},{1,0},{2,3},{3,2},{4,5},{5,4},{6,7},{7,6},{8,9},{9,8},{10,11... | collective-permute-start | bytes 393224 | tf_op jit(solution)/shard_map/ppermute | solution.py:296
  32.0 11.2 %collective-permute-start.23 = (bf16[256,256]{1,0:T(8,128)(2,1)}, bf16[256,256]{1,0:T(8,128)(2,1)S(1)}, u32[]{:S(2)}, u32[]{:S(2)}) collective-permute-start(bf16[256,256]{1,0:T(8,128)(2,1)} %get-tuple-element.91.rest_0_), channel_id=1, source_target_pairs={{0,2},{1,3},{2,0},{3,1},{4,6},{5,7},{6,4},{7,5},{8,10},{9,11},{10,... | collective-permute-start | bytes 393224 | tf_op jit(solution)/shard_map/ppermute | solution.py:296
  37.6 14.3 %collective-permute-start.13 = (bf16[128,1024]{1,0:T(8,128)(2,1)S(1)}, bf16[128,1024]{1,0:T(8,128)(2,1)}, u32[]{:S(2)}, u32[]{:S(2)}) collective-permute-start(bf16[128,1024]{1,0:T(8,128)(2,1)S(1)} %dynamic-slice_bitcast_fusion.rest_0_), channel_id=1, source_target_pairs={{0,1},{1,0},{2,3},{3,2},{4,5},{5,4},{6,7},{7,6},{8,9},{9,8},{10,11... | collective-permute-start | bytes 786440 | tf_op jit(solution)/shard_map/ppermute | solution.py:296
  39.4 11.2 %collective-permute-start.24 = (bf16[256,256]{1,0:T(8,128)(2,1)}, bf16[256,256]{1,0:T(8,128)(2,1)S(1)}, u32[]{:S(2)}, u32[]{:S(2)}) collective-permute-start(bf16[256,256]{1,0:T(8,128)(2,1)} %get-tuple-element.91.rest_0_), channel_id=1, source_target_pairs={{0,3},{1,2},{2,1},{3,0},{4,7},{5,6},{6,5},{7,4},{8,11},{9,10},{10,... | collective-permute-start | bytes 393224 | tf_op jit(solution)/shard_map/ppermute | solution.py:296
  43.2 15.3 %collective-permute-start.14 = (bf16[128,1024]{1,0:T(8,128)(2,1)S(1)}, bf16[128,1024]{1,0:T(8,128)(2,1)}, u32[]{:S(2)}, u32[]{:S(2)}) collective-permute-start(bf16[128,1024]{1,0:T(8,128)(2,1)S(1)} %dynamic-slice_bitcast_fusion.rest_0_), channel_id=1, source_target_pairs={{0,2},{1,3},{2,0},{3,1},{4,6},{5,7},{6,4},{7,5},{8,10},{9,11},{10,... | collective-permute-start | bytes 786440 | tf_op jit(solution)/shard_map/ppermute | solution.py:296
  43.9 20.0 %collective-permute-start.15 = (bf16[128,1024]{1,0:T(8,128)(2,1)S(1)}, bf16[128,1024]{1,0:T(8,128)(2,1)}, u32[]{:S(2)}, u32[]{:S(2)}) collective-permute-start(bf16[128,1024]{1,0:T(8,128)(2,1)S(1)} %dynamic-slice_bitcast_fusion.rest_0_), channel_id=1, source_target_pairs={{0,3},{1,2},{2,1},{3,0},{4,7},{5,6},{6,5},{7,4},{8,11},{9,10},{10,... | collective-permute-start | bytes 786440 | tf_op jit(solution)/shard_map/ppermute | solution.py:296
  50.6 15.2 %collective-permute-start.10 = (bf16[2,1024,128]{2,1,0:T(8,128)(2,1)}, bf16[2,1024,128]{2,1,0:T(8,128)(2,1)S(1)}, u32[]{:S(2)}, u32[]{:S(2)}) collective-permute-start(bf16[2,1024,128]{2,1,0:T(8,128)(2,1)} %get-tuple-element.79.rest_0_), channel_id=1, source_target_pairs={{0,8},{4,12},{8,16},{12,20},{16,24},{20,28},{1,9},{5,13},{9,17},{1... | collective-permute-start | bytes 1572872 | tf_op jit(solution)/shard_map/ppermute | solution.py:307
  51.9 23.3 %collective-permute-start.18 = (bf16[2,1024,128]{2,1,0:T(8,128)(2,1)}, bf16[2,1024,128]{2,1,0:T(8,128)(2,1)S(1)}, u32[]{:S(2)}, u32[]{:S(2)}) collective-permute-start(bf16[2,1024,128]{2,1,0:T(8,128)(2,1)} %get-tuple-element.85.rest_0_), channel_id=1, source_target_pairs={{0,8},{4,12},{8,16},{12,20},{16,24},{20,28},{1,9},{5,13},{9,17},{1... | collective-permute-start | bytes 1572872 | tf_op jit(solution)/shard_map/ppermute | solution.py:307
  58.6 22.3 %collective-permute-start.25 = (bf16[2,1024,128]{2,1,0:T(8,128)(2,1)}, bf16[2,1024,128]{2,1,0:T(8,128)(2,1)S(1)}, u32[]{:S(2)}, u32[]{:S(2)}) collective-permute-start(bf16[2,1024,128]{2,1,0:T(8,128)(2,1)} %get-tuple-element.92.rest_0_), channel_id=1, source_target_pairs={{0,8},{4,12},{8,16},{12,20},{16,24},{20,28},{1,9},{5,13},{9,17},{1... | collective-permute-start | bytes 1572872 | tf_op jit(solution)/shard_map/ppermute | solution.py:307
  63.9 22.6 %collective-permute-start.29 = (bf16[2,1024,128]{2,1,0:T(8,128)(2,1)}, bf16[2,1024,128]{2,1,0:T(8,128)(2,1)S(1)}, u32[]{:S(2)}, u32[]{:S(2)}) collective-permute-start(bf16[2,1024,128]{2,1,0:T(8,128)(2,1)} %get-tuple-element.98.rest_0_), channel_id=1, source_target_pairs={{0,8},{4,12},{8,16},{12,20},{16,24},{20,28},{1,9},{5,13},{9,17},{1... | collective-permute-start | bytes 1572872 | tf_op jit(solution)/shard_map/ppermute | solution.py:307
  65.8 30.9 %collective-permute-start.11 = (bf16[2,1024,128]{2,1,0:T(8,128)(2,1)S(1)}, bf16[2,1024,128]{2,1,0:T(8,128)(2,1)}, u32[]{:S(2)}, u32[]{:S(2)}) collective-permute-start(bf16[2,1024,128]{2,1,0:T(8,128)(2,1)S(1)} %collective-permute-done.10.rest_1_), channel_id=1, source_target_pairs={{8,16},{12,20},{16,24},{20,28},{9,17},{13,21},{17,25},{21,29},{10,... | collective-permute-start | bytes 1572872 | tf_op jit(solution)/shard_map/ppermute | solution.py:307
  75.2 28.1 %collective-permute-start.19 = (bf16[2,1024,128]{2,1,0:T(8,128)(2,1)S(1)}, bf16[2,1024,128]{2,1,0:T(8,128)(2,1)}, u32[]{:S(2)}, u32[]{:S(2)}) collective-permute-start(bf16[2,1024,128]{2,1,0:T(8,128)(2,1)S(1)} %collective-permute-done.18.rest_1_), channel_id=1, source_target_pairs={{8,16},{12,20},{16,24},{20,28},{9,17},{13,21},{17,25},{21,29},{10,... | collective-permute-start | bytes 1572872 | tf_op jit(solution)/shard_map/ppermute | solution.py:307
  80.8 29.0 %collective-permute-start.26 = (bf16[2,1024,128]{2,1,0:T(8,128)(2,1)S(1)}, bf16[2,1024,128]{2,1,0:T(8,128)(2,1)S(1)}, u32[]{:S(2)}, u32[]{:S(2)}) collective-permute-start(bf16[2,1024,128]{2,1,0:T(8,128)(2,1)S(1)} %collective-permute-done.25.rest_1_), channel_id=1, source_target_pairs={{8,16},{12,20},{16,24},{20,28},{9,17},{13,21},{17,25},{21,29},{10,... | collective-permute-start | bytes 1572872 | tf_op jit(solution)/shard_map/ppermute | solution.py:307
  86.5 30.9 %collective-permute-start.30 = (bf16[2,1024,128]{2,1,0:T(8,128)(2,1)S(1)}, bf16[2,1024,128]{2,1,0:T(8,128)(2,1)S(1)}, u32[]{:S(2)}, u32[]{:S(2)}) collective-permute-start(bf16[2,1024,128]{2,1,0:T(8,128)(2,1)S(1)} %collective-permute-done.29.rest_1_), channel_id=1, source_target_pairs={{8,16},{12,20},{16,24},{20,28},{9,17},{13,21},{17,25},{21,29},{10,... | collective-permute-start | bytes 1572872 | tf_op jit(solution)/shard_map/ppermute | solution.py:307
  132.1 9.2 %collective-permute-start.37 = (bf16[128,1024]{1,0:T(8,128)(2,1)}, bf16[128,1024]{1,0:T(8,128)(2,1)S(1)}, u32[]{:S(2)}, u32[]{:S(2)}) collective-permute-start(bf16[128,1024]{1,0:T(8,128)(2,1)} %get-tuple-element.117), channel_id=1, source_target_pairs={{0,1},{1,0},{2,3},{3,2},{4,5},{5,4},{6,7},{7,6},{8,9},{9,8},{10,11... | collective-permute-start | bytes 786440 | tf_op jit(solution)/shard_map/ppermute | solution.py:296
  132.8 31.4 %collective-permute-start.16 = (bf16[2,1024,128]{2,1,0:T(8,128)(2,1)S(1)}, bf16[2,1024,128]{2,1,0:T(8,128)(2,1)}, u32[]{:S(2)}, u32[]{:S(2)}) collective-permute-start(bf16[2,1024,128]{2,1,0:T(8,128)(2,1)S(1)} %copy-done.9), channel_id=1, source_target_pairs={{8,0},{12,4},{16,8},{20,12},{24,16},{28,20},{9,1},{13,5},{17,9},{2... | collective-permute-start | bytes 1572872 | tf_op jit(solution)/shard_map/ppermute | solution.py:310
  134.1 41.3 %collective-permute-start.20 = (bf16[2,1024,128]{2,1,0:T(8,128)(2,1)S(1)}, bf16[2,1024,128]{2,1,0:T(8,128)(2,1)}, u32[]{:S(2)}, u32[]{:S(2)}) collective-permute-start(bf16[2,1024,128]{2,1,0:T(8,128)(2,1)S(1)} %copy-done.8), channel_id=1, source_target_pairs={{8,0},{12,4},{16,8},{20,12},{24,16},{28,20},{9,1},{13,5},{17,9},{2... | collective-permute-start | bytes 1572872 | tf_op jit(solution)/shard_map/ppermute | solution.py:310
  135.4 51.2 %collective-permute-start.27 = (bf16[2,1024,128]{2,1,0:T(8,128)(2,1)S(1)}, bf16[2,1024,128]{2,1,0:T(8,128)(2,1)S(1)}, u32[]{:S(2)}, u32[]{:S(2)}) collective-permute-start(bf16[2,1024,128]{2,1,0:T(8,128)(2,1)S(1)} %copy-done.6), channel_id=1, source_target_pairs={{8,0},{12,4},{16,8},{20,12},{24,16},{28,20},{9,1},{13,5},{17,9},{2... | collective-permute-start | bytes 1572872 | tf_op jit(solution)/shard_map/ppermute | solution.py:310
  136.7 61.1 %collective-permute-start.31 = (bf16[2,1024,128]{2,1,0:T(8,128)(2,1)S(1)}, bf16[2,1024,128]{2,1,0:T(8,128)(2,1)S(1)}, u32[]{:S(2)}, u32[]{:S(2)}) collective-permute-start(bf16[2,1024,128]{2,1,0:T(8,128)(2,1)S(1)} %copy-done.5), channel_id=1, source_target_pairs={{8,0},{12,4},{16,8},{20,12},{24,16},{28,20},{9,1},{13,5},{17,9},{2... | collective-permute-start | bytes 1572872 | tf_op jit(solution)/shard_map/ppermute | solution.py:310
  141.3 6.6 %collective-permute-start.38 = (bf16[128,1024]{1,0:T(8,128)(2,1)}, bf16[128,1024]{1,0:T(8,128)(2,1)S(1)}, u32[]{:S(2)}, u32[]{:S(2)}) collective-permute-start(bf16[128,1024]{1,0:T(8,128)(2,1)} %get-tuple-element.118), channel_id=1, source_target_pairs={{0,2},{1,3},{2,0},{3,1},{4,6},{5,7},{6,4},{7,5},{8,10},{9,11},{10,... | collective-permute-start | bytes 786440 | tf_op jit(solution)/shard_map/ppermute | solution.py:296
  147.9 51.3 %collective-permute-start.39 = (bf16[128,1024]{1,0:T(8,128)(2,1)}, bf16[128,1024]{1,0:T(8,128)(2,1)}, u32[]{:S(2)}, u32[]{:S(2)}) collective-permute-start(bf16[128,1024]{1,0:T(8,128)(2,1)} %get-tuple-element.119), channel_id=1, source_target_pairs={{0,3},{1,2},{2,1},{3,0},{4,7},{5,6},{6,5},{7,4},{8,11},{9,10},{10,... | collective-permute-start | bytes 786440 | tf_op jit(solution)/shard_map/ppermute | solution.py:296
  164.1 83.4 %collective-permute-start.17 = (bf16[2,1024,128]{2,1,0:T(8,128)(2,1)}, bf16[2,1024,128]{2,1,0:T(8,128)(2,1)}, u32[]{:S(2)}, u32[]{:S(2)}) collective-permute-start(bf16[2,1024,128]{2,1,0:T(8,128)(2,1)} %collective-permute-done.16.rest_1_), channel_id=1, source_target_pairs={{8,0},{12,4},{16,8},{20,12},{9,1},{13,5},{17,9},{21,13},{10,2},{14... | collective-permute-start | bytes 1572872 | tf_op jit(solution)/shard_map/ppermute | solution.py:310
  175.4 77.2 %collective-permute-start.21 = (bf16[2,1024,128]{2,1,0:T(8,128)(2,1)}, bf16[2,1024,128]{2,1,0:T(8,128)(2,1)S(1)}, u32[]{:S(2)}, u32[]{:S(2)}) collective-permute-start(bf16[2,1024,128]{2,1,0:T(8,128)(2,1)} %collective-permute-done.20.rest_1_), channel_id=1, source_target_pairs={{8,0},{12,4},{16,8},{20,12},{9,1},{13,5},{17,9},{21,13},{10,2},{14... | collective-permute-start | bytes 1572872 | tf_op jit(solution)/shard_map/ppermute | solution.py:310
  186.5 80.1 %collective-permute-start.28 = (bf16[2,1024,128]{2,1,0:T(8,128)(2,1)S(1)}, bf16[2,1024,128]{2,1,0:T(8,128)(2,1)S(1)}, u32[]{:S(2)}, u32[]{:S(2)}) collective-permute-start(bf16[2,1024,128]{2,1,0:T(8,128)(2,1)S(1)} %collective-permute-done.27.rest_1_), channel_id=1, source_target_pairs={{8,0},{12,4},{16,8},{20,12},{9,1},{13,5},{17,9},{21,13},{10,2},{14... | collective-permute-start | bytes 1572872 | tf_op jit(solution)/shard_map/ppermute | solution.py:310
  197.8 74.8 %collective-permute-start.32 = (bf16[2,1024,128]{2,1,0:T(8,128)(2,1)S(1)}, bf16[2,1024,128]{2,1,0:T(8,128)(2,1)S(1)}, u32[]{:S(2)}, u32[]{:S(2)}) collective-permute-start(bf16[2,1024,128]{2,1,0:T(8,128)(2,1)S(1)} %collective-permute-done.31.rest_1_), channel_id=1, source_target_pairs={{8,0},{12,4},{16,8},{20,12},{9,1},{13,5},{17,9},{21,13},{10,2},{14... | collective-permute-start | bytes 1572872 | tf_op jit(solution)/shard_map/ppermute | solution.py:310
  201.4 30.1 %collective-permute-start.40 = (bf16[32,1024]{1,0:T(8,128)(2,1)}, bf16[32,1024]{1,0:T(8,128)(2,1)S(1)}, u32[]{:S(2)}, u32[]{:S(2)}) collective-permute-start(bf16[32,1024]{1,0:T(8,128)(2,1)} %get-tuple-element.121), channel_id=1, source_target_pairs={{0,8},{4,12},{8,0},{12,4},{16,24},{20,28},{24,16},{28,20},{1,9},{5... | collective-permute-start | bytes 196616 | tf_op jit(solution)/shard_map/ppermute | solution.py:303
  231.6 5.4 %collective-permute-start.41 = (bf16[32,1024]{1,0:T(8,128)(2,1)}, bf16[32,1024]{1,0:T(8,128)(2,1)S(1)}, u32[]{:S(2)}, u32[]{:S(2)}) collective-permute-start(bf16[32,1024]{1,0:T(8,128)(2,1)} %get-tuple-element.122), channel_id=1, source_target_pairs={{0,16},{4,20},{8,24},{12,28},{16,0},{20,4},{24,8},{28,12},{1,17},{... | collective-permute-start | bytes 196616 | tf_op jit(solution)/shard_map/ppermute | solution.py:303
  237.0 6.6 %collective-permute-start.42 = (bf16[32,1024]{1,0:T(8,128)(2,1)}, bf16[32,1024]{1,0:T(8,128)(2,1)S(1)}, u32[]{:S(2)}, u32[]{:S(2)}) collective-permute-start(bf16[32,1024]{1,0:T(8,128)(2,1)} %get-tuple-element.123), channel_id=1, source_target_pairs={{0,24},{4,28},{8,16},{12,20},{16,8},{20,12},{24,0},{28,4},{1,25},{... | collective-permute-start | bytes 196616 | tf_op jit(solution)/shard_map/ppermute | solution.py:303
  245.8 10.4 %collective-permute-start.43 = (bf16[32,1024]{1,0:T(8,128)(2,1)}, bf16[32,1024]{1,0:T(8,128)(2,1)S(1)}, u32[]{:S(2)}, u32[]{:S(2)}) collective-permute-start(bf16[32,1024]{1,0:T(8,128)(2,1)} %shard_map.119.rest_0_), channel_id=1, source_target_pairs={{0,8},{4,12},{8,0},{12,4},{16,24},{20,28},{24,16},{28,20},{1,9},{5... | collective-permute-start | bytes 196616 | tf_op jit(solution)/shard_map/ppermute | solution.py:303
  247.5 28.8 %collective-permute-start.67 = (bf16[2,128,128]{2,1,0:T(8,128)(2,1)}, bf16[2,128,128]{2,1,0:T(8,128)(2,1)S(1)}, u32[]{:S(2)}, u32[]{:S(2)}) collective-permute-start(bf16[2,128,128]{2,1,0:T(8,128)(2,1)} %get-tuple-element.147), channel_id=1, source_target_pairs={{0,8},{4,12},{8,0},{12,4},{16,24},{20,28},{24,16},{28,20},{1,9},{5... | collective-permute-start | bytes 196616 | tf_op jit(solution)/shard_map/ppermute | solution.py:303
  252.6 11.0 %collective-permute-start.44 = (bf16[32,1024]{1,0:T(8,128)(2,1)S(1)}, bf16[32,1024]{1,0:T(8,128)(2,1)S(1)}, u32[]{:S(2)}, u32[]{:S(2)}) collective-permute-start(bf16[32,1024]{1,0:T(8,128)(2,1)S(1)} %copy-done.21), channel_id=1, source_target_pairs={{0,16},{4,20},{8,24},{12,28},{16,0},{20,4},{24,8},{28,12},{1,17},{... | collective-permute-start | bytes 196616 | tf_op jit(solution)/shard_map/ppermute | solution.py:303
  256.2 8.1 %collective-permute-start.45 = (bf16[32,1024]{1,0:T(8,128)(2,1)S(1)}, bf16[32,1024]{1,0:T(8,128)(2,1)S(1)}, u32[]{:S(2)}, u32[]{:S(2)}) collective-permute-start(bf16[32,1024]{1,0:T(8,128)(2,1)S(1)} %copy-done.21), channel_id=1, source_target_pairs={{0,24},{4,28},{8,16},{12,20},{16,8},{20,12},{24,0},{28,4},{1,25},{... | collective-permute-start | bytes 196616 | tf_op jit(solution)/shard_map/ppermute | solution.py:303
  263.6 22.1 %collective-permute-start.47 = (bf16[256,256]{1,0:T(8,128)(2,1)}, bf16[256,256]{1,0:T(8,128)(2,1)S(1)}, u32[]{:S(2)}, u32[]{:S(2)}) collective-permute-start(bf16[256,256]{1,0:T(8,128)(2,1)} %get-tuple-element.125), channel_id=1, source_target_pairs={{0,1},{1,0},{2,3},{3,2},{4,5},{5,4},{6,7},{7,6},{8,9},{9,8},{10,11... | collective-permute-start | bytes 393224 | tf_op jit(solution)/shard_map/ppermute | solution.py:296
  264.3 19.5 %collective-permute-start.68 = (bf16[2,128,128]{2,1,0:T(8,128)(2,1)S(1)}, bf16[2,128,128]{2,1,0:T(8,128)(2,1)S(1)}, u32[]{:S(2)}, u32[]{:S(2)}) collective-permute-start(bf16[2,128,128]{2,1,0:T(8,128)(2,1)S(1)} %copy-done.67), channel_id=1, source_target_pairs={{0,16},{4,20},{8,24},{12,28},{16,0},{20,4},{24,8},{28,12},{1,17},{... | collective-permute-start | bytes 196616 | tf_op jit(solution)/shard_map/ppermute | solution.py:303
  266.6 18.4 %collective-permute-start.69 = (bf16[2,128,128]{2,1,0:T(8,128)(2,1)S(1)}, bf16[2,128,128]{2,1,0:T(8,128)(2,1)S(1)}, u32[]{:S(2)}, u32[]{:S(2)}) collective-permute-start(bf16[2,128,128]{2,1,0:T(8,128)(2,1)S(1)} %copy-done.66), channel_id=1, source_target_pairs={{0,24},{4,28},{8,16},{12,20},{16,8},{20,12},{24,0},{28,4},{1,25},{... | collective-permute-start | bytes 196616 | tf_op jit(solution)/shard_map/ppermute | solution.py:303
  272.6 31.4 %collective-permute-start.46 = (bf16[4,32,1024]{2,1,0:T(8,128)(2,1)S(1)}, bf16[4,32,1024]{2,1,0:T(8,128)(2,1)S(1)}, u32[]{:S(2)}, u32[]{:S(2)}) collective-permute-start(bf16[4,32,1024]{2,1,0:T(8,128)(2,1)S(1)} %copy-done.2), channel_id=1, source_target_pairs={{0,4},{4,0},{8,12},{12,8},{16,20},{20,16},{24,28},{28,24},{1,5},{5... | collective-permute-start | bytes 786440 | tf_op jit(solution)/shard_map/ppermute | solution.py:290
  276.4 11.0 %collective-permute-start.48 = (bf16[256,256]{1,0:T(8,128)(2,1)S(1)}, bf16[256,256]{1,0:T(8,128)(2,1)S(1)}, u32[]{:S(2)}, u32[]{:S(2)}) collective-permute-start(bf16[256,256]{1,0:T(8,128)(2,1)S(1)} %copy-done.65), channel_id=1, source_target_pairs={{0,2},{1,3},{2,0},{3,1},{4,6},{5,7},{6,4},{7,5},{8,10},{9,11},{10,... | collective-permute-start | bytes 393224 | tf_op jit(solution)/shard_map/ppermute | solution.py:296
  283.8 7.3 %collective-permute-start.49 = (bf16[256,256]{1,0:T(8,128)(2,1)S(1)}, bf16[256,256]{1,0:T(8,128)(2,1)S(1)}, u32[]{:S(2)}, u32[]{:S(2)}) collective-permute-start(bf16[256,256]{1,0:T(8,128)(2,1)S(1)} %copy-done.64), channel_id=1, source_target_pairs={{0,3},{1,2},{2,1},{3,0},{4,7},{5,6},{6,5},{7,4},{8,11},{9,10},{10,... | collective-permute-start | bytes 393224 | tf_op jit(solution)/shard_map/ppermute | solution.py:296
  285.1 7.8 %collective-permute-start.57 = (bf16[256,256]{1,0:T(8,128)(2,1)}, bf16[256,256]{1,0:T(8,128)(2,1)S(1)}, u32[]{:S(2)}, u32[]{:S(2)}) collective-permute-start(bf16[256,256]{1,0:T(8,128)(2,1)} %get-tuple-element.133), channel_id=1, source_target_pairs={{0,1},{1,0},{2,3},{3,2},{4,5},{5,4},{6,7},{7,6},{8,9},{9,8},{10,11... | collective-permute-start | bytes 393224 | tf_op jit(solution)/shard_map/ppermute | solution.py:296
  285.7 9.3 %collective-permute-start.58 = (bf16[256,256]{1,0:T(8,128)(2,1)}, bf16[256,256]{1,0:T(8,128)(2,1)S(1)}, u32[]{:S(2)}, u32[]{:S(2)}) collective-permute-start(bf16[256,256]{1,0:T(8,128)(2,1)} %get-tuple-element.134), channel_id=1, source_target_pairs={{0,2},{1,3},{2,0},{3,1},{4,6},{5,7},{6,4},{7,5},{8,10},{9,11},{10,... | collective-permute-start | bytes 393224 | tf_op jit(solution)/shard_map/ppermute | solution.py:296
  287.4 10.2 %collective-permute-start.59 = (bf16[256,256]{1,0:T(8,128)(2,1)}, bf16[256,256]{1,0:T(8,128)(2,1)S(1)}, u32[]{:S(2)}, u32[]{:S(2)}) collective-permute-start(bf16[256,256]{1,0:T(8,128)(2,1)} %get-tuple-element.135), channel_id=1, source_target_pairs={{0,3},{1,2},{2,1},{3,0},{4,7},{5,6},{6,5},{7,4},{8,11},{9,10},{10,... | collective-permute-start | bytes 393224 | tf_op jit(solution)/shard_map/ppermute | solution.py:296
  291.2 9.0 %collective-permute-start.70 = (bf16[2,128,128]{2,1,0:T(8,128)(2,1)}, bf16[2,128,128]{2,1,0:T(8,128)(2,1)S(1)}, u32[]{:S(2)}, u32[]{:S(2)}) collective-permute-start(bf16[2,128,128]{2,1,0:T(8,128)(2,1)} %shard_map.129.rest_0_), channel_id=1, source_target_pairs={{0,1},{1,0},{2,3},{3,2},{4,5},{5,4},{6,7},{7,6},{8,9},{9,8},{10,11... | collective-permute-start | bytes 196616 | tf_op jit(solution)/shard_map/ppermute | solution.py:296
  292.8 8.3 %collective-permute-start.71 = (bf16[2,128,128]{2,1,0:T(8,128)(2,1)}, bf16[2,128,128]{2,1,0:T(8,128)(2,1)S(1)}, u32[]{:S(2)}, u32[]{:S(2)}) collective-permute-start(bf16[2,128,128]{2,1,0:T(8,128)(2,1)} %shard_map.129.rest_0_), channel_id=1, source_target_pairs={{0,2},{1,3},{2,0},{3,1},{4,6},{5,7},{6,4},{7,5},{8,10},{9,11},{10,... | collective-permute-start | bytes 196616 | tf_op jit(solution)/shard_map/ppermute | solution.py:296
  295.0 9.0 %collective-permute-start.72 = (bf16[2,128,128]{2,1,0:T(8,128)(2,1)}, bf16[2,128,128]{2,1,0:T(8,128)(2,1)S(1)}, u32[]{:S(2)}, u32[]{:S(2)}) collective-permute-start(bf16[2,128,128]{2,1,0:T(8,128)(2,1)} %shard_map.129.rest_0_), channel_id=1, source_target_pairs={{0,3},{1,2},{2,1},{3,0},{4,7},{5,6},{6,5},{7,4},{8,11},{9,10},{10,... | collective-permute-start | bytes 196616 | tf_op jit(solution)/shard_map/ppermute | solution.py:296
  297.6 7.9 %collective-permute-start.50 = (bf16[64,256]{1,0:T(8,128)(2,1)}, bf16[64,256]{1,0:T(8,128)(2,1)S(1)}, u32[]{:S(2)}, u32[]{:S(2)}) collective-permute-start(bf16[64,256]{1,0:T(8,128)(2,1)} %get-tuple-element.129), channel_id=1, source_target_pairs={{0,8},{4,12},{8,0},{12,4},{16,24},{20,28},{24,16},{28,20},{1,9},{5... | collective-permute-start | bytes 98312 | tf_op jit(solution)/shard_map/ppermute | solution.py:303
  300.1 5.5 %collective-permute-start.51 = (bf16[64,256]{1,0:T(8,128)(2,1)}, bf16[64,256]{1,0:T(8,128)(2,1)S(1)}, u32[]{:S(2)}, u32[]{:S(2)}) collective-permute-start(bf16[64,256]{1,0:T(8,128)(2,1)} %get-tuple-element.130), channel_id=1, source_target_pairs={{0,16},{4,20},{8,24},{12,28},{16,0},{20,4},{24,8},{28,12},{1,17},{... | collective-permute-start | bytes 98312 | tf_op jit(solution)/shard_map/ppermute | solution.py:303
  301.1 5.9 %collective-permute-start.52 = (bf16[64,256]{1,0:T(8,128)(2,1)}, bf16[64,256]{1,0:T(8,128)(2,1)S(1)}, u32[]{:S(2)}, u32[]{:S(2)}) collective-permute-start(bf16[64,256]{1,0:T(8,128)(2,1)} %get-tuple-element.131), channel_id=1, source_target_pairs={{0,24},{4,28},{8,16},{12,20},{16,8},{20,12},{24,0},{28,4},{1,25},{... | collective-permute-start | bytes 98312 | tf_op jit(solution)/shard_map/ppermute | solution.py:303
  305.6 47.4 %collective-permute-start.35 = (bf16[1024,256]{1,0:T(8,128)(2,1)S(1)}, bf16[1024,256]{1,0:T(8,128)(2,1)S(1)}, u32[]{:S(2)}, u32[]{:S(2)}) collective-permute-start(bf16[1024,256]{1,0:T(8,128)(2,1)S(1)} %copy-done.3), channel_id=1, source_target_pairs={{0,4},{4,0},{8,12},{12,8},{16,20},{20,16},{24,28},{28,24},{1,5},{5... | collective-permute-start | bytes 1572872 | tf_op jit(solution)/shard_map/ppermute | solution.py:290
  305.7 47.3 %collective-permute-start.36 = (bf16[1024,256]{1,0:T(8,128)(2,1)S(1)}, bf16[1024,256]{1,0:T(8,128)(2,1)S(1)}, u32[]{:S(2)}, u32[]{:S(2)}) collective-permute-start(bf16[1024,256]{1,0:T(8,128)(2,1)S(1)} %copy-done.4), channel_id=1, source_target_pairs={{0,4},{4,0},{8,12},{12,8},{16,20},{20,16},{24,28},{28,24},{1,5},{5... | collective-permute-start | bytes 1572872 | tf_op jit(solution)/shard_map/ppermute | solution.py:290
  307.1 45.9 %collective-permute-start.33 = (bf16[1024,256]{1,0:T(8,128)(2,1)}, bf16[1024,256]{1,0:T(8,128)(2,1)S(1)}, u32[]{:S(2)}, u32[]{:S(2)}) collective-permute-start(bf16[1024,256]{1,0:T(8,128)(2,1)} %get-tuple-element.106), channel_id=1, source_target_pairs={{0,4},{4,0},{8,12},{12,8},{16,20},{20,16},{24,28},{28,24},{1,5},{5... | collective-permute-start | bytes 1572872 | tf_op jit(solution)/shard_map/ppermute | solution.py:290
  308.8 44.2 %collective-permute-start.34 = (bf16[1024,256]{1,0:T(8,128)(2,1)}, bf16[1024,256]{1,0:T(8,128)(2,1)S(1)}, u32[]{:S(2)}, u32[]{:S(2)}) collective-permute-start(bf16[1024,256]{1,0:T(8,128)(2,1)} %get-tuple-element.109), channel_id=1, source_target_pairs={{0,4},{4,0},{8,12},{12,8},{16,20},{20,16},{24,28},{28,24},{1,5},{5... | collective-permute-start | bytes 1572872 | tf_op jit(solution)/shard_map/ppermute | solution.py:290
  309.3 6.0 %collective-permute-start.62 = (bf16[64,256]{1,0:T(8,128)(2,1)}, bf16[64,256]{1,0:T(8,128)(2,1)}, u32[]{:S(2)}, u32[]{:S(2)}) collective-permute-start(bf16[64,256]{1,0:T(8,128)(2,1)} %get-tuple-element.139), channel_id=1, source_target_pairs={{0,24},{4,28},{8,16},{12,20},{16,8},{20,12},{24,0},{28,4},{1,25},{... | collective-permute-start | bytes 98312 | tf_op jit(solution)/shard_map/ppermute | solution.py:303
  319.5 5.4 %collective-permute-start.54 = (bf16[64,256]{1,0:T(8,128)(2,1)}, bf16[64,256]{1,0:T(8,128)(2,1)}, u32[]{:S(2)}, u32[]{:S(2)}) collective-permute-start(bf16[64,256]{1,0:T(8,128)(2,1)} %shard_map.122.rest_0_), channel_id=1, source_target_pairs={{0,16},{4,20},{8,24},{12,28},{16,0},{20,4},{24,8},{28,12},{1,17},{... | collective-permute-start | bytes 98312 | tf_op jit(solution)/shard_map/ppermute | solution.py:303
  324.9 6.0 %collective-permute-start.55 = (bf16[64,256]{1,0:T(8,128)(2,1)}, bf16[64,256]{1,0:T(8,128)(2,1)}, u32[]{:S(2)}, u32[]{:S(2)}) collective-permute-start(bf16[64,256]{1,0:T(8,128)(2,1)} %shard_map.122.rest_0_), channel_id=1, source_target_pairs={{0,24},{4,28},{8,16},{12,20},{16,8},{20,12},{24,0},{28,4},{1,25},{... | collective-permute-start | bytes 98312 | tf_op jit(solution)/shard_map/ppermute | solution.py:303
  340.3 6.0 %collective-permute-start.65 = (bf16[64,256]{1,0:T(8,128)(2,1)}, bf16[64,256]{1,0:T(8,128)(2,1)}, u32[]{:S(2)}, u32[]{:S(2)}) collective-permute-start(bf16[64,256]{1,0:T(8,128)(2,1)} %shard_map.125.rest_0_), channel_id=1, source_target_pairs={{0,24},{4,28},{8,16},{12,20},{16,8},{20,12},{24,0},{28,4},{1,25},{... | collective-permute-start | bytes 98312 | tf_op jit(solution)/shard_map/ppermute | solution.py:303
  (77 other events, 1080.5 us)
where the time goes:
time: 363 us; the launch traced here: 361 us
  waiting for transfers between devices  162 us (45%)
  Pallas kernels  108 us (30%)
  starting transfers between devices  81.3 us (22%)
  local copies, waits for them, and re-layouts  6.9 us (2%)
    pallas_call x29, Pallas kernels, call(): pl.pallas_call(body, out_shape=tuple(outs), in_specs=[SM] * scalars + [VM...  102 us
    ppermute x27, waiting for transfers between devices, from_chips(): got.append(lax.ppermute(blocks[k], 'seq', pairs))  81 us
    ppermute x8, waiting for transfers between devices, down(): lax.ppermute(x, 'seq', [(i + 2, i) for i in range(seq_size - 2 * hop)])  44.7 us
    ppermute x27, starting transfers between devices, from_chips(): got.append(lax.ppermute(blocks[k], 'seq', pairs))  31.8 us
    ppermute x21, starting transfers between devices, from_fsdp(): got.append(lax.ppermute(blocks[k], 'fsdp', pairs))  23.2 us
    ppermute x21, waiting for transfers between devices, from_fsdp(): got.append(lax.ppermute(blocks[k], 'fsdp', pairs))  19.6 us
    ppermute x8, waiting for transfers between devices, up(): lax.ppermute(x, 'seq', [(i, i + 2) for i in range(2 * (hop - 1), seq_size...  17 us
    ppermute x8, starting transfers between devices, up(): lax.ppermute(x, 'seq', [(i, i + 2) for i in range(2 * (hop - 1), seq_size...  14.1 us
  transfers between devices with their start and end apart: 73, of which 33 were waited for; matrix products, arithmetic and copies ran while one was open for 0% of the time, Pallas kernels for 24%

commit v1 on v0

--- a/solution.py
+++ b/solution.py
@@ -38,45 +38,64 @@
     return jax.ShapeDtypeStruct(dims, kind)
 
 
-def forward_body(parts, tile, meta, own, partner, *rest):
+def tiled(body, steps, outs, ins, scratch=(), flops=0):
+    moved = sum(math.prod(x[0].shape) * x[0].dtype.itemsize for x in list(ins) + list(outs))
+    return pl.pallas_call(
+        body,
+        grid=(steps,),
+        out_shape=tuple(x[0] for x in outs),
+        in_specs=[SM] + [pl.BlockSpec(x[1], x[2]) for x in ins[1:]],
+        out_specs=tuple(pl.BlockSpec(x[1], x[2]) for x in outs),
+        scratch_shapes=list(scratch),
+        cost_estimate=pl.CostEstimate(flops=flops, bytes_accessed=moved, transcendentals=0),
+        compiler_params=pltpu.CompilerParams(vmem_limit_bytes=60 * 1024 * 1024),
+    )(*[x[0] for x in ins])
+
+
+def fixed(x):
+    return (x, x.shape, lambda i: (0,) * len(x.shape))
+
+
+def forward_body(parts, steps, meta, own, partner, *rest):
     weights, outs = rest[:parts], rest[parts:]
-    me = meta[0]
+    targets, panel = outs[:-1], outs[-1]
     rows = weights[0].shape[0]
-    panel = outs[-1]
-    for k in range(parts):
-        panel[pl.ds(pl.multiple_of((me ^ k) * rows, rows), rows), :] = weights[k][...]
-    targets = outs[:-1]
-    for source, slot in ((own, 0), (partner, 1)):
-
-        def step(i, carry, source=source, slot=slot):
-            at = pl.multiple_of(i * tile, tile)
-            got = dot(source[pl.ds(at, tile), :], panel[...], 1, 0).astype(BF)
-            for j, target in enumerate(targets):
-                target[slot, pl.ds(at, tile), :] = got[:, j * LANES : (j + 1) * LANES]
-            return carry
-
-        lax.fori_loop(0, source.shape[0] // tile, step, 0)
-
-
-def upstream_body(parts, tile, meta, own, partner, *rest):
+    at = pl.program_id(0)
+
+    @pl.when(at == 0)
+    def _():
+        for k in range(parts):
+            start = pl.multiple_of((meta[0] ^ k) * rows, rows)
+            panel[pl.ds(start, rows), :] = weights[k][...]
+
+    def work(source):
+        got = dot(source[...], panel[...], 1, 0).astype(BF)
+        for j, target in enumerate(targets):
+            target[0] = got[:, j * LANES : (j + 1) * LANES]
+
+    pl.when(at < steps)(lambda: work(own))
+    pl.when(at >= steps)(lambda: work(partner))
+
+
+def upstream_body(parts, steps, meta, own, partner, *rest):
     weights, outs = rest[:parts], rest[parts:]
-    me = meta[0]
+    targets, panel = outs[:-1], outs[-1]
     rows = weights[0].shape[0]
-    panel = outs[-1]
-    targets = outs[:-1]
-    for k in range(parts):
-        panel[me ^ k] = weights[k][...]
-    for source, slot in ((own, 0), (partner, 1)):
-
-        def step(i, carry, source=source, slot=slot):
-            at = pl.multiple_of(i * tile, tile)
-            whole = panel[...].reshape(parts * rows, panel.shape[2])
-            got = dot(source[pl.ds(at, tile), :], whole, 1, 1).astype(BF)
-            for j, target in enumerate(targets):
-                target[slot, pl.ds(at, tile), :] = got[:, j * LANES : (j + 1) * LANES]
-            return carry
-
-        lax.fori_loop(0, source.shape[0] // tile, step, 0)
+    at = pl.program_id(0)
+
+    @pl.when(at == 0)
+    def _():
+        for k in range(parts):
+            start = pl.multiple_of((meta[0] ^ k) * rows, rows)
+            panel[pl.ds(start, rows), :] = weights[k][...]
+
+    def work(source):
+        got = dot(source[...], panel[...], 1, 1).astype(BF)
+        for j, target in enumerate(targets):
+            target[0] = got[:, j * LANES : (j + 1) * LANES]
+
+    pl.when(at < steps)(lambda: work(own))
+    pl.when(at >= steps)(lambda: work(partner))
 
 
 def select_lanes(a, b):
@@ -160,36 +179,40 @@
         lax.fori_loop(0, half // tile, step, 0)
 
 
-def outer_body(chunks, parts, tile, by_rows, split, meta, *rest):
+def outer_body(chunks, parts, steps, by_rows, split, meta, *rest):
     count = chunks * (2 if split else 1)
     lefts, rest = rest[:count], rest[count:]
     rights, outs, total = rest[:2], rest[2:-1], rest[-1]
-    me = meta[0]
-    total[...] = jnp.zeros_like(total)
-    for slot in range(2):
-
-        def step(i, carry, slot=slot):
-            at = pl.multiple_of(i * tile, tile)
-            if split:
-                left = [lefts[2 * j + slot][pl.ds(at, tile), :] for j in range(chunks)]
+    at = pl.program_id(0)
+
+    @pl.when(at == 0)
+    def _():
+        total[...] = jnp.zeros_like(total)
+
+    def work(slot):
+        if split:
+            left = [lefts[2 * j + slot][...] for j in range(chunks)]
+        else:
+            left = [lefts[j][0] for j in range(chunks)]
+        left = jnp.concatenate(left, axis=1)
+        if split and slot == 1:
+            outs[parts][...] = left
+        total[...] += dot(left, rights[slot][...], 0, 0)
+
+    pl.when(at < steps)(lambda: work(0))
+    pl.when(at >= steps)(lambda: work(1))
+
+    @pl.when(at == 2 * steps - 1)
+    def _():
+        rows, columns = outs[0].shape
+        for k in range(parts):
+            if by_rows:
+                start = pl.multiple_of((meta[0] ^ k) * rows, rows)
+                got = total[pl.ds(start, rows), :]
             else:
-                left = [lefts[j][slot, pl.ds(at, tile), :] for j in range(chunks)]
-            left = jnp.concatenate(left, axis=1)
-            if split and slot == 1:
-                outs[parts][pl.ds(at, tile), :] = left
-            total[...] += dot(left, rights[slot][pl.ds(at, tile), :], 0, 0)
-            return carry
-
-        lax.fori_loop(0, rights[slot].shape[0] // tile, step, 0)
-    rows, columns = outs[0].shape
-    for k in range(parts):
-        if by_rows:
-            at = pl.multiple_of((me ^ k) * rows, rows)
-            got = total[pl.ds(at, rows), :]
-        else:
-            at = pl.multiple_of((me ^ k) * columns, columns)
-            got = total[:, pl.ds(at, columns)]
-        outs[k][...] = got.astype(outs[k].dtype)
+                start = pl.multiple_of((meta[0] ^ k) * columns, columns)
+                got = total[:, pl.ds(start, columns)]
+            outs[k][...] = got.astype(outs[k].dtype)
 
 
 def tree(values):
@@ -205,6 +228,38 @@
     for k in range(parts):
         at = pl.multiple_of((meta[1] ^ k) * rows, rows)
         outs[k][...] = total[pl.ds(at, rows), :].astype(outs[k].dtype)
+
+
+def gather_body(count, chips, pairs, meta, *rest):
+    first, second = rest[:count], rest[count : 2 * count]
+    kernels, rest = rest[2 * count : 2 * count + pairs], rest[2 * count + pairs :]
+    outs, (sum_one, sum_two, held) = rest[:-3], rest[-3:]
+    sum_one[...] = tree([x[...].astype(F32) for x in first])
+    sum_two[...] = tree([x[...].astype(F32) for x in second])
+    width = sum_one.shape[1]
+    one, two, taps = sum_one.shape[0] // chips, sum_two.shape[0] // chips, held.shape[2]
+    for j in range(pairs):
+        for n in range(LANES // taps):
+            held[j * (LANES // taps) + n] = kernels[j][:, n * taps : (n + 1) * taps, :]
+    for k in range(chips):
+        at, kind = meta[1] ^ k, outs[k].dtype
+        outs[k][:one, :] = sum_one[pl.ds(pl.multiple_of(at * one, 8), one), :].astype(kind)
+        block = sum_two[pl.ds(pl.multiple_of(at * two, 8), two), :].astype(kind)
+        top = one
+        for n in range(block.shape[1] // width):
+            outs[k][top : top + two, :] = block[:, n * width : (n + 1) * width]
+            top += two
+        for tap in range(2):
+            column = (tap * LANES) % width
+            row = top + (tap * LANES) // width * taps
+            outs[k][row : row + taps, column : column + LANES] = held[at, tap].astype(kind)
+
+
+def divide_body(count, *rest):
+    got = tree([x[...].astype(F32) for x in rest[:count]]).astype(BF)
+    rows = rest[count].shape[0]
+    rest[count][...] = got[:rows, :]
+    rest[count + 1][...] = got[rows:, :]
 
 
 def sum_body(count, factor, *rest):
@@ -254,17 +309,6 @@
                         zero = jnp.zeros_like(block)
                         out[top : top + width, :LANES] = jnp.where(here, left, zero).astype(BF)
                         out[top : top + width, LANES:] = jnp.where(here, right, zero).astype(BF)
-
-
-def pick_body(chips, count, meta, *rest):
-    ins, outs, held = rest[:count], rest[count:-1], rest[-1]
-    rows = outs[0].shape[1]
-    each = LANES // rows
-    for j in range(count):
-        for n in range(each):
-            held[j * each + n] = ins[j][:, n * rows : (n + 1) * rows, :]
-    for k in range(chips):
-        outs[k][...] = held[meta[1] ^ k]
 
 
 def local_step(signal, cotangent, w_in, w_conv, w_out, dilation, lengths):
@@ -312,16 +356,14 @@
     where = jnp.stack([fsdp_at, chip, core, lengths[0] - chip * block]).astype(jnp.int32)
     wide = per_half * LANES
     halves = range(0, chunks, per_half)
-    in_shares = call(
-        functools.partial(share_body, fsdp_size),
-        [shape((w_in.shape[0], wide), BF)] * len(halves),
-        [where, w_in],
+    (in_share,) = call(
+        functools.partial(share_body, fsdp_size), [shape((w_in.shape[0], share), BF)], [where, w_in]
     )
     out_share = lax.dynamic_index_in_dim(
         w_out.reshape(2, piece, channels), core, 0, keepdims=False
     )
     record_far = to_partner(record)
-    in_parts = [from_fsdp([x] * fsdp_size) for x in in_shares]
+    in_parts = from_fsdp([in_share] * fsdp_size)
     upstream_far = to_partner(upstream)
     out_parts = from_fsdp([out_share] * fsdp_size)
     delays = from_chips([dilation] * chips)
@@ -336,25 +378,37 @@
     amounts, kernels = taps[0], taps[1:]
 
     series = shape((2, samples, LANES), BF)
-    tile = min(512, samples)
-    projected, panels = [], []
-    for n in range(len(halves)):
-        got = call(
-            functools.partial(forward_body, fsdp_size, tile),
-            [series] * per_half + [shape((channels, wide), BF)],
-            [where, record, record_far] + in_parts[n],
-            flops=2 * block * channels * wide,
-        )
-        projected += got[:-1]
-        panels.append(got[-1])
-    grad_gated = call(
-        functools.partial(upstream_body, fsdp_size, tile),
-        [series] * chunks,
-        [where, upstream, upstream_far] + out_parts,
-        scratch=[pltpu.VMEM((fsdp_size, piece, channels), BF)],
+    tile = min(256, samples)
+    steps = samples // tile
+
+    def near(x):
+        block_shape = (tile, x.shape[1])
+        return (x, block_shape, lambda i: (jnp.minimum(i, steps - 1), 0))
+
+    def far(x):
+        block_shape = (tile, x.shape[1])
+        return (x, block_shape, lambda i: (jnp.maximum(i - steps, 0), 0))
+
+    def both(x):
+        return (x, (1, tile, LANES), lambda i: (i // steps, i % steps, 0))
+
+    got = tiled(
+        functools.partial(forward_body, fsdp_size, steps),
+        2 * steps,
+        [both(series)] * chunks + [fixed(shape((channels, share), BF))],
+        [(where,), near(record), far(record_far)] + [fixed(x) for x in in_parts],
         flops=2 * block * channels * share,
     )
-    panels_far = [to_partner(x) for x in panels]
+    projected, panel = got[:-1], got[-1]
+    grad_gated = tiled(
+        functools.partial(upstream_body, fsdp_size, steps),
+        2 * steps,
+        [both(series)] * chunks,
+        [(where,), near(upstream), far(upstream_far)] + [fixed(x) for x in out_parts],
+        scratch=[pltpu.VMEM((share, channels), BF)],
+        flops=2 * block * channels * share,
+    )
+    panel_far = to_partner(panel)
 
     tile = min(256, samples)
     gated, own_mixed, far_mixed, kernel_grads = [], [], [], []
@@ -376,7 +430,7 @@
         back = [tap_one]
         for hop in range(1, hops + 1):
             back.append(down(back[-1], hop))
-        own, far = call(
+        own, other = call(
             functools.partial(mixed_body, hops, tile, j),
             [shape((samples, LANES), BF)] * 2,
             [where, amounts, tap_zero] + back,
@@ -384,91 +438,94 @@
             scalars=2,
         )
         own_mixed.append(own)
-        far_mixed.append(far)
-
-    def over_all(blocks):
-        got = from_fsdp(blocks)
-        rows, columns = blocks[0].shape
-        part = rows // chips
-        cut = call(
-            functools.partial(split_body, fsdp_size, chips),
-            [shape((part, columns), F32)] + [shape((part, columns), BF)] * (chips - 1),
-            [where] + got,
-            scratch=[pltpu.VMEM((rows, columns), F32)],
-        )
-        got = from_chips(cut)
-        (mine,) = call(
-            functools.partial(sum_body, chips, None), [shape((part, columns), BF)], got, scalars=0
-        )
-        got = from_chips([mine] * chips)
-        (packed,) = call(
-            functools.partial(pack_body, chips), [shape((chips, part, columns), BF)], [where] + got
-        )
-        return [packed, to_partner(packed)]
-
-    def outer(lefts, rights, by_rows, split, tile):
+        far_mixed.append(other)
+
+    tile = min(256, samples)
+
+    def outer(lefts, rights, by_rows, split):
         count = len(lefts) // 2 if split else len(lefts)
         rows, columns = LANES * count, channels
         one = (piece, columns) if by_rows else (rows, columns // fsdp_size)
-        return call(
-            functools.partial(outer_body, count, fsdp_size, tile, by_rows, split),
-            [shape(one, F32)]
-            + [shape(one, BF)] * (fsdp_size - 1)
-            + ([shape((samples, rows), BF)] if split else []),
-            [where] + lefts + list(rights),
+        outs = [fixed(shape(one, F32))] + [fixed(shape(one, BF))] * (fsdp_size - 1)
+        if split:
+            outs.append(far(shape((samples, rows), BF)))
+            lefts = [(near, far)[n % 2](x) for n, x in enumerate(lefts)]
+        else:
+            lefts = [both(x) for x in lefts]
+        return tiled(
+            functools.partial(outer_body, count, fsdp_size, steps, by_rows, split),
+            2 * steps,
+            outs,
+            [(where,)] + lefts + [near(rights[0]), far(rights[1])],
             scratch=[pltpu.VMEM((rows, columns), F32)],
             flops=2 * block * rows * columns,
         )
 
-    tile = min(512, samples)
-    finals = over_all(outer(gated, (upstream, upstream_far), True, False, tile))
-    mixed_in = []
+    def finish_sum(mine):
+        rows, columns = mine.shape
+        got = from_chips([mine] * chips)
+        (packed,) = call(
+            functools.partial(pack_body, chips), [shape((chips, rows, columns), BF)], [where] + got
+        )
+        return [packed, to_partner(packed)]
+
+    mixed_in, flats = [], []
     for start in halves:
         sides = []
         for j in range(start, start + per_half):
             sides += [own_mixed[j], far_mixed[j]]
-        got = outer(sides, (record, record_far), False, True, tile)
+        got = outer(sides, (record, record_far), False, True)
         mixed_in.append(to_partner(got[-1]))
-        finals += over_all(got[:fsdp_size])
-
-    cuts = call(
-        functools.partial(pick_body, chips, chunks),
-        [shape((2, conv_chans, LANES), BF)] * chips,
-        [where] + kernel_grads,
-        scratch=[pltpu.VMEM((chips, 2, conv_chans, LANES), BF)],
-    )
-    got = from_chips(cuts)
+        flats.append(from_fsdp(got[:fsdp_size]))
+    got = outer(gated, (upstream, upstream_far), True, False)
+    flat_out = from_fsdp(got)
+
+    own_rows = channels // fsdp_size
+    in_part, out_part = wide // chips, piece // chips
+    panel_rows = in_part + out_part * (channels // own_rows)
+    kernel_rows = 2 * LANES * conv_chans // own_rows
+    whole = (panel_rows + kernel_rows, own_rows)
+    cut = call(
+        functools.partial(gather_body, fsdp_size, chips, chunks),
+        [shape(whole, F32)] + [shape(whole, BF)] * (chips - 1),
+        [where] + flats[0] + flat_out + kernel_grads,
+        scratch=[
+            pltpu.VMEM((wide, own_rows), F32),
+            pltpu.VMEM((piece, channels), F32),
+            pltpu.VMEM((chips, 2, conv_chans, LANES), BF),
+        ],
+    )
+    mine, mine_kernel = call(
+        functools.partial(divide_body, chips),
+        [shape((panel_rows, own_rows), BF), shape((kernel_rows, own_rows), BF)],
+        from_chips(cut),
+        scalars=0,
+    )
+    kernel_parts = from_fsdp([mine_kernel] * fsdp_size)
+    finals = finish_sum(mine)
+
+    last = (wide // chips, own_rows)
+    cut = call(
+        functools.partial(split_body, fsdp_size, chips),
+        [shape(last, F32)] + [shape(last, BF)] * (chips - 1),
+        [where] + flats[1],
+        scratch=[pltpu.VMEM((wide, own_rows), F32)],
+    )
     (mine,) = call(
-        functools.partial(sum_body, chips, None),
-        [shape((2, conv_chans, LANES), BF)],
-        got,
-        scalars=0,
-    )
-    got = from_fsdp([mine] * fsdp_size)
-    (grad_conv,) = call(
-        functools.partial(sum_body, fsdp_size, factor),
-        [shape((2, conv_chans, LANES), F32)],
-        got,
-        scalars=0,
-    )
+        functools.partial(sum_body, chips, None), [shape(last, BF)], from_chips(cut), scalars=0
+    )
+    finals += finish_sum(mine)
 
     tile = min(256, samples)
 
     def signal_body(base, *rest):
-        target = rest[-1]
-        mixes, others, sides = rest[:chunks], rest[chunks : chunks + len(halves)], rest[
-            chunks + len(halves) : -1
-        ]
-        acc = base[...].astype(F32)
-        for n in range(len(halves)):
-            mix = jnp.concatenate(
-                [mixes[n * per_half + j][...] for j in range(per_half)], axis=1
-            )
-            acc += dot(mix, sides[n][...], 1, 1)
-            acc += dot(others[n][...], sides[len(halves) + n][...], 1, 1)
-        target[...] = acc.astype(BF)
-
-    sides = panels + panels_far
+        mixes, others = rest[:chunks], rest[chunks : chunks + len(halves)]
+        side, side_far, target = rest[-3:]
+        mix = jnp.concatenate([x[...] for x in mixes], axis=1)
+        other = jnp.concatenate([x[...] for x in others], axis=1)
+        acc = base[...].astype(F32) + dot(mix, side[...], 1, 1)
+        target[...] = (acc + dot(other, side_far[...], 1, 1)).astype(BF)
+
     grad_signal = pl.pallas_call(
         signal_body,
         grid=(samples // tile,),
@@ -476,7 +533,7 @@
         in_specs=[pl.BlockSpec((tile, channels), lambda i: (i, 0))]
         + [pl.BlockSpec((tile, LANES), lambda i: (i, 0))] * chunks
         + [pl.BlockSpec((tile, wide), lambda i: (i, 0))] * len(halves)
-        + [pl.BlockSpec(x.shape, lambda i: (0, 0)) for x in sides],
+        + [pl.BlockSpec(panel.shape, lambda i: (0, 0))] * 2,
         out_specs=pl.BlockSpec((tile, channels), lambda i: (i, 0)),
         cost_estimate=pl.CostEstimate(
             flops=2 * samples * channels * channels,
@@ -485,31 +542,38 @@
         ),
         compiler_params=pltpu.CompilerParams(vmem_limit_bytes=60 * 1024 * 1024),
         name="signal",
-    )(upstream, *own_mixed, *mixed_in, *sides)
+    )(upstream, *own_mixed, *mixed_in, panel, panel_far)
 
     def finish_body(meta, *rest):
-        ins, (grad_in, grad_out, turned) = rest[:-3], rest[-3:]
+        packs, parts = rest[:4], rest[4 : 4 + fsdp_size]
+        grad_in, grad_out, grad_conv, turned = rest[4 + fsdp_size :]
         core_at = meta[2]
         for side in range(2):
-            whole = ins[side][...].astype(F32) * factor
-            at = pl.multiple_of((side ^ core_at) * piece, piece)
-            grad_out[pl.ds(at, piece), :] = whole.reshape(piece, channels)
-            for n in range(len(halves)):
-                whole = ins[2 * (n + 1) + side][...].astype(F32) * factor
-                turned[side ^ core_at, n * wide : (n + 1) * wide, :] = whole.reshape(
-                    wide, turned.shape[2]
-                )
+            first = packs[side][...].astype(F32) * factor
+            second = packs[2 + side][...].astype(F32) * factor
+            for p in range(chips):
+                at = pl.multiple_of((side ^ core_at) * piece + p * out_part, 8)
+                for n in range(channels // own_rows):
+                    top = in_part + n * out_part
+                    grad_out[pl.ds(at, out_part), n * own_rows : (n + 1) * own_rows] = first[
+                        p, top : top + out_part, :
+                    ]
+                at = p * in_part
+                turned[side ^ core_at, at : at + in_part, :] = first[p, :in_part, :]
+                turned[side ^ core_at, wide + at : wide + at + in_part, :] = second[p]
         for f in range(fsdp_size):
-            both = jnp.concatenate(
-                [turned[c, f * piece : (f + 1) * piece, :] for c in range(2)], axis=0
-            )
-            grad_in[:, 2 * f * piece : 2 * (f + 1) * piece] = both.T
-
-    own_rows = channels // fsdp_size
-    grad_in, grad_out = call(
+            pair = [turned[c, f * piece : (f + 1) * piece, :] for c in range(2)]
+            grad_in[:, 2 * f * piece : 2 * (f + 1) * piece] = jnp.concatenate(pair, axis=0).T
+        total = tree([x[...].astype(F32) for x in parts]) * factor
+        for tap in range(2):
+            column = (tap * LANES) % own_rows
+            row = (tap * LANES) // own_rows * conv_chans
+            grad_conv[tap] = total[row : row + conv_chans, column : column + LANES]
+
+    grad_in, grad_out, grad_conv = call(
         finish_body,
-        [shape((own_rows, channels), F32)] * 2,
-        [where] + finals,
+        [shape((own_rows, channels), F32)] * 2 + [shape((2, conv_chans, LANES), F32)],
+        [where] + finals + kernel_parts,
         scratch=[pltpu.VMEM((2, share, own_rows), F32)],
     )
     return (grad_signal[None], grad_in, grad_out, grad_conv)

time: 363 us -> 296 us (0.82)
  waiting for transfers between devices: 162 us -> 101 us
    ppermute x27 -> x18, waiting for transfers between devices: 81 us -> 27 us  [from_chips(): got.append(lax.ppermute(blocks[k], 'seq', pairs))]
    pallas_call x29 -> x17, Pallas kernels: 102 us -> 57 us  [call(): pl.pallas_call(body, out_shape=tuple(outs), in_specs=[SM] * scalars + [VM...]
    pallas_call x0 -> x5, Pallas kernels: none -> 41.5 us  [tiled(): pl.pallas_call(body, grid=(steps,), out_shape=tuple((x[0] for x in outs))...]
    ppermute x8, waiting for transfers between devices: 17 us -> 26.1 us  [up(): lax.ppermute(x, 'seq', [(i, i + 2) for i in range(2 * (hop - 1), seq_size...]
    ppermute x21 -> x18, waiting for transfers between devices: 19.6 us -> 10.5 us  [from_fsdp(): got.append(lax.ppermute(blocks[k], 'fsdp', pairs))]
    ppermute x8, waiting for transfers between devices: 44.7 us -> 37.8 us  [down(): lax.ppermute(x, 'seq', [(i + 2, i) for i in range(seq_size - 2 * hop)])]
    ppermute x21 -> x18, starting transfers between devices: 23.2 us -> 21.6 us  [from_fsdp(): got.append(lax.ppermute(blocks[k], 'fsdp', pairs))]
    ppermute x27 -> x18, starting transfers between devices: 31.8 us -> 31.4 us  [from_chips(): got.append(lax.ppermute(blocks[k], 'seq', pairs))]
  transfers between devices with their start and end apart: 73 -> 59, of which waited for: 33 -> 25; matrix products, arithmetic and copies ran while one was open for 0% -> 0% of each run, Pallas kernels for 24% -> 35%
where the time goes in v1:
time: 296 us; the launch traced here: 294 us
  Pallas kernels  105 us (35%)
  waiting for transfers between devices  101 us (34%)
  starting transfers between devices  80.8 us (27%)
  local copies, waits for them, and re-layouts  4.54 us (2%)
    pallas_call x17, Pallas kernels, call(): pl.pallas_call(body, out_shape=tuple(outs), in_specs=[SM] * scalars + [VM...  57 us
    pallas_call x5, Pallas kernels, tiled(): pl.pallas_call(body, grid=(steps,), out_shape=tuple((x[0] for x in outs))...  41.5 us
    ppermute x8, waiting for transfers between devices, down(): lax.ppermute(x, 'seq', [(i + 2, i) for i in range(seq_size - 2 * hop)])  37.8 us
    ppermute x18, starting transfers between devices, from_chips(): got.append(lax.ppermute(blocks[k], 'seq', pairs))  31.4 us
    ppermute x18, waiting for transfers between devices, from_chips(): got.append(lax.ppermute(blocks[k], 'seq', pairs))  27 us
    ppermute x8, waiting for transfers between devices, up(): lax.ppermute(x, 'seq', [(i, i + 2) for i in range(2 * (hop - 1), seq_size...  26.1 us
    ppermute x18, starting transfers between devices, from_fsdp(): got.append(lax.ppermute(blocks[k], 'fsdp', pairs))  21.6 us
    ppermute x8, starting transfers between devices, up(): lax.ppermute(x, 'seq', [(i, i + 2) for i in range(2 * (hop - 1), seq_size...  16.3 us
  transfers between devices with their start and end apart: 59, of which 25 were waited for; matrix products, arithmetic and copies ran while one was open for 0% of the time, Pallas kernels for 35%

profile of v1, /device:TPU:0, one launch (start us, length us, event | category | flops | bytes accessed | tf_op | source)
XLA Modules:
  0.0 294.4 jit_solution(10254841146551730500)
XLA Ops:
  1.3 3.0 %collective-permute-start = (s32[2]{0:T(128)}, s32[2]{0:T(128)S(1)}, u32[]{:S(2)}, u32[]{:S(2)}) collective-permute-start(s32[2]{0:T(128)} %rest_0_.1), channel_id=1, source_target_pairs={{0,8},{4,12},{8,0},{12,4},{16,24},{20,28},{24,16},{28,20},{1,9},{5... | collective-permute-start | bytes 32 | tf_op jit(solution)/shard_map/ppermute | solution.py:347
  4.3 2.6 collective-permute-start.1
  8.6 1.8 shard_map.103.rest_0_
  11.8 1.5 collective-permute-start.7
  13.3 2.7 collective-permute-done.2.rest_3_
  15.9 1.5 collective-permute-start.8
  20.3 2.6 collective-permute-start.4
  22.9 5.2 %collective-permute-done.8.rest_2_ = bf16[256,512]{1,0:T(8,128)(2,1)S(1)} collective-permute-done((bf16[256,512]{1,0:T(8,128)(2,1)}, bf16[256,512]{1,0:T(8,128)(2,1)S(1)}, u32[]{:S(2)}, u32[]{:S(2)}) %collective-permute-start.8) | collective-permute-done | bytes 262176 | tf_op jit(solution)/shard_map/ppermute | solution.py:340
  29.4 1.5 collective-permute-start.13
  30.9 1.6 collective-permute-start.14
  32.5 8.6 %shard_map.104 = (bf16[2,1024,128]{2,1,0:T(8,128)(2,1)}, bf16[2,1024,128]{2,1,0:T(8,128)(2,1)}, bf16[2,1024,128]{2,1,0:T(8,128)(2,1)}, bf16[2,1024,128]{2,1,0:T(8,128)(2,1)}, bf16[1024,512]{1,0:T(8,128)(2,1)}) custom-call(s32[4]{0:T(128)} %pad_add_fusion.meta, bf16[1024,1024]{1,0:T(8,128)(2,1)} %bitcast.14, bf16[1024,1024]{1,0:T(8,128)(2,1)} %copy-done.1, ...), custom_call_target="tpu_custom_call" | custom-call | flops 2147483648 | bytes 8388624 | tf_op jit(solution)/shard_map/pallas_call | solution.py:43
  43.9 3.0 %collective-permute-start.18 = (bf16[2,1024,128]{2,1,0:T(8,128)(2,1)}, bf16[2,1024,128]{2,1,0:T(8,128)(2,1)S(1)}, u32[]{:S(2)}, u32[]{:S(2)}) collective-permute-start(bf16[2,1024,128]{2,1,0:T(8,128)(2,1)} %get-tuple-element.76.rest_0_), channel_id=1, source_target_pairs={{0,8},{4,12},{8,16},{12,20},{16,24},{20,28},{1,9},{5,13},{9,17},{1... | collective-permute-start | bytes 1572872 | tf_op jit(solution)/shard_map/ppermute | solution.py:351
  46.9 5.1 %collective-permute-start.22 = (bf16[2,1024,128]{2,1,0:T(8,128)(2,1)}, bf16[2,1024,128]{2,1,0:T(8,128)(2,1)S(1)}, u32[]{:S(2)}, u32[]{:S(2)}) collective-permute-start(bf16[2,1024,128]{2,1,0:T(8,128)(2,1)} %get-tuple-element.82.rest_0_), channel_id=1, source_target_pairs={{0,8},{4,12},{8,16},{12,20},{16,24},{20,28},{1,9},{5,13},{9,17},{1... | collective-permute-start | bytes 1572872 | tf_op jit(solution)/shard_map/ppermute | solution.py:351
  52.6 1.9 collective-permute-start.26
  55.1 1.5 collective-permute-start.11
  56.6 9.8 %collective-permute-done.18.rest_1_ = bf16[2,1024,128]{2,1,0:T(8,128)(2,1)S(1)} collective-permute-done((bf16[2,1024,128]{2,1,0:T(8,128)(2,1)}, bf16[2,1024,128]{2,1,0:T(8,128)(2,1)S(1)}, u32[]{:S(2)}, u32[]{:S(2)}) %collective-permute-start.18) | collective-permute-done | bytes 524320 | tf_op jit(solution)/shard_map/ppermute | solution.py:351
  66.4 1.4 collective-permute-start.19
  67.8 9.8 %collective-permute-done.22.rest_1_ = bf16[2,1024,128]{2,1,0:T(8,128)(2,1)S(1)} collective-permute-done((bf16[2,1024,128]{2,1,0:T(8,128)(2,1)}, bf16[2,1024,128]{2,1,0:T(8,128)(2,1)S(1)}, u32[]{:S(2)}, u32[]{:S(2)}) %collective-permute-start.22) | collective-permute-done | bytes 524320 | tf_op jit(solution)/shard_map/ppermute | solution.py:351
  77.6 1.4 collective-permute-start.23
  79.1 6.0 %collective-permute-done.26.rest_1_ = bf16[2,1024,128]{2,1,0:T(8,128)(2,1)S(1)} collective-permute-done((bf16[2,1024,128]{2,1,0:T(8,128)(2,1)}, bf16[2,1024,128]{2,1,0:T(8,128)(2,1)S(1)}, u32[]{:S(2)}, u32[]{:S(2)}) %collective-permute-start.26) | collective-permute-done | bytes 524320 | tf_op jit(solution)/shard_map/ppermute | solution.py:351
  85.8 2.6 shard_map.102
  88.4 8.5 %shard_map.105 = (bf16[2,1024,128]{2,1,0:T(8,128)(2,1)}, bf16[2,1024,128]{2,1,0:T(8,128)(2,1)}, bf16[2,1024,128]{2,1,0:T(8,128)(2,1)}, bf16[2,1024,128]{2,1,0:T(8,128)(2,1)}) custom-call(s32[4]{0:T(128)} %pad_add_fusion.meta, bf16[1024,1024]{1,0:T(8,128)(2,1)} %bitcast.18, bf16[1024,1024]{1,0:T(8,128)(2,1)} %collective-permute-done.12.partner.rest_5_, ...), custom_call_target="tpu_custom_call" | custom-call | flops 2147483648 | bytes 7340048 | tf_op jit(solution)/shard_map/pallas_call | solution.py:43
  96.9 6.5 %shard_map.106 = (bf16[2,1024,128]{2,1,0:T(8,128)(2,1)}, f32[2,1024,128]{2,1,0:T(8,128)}, bf16[2,1024,128]{2,1,0:T(8,128)(2,1)}, bf16[2,128,128]{2,1,0:T(8,128)(2,1)}) custom-call(s32[4]{0:T(128)} %pad_add_fusion.meta, s32[8]{0:T(128)} %get-tuple-element.69.amounts, bf16[2,1024,128]{2,1,0:T(8,128)(2,1)} %get-tuple-element.70.rest_0_, ...), custom_call_target="tpu_custom_call" | custom-call | flops 805306368 | bytes 4390960 | tf_op jit(solution)/shard_map/pallas_call | solution.py:26
  104.7 6.6 %shard_map.108 = (bf16[2,1024,128]{2,1,0:T(8,128)(2,1)}, f32[2,1024,128]{2,1,0:T(8,128)}, bf16[2,1024,128]{2,1,0:T(8,128)(2,1)}, bf16[2,128,128]{2,1,0:T(8,128)(2,1)}) custom-call(s32[4]{0:T(128)} %pad_add_fusion.meta, s32[8]{0:T(128)} %get-tuple-element.69.amounts, bf16[2,1024,128]{2,1,0:T(8,128)(2,1)} %get-tuple-element.76.rest_0_, ...), custom_call_target="tpu_custom_call" | custom-call | flops 805306368 | bytes 4390960 | tf_op jit(solution)/shard_map/pallas_call | solution.py:26
  112.6 6.6 %shard_map.110 = (bf16[2,1024,128]{2,1,0:T(8,128)(2,1)}, f32[2,1024,128]{2,1,0:T(8,128)}, bf16[2,1024,128]{2,1,0:T(8,128)(2,1)}, bf16[2,128,128]{2,1,0:T(8,128)(2,1)}) custom-call(s32[4]{0:T(128)} %pad_add_fusion.meta, s32[8]{0:T(128)} %get-tuple-element.69.amounts, bf16[2,1024,128]{2,1,0:T(8,128)(2,1)} %get-tuple-element.82.rest_0_, ...), custom_call_target="tpu_custom_call" | custom-call | flops 805306368 | bytes 4390960 | tf_op jit(solution)/shard_map/pallas_call | solution.py:26
  121.3 6.6 %shard_map.112 = (bf16[2,1024,128]{2,1,0:T(8,128)(2,1)}, f32[2,1024,128]{2,1,0:T(8,128)}, bf16[2,1024,128]{2,1,0:T(8,128)(2,1)}, bf16[2,128,128]{2,1,0:T(8,128)(2,1)}) custom-call(s32[4]{0:T(128)} %pad_add_fusion.meta, s32[8]{0:T(128)} %get-tuple-element.69.amounts, bf16[2,1024,128]{2,1,0:T(8,128)(2,1)} %get-tuple-element.88.rest_0_, ...), custom_call_target="tpu_custom_call" | custom-call | flops 805306368 | bytes 4390960 | tf_op jit(solution)/shard_map/pallas_call | solution.py:26
  130.6 8.0 %collective-permute-done.20.rest_1_ = bf16[2,1024,128]{2,1,0:T(8,128)(2,1)} collective-permute-done((bf16[2,1024,128]{2,1,0:T(8,128)(2,1)}, bf16[2,1024,128]{2,1,0:T(8,128)(2,1)}, u32[]{:S(2)}, u32[]{:S(2)}) %collective-permute-start.20) | collective-permute-done | bytes 524320 | tf_op jit(solution)/shard_map/ppermute | solution.py:354
  139.9 8.9 %shard_map.116 = (f32[128,1024]{1,0:T(8,128)}, bf16[128,1024]{1,0:T(8,128)(2,1)}, bf16[128,1024]{1,0:T(8,128)(2,1)}, bf16[128,1024]{1,0:T(8,128)(2,1)}) custom-call(s32[4]{0:T(128)} %pad_add_fusion.meta, bf16[2,1024,128]{2,1,0:T(8,128)(2,1)} %get-tuple-element.105.rest_0_, bf16[2,1024,128]{2,1,0:T(8,128)(2,1)} %get-tuple-element.106.rest_1_, ...), custom_call_target="tpu_custom_call" | custom-call | flops 2147483648 | bytes 7602192 | tf_op jit(solution)/shard_map/pallas_call | solution.py:43
  151.0 9.9 %collective-permute-done.28.rest_1_ = bf16[2,1024,128]{2,1,0:T(8,128)(2,1)S(1)} collective-permute-done((bf16[2,1024,128]{2,1,0:T(8,128)(2,1)}, bf16[2,1024,128]{2,1,0:T(8,128)(2,1)S(1)}, u32[]{:S(2)}, u32[]{:S(2)}) %collective-permute-start.28) | collective-permute-done | bytes 524320 | tf_op jit(solution)/shard_map/ppermute | solution.py:354
  160.9 1.5 collective-permute-start.29
  163.2 9.0 %collective-permute-done.17.rest_2_ = bf16[2,1024,128]{2,1,0:T(8,128)(2,1)S(1)} collective-permute-done((bf16[2,1024,128]{2,1,0:T(8,128)(2,1)S(1)}, bf16[2,1024,128]{2,1,0:T(8,128)(2,1)S(1)}, u32[]{:S(2)}, u32[]{:S(2)}) %collective-permute-start.17) | collective-permute-done | bytes 524320 | tf_op jit(solution)/shard_map/ppermute | solution.py:354
  173.0 10.5 %collective-permute-done.21.rest_2_ = bf16[2,1024,128]{2,1,0:T(8,128)(2,1)} collective-permute-done((bf16[2,1024,128]{2,1,0:T(8,128)(2,1)}, bf16[2,1024,128]{2,1,0:T(8,128)(2,1)}, u32[]{:S(2)}, u32[]{:S(2)}) %collective-permute-start.21) | collective-permute-done | bytes 524320 | tf_op jit(solution)/shard_map/ppermute | solution.py:354
  184.2 3.0 %shard_map.107 = (bf16[1024,128]{1,0:T(8,128)(2,1)}, bf16[1024,128]{1,0:T(8,128)(2,1)}) custom-call(s32[4]{0:T(128)} %pad_add_fusion.meta, s32[8]{0:T(128)} %get-tuple-element.69.amounts, f32[2,1024,128]{2,1,0:T(8,128)} %get-tuple-element.73.tap_zero, bf16[2,1024,128]{2,1,0:T(8,128)(2,1)} %get-tuple-element.74.rest_0_, bf16[2,1024,128]{2,1,0:T(8,128)(2,1)} %copy-done.8, ...), custom_call_target="tpu_custom_call" | custom-call | bytes 3145776 | tf_op jit(solution)/shard_map/pallas_call | solution.py:26
  187.1 2.9 shard_map.109
  190.0 7.8 %shard_map.114 = (f32[256,256]{1,0:T(8,128)}, bf16[256,256]{1,0:T(8,128)(2,1)}, bf16[256,256]{1,0:T(8,128)(2,1)}, bf16[256,256]{1,0:T(8,128)(2,1)}, bf16[1024,256]{1,0:T(8,128)(2,1)}) custom-call(s32[4]{0:T(128)} %pad_add_fusion.meta, bf16[1024,128]{1,0:T(8,128)(2,1)} %get-tuple-element.75.rest_0_, bf16[1024,128]{1,0:T(8,128)(2,1)} %get-tuple-element.94.rest_1_, ...), custom_call_target="tpu_custom_call" | custom-call | flops 1073741824 | bytes 6422544 | tf_op jit(solution)/shard_map/pallas_call | solution.py:43
  197.8 1.6 collective-permute-start.33
  201.9 3.0 %shard_map.111 = (bf16[1024,128]{1,0:T(8,128)(2,1)}, bf16[1024,128]{1,0:T(8,128)(2,1)}) custom-call(s32[4]{0:T(128)} %pad_add_fusion.meta, s32[8]{0:T(128)} %get-tuple-element.69.amounts, f32[2,1024,128]{2,1,0:T(8,128)} %get-tuple-element.85.tap_zero, bf16[2,1024,128]{2,1,0:T(8,128)(2,1)} %get-tuple-element.86.rest_0_, bf16[2,1024,128]{2,1,0:T(8,128)(2,1)} %copy-done.6, ...), custom_call_target="tpu_custom_call" | custom-call | bytes 3145776 | tf_op jit(solution)/shard_map/pallas_call | solution.py:26
  204.9 3.0 %shard_map.113 = (bf16[1024,128]{1,0:T(8,128)(2,1)}, bf16[1024,128]{1,0:T(8,128)(2,1)}) custom-call(s32[4]{0:T(128)} %pad_add_fusion.meta, s32[8]{0:T(128)} %get-tuple-element.69.amounts, f32[2,1024,128]{2,1,0:T(8,128)} %get-tuple-element.91.tap_zero, bf16[2,1024,128]{2,1,0:T(8,128)(2,1)} %get-tuple-element.92.rest_0_, bf16[2,1024,128]{2,1,0:T(8,128)(2,1)} %copy-done.7, ...), custom_call_target="tpu_custom_call" | custom-call | bytes 3145776 | tf_op jit(solution)/shard_map/pallas_call | solution.py:26
  208.6 2.8 shard_map.117
  211.3 2.4 collective-permute-start.39
  213.7 7.7 %shard_map.115 = (f32[256,256]{1,0:T(8,128)}, bf16[256,256]{1,0:T(8,128)(2,1)}, bf16[256,256]{1,0:T(8,128)(2,1)}, bf16[256,256]{1,0:T(8,128)(2,1)}, bf16[1024,256]{1,0:T(8,128)(2,1)}) custom-call(s32[4]{0:T(128)} %pad_add_fusion.meta, bf16[1024,128]{1,0:T(8,128)(2,1)} %get-tuple-element.87.rest_0_.rest_2_, bf16[1024,128]{1,0:T(8,128)(2,1)} %get-tuple-element.97.rest_1_, ...), custom_call_target="tpu_custom_call" | custom-call | flops 1073741824 | bytes 6422544 | tf_op jit(solution)/shard_map/pallas_call | solution.py:43
  221.4 1.5 collective-permute-start.46
  223.0 2.4 collective-permute-start.41
  228.0 2.5 collective-permute-done.41.rest_3_
  231.3 1.9 shard_map.118
  236.7 2.8 collective-permute-start.43
  240.0 1.8 collective-permute-start.44
  241.8 1.9 shard_map.120
  243.7 1.7 collective-permute-done.43.rest_2_
  246.9 1.8 shard_map.119.rest_0_
  249.6 2.0 collective-permute-start.50
  251.6 3.0 %collective-permute-done.50.rest_2_ = bf16[64,256]{1,0:T(8,128)(2,1)S(1)} collective-permute-done((bf16[64,256]{1,0:T(8,128)(2,1)}, bf16[64,256]{1,0:T(8,128)(2,1)S(1)}, u32[]{:S(2)}, u32[]{:S(2)}) %collective-permute-start.50) | collective-permute-done | bytes 32800 | tf_op jit(solution)/shard_map/ppermute | solution.py:347
  254.6 3.4 %collective-permute-start.51 = (bf16[64,256]{1,0:T(8,128)(2,1)}, bf16[64,256]{1,0:T(8,128)(2,1)}, u32[]{:S(2)}, u32[]{:S(2)}) collective-permute-start(bf16[64,256]{1,0:T(8,128)(2,1)} %get-tuple-element.129), channel_id=1, source_target_pairs={{0,24},{4,28},{8,16},{12,20},{16,8},{20,12},{24,0},{28,4},{1,25},{... | collective-permute-start | bytes 98312 | tf_op jit(solution)/shard_map/ppermute | solution.py:347
  258.1 2.6 collective-permute-done.51.rest_3_
  260.7 1.5 shard_map.121.rest_0_
  262.2 4.3 %collective-permute-done.52.rest_1_ = bf16[64,256]{1,0:T(8,128)(2,1)S(1)} collective-permute-done((bf16[64,256]{1,0:T(8,128)(2,1)}, bf16[64,256]{1,0:T(8,128)(2,1)S(1)}, u32[]{:S(2)}, u32[]{:S(2)}) %collective-permute-start.52) | collective-permute-done | bytes 32800 | tf_op jit(solution)/shard_map/ppermute | solution.py:347
  266.4 1.8 collective-permute-start.53
  268.3 3.9 %collective-permute-done.53.rest_2_ = bf16[64,256]{1,0:T(8,128)(2,1)S(1)} collective-permute-done((bf16[64,256]{1,0:T(8,128)(2,1)}, bf16[64,256]{1,0:T(8,128)(2,1)S(1)}, u32[]{:S(2)}, u32[]{:S(2)}) %collective-permute-start.53) | collective-permute-done | bytes 32800 | tf_op jit(solution)/shard_map/ppermute | solution.py:347
  272.2 2.6 collective-permute-start.54
  274.8 3.4 %collective-permute-done.54.rest_3_ = bf16[64,256]{1,0:T(8,128)(2,1)} collective-permute-done((bf16[64,256]{1,0:T(8,128)(2,1)}, bf16[64,256]{1,0:T(8,128)(2,1)}, u32[]{:S(2)}, u32[]{:S(2)}) %collective-permute-start.54) | collective-permute-done | bytes 32800 | tf_op jit(solution)/shard_map/ppermute | solution.py:347
  278.2 1.5 shard_map.122.rest_2_
  281.0 2.3 collective-permute-start.58
  283.3 6.6 %signal.1 = bf16[1024,1024]{1,0:T(8,128)(2,1)} custom-call(bf16[1024,1024]{1,0:T(8,128)(2,1)} %bitcast.20, bf16[1024,128]{1,0:T(8,128)(2,1)} %get-tuple-element.75.rest_0_, bf16[1024,128]{1,0:T(8,128)(2,1)} %get-tuple-element.81.rest_2_.rest_1_, bf16[1024,128]{1,0:T(8,128)(2,1)} %get-tuple-element.87.rest_0_.rest_2_, ...), custom_call_target="tpu_custom_call" | custom-call | flops 2147483648 | bytes 8388608 | tf_op jit(solution)/shard_map/signal/pallas_call | solution.py:529
  291.3 3.0 %shard_map.123 = (f32[256,1024]{1,0:T(8,128)}, f32[256,1024]{1,0:T(8,128)}, f32[2,128,128]{2,1,0:T(8,128)}) custom-call(s32[4]{0:T(128)} %pad_add_fusion.meta, bf16[4,192,256]{2,1,0:T(8,128)(2,1)} %shard_map.119.rest_0_, bf16[4,192,256]{2,1,0:T(8,128)(2,1)} %copy-done.10, bf16[4,64,256]{2,1,0:T(8,128)(2,1)} %shard_map.122.rest_2_, ...), custom_call_target="tpu_custom_call" | custom-call | bytes 3538960 | tf_op jit(solution)/shard_map/pallas_call | solution.py:26
  (167 shorter events, 40.5 us)
Async XLA Ops:
  0.6 30.3 %collective-permute-start.6 = (bf16[1024,1024]{1,0:T(8,128)(2,1)}, bf16[1024,1024]{1,0:T(8,128)(2,1)S(1)}, u32[]{:S(2)}, u32[]{:S(2)}) collective-permute-start(bf16[1024,1024]{1,0:T(8,128)(2,1)} %bitcast.13), channel_id=1, source_target_pairs={{0,4},{4,0},{8,12},{12,8},{16,20},{20,16},{24,28},{28,24},{1,5},{5... | collective-permute-start | bytes 6291464 | tf_op jit(solution)/shard_map/ppermute | solution.py:334
  1.2 87.1 %collective-permute-start.12 = (bf16[1024,1024]{1,0:T(8,128)(2,1)}, bf16[1024,1024]{1,0:T(8,128)(2,1)}, u32[]{:S(2)}, u32[]{:S(2)}) collective-permute-start(bf16[1024,1024]{1,0:T(8,128)(2,1)} %bitcast.17), channel_id=1, source_target_pairs={{0,4},{4,0},{8,12},{12,8},{16,20},{20,16},{24,28},{28,24},{1,5},{5... | collective-permute-start | bytes 6291464 | tf_op jit(solution)/shard_map/ppermute | solution.py:334
  1.3 9.1 %collective-permute-start = (s32[2]{0:T(128)}, s32[2]{0:T(128)S(1)}, u32[]{:S(2)}, u32[]{:S(2)}) collective-permute-start(s32[2]{0:T(128)} %rest_0_.1), channel_id=1, source_target_pairs={{0,8},{4,12},{8,0},{12,4},{16,24},{20,28},{24,16},{28,20},{1,9},{5... | collective-permute-start | bytes 32 | tf_op jit(solution)/shard_map/ppermute | solution.py:347
  4.3 7.5 %collective-permute-start.1 = (s32[2]{0:T(128)}, s32[2]{0:T(128)S(1)}, u32[]{:S(2)}, u32[]{:S(2)}) collective-permute-start(s32[2]{0:T(128)} %rest_0_.1), channel_id=1, source_target_pairs={{0,16},{4,20},{8,24},{12,28},{16,0},{20,4},{24,8},{28,12},{1,17},{... | collective-permute-start | bytes 32 | tf_op jit(solution)/shard_map/ppermute | solution.py:347
  6.9 10.6 %collective-permute-start.3 = (bf16[2,128,128]{2,1,0:T(8,128)(2,1)}, bf16[2,128,128]{2,1,0:T(8,128)(2,1)S(1)}, u32[]{:S(2)}, u32[]{:S(2)}) collective-permute-start(bf16[2,128,128]{2,1,0:T(8,128)(2,1)} %rest_4_.1), channel_id=1, source_target_pairs={{0,8},{4,12},{8,0},{12,4},{16,24},{20,28},{24,16},{28,20},{1,9},{5... | collective-permute-start | bytes 196616 | tf_op jit(solution)/shard_map/ppermute | solution.py:347
  10.4 5.5 %collective-permute-start.2 = (s32[2]{0:T(128)}, s32[2]{0:T(128)S(1)}, u32[]{:S(2)}, u32[]{:S(2)}) collective-permute-start(s32[2]{0:T(128)} %rest_0_.1), channel_id=1, source_target_pairs={{0,24},{4,28},{8,16},{12,20},{16,8},{20,12},{24,0},{28,4},{1,25},{... | collective-permute-start | bytes 32 | tf_op jit(solution)/shard_map/ppermute | solution.py:347
  11.8 8.5 %collective-permute-start.7 = (bf16[256,512]{1,0:T(8,128)(2,1)}, bf16[256,512]{1,0:T(8,128)(2,1)S(1)}, u32[]{:S(2)}, u32[]{:S(2)}) collective-permute-start(bf16[256,512]{1,0:T(8,128)(2,1)} %shard_map.103.rest_0_), channel_id=1, source_target_pairs={{0,1},{1,0},{2,3},{3,2},{4,5},{5,4},{6,7},{7,6},{8,9},{9,8},{10,11... | collective-permute-start | bytes 786440 | tf_op jit(solution)/shard_map/ppermute | solution.py:340
  15.9 12.1 %collective-permute-start.8 = (bf16[256,512]{1,0:T(8,128)(2,1)}, bf16[256,512]{1,0:T(8,128)(2,1)S(1)}, u32[]{:S(2)}, u32[]{:S(2)}) collective-permute-start(bf16[256,512]{1,0:T(8,128)(2,1)} %shard_map.103.rest_0_), channel_id=1, source_target_pairs={{0,2},{1,3},{2,0},{3,1},{4,6},{5,7},{6,4},{7,5},{8,10},{9,11},{10,... | collective-permute-start | bytes 786440 | tf_op jit(solution)/shard_map/ppermute | solution.py:340
  17.5 12.0 %collective-permute-start.9 = (bf16[256,512]{1,0:T(8,128)(2,1)}, bf16[256,512]{1,0:T(8,128)(2,1)}, u32[]{:S(2)}, u32[]{:S(2)}) collective-permute-start(bf16[256,512]{1,0:T(8,128)(2,1)} %shard_map.103.rest_0_), channel_id=1, source_target_pairs={{0,3},{1,2},{2,1},{3,0},{4,7},{5,6},{6,5},{7,4},{8,11},{9,10},{10,... | collective-permute-start | bytes 786440 | tf_op jit(solution)/shard_map/ppermute | solution.py:340
  18.9 69.4 %copy-start.12 = (bf16[128,1024]{1,0:T(8,128)(2,1)}, bf16[128,1024]{1,0:T(8,128)(2,1)S(1)}, u32[]{:S(2)}) copy-start(bf16[128,1024]{1,0:T(8,128)(2,1)S(1)} %dynamic-slice_bitcast_fusion.rest_0_) | copy-start | bytes 786436
  20.3 20.9 %collective-permute-start.4 = (bf16[2,128,128]{2,1,0:T(8,128)(2,1)}, bf16[2,128,128]{2,1,0:T(8,128)(2,1)S(1)}, u32[]{:S(2)}, u32[]{:S(2)}) collective-permute-start(bf16[2,128,128]{2,1,0:T(8,128)(2,1)} %rest_4_.1), channel_id=1, source_target_pairs={{0,16},{4,20},{8,24},{12,28},{16,0},{20,4},{24,8},{28,12},{1,17},{... | collective-permute-start | bytes 196616 | tf_op jit(solution)/shard_map/ppermute | solution.py:347
  28.1 14.5 %collective-permute-start.5 = (bf16[2,128,128]{2,1,0:T(8,128)(2,1)}, bf16[2,128,128]{2,1,0:T(8,128)(2,1)S(1)}, u32[]{:S(2)}, u32[]{:S(2)}) collective-permute-start(bf16[2,128,128]{2,1,0:T(8,128)(2,1)} %rest_4_.1), channel_id=1, source_target_pairs={{0,24},{4,28},{8,16},{12,20},{16,8},{20,12},{24,0},{28,4},{1,25},{... | collective-permute-start | bytes 196616 | tf_op jit(solution)/shard_map/ppermute | solution.py:347
  29.4 14.4 %collective-permute-start.13 = (bf16[128,1024]{1,0:T(8,128)(2,1)S(1)}, bf16[128,1024]{1,0:T(8,128)(2,1)S(1)}, u32[]{:S(2)}, u32[]{:S(2)}) collective-permute-start(bf16[128,1024]{1,0:T(8,128)(2,1)S(1)} %dynamic-slice_bitcast_fusion.rest_0_), channel_id=1, source_target_pairs={{0,1},{1,0},{2,3},{3,2},{4,5},{5,4},{6,7},{7,6},{8,9},{9,8},{10,11... | collective-permute-start | bytes 786440 | tf_op jit(solution)/shard_map/ppermute | solution.py:340
  30.9 15.9 %collective-permute-start.14 = (bf16[128,1024]{1,0:T(8,128)(2,1)S(1)}, bf16[128,1024]{1,0:T(8,128)(2,1)S(1)}, u32[]{:S(2)}, u32[]{:S(2)}) collective-permute-start(bf16[128,1024]{1,0:T(8,128)(2,1)S(1)} %dynamic-slice_bitcast_fusion.rest_0_), channel_id=1, source_target_pairs={{0,2},{1,3},{2,0},{3,1},{4,6},{5,7},{6,4},{7,5},{8,10},{9,11},{10,... | collective-permute-start | bytes 786440 | tf_op jit(solution)/shard_map/ppermute | solution.py:340
  41.2 44.5 %copy-start.25 = (bf16[2,128,128]{2,1,0:T(8,128)(2,1)}, bf16[2,128,128]{2,1,0:T(8,128)(2,1)S(1)}, u32[]{:S(2)}) copy-start(bf16[2,128,128]{2,1,0:T(8,128)(2,1)S(1)} %collective-permute-done.4.rest_6_) | copy-start | bytes 196612
  41.2 13.9 %collective-permute-start.10 = (bf16[2,1024,128]{2,1,0:T(8,128)(2,1)}, bf16[2,1024,128]{2,1,0:T(8,128)(2,1)S(1)}, u32[]{:S(2)}, u32[]{:S(2)}) collective-permute-start(bf16[2,1024,128]{2,1,0:T(8,128)(2,1)} %get-tuple-element.70.rest_0_), channel_id=1, source_target_pairs={{0,8},{4,12},{8,16},{12,20},{16,24},{20,28},{1,9},{5,13},{9,17},{1... | collective-permute-start | bytes 1572872 | tf_op jit(solution)/shard_map/ppermute | solution.py:351
  42.6 43.2 %copy-start.26 = (bf16[2,128,128]{2,1,0:T(8,128)(2,1)}, bf16[2,128,128]{2,1,0:T(8,128)(2,1)S(1)}, u32[]{:S(2)}) copy-start(bf16[2,128,128]{2,1,0:T(8,128)(2,1)S(1)} %collective-permute-done.5.rest_7_) | copy-start | bytes 196612
  42.6 9.4 %collective-permute-start.15 = (bf16[128,1024]{1,0:T(8,128)(2,1)S(1)}, bf16[128,1024]{1,0:T(8,128)(2,1)S(1)}, u32[]{:S(2)}, u32[]{:S(2)}) collective-permute-start(bf16[128,1024]{1,0:T(8,128)(2,1)S(1)} %dynamic-slice_bitcast_fusion.rest_0_), channel_id=1, source_target_pairs={{0,3},{1,2},{2,1},{3,0},{4,7},{5,6},{6,5},{7,4},{8,11},{9,10},{10,... | collective-permute-start | bytes 786440 | tf_op jit(solution)/shard_map/ppermute | solution.py:340
  43.9 44.5 %copy-start.39 = (bf16[128,1024]{1,0:T(8,128)(2,1)}, bf16[128,1024]{1,0:T(8,128)(2,1)S(1)}, u32[]{:S(2)}) copy-start(bf16[128,1024]{1,0:T(8,128)(2,1)S(1)} %collective-permute-done.13.rest_1_) | copy-start | bytes 786436
  43.9 22.5 %collective-permute-start.18 = (bf16[2,1024,128]{2,1,0:T(8,128)(2,1)}, bf16[2,1024,128]{2,1,0:T(8,128)(2,1)S(1)}, u32[]{:S(2)}, u32[]{:S(2)}) collective-permute-start(bf16[2,1024,128]{2,1,0:T(8,128)(2,1)} %get-tuple-element.76.rest_0_), channel_id=1, source_target_pairs={{0,8},{4,12},{8,16},{12,20},{16,24},{20,28},{1,9},{5,13},{9,17},{1... | collective-permute-start | bytes 1572872 | tf_op jit(solution)/shard_map/ppermute | solution.py:351
  46.9 30.7 %collective-permute-start.22 = (bf16[2,1024,128]{2,1,0:T(8,128)(2,1)}, bf16[2,1024,128]{2,1,0:T(8,128)(2,1)S(1)}, u32[]{:S(2)}, u32[]{:S(2)}) collective-permute-start(bf16[2,1024,128]{2,1,0:T(8,128)(2,1)} %get-tuple-element.82.rest_0_), channel_id=1, source_target_pairs={{0,8},{4,12},{8,16},{12,20},{16,24},{20,28},{1,9},{5,13},{9,17},{1... | collective-permute-start | bytes 1572872 | tf_op jit(solution)/shard_map/ppermute | solution.py:351
  52.6 32.4 %collective-permute-start.26 = (bf16[2,1024,128]{2,1,0:T(8,128)(2,1)}, bf16[2,1024,128]{2,1,0:T(8,128)(2,1)S(1)}, u32[]{:S(2)}, u32[]{:S(2)}) collective-permute-start(bf16[2,1024,128]{2,1,0:T(8,128)(2,1)} %get-tuple-element.88.rest_0_), channel_id=1, source_target_pairs={{0,8},{4,12},{8,16},{12,20},{16,24},{20,28},{1,9},{5,13},{9,17},{1... | collective-permute-start | bytes 1572872 | tf_op jit(solution)/shard_map/ppermute | solution.py:351
  55.1 41.7 %collective-permute-start.11 = (bf16[2,1024,128]{2,1,0:T(8,128)(2,1)S(1)}, bf16[2,1024,128]{2,1,0:T(8,128)(2,1)}, u32[]{:S(2)}, u32[]{:S(2)}) collective-permute-start(bf16[2,1024,128]{2,1,0:T(8,128)(2,1)S(1)} %collective-permute-done.10.rest_1_), channel_id=1, source_target_pairs={{8,16},{12,20},{16,24},{20,28},{9,17},{13,21},{17,25},{21,29},{10,... | collective-permute-start | bytes 1572872 | tf_op jit(solution)/shard_map/ppermute | solution.py:351
  66.4 38.3 %collective-permute-start.19 = (bf16[2,1024,128]{2,1,0:T(8,128)(2,1)S(1)}, bf16[2,1024,128]{2,1,0:T(8,128)(2,1)}, u32[]{:S(2)}, u32[]{:S(2)}) collective-permute-start(bf16[2,1024,128]{2,1,0:T(8,128)(2,1)S(1)} %collective-permute-done.18.rest_1_), channel_id=1, source_target_pairs={{8,16},{12,20},{16,24},{20,28},{9,17},{13,21},{17,25},{21,29},{10,... | collective-permute-start | bytes 1572872 | tf_op jit(solution)/shard_map/ppermute | solution.py:351
  77.6 35.0 %collective-permute-start.23 = (bf16[2,1024,128]{2,1,0:T(8,128)(2,1)S(1)}, bf16[2,1024,128]{2,1,0:T(8,128)(2,1)}, u32[]{:S(2)}, u32[]{:S(2)}) collective-permute-start(bf16[2,1024,128]{2,1,0:T(8,128)(2,1)S(1)} %collective-permute-done.22.rest_1_), channel_id=1, source_target_pairs={{8,16},{12,20},{16,24},{20,28},{9,17},{13,21},{17,25},{21,29},{10,... | collective-permute-start | bytes 1572872 | tf_op jit(solution)/shard_map/ppermute | solution.py:351
  85.0 35.5 %collective-permute-start.27 = (bf16[2,1024,128]{2,1,0:T(8,128)(2,1)S(1)}, bf16[2,1024,128]{2,1,0:T(8,128)(2,1)S(1)}, u32[]{:S(2)}, u32[]{:S(2)}) collective-permute-start(bf16[2,1024,128]{2,1,0:T(8,128)(2,1)S(1)} %collective-permute-done.26.rest_1_), channel_id=1, source_target_pairs={{8,16},{12,20},{16,24},{20,28},{9,17},{13,21},{17,25},{21,29},{10,... | collective-permute-start | bytes 1572872 | tf_op jit(solution)/shard_map/ppermute | solution.py:351
  103.4 25.9 %collective-permute-start.16 = (bf16[2,1024,128]{2,1,0:T(8,128)(2,1)}, bf16[2,1024,128]{2,1,0:T(8,128)(2,1)S(1)}, u32[]{:S(2)}, u32[]{:S(2)}) collective-permute-start(bf16[2,1024,128]{2,1,0:T(8,128)(2,1)} %get-tuple-element.74.rest_0_), channel_id=1, source_target_pairs={{8,0},{12,4},{16,8},{20,12},{24,16},{28,20},{9,1},{13,5},{17,9},{2... | collective-permute-start | bytes 1572872 | tf_op jit(solution)/shard_map/ppermute | solution.py:354
  111.3 27.3 %collective-permute-start.20 = (bf16[2,1024,128]{2,1,0:T(8,128)(2,1)}, bf16[2,1024,128]{2,1,0:T(8,128)(2,1)}, u32[]{:S(2)}, u32[]{:S(2)}) collective-permute-start(bf16[2,1024,128]{2,1,0:T(8,128)(2,1)} %get-tuple-element.80.rest_0_), channel_id=1, source_target_pairs={{8,0},{12,4},{16,8},{20,12},{24,16},{28,20},{9,1},{13,5},{17,9},{2... | collective-permute-start | bytes 1572872 | tf_op jit(solution)/shard_map/ppermute | solution.py:354
  119.2 30.5 %collective-permute-start.24 = (bf16[2,1024,128]{2,1,0:T(8,128)(2,1)}, bf16[2,1024,128]{2,1,0:T(8,128)(2,1)S(1)}, u32[]{:S(2)}, u32[]{:S(2)}) collective-permute-start(bf16[2,1024,128]{2,1,0:T(8,128)(2,1)} %get-tuple-element.86.rest_0_), channel_id=1, source_target_pairs={{8,0},{12,4},{16,8},{20,12},{24,16},{28,20},{9,1},{13,5},{17,9},{2... | collective-permute-start | bytes 1572872 | tf_op jit(solution)/shard_map/ppermute | solution.py:354
  128.0 33.0 %collective-permute-start.28 = (bf16[2,1024,128]{2,1,0:T(8,128)(2,1)}, bf16[2,1024,128]{2,1,0:T(8,128)(2,1)S(1)}, u32[]{:S(2)}, u32[]{:S(2)}) collective-permute-start(bf16[2,1024,128]{2,1,0:T(8,128)(2,1)} %get-tuple-element.92.rest_0_), channel_id=1, source_target_pairs={{8,0},{12,4},{16,8},{20,12},{24,16},{28,20},{9,1},{13,5},{17,9},{2... | collective-permute-start | bytes 1572872 | tf_op jit(solution)/shard_map/ppermute | solution.py:354
  129.3 42.9 %collective-permute-start.17 = (bf16[2,1024,128]{2,1,0:T(8,128)(2,1)S(1)}, bf16[2,1024,128]{2,1,0:T(8,128)(2,1)S(1)}, u32[]{:S(2)}, u32[]{:S(2)}) collective-permute-start(bf16[2,1024,128]{2,1,0:T(8,128)(2,1)S(1)} %collective-permute-done.16.rest_1_), channel_id=1, source_target_pairs={{8,0},{12,4},{16,8},{20,12},{9,1},{13,5},{17,9},{21,13},{10,2},{14... | collective-permute-start | bytes 1572872 | tf_op jit(solution)/shard_map/ppermute | solution.py:354
  138.6 44.9 %collective-permute-start.21 = (bf16[2,1024,128]{2,1,0:T(8,128)(2,1)}, bf16[2,1024,128]{2,1,0:T(8,128)(2,1)}, u32[]{:S(2)}, u32[]{:S(2)}) collective-permute-start(bf16[2,1024,128]{2,1,0:T(8,128)(2,1)} %collective-permute-done.20.rest_1_), channel_id=1, source_target_pairs={{8,0},{12,4},{16,8},{20,12},{9,1},{13,5},{17,9},{21,13},{10,2},{14... | collective-permute-start | bytes 1572872 | tf_op jit(solution)/shard_map/ppermute | solution.py:354
  148.8 13.6 %collective-permute-start.36 = (bf16[128,1024]{1,0:T(8,128)(2,1)}, bf16[128,1024]{1,0:T(8,128)(2,1)S(1)}, u32[]{:S(2)}, u32[]{:S(2)}) collective-permute-start(bf16[128,1024]{1,0:T(8,128)(2,1)} %get-tuple-element.110), channel_id=1, source_target_pairs={{0,1},{1,0},{2,3},{3,2},{4,5},{5,4},{6,7},{7,6},{8,9},{9,8},{10,11... | collective-permute-start | bytes 786440 | tf_op jit(solution)/shard_map/ppermute | solution.py:340
  149.7 49.6 %collective-permute-start.25 = (bf16[2,1024,128]{2,1,0:T(8,128)(2,1)S(1)}, bf16[2,1024,128]{2,1,0:T(8,128)(2,1)}, u32[]{:S(2)}, u32[]{:S(2)}) collective-permute-start(bf16[2,1024,128]{2,1,0:T(8,128)(2,1)S(1)} %collective-permute-done.24.rest_1_), channel_id=1, source_target_pairs={{8,0},{12,4},{16,8},{20,12},{9,1},{13,5},{17,9},{21,13},{10,2},{14... | collective-permute-start | bytes 1572872 | tf_op jit(solution)/shard_map/ppermute | solution.py:354
  160.9 39.7 %collective-permute-start.29 = (bf16[2,1024,128]{2,1,0:T(8,128)(2,1)S(1)}, bf16[2,1024,128]{2,1,0:T(8,128)(2,1)}, u32[]{:S(2)}, u32[]{:S(2)}) collective-permute-start(bf16[2,1024,128]{2,1,0:T(8,128)(2,1)S(1)} %collective-permute-done.28.rest_1_), channel_id=1, source_target_pairs={{8,0},{12,4},{16,8},{20,12},{9,1},{13,5},{17,9},{21,13},{10,2},{14... | collective-permute-start | bytes 1572872 | tf_op jit(solution)/shard_map/ppermute | solution.py:354
  162.4 42.4 %copy-start.11 = (bf16[128,1024]{1,0:T(8,128)(2,1)}, bf16[128,1024]{1,0:T(8,128)(2,1)S(1)}, u32[]{:S(2)}) copy-start(bf16[128,1024]{1,0:T(8,128)(2,1)S(1)} %collective-permute-done.36.rest_5_) | copy-start | bytes 786436
  162.4 35.3 %collective-permute-start.37 = (bf16[128,1024]{1,0:T(8,128)(2,1)}, bf16[128,1024]{1,0:T(8,128)(2,1)}, u32[]{:S(2)}, u32[]{:S(2)}) collective-permute-start(bf16[128,1024]{1,0:T(8,128)(2,1)} %get-tuple-element.111), channel_id=1, source_target_pairs={{0,2},{1,3},{2,0},{3,1},{4,6},{5,7},{6,4},{7,5},{8,10},{9,11},{10,... | collective-permute-start | bytes 786440 | tf_op jit(solution)/shard_map/ppermute | solution.py:340
  173.0 106.7 %collective-permute-start.32 = (bf16[1024,512]{1,0:T(8,128)(2,1)S(1)}, bf16[1024,512]{1,0:T(8,128)(2,1)S(1)}, u32[]{:S(2)}, u32[]{:S(2)}) collective-permute-start(bf16[1024,512]{1,0:T(8,128)(2,1)S(1)} %copy-done.2), channel_id=1, source_target_pairs={{0,4},{4,0},{8,12},{12,8},{16,20},{20,16},{24,28},{28,24},{1,5},{5... | collective-permute-start | bytes 3145736 | tf_op jit(solution)/shard_map/ppermute | solution.py:334
  183.5 24.3 %collective-permute-start.38 = (bf16[128,1024]{1,0:T(8,128)(2,1)}, bf16[128,1024]{1,0:T(8,128)(2,1)}, u32[]{:S(2)}, u32[]{:S(2)}) collective-permute-start(bf16[128,1024]{1,0:T(8,128)(2,1)} %get-tuple-element.112), channel_id=1, source_target_pairs={{0,3},{1,2},{2,1},{3,0},{4,7},{5,6},{6,5},{7,4},{8,11},{9,10},{10,... | collective-permute-start | bytes 786440 | tf_op jit(solution)/shard_map/ppermute | solution.py:340
  197.8 10.0 %collective-permute-start.33 = (bf16[256,256]{1,0:T(8,128)(2,1)}, bf16[256,256]{1,0:T(8,128)(2,1)S(1)}, u32[]{:S(2)}, u32[]{:S(2)}) collective-permute-start(bf16[256,256]{1,0:T(8,128)(2,1)} %get-tuple-element.102), channel_id=1, source_target_pairs={{0,1},{1,0},{2,3},{3,2},{4,5},{5,4},{6,7},{7,6},{8,9},{9,8},{10,11... | collective-permute-start | bytes 393224 | tf_op jit(solution)/shard_map/ppermute | solution.py:340
  199.3 8.5 %collective-permute-start.34 = (bf16[256,256]{1,0:T(8,128)(2,1)}, bf16[256,256]{1,0:T(8,128)(2,1)S(1)}, u32[]{:S(2)}, u32[]{:S(2)}) collective-permute-start(bf16[256,256]{1,0:T(8,128)(2,1)} %get-tuple-element.103), channel_id=1, source_target_pairs={{0,2},{1,3},{2,0},{3,1},{4,6},{5,7},{6,4},{7,5},{8,10},{9,11},{10,... | collective-permute-start | bytes 393224 | tf_op jit(solution)/shard_map/ppermute | solution.py:340
  200.7 7.2 %collective-permute-start.35 = (bf16[256,256]{1,0:T(8,128)(2,1)}, bf16[256,256]{1,0:T(8,128)(2,1)S(1)}, u32[]{:S(2)}, u32[]{:S(2)}) collective-permute-start(bf16[256,256]{1,0:T(8,128)(2,1)} %get-tuple-element.104), channel_id=1, source_target_pairs={{0,3},{1,2},{2,1},{3,0},{4,7},{5,6},{6,5},{7,4},{8,11},{9,10},{10,... | collective-permute-start | bytes 393224 | tf_op jit(solution)/shard_map/ppermute | solution.py:340
  211.3 15.3 %collective-permute-start.39 = (bf16[320,256]{1,0:T(8,128)(2,1)}, bf16[320,256]{1,0:T(8,128)(2,1)S(1)}, u32[]{:S(2)}, u32[]{:S(2)}) collective-permute-start(bf16[320,256]{1,0:T(8,128)(2,1)} %get-tuple-element.118), channel_id=1, source_target_pairs={{0,8},{4,12},{8,0},{12,4},{16,24},{20,28},{24,16},{28,20},{1,9},{5... | collective-permute-start | bytes 491528 | tf_op jit(solution)/shard_map/ppermute | solution.py:347
  213.7 13.5 %collective-permute-start.40 = (bf16[320,256]{1,0:T(8,128)(2,1)}, bf16[320,256]{1,0:T(8,128)(2,1)S(1)}, u32[]{:S(2)}, u32[]{:S(2)}) collective-permute-start(bf16[320,256]{1,0:T(8,128)(2,1)} %get-tuple-element.119), channel_id=1, source_target_pairs={{0,16},{4,20},{8,24},{12,28},{16,0},{20,4},{24,8},{28,12},{1,17},{... | collective-permute-start | bytes 491528 | tf_op jit(solution)/shard_map/ppermute | solution.py:347
  221.4 5.2 %collective-permute-start.46 = (bf16[256,256]{1,0:T(8,128)(2,1)}, bf16[256,256]{1,0:T(8,128)(2,1)S(1)}, u32[]{:S(2)}, u32[]{:S(2)}) collective-permute-start(bf16[256,256]{1,0:T(8,128)(2,1)} %get-tuple-element.123), channel_id=1, source_target_pairs={{0,1},{1,0},{2,3},{3,2},{4,5},{5,4},{6,7},{7,6},{8,9},{9,8},{10,11... | collective-permute-start | bytes 393224 | tf_op jit(solution)/shard_map/ppermute | solution.py:340
  223.0 7.5 %collective-permute-start.41 = (bf16[320,256]{1,0:T(8,128)(2,1)}, bf16[320,256]{1,0:T(8,128)(2,1)}, u32[]{:S(2)}, u32[]{:S(2)}) collective-permute-start(bf16[320,256]{1,0:T(8,128)(2,1)} %get-tuple-element.120), channel_id=1, source_target_pairs={{0,24},{4,28},{8,16},{12,20},{16,8},{20,12},{24,0},{28,4},{1,25},{... | collective-permute-start | bytes 491528 | tf_op jit(solution)/shard_map/ppermute | solution.py:347
  226.7 54.3 %collective-permute-start.30 = (bf16[1024,256]{1,0:T(8,128)(2,1)}, bf16[1024,256]{1,0:T(8,128)(2,1)S(1)}, u32[]{:S(2)}, u32[]{:S(2)}) collective-permute-start(bf16[1024,256]{1,0:T(8,128)(2,1)} %get-tuple-element.96), channel_id=1, source_target_pairs={{0,4},{4,0},{8,12},{12,8},{16,20},{20,16},{24,28},{28,24},{1,5},{5... | collective-permute-start | bytes 1572872 | tf_op jit(solution)/shard_map/ppermute | solution.py:334
  226.7 54.3 %collective-permute-start.31 = (bf16[1024,256]{1,0:T(8,128)(2,1)}, bf16[1024,256]{1,0:T(8,128)(2,1)S(1)}, u32[]{:S(2)}, u32[]{:S(2)}) collective-permute-start(bf16[1024,256]{1,0:T(8,128)(2,1)} %get-tuple-element.99), channel_id=1, source_target_pairs={{0,4},{4,0},{8,12},{12,8},{16,20},{20,16},{24,28},{28,24},{1,5},{5... | collective-permute-start | bytes 1572872 | tf_op jit(solution)/shard_map/ppermute | solution.py:334
  227.2 7.2 %collective-permute-start.47 = (bf16[256,256]{1,0:T(8,128)(2,1)}, bf16[256,256]{1,0:T(8,128)(2,1)}, u32[]{:S(2)}, u32[]{:S(2)}) collective-permute-start(bf16[256,256]{1,0:T(8,128)(2,1)} %get-tuple-element.124), channel_id=1, source_target_pairs={{0,2},{1,3},{2,0},{3,1},{4,6},{5,7},{6,4},{7,5},{8,10},{9,11},{10,... | collective-permute-start | bytes 393224 | tf_op jit(solution)/shard_map/ppermute | solution.py:340
  230.5 6.2 %collective-permute-start.48 = (bf16[256,256]{1,0:T(8,128)(2,1)}, bf16[256,256]{1,0:T(8,128)(2,1)}, u32[]{:S(2)}, u32[]{:S(2)}) collective-permute-start(bf16[256,256]{1,0:T(8,128)(2,1)} %get-tuple-element.125), channel_id=1, source_target_pairs={{0,3},{1,2},{2,1},{3,0},{4,7},{5,6},{6,5},{7,4},{8,11},{9,10},{10,... | collective-permute-start | bytes 393224 | tf_op jit(solution)/shard_map/ppermute | solution.py:340
  234.4 5.6 %collective-permute-start.42 = (bf16[192,256]{1,0:T(8,128)(2,1)}, bf16[192,256]{1,0:T(8,128)(2,1)S(1)}, u32[]{:S(2)}, u32[]{:S(2)}) collective-permute-start(bf16[192,256]{1,0:T(8,128)(2,1)} %get-tuple-element.121.rest_0_), channel_id=1, source_target_pairs={{0,8},{4,12},{8,0},{12,4},{16,24},{20,28},{24,16},{28,20},{1,9},{5... | collective-permute-start | bytes 294920 | tf_op jit(solution)/shard_map/ppermute | solution.py:347
  236.7 8.8 %collective-permute-start.43 = (bf16[192,256]{1,0:T(8,128)(2,1)}, bf16[192,256]{1,0:T(8,128)(2,1)S(1)}, u32[]{:S(2)}, u32[]{:S(2)}) collective-permute-start(bf16[192,256]{1,0:T(8,128)(2,1)} %get-tuple-element.121.rest_0_), channel_id=1, source_target_pairs={{0,16},{4,20},{8,24},{12,28},{16,0},{20,4},{24,8},{28,12},{1,17},{... | collective-permute-start | bytes 294920 | tf_op jit(solution)/shard_map/ppermute | solution.py:347
  240.0 6.8 %collective-permute-start.44 = (bf16[192,256]{1,0:T(8,128)(2,1)}, bf16[192,256]{1,0:T(8,128)(2,1)}, u32[]{:S(2)}, u32[]{:S(2)}) collective-permute-start(bf16[192,256]{1,0:T(8,128)(2,1)} %get-tuple-element.121.rest_0_), channel_id=1, source_target_pairs={{0,24},{4,28},{8,16},{12,20},{16,8},{20,12},{24,0},{28,4},{1,25},{... | collective-permute-start | bytes 294920 | tf_op jit(solution)/shard_map/ppermute | solution.py:347
  245.5 4.1 %collective-permute-start.49 = (bf16[64,256]{1,0:T(8,128)(2,1)}, bf16[64,256]{1,0:T(8,128)(2,1)S(1)}, u32[]{:S(2)}, u32[]{:S(2)}) collective-permute-start(bf16[64,256]{1,0:T(8,128)(2,1)} %get-tuple-element.127), channel_id=1, source_target_pairs={{0,8},{4,12},{8,0},{12,4},{16,24},{20,28},{24,16},{28,20},{1,9},{5... | collective-permute-start | bytes 98312 | tf_op jit(solution)/shard_map/ppermute | solution.py:347
  248.7 41.2 %collective-permute-start.45 = (bf16[4,192,256]{2,1,0:T(8,128)(2,1)}, bf16[4,192,256]{2,1,0:T(8,128)(2,1)S(1)}, u32[]{:S(2)}, u32[]{:S(2)}) collective-permute-start(bf16[4,192,256]{2,1,0:T(8,128)(2,1)} %shard_map.119.rest_0_), channel_id=1, source_target_pairs={{0,4},{4,0},{8,12},{12,8},{16,20},{20,16},{24,28},{28,24},{1,5},{5... | collective-permute-start | bytes 1179656 | tf_op jit(solution)/shard_map/ppermute | solution.py:334
  249.6 5.0 %collective-permute-start.50 = (bf16[64,256]{1,0:T(8,128)(2,1)}, bf16[64,256]{1,0:T(8,128)(2,1)S(1)}, u32[]{:S(2)}, u32[]{:S(2)}) collective-permute-start(bf16[64,256]{1,0:T(8,128)(2,1)} %get-tuple-element.128), channel_id=1, source_target_pairs={{0,16},{4,20},{8,24},{12,28},{16,0},{20,4},{24,8},{28,12},{1,17},{... | collective-permute-start | bytes 98312 | tf_op jit(solution)/shard_map/ppermute | solution.py:347
  254.6 6.0 %collective-permute-start.51 = (bf16[64,256]{1,0:T(8,128)(2,1)}, bf16[64,256]{1,0:T(8,128)(2,1)}, u32[]{:S(2)}, u32[]{:S(2)}) collective-permute-start(bf16[64,256]{1,0:T(8,128)(2,1)} %get-tuple-element.129), channel_id=1, source_target_pairs={{0,24},{4,28},{8,16},{12,20},{16,8},{20,12},{24,0},{28,4},{1,25},{... | collective-permute-start | bytes 98312 | tf_op jit(solution)/shard_map/ppermute | solution.py:347
  262.2 4.3 %collective-permute-start.52 = (bf16[64,256]{1,0:T(8,128)(2,1)}, bf16[64,256]{1,0:T(8,128)(2,1)S(1)}, u32[]{:S(2)}, u32[]{:S(2)}) collective-permute-start(bf16[64,256]{1,0:T(8,128)(2,1)} %shard_map.121.rest_0_), channel_id=1, source_target_pairs={{0,8},{4,12},{8,0},{12,4},{16,24},{20,28},{24,16},{28,20},{1,9},{5... | collective-permute-start | bytes 98312 | tf_op jit(solution)/shard_map/ppermute | solution.py:347
  266.4 5.7 %collective-permute-start.53 = (bf16[64,256]{1,0:T(8,128)(2,1)}, bf16[64,256]{1,0:T(8,128)(2,1)S(1)}, u32[]{:S(2)}, u32[]{:S(2)}) collective-permute-start(bf16[64,256]{1,0:T(8,128)(2,1)} %shard_map.121.rest_0_), channel_id=1, source_target_pairs={{0,16},{4,20},{8,24},{12,28},{16,0},{20,4},{24,8},{28,12},{1,17},{... | collective-permute-start | bytes 98312 | tf_op jit(solution)/shard_map/ppermute | solution.py:347
  272.2 6.0 %collective-permute-start.54 = (bf16[64,256]{1,0:T(8,128)(2,1)}, bf16[64,256]{1,0:T(8,128)(2,1)}, u32[]{:S(2)}, u32[]{:S(2)}) collective-permute-start(bf16[64,256]{1,0:T(8,128)(2,1)} %shard_map.121.rest_0_), channel_id=1, source_target_pairs={{0,24},{4,28},{8,16},{12,20},{16,8},{20,12},{24,0},{28,4},{1,25},{... | collective-permute-start | bytes 98312 | tf_op jit(solution)/shard_map/ppermute | solution.py:347
  279.7 10.2 %collective-permute-start.55 = (bf16[4,64,256]{2,1,0:T(8,128)(2,1)}, bf16[4,64,256]{2,1,0:T(8,128)(2,1)}, u32[]{:S(2)}, u32[]{:S(2)}) collective-permute-start(bf16[4,64,256]{2,1,0:T(8,128)(2,1)} %shard_map.122.rest_2_), channel_id=1, source_target_pairs={{0,4},{4,0},{8,12},{12,8},{16,20},{20,16},{24,28},{28,24},{1,5},{5... | collective-permute-start | bytes 393224 | tf_op jit(solution)/shard_map/ppermute | solution.py:334
  279.7 10.2 %collective-permute-start.56 = (bf16[128,256]{1,0:T(8,128)(2,1)}, bf16[128,256]{1,0:T(8,128)(2,1)S(1)}, u32[]{:S(2)}, u32[]{:S(2)}) collective-permute-start(bf16[128,256]{1,0:T(8,128)(2,1)} %get-tuple-element.130.rest_4_), channel_id=1, source_target_pairs={{0,1},{1,0},{2,3},{3,2},{4,5},{5,4},{6,7},{7,6},{8,9},{9,8},{10,11... | collective-permute-start | bytes 196616 | tf_op jit(solution)/shard_map/ppermute | solution.py:340
  280.9 9.0 %collective-permute-start.57 = (bf16[128,256]{1,0:T(8,128)(2,1)}, bf16[128,256]{1,0:T(8,128)(2,1)S(1)}, u32[]{:S(2)}, u32[]{:S(2)}) collective-permute-start(bf16[128,256]{1,0:T(8,128)(2,1)} %get-tuple-element.130.rest_4_), channel_id=1, source_target_pairs={{0,2},{1,3},{2,0},{3,1},{4,6},{5,7},{6,4},{7,5},{8,10},{9,11},{10,... | collective-permute-start | bytes 196616 | tf_op jit(solution)/shard_map/ppermute | solution.py:340
  281.0 9.0 %collective-permute-start.58 = (bf16[128,256]{1,0:T(8,128)(2,1)}, bf16[128,256]{1,0:T(8,128)(2,1)S(1)}, u32[]{:S(2)}, u32[]{:S(2)}) collective-permute-start(bf16[128,256]{1,0:T(8,128)(2,1)} %get-tuple-element.130.rest_4_), channel_id=1, source_target_pairs={{0,3},{1,2},{2,1},{3,0},{4,7},{5,6},{6,5},{7,4},{8,11},{9,10},{10,... | collective-permute-start | bytes 196616 | tf_op jit(solution)/shard_map/ppermute | solution.py:340
  (39 other events, 480.6 us)

commit v2 on v1

--- a/solution.py
+++ b/solution.py
@@ -30,7 +30,7 @@
         out_specs=tuple([SM] * small + [VM] * (len(outs) - small)),
         scratch_shapes=list(scratch),
         cost_estimate=pl.CostEstimate(flops=flops, bytes_accessed=moved, transcendentals=0),
-        compiler_params=pltpu.CompilerParams(vmem_limit_bytes=60 * 1024 * 1024),
+        compiler_params=pltpu.CompilerParams(vmem_limit_bytes=20 * 1024 * 1024),
     )(*ins)
 
 
@@ -38,64 +38,23 @@
     return jax.ShapeDtypeStruct(dims, kind)
 
 
-def tiled(body, steps, outs, ins, scratch=(), flops=0):
-    moved = sum(math.prod(x[0].shape) * x[0].dtype.itemsize for x in list(ins) + list(outs))
-    return pl.pallas_call(
-        body,
-        grid=(steps,),
-        out_shape=tuple(x[0] for x in outs),
-        in_specs=[SM] + [pl.BlockSpec(x[1], x[2]) for x in ins[1:]],
-        out_specs=tuple(pl.BlockSpec(x[1], x[2]) for x in outs),
-        scratch_shapes=list(scratch),
-        cost_estimate=pl.CostEstimate(flops=flops, bytes_accessed=moved, transcendentals=0),
-        compiler_params=pltpu.CompilerParams(vmem_limit_bytes=60 * 1024 * 1024),
-    )(*[x[0] for x in ins])
-
-
-def fixed(x):
-    return (x, x.shape, lambda i: (0,) * len(x.shape))
-
-
-def forward_body(parts, steps, meta, own, partner, *rest):
+def product_body(parts, tile, turned, meta, own, partner, *rest):
     weights, outs = rest[:parts], rest[parts:]
     targets, panel = outs[:-1], outs[-1]
     rows = weights[0].shape[0]
-    at = pl.program_id(0)
-
-    @pl.when(at == 0)
-    def _():
-        for k in range(parts):
-            start = pl.multiple_of((meta[0] ^ k) * rows, rows)
-            panel[pl.ds(start, rows), :] = weights[k][...]
-
-    def work(source):
-        got = dot(source[...], panel[...], 1, 0).astype(BF)
-        for j, target in enumerate(targets):
-            target[0] = got[:, j * LANES : (j + 1) * LANES]
-
-    pl.when(at < steps)(lambda: work(own))
-    pl.when(at >= steps)(lambda: work(partner))
-
-
-def upstream_body(parts, steps, meta, own, partner, *rest):
-    weights, outs = rest[:parts], rest[parts:]
-    targets, panel = outs[:-1], outs[-1]
-    rows = weights[0].shape[0]
-    at = pl.program_id(0)
-
-    @pl.when(at == 0)
-    def _():
-        for k in range(parts):
-            start = pl.multiple_of((meta[0] ^ k) * rows, rows)
-            panel[pl.ds(start, rows), :] = weights[k][...]
-
-    def work(source):
-        got = dot(source[...], panel[...], 1, 1).astype(BF)
-        for j, target in enumerate(targets):
-            target[0] = got[:, j * LANES : (j + 1) * LANES]
-
-    pl.when(at < steps)(lambda: work(own))
-    pl.when(at >= steps)(lambda: work(partner))
+    for k in range(parts):
+        start = pl.multiple_of((meta[0] ^ k) * rows, rows)
+        panel[pl.ds(start, rows), :] = weights[k][...]
+    for slot, source in enumerate((own, partner)):
+
+        def step(i, carry, slot=slot, source=source):
+            at = pl.multiple_of(i * tile, tile)
+            got = dot(source[pl.ds(at, tile), :], panel[...], 1, int(turned)).astype(BF)
+            for j, target in enumerate(targets):
+                target[slot, pl.ds(at, tile), :] = got[:, j * LANES : (j + 1) * LANES]
+            return carry
+
+        lax.fori_loop(0, source.shape[0] // tile, step, 0)
 
 
 def select_lanes(a, b):
@@ -179,40 +138,51 @@
         lax.fori_loop(0, half // tile, step, 0)
 
 
-def outer_body(chunks, parts, steps, by_rows, split, meta, *rest):
+def outer_body(chunks, parts, tile, by_rows, split, meta, *rest):
     count = chunks * (2 if split else 1)
     lefts, rest = rest[:count], rest[count:]
     rights, outs, total = rest[:2], rest[2:-1], rest[-1]
-    at = pl.program_id(0)
-
-    @pl.when(at == 0)
-    def _():
-        total[...] = jnp.zeros_like(total)
-
-    def work(slot):
-        if split:
-            left = [lefts[2 * j + slot][...] for j in range(chunks)]
+    total[...] = jnp.zeros_like(total)
+    for slot in range(2):
+
+        def step(i, carry, slot=slot):
+            at = pl.multiple_of(i * tile, tile)
+            if split:
+                left = [lefts[2 * j + slot][pl.ds(at, tile), :] for j in range(chunks)]
+            else:
+                left = [lefts[j][slot, pl.ds(at, tile), :] for j in range(chunks)]
+            left = jnp.concatenate(left, axis=1)
+            if split and slot == 1:
+                outs[parts][pl.ds(at, tile), :] = left
+            total[...] += dot(left, rights[slot][pl.ds(at, tile), :], 0, 0)
+            return carry
+
+        lax.fori_loop(0, rights[slot].shape[0] // tile, step, 0)
+    rows, columns = outs[0].shape
+    for k in range(parts):
+        if by_rows:
+            start = pl.multiple_of((meta[0] ^ k) * rows, rows)
+            got = total[pl.ds(start, rows), :]
         else:
-            left = [lefts[j][0] for j in range(chunks)]
-        left = jnp.concatenate(left, axis=1)
-        if split and slot == 1:
-            outs[parts][...] = left
-        total[...] += dot(left, rights[slot][...], 0, 0)
-
-    pl.when(at < steps)(lambda: work(0))
-    pl.when(at >= steps)(lambda: work(1))
-
-    @pl.when(at == 2 * steps - 1)
-    def _():
-        rows, columns = outs[0].shape
-        for k in range(parts):
-            if by_rows:
-                start = pl.multiple_of((meta[0] ^ k) * rows, rows)
-                got = total[pl.ds(start, rows), :]
-            else:
-                start = pl.multiple_of((meta[0] ^ k) * columns, columns)
-                got = total[:, pl.ds(start, columns)]
-            outs[k][...] = got.astype(outs[k].dtype)
+            start = pl.multiple_of((meta[0] ^ k) * columns, columns)
+            got = total[:, pl.ds(start, columns)]
+        outs[k][...] = got.astype(outs[k].dtype)
+
+
+def signal_body(tile, base, *rest):
+    side, side_far, target = rest[-3:]
+    count = (len(rest) - 3) // 3 * 2
+    mixes, others = rest[:count], rest[count:-3]
+
+    def step(i, carry):
+        at = pl.multiple_of(i * tile, tile)
+        mix = jnp.concatenate([x[pl.ds(at, tile), :] for x in mixes], axis=1)
+        other = jnp.concatenate([x[pl.ds(at, tile), :] for x in others], axis=1)
+        acc = base[pl.ds(at, tile), :].astype(F32) + dot(mix, side[...], 1, 1)
+        target[pl.ds(at, tile), :] = (acc + dot(other, side_far[...], 1, 1)).astype(BF)
+        return carry
+
+    lax.fori_loop(0, base.shape[0] // tile, step, 0)
 
 
 def tree(values):
@@ -378,33 +348,18 @@
     amounts, kernels = taps[0], taps[1:]
 
     series = shape((2, samples, LANES), BF)
-    tile = min(256, samples)
-    steps = samples // tile
-
-    def near(x):
-        block_shape = (tile, x.shape[1])
-        return (x, block_shape, lambda i: (jnp.minimum(i, steps - 1), 0))
-
-    def far(x):
-        block_shape = (tile, x.shape[1])
-        return (x, block_shape, lambda i: (jnp.maximum(i - steps, 0), 0))
-
-    def both(x):
-        return (x, (1, tile, LANES), lambda i: (i // steps, i % steps, 0))
-
-    got = tiled(
-        functools.partial(forward_body, fsdp_size, steps),
-        2 * steps,
-        [both(series)] * chunks + [fixed(shape((channels, share), BF))],
-        [(where,), near(record), far(record_far)] + [fixed(x) for x in in_parts],
+    tile = min(512, samples)
+    got = call(
+        functools.partial(product_body, fsdp_size, tile, False),
+        [series] * chunks + [shape((channels, share), BF)],
+        [where, record, record_far] + in_parts,
         flops=2 * block * channels * share,
     )
     projected, panel = got[:-1], got[-1]
-    grad_gated = tiled(
-        functools.partial(upstream_body, fsdp_size, steps),
-        2 * steps,
-        [both(series)] * chunks,
-        [(where,), near(upstream), far(upstream_far)] + [fixed(x) for x in out_parts],
+    grad_gated = call(
+        functools.partial(product_body, fsdp_size, tile, True),
+        [series] * chunks,
+        [where, upstream, upstream_far] + out_parts,
         scratch=[pltpu.VMEM((share, channels), BF)],
         flops=2 * block * channels * share,
     )
@@ -440,23 +395,18 @@
         own_mixed.append(own)
         far_mixed.append(other)
 
-    tile = min(256, samples)
+    tile = min(512, samples)
 
     def outer(lefts, rights, by_rows, split):
         count = len(lefts) // 2 if split else len(lefts)
         rows, columns = LANES * count, channels
         one = (piece, columns) if by_rows else (rows, columns // fsdp_size)
-        outs = [fixed(shape(one, F32))] + [fixed(shape(one, BF))] * (fsdp_size - 1)
-        if split:
-            outs.append(far(shape((samples, rows), BF)))
-            lefts = [(near, far)[n % 2](x) for n, x in enumerate(lefts)]
-        else:
-            lefts = [both(x) for x in lefts]
-        return tiled(
-            functools.partial(outer_body, count, fsdp_size, steps, by_rows, split),
-            2 * steps,
-            outs,
-            [(where,)] + lefts + [near(rights[0]), far(rights[1])],
+        return call(
+            functools.partial(outer_body, count, fsdp_size, tile, by_rows, split),
+            [shape(one, F32)]
+            + [shape(one, BF)] * (fsdp_size - 1)
+            + ([shape((samples, rows), BF)] if split else []),
+            [where] + list(lefts) + list(rights),
             scratch=[pltpu.VMEM((rows, columns), F32)],
             flops=2 * block * rows * columns,
         )
@@ -518,31 +468,13 @@
 
     tile = min(256, samples)
 
-    def signal_body(base, *rest):
-        mixes, others = rest[:chunks], rest[chunks : chunks + len(halves)]
-        side, side_far, target = rest[-3:]
-        mix = jnp.concatenate([x[...] for x in mixes], axis=1)
-        other = jnp.concatenate([x[...] for x in others], axis=1)
-        acc = base[...].astype(F32) + dot(mix, side[...], 1, 1)
-        target[...] = (acc + dot(other, side_far[...], 1, 1)).astype(BF)
-
-    grad_signal = pl.pallas_call(
-        signal_body,
-        grid=(samples // tile,),
-        out_shape=shape((samples, channels), BF),
-        in_specs=[pl.BlockSpec((tile, channels), lambda i: (i, 0))]
-        + [pl.BlockSpec((tile, LANES), lambda i: (i, 0))] * chunks
-        + [pl.BlockSpec((tile, wide), lambda i: (i, 0))] * len(halves)
-        + [pl.BlockSpec(panel.shape, lambda i: (0, 0))] * 2,
-        out_specs=pl.BlockSpec((tile, channels), lambda i: (i, 0)),
-        cost_estimate=pl.CostEstimate(
-            flops=2 * samples * channels * channels,
-            bytes_accessed=8 * samples * channels,
-            transcendentals=0,
-        ),
-        compiler_params=pltpu.CompilerParams(vmem_limit_bytes=60 * 1024 * 1024),
-        name="signal",
-    )(upstream, *own_mixed, *mixed_in, panel, panel_far)
+    (grad_signal,) = call(
+        functools.partial(signal_body, tile),
+        [shape((samples, channels), BF)],
+        [upstream] + own_mixed + mixed_in + [panel, panel_far],
+        scalars=0,
+        flops=2 * samples * channels * channels,
+    )
 
     def finish_body(meta, *rest):
         packs, parts = rest[:4], rest[4 : 4 + fsdp_size]

time: 296 us -> 268 us (0.905)
  Pallas kernels: 105 us -> 52.7 us
  waiting for transfers between devices: 101 us -> 142 us
  starting transfers between devices: 80.8 us -> 68.2 us
    pallas_call x6 -> x0, Pallas kernels: 48.1 us -> none  [the longest x5 41.5 us: tiled(): pl.pallas_call(body, grid=(steps,), out_shape=tuple((x[0] for x in outs))...]
    ppermute x8, waiting for transfers between devices: 37.8 us -> 59.1 us  [down(): lax.ppermute(x, 'seq', [(i + 2, i) for i in range(seq_size - 2 * hop)])]
    ppermute x18, waiting for transfers between devices: 27 us -> 38.7 us  [from_chips(): got.append(lax.ppermute(blocks[k], 'seq', pairs))]
    ppermute x18, starting transfers between devices: 31.4 us -> 22.2 us  [from_chips(): got.append(lax.ppermute(blocks[k], 'seq', pairs))]
    ppermute x18, waiting for transfers between devices: 10.5 us -> 15.5 us  [from_fsdp(): got.append(lax.ppermute(blocks[k], 'fsdp', pairs))]
    pallas_call x17 -> x23, Pallas kernels: 57 us -> 52.7 us  [call(): pl.pallas_call(body, out_shape=tuple(outs), in_specs=[SM] * scalars + [VM...]
  transfers between devices with their start and end apart: 59 -> 59, of which waited for: 25 -> 26; matrix products, arithmetic and copies ran while one was open for 0% -> 0% of each run, Pallas kernels for 35% -> 19%
where the time goes in v2:
time: 268 us
  waiting for transfers between devices  142 us (53%)
  starting transfers between devices  68.2 us (25%)
  Pallas kernels  52.7 us (20%)
  local copies, waits for them, and re-layouts  2.68 us (1%)
    ppermute x8, waiting for transfers between devices, down(): lax.ppermute(x, 'seq', [(i + 2, i) for i in range(seq_size - 2 * hop)])  59.1 us
    pallas_call x23, Pallas kernels, call(): pl.pallas_call(body, out_shape=tuple(outs), in_specs=[SM] * scalars + [VM...  52.7 us
    ppermute x18, waiting for transfers between devices, from_chips(): got.append(lax.ppermute(blocks[k], 'seq', pairs))  38.7 us
    ppermute x8, waiting for transfers between devices, up(): lax.ppermute(x, 'seq', [(i, i + 2) for i in range(2 * (hop - 1), seq_size...  28.9 us
    ppermute x18, starting transfers between devices, from_chips(): got.append(lax.ppermute(blocks[k], 'seq', pairs))  22.2 us
    ppermute x18, starting transfers between devices, from_fsdp(): got.append(lax.ppermute(blocks[k], 'fsdp', pairs))  20.3 us
    ppermute x18, waiting for transfers between devices, from_fsdp(): got.append(lax.ppermute(blocks[k], 'fsdp', pairs))  15.5 us
    ppermute x8, starting transfers between devices, up(): lax.ppermute(x, 'seq', [(i, i + 2) for i in range(2 * (hop - 1), seq_size...  14 us
  transfers between devices with their start and end apart: 59, of which 26 were waited for; matrix products, arithmetic and copies ran while one was open for 0% of the time, Pallas kernels for 19%

profile of v2, /device:TPU:0, one launch (start us, length us, event | category | flops | bytes accessed | tf_op | source)
XLA Modules:
  0.0 267.5 jit_solution(15006528089829266636)
XLA Ops:
  1.3 3.0 %collective-permute-start = (s32[2]{0:T(128)}, s32[2]{0:T(128)S(1)}, u32[]{:S(2)}, u32[]{:S(2)}) collective-permute-start(s32[2]{0:T(128)} %rest_0_.1), channel_id=1, source_target_pairs={{0,8},{4,12},{8,0},{12,4},{16,24},{20,28},{24,16},{28,20},{1,9},{5... | collective-permute-start | bytes 32 | tf_op jit(solution)/shard_map/ppermute | solution.py:317
  4.3 2.6 collective-permute-start.1
  9.7 1.4 collective-permute-start.2
  11.1 1.5 collective-permute-start.7
  12.6 2.7 collective-permute-done.2.rest_3_
  15.3 1.5 collective-permute-start.8
  16.8 1.4 collective-permute-start.9
  19.4 2.6 collective-permute-start.4
  22.0 5.2 %collective-permute-done.8.rest_2_ = bf16[256,512]{1,0:T(8,128)(2,1)S(1)} collective-permute-done((bf16[256,512]{1,0:T(8,128)(2,1)S(1)}, bf16[256,512]{1,0:T(8,128)(2,1)S(1)}, u32[]{:S(2)}, u32[]{:S(2)}) %collective-permute-start.8) | collective-permute-done | bytes 262176 | tf_op jit(solution)/shard_map/ppermute | solution.py:310
  27.2 1.3 collective-permute-start.5
  28.5 1.5 collective-permute-start.13
  30.0 1.5 collective-permute-start.14
  31.6 1.6 copy-done.1
  33.2 4.0 %shard_map.104 = (bf16[2,1024,128]{2,1,0:T(8,128)(2,1)S(1)}, bf16[2,1024,128]{2,1,0:T(8,128)(2,1)S(1)}, bf16[2,1024,128]{2,1,0:T(8,128)(2,1)S(1)}, bf16[2,1024,1...) custom-call(s32[4]{0:T(128)S(1)} %pad_add_fusion.meta, bf16[1024,1024]{1,0:T(8,128)(2,1)S(1)} %bitcast.14, ...), custom_call_target="tpu_custom_call" | custom-call | flops 2147483648 | bytes 8388624 | tf_op jit(solution)/shard_map/pallas_call | solution.py:26
  37.2 1.3 collective-permute-start.10
  39.1 3.0 %collective-permute-start.18 = (bf16[2,1024,128]{2,1,0:T(8,128)(2,1)S(1)}, bf16[2,1024,128]{2,1,0:T(8,128)(2,1)S(1)}, u32[]{:S(2)}, u32[]{:S(2)}) collective-permute-start(bf16[2,1024,128]{2,1,0:T(8,128)(2,1)S(1)} %get-tuple-element.76.rest_0_), channel_id=1, source_target_pairs={{0,8},{4,12},{8,16},{12,20},{16,24},{20,28},{1,9},{5,13},{9,17},{1... | collective-permute-start | bytes 1572872 | tf_op jit(solution)/shard_map/ppermute | solution.py:321
  42.1 5.1 %collective-permute-start.22 = (bf16[2,1024,128]{2,1,0:T(8,128)(2,1)S(1)}, bf16[2,1024,128]{2,1,0:T(8,128)(2,1)S(1)}, u32[]{:S(2)}, u32[]{:S(2)}) collective-permute-start(bf16[2,1024,128]{2,1,0:T(8,128)(2,1)S(1)} %get-tuple-element.82.rest_0_), channel_id=1, source_target_pairs={{0,8},{4,12},{8,16},{12,20},{16,24},{20,28},{1,9},{5,13},{9,17},{1... | collective-permute-start | bytes 1572872 | tf_op jit(solution)/shard_map/ppermute | solution.py:321
  47.2 1.9 collective-permute-start.26
  49.1 1.7 collective-permute-done.10.rest_1_
  51.5 10.5 %collective-permute-done.18.rest_1_ = bf16[2,1024,128]{2,1,0:T(8,128)(2,1)S(1)} collective-permute-done((bf16[2,1024,128]{2,1,0:T(8,128)(2,1)S(1)}, bf16[2,1024,128]{2,1,0:T(8,128)(2,1)S(1)}, u32[]{:S(2)}, u32[]{:S(2)}) %collective-permute-start.18) | collective-permute-done | bytes 524320 | tf_op jit(solution)/shard_map/ppermute | solution.py:321
  62.7 10.5 %collective-permute-done.22.rest_1_ = bf16[2,1024,128]{2,1,0:T(8,128)(2,1)S(1)} collective-permute-done((bf16[2,1024,128]{2,1,0:T(8,128)(2,1)S(1)}, bf16[2,1024,128]{2,1,0:T(8,128)(2,1)S(1)}, u32[]{:S(2)}, u32[]{:S(2)}) %collective-permute-start.22) | collective-permute-done | bytes 524320 | tf_op jit(solution)/shard_map/ppermute | solution.py:321
  74.0 6.1 %collective-permute-done.26.rest_1_ = bf16[2,1024,128]{2,1,0:T(8,128)(2,1)S(1)} collective-permute-done((bf16[2,1024,128]{2,1,0:T(8,128)(2,1)S(1)}, bf16[2,1024,128]{2,1,0:T(8,128)(2,1)S(1)}, u32[]{:S(2)}, u32[]{:S(2)}) %collective-permute-start.26) | collective-permute-done | bytes 524320 | tf_op jit(solution)/shard_map/ppermute | solution.py:321
  80.7 2.0 shard_map.102
  82.7 4.7 %shard_map.105 = (bf16[2,1024,128]{2,1,0:T(8,128)(2,1)S(1)}, bf16[2,1024,128]{2,1,0:T(8,128)(2,1)S(1)}, bf16[2,1024,128]{2,1,0:T(8,128)(2,1)S(1)}, bf16[2,1024,128]{2,1,0:T(8,128)(2,1)S(1)}) custom-call(s32[4]{0:T(128)S(1)} %pad_add_fusion.meta, bf16[1024,1024]{1,0:T(8,128)(2,1)S(1)} %bitcast.18, bf16[1024,1024]{1,0:T(8,128)(2,1)} %collective-permute-done.12.partner.rest_5_, ...), custom_call_target="tpu_custom_call" | custom-call | flops 2147483648 | bytes 7340048 | tf_op jit(solution)/shard_map/pallas_call | solution.py:26
  87.4 4.5 %shard_map.106 = (bf16[2,1024,128]{2,1,0:T(8,128)(2,1)S(1)}, f32[2,1024,128]{2,1,0:T(8,128)S(1)}, bf16[2,1024,128]{2,1,0:T(8,128)(2,1)S(1)}, bf16[2,128,128]{2,1,0:T(8,128)(2,1)S(1)}) custom-call(s32[4]{0:T(128)S(1)} %pad_add_fusion.meta, s32[8]{0:T(128)S(1)} %get-tuple-element.69.amounts, bf16[2,1024,128]{2,1,0:T(8,128)(2,1)S(1)} %get-tuple-element.70.rest_0_, ...), custom_call_target="tpu_custom_call" | custom-call | flops 805306368 | bytes 4390960 | tf_op jit(solution)/shard_map/pallas_call | solution.py:26
  91.9 1.3 collective-permute-start.16
  93.2 4.5 %shard_map.108 = (bf16[2,1024,128]{2,1,0:T(8,128)(2,1)S(1)}, f32[2,1024,128]{2,1,0:T(8,128)S(1)}, bf16[2,1024,128]{2,1,0:T(8,128)(2,1)S(1)}, bf16[2,128,128]{2,1,0:T(8,128)(2,1)S(1)}) custom-call(s32[4]{0:T(128)S(1)} %pad_add_fusion.meta, s32[8]{0:T(128)S(1)} %get-tuple-element.69.amounts, bf16[2,1024,128]{2,1,0:T(8,128)(2,1)S(1)} %get-tuple-element.76.rest_0_, ...), custom_call_target="tpu_custom_call" | custom-call | flops 805306368 | bytes 4390960 | tf_op jit(solution)/shard_map/pallas_call | solution.py:26
  97.7 1.3 collective-permute-start.20
  99.0 4.5 %shard_map.110 = (bf16[2,1024,128]{2,1,0:T(8,128)(2,1)S(1)}, f32[2,1024,128]{2,1,0:T(8,128)S(1)}, bf16[2,1024,128]{2,1,0:T(8,128)(2,1)S(1)}, bf16[2,128,128]{2,1,0:T(8,128)(2,1)S(1)}) custom-call(s32[4]{0:T(128)S(1)} %pad_add_fusion.meta, s32[8]{0:T(128)S(1)} %get-tuple-element.69.amounts, bf16[2,1024,128]{2,1,0:T(8,128)(2,1)S(1)} %get-tuple-element.82.rest_0_, ...), custom_call_target="tpu_custom_call" | custom-call | flops 805306368 | bytes 4390960 | tf_op jit(solution)/shard_map/pallas_call | solution.py:26
  103.6 1.3 collective-permute-start.24
  104.9 4.5 %shard_map.112 = (bf16[2,1024,128]{2,1,0:T(8,128)(2,1)S(1)}, f32[2,1024,128]{2,1,0:T(8,128)S(1)}, bf16[2,1024,128]{2,1,0:T(8,128)(2,1)S(1)}, bf16[2,128,128]{2,1,0:T(8,128)(2,1)S(1)}) custom-call(s32[4]{0:T(128)S(1)} %pad_add_fusion.meta, s32[8]{0:T(128)S(1)} %get-tuple-element.69.amounts, bf16[2,1024,128]{2,1,0:T(8,128)(2,1)S(1)} %get-tuple-element.88.rest_0_, ...), custom_call_target="tpu_custom_call" | custom-call | flops 805306368 | bytes 4390960 | tf_op jit(solution)/shard_map/pallas_call | solution.py:26
  110.7 3.5 %collective-permute-done.16.rest_1_ = bf16[2,1024,128]{2,1,0:T(8,128)(2,1)S(1)} collective-permute-done((bf16[2,1024,128]{2,1,0:T(8,128)(2,1)S(1)}, bf16[2,1024,128]{2,1,0:T(8,128)(2,1)S(1)}, u32[]{:S(2)}, u32[]{:S(2)}) %collective-permute-start.16) | collective-permute-done | bytes 524320 | tf_op jit(solution)/shard_map/ppermute | solution.py:324
  115.4 9.9 %collective-permute-done.20.rest_1_ = bf16[2,1024,128]{2,1,0:T(8,128)(2,1)S(1)} collective-permute-done((bf16[2,1024,128]{2,1,0:T(8,128)(2,1)S(1)}, bf16[2,1024,128]{2,1,0:T(8,128)(2,1)S(1)}, u32[]{:S(2)}, u32[]{:S(2)}) %collective-permute-start.20) | collective-permute-done | bytes 524320 | tf_op jit(solution)/shard_map/ppermute | solution.py:324
  126.6 4.8 %shard_map.117 = (f32[128,1024]{1,0:T(8,128)S(1)}, bf16[128,1024]{1,0:T(8,128)(2,1)S(1)}, bf16[128,1024]{1,0:T(8,128)(2,1)S(1)}, bf16[128,1024]{1,0:T(8,128)(2,1)S(1)}) custom-call(s32[4]{0:T(128)S(1)} %pad_add_fusion.meta, bf16[2,1024,128]{2,1,0:T(8,128)(2,1)S(1)} %get-tuple-element.105.rest_0_, bf16[2,1024,128]{2,1,0:T(8,128)(2,1)S(1)} %get-tuple-element.106.rest_1_, ...), custom_call_target="tpu_custom_call" | custom-call | flops 2147483648 | bytes 7602192 | tf_op jit(solution)/shard_map/pallas_call | solution.py:26
  132.0 4.5 %collective-permute-done.24.rest_1_ = bf16[2,1024,128]{2,1,0:T(8,128)(2,1)S(1)} collective-permute-done((bf16[2,1024,128]{2,1,0:T(8,128)(2,1)S(1)}, bf16[2,1024,128]{2,1,0:T(8,128)(2,1)S(1)}, u32[]{:S(2)}, u32[]{:S(2)}) %collective-permute-start.24) | collective-permute-done | bytes 524320 | tf_op jit(solution)/shard_map/ppermute | solution.py:324
  137.9 9.9 %collective-permute-done.28.rest_1_ = bf16[2,1024,128]{2,1,0:T(8,128)(2,1)S(1)} collective-permute-done((bf16[2,1024,128]{2,1,0:T(8,128)(2,1)S(1)}, bf16[2,1024,128]{2,1,0:T(8,128)(2,1)S(1)}, u32[]{:S(2)}, u32[]{:S(2)}) %collective-permute-start.28) | collective-permute-done | bytes 524320 | tf_op jit(solution)/shard_map/ppermute | solution.py:324
  147.8 1.5 collective-permute-start.29
  150.3 8.7 %collective-permute-done.17.rest_2_ = bf16[2,1024,128]{2,1,0:T(8,128)(2,1)S(1)} collective-permute-done((bf16[2,1024,128]{2,1,0:T(8,128)(2,1)S(1)}, bf16[2,1024,128]{2,1,0:T(8,128)(2,1)S(1)}, u32[]{:S(2)}, u32[]{:S(2)}) %collective-permute-start.17) | collective-permute-done | bytes 524320 | tf_op jit(solution)/shard_map/ppermute | solution.py:324
  159.0 11.2 %collective-permute-done.21.rest_2_ = bf16[2,1024,128]{2,1,0:T(8,128)(2,1)S(1)} collective-permute-done((bf16[2,1024,128]{2,1,0:T(8,128)(2,1)S(1)}, bf16[2,1024,128]{2,1,0:T(8,128)(2,1)S(1)}, u32[]{:S(2)}, u32[]{:S(2)}) %collective-permute-start.21) | collective-permute-done | bytes 524320 | tf_op jit(solution)/shard_map/ppermute | solution.py:324
  173.1 2.5 shard_map.114
  175.6 1.7 collective-permute-start.33
  177.4 4.1 %collective-permute-done.25.rest_2_ = bf16[2,1024,128]{2,1,0:T(8,128)(2,1)S(1)} collective-permute-done((bf16[2,1024,128]{2,1,0:T(8,128)(2,1)S(1)}, bf16[2,1024,128]{2,1,0:T(8,128)(2,1)S(1)}, u32[]{:S(2)}, u32[]{:S(2)}) %collective-permute-start.25) | collective-permute-done | bytes 524320 | tf_op jit(solution)/shard_map/ppermute | solution.py:324
  182.5 7.1 %collective-permute-done.29.rest_2_ = bf16[2,1024,128]{2,1,0:T(8,128)(2,1)S(1)} collective-permute-done((bf16[2,1024,128]{2,1,0:T(8,128)(2,1)S(1)}, bf16[2,1024,128]{2,1,0:T(8,128)(2,1)S(1)}, u32[]{:S(2)}, u32[]{:S(2)}) %collective-permute-start.29) | collective-permute-done | bytes 524320 | tf_op jit(solution)/shard_map/ppermute | solution.py:324
  192.1 3.3 %collective-permute-done.35.rest_3_ = bf16[256,256]{1,0:T(8,128)(2,1)S(1)} collective-permute-done((bf16[256,256]{1,0:T(8,128)(2,1)S(1)}, bf16[256,256]{1,0:T(8,128)(2,1)S(1)}, u32[]{:S(2)}, u32[]{:S(2)}) %collective-permute-start.35) | collective-permute-done | bytes 131104 | tf_op jit(solution)/shard_map/ppermute | solution.py:310
  196.4 2.6 collective-permute-start.39
  199.0 2.6 shard_map.115
  202.2 2.4 collective-permute-start.41
  204.6 2.0 collective-permute-done.46.rest_1_
  207.1 3.8 %collective-permute-done.40.rest_2_ = bf16[320,256]{1,0:T(8,128)(2,1)S(1)} collective-permute-done((bf16[320,256]{1,0:T(8,128)(2,1)S(1)}, bf16[320,256]{1,0:T(8,128)(2,1)S(1)}, u32[]{:S(2)}, u32[]{:S(2)}) %collective-permute-start.40) | collective-permute-done | bytes 163872 | tf_op jit(solution)/shard_map/ppermute | solution.py:317
  211.0 2.5 collective-permute-start.48
  213.6 3.8 %collective-permute-done.47.rest_2_ = bf16[256,256]{1,0:T(8,128)(2,1)S(1)} collective-permute-done((bf16[256,256]{1,0:T(8,128)(2,1)S(1)}, bf16[256,256]{1,0:T(8,128)(2,1)S(1)}, u32[]{:S(2)}, u32[]{:S(2)}) %collective-permute-start.47) | collective-permute-done | bytes 131104 | tf_op jit(solution)/shard_map/ppermute | solution.py:310
  217.3 2.1 collective-permute-start.43
  219.4 4.9 %collective-permute-done.42.rest_1_ = bf16[192,256]{1,0:T(8,128)(2,1)S(1)} collective-permute-done((bf16[192,256]{1,0:T(8,128)(2,1)S(1)}, bf16[192,256]{1,0:T(8,128)(2,1)S(1)}, u32[]{:S(2)}, u32[]{:S(2)}) %collective-permute-start.42) | collective-permute-done | bytes 98336 | tf_op jit(solution)/shard_map/ppermute | solution.py:317
  225.2 5.6 %collective-permute-done.44.rest_3_ = bf16[192,256]{1,0:T(8,128)(2,1)S(1)} collective-permute-done((bf16[192,256]{1,0:T(8,128)(2,1)S(1)}, bf16[192,256]{1,0:T(8,128)(2,1)S(1)}, u32[]{:S(2)}, u32[]{:S(2)}) %collective-permute-start.44) | collective-permute-done | bytes 98336 | tf_op jit(solution)/shard_map/ppermute | solution.py:317
  231.7 4.6 %collective-permute-done.50.rest_2_ = bf16[64,256]{1,0:T(8,128)(2,1)S(1)} collective-permute-done((bf16[64,256]{1,0:T(8,128)(2,1)S(1)}, bf16[64,256]{1,0:T(8,128)(2,1)S(1)}, u32[]{:S(2)}, u32[]{:S(2)}) %collective-permute-start.50) | collective-permute-done | bytes 32800 | tf_op jit(solution)/shard_map/ppermute | solution.py:317
  236.3 1.4 collective-permute-start.51
  237.8 4.3 %collective-permute-done.51.rest_3_ = bf16[64,256]{1,0:T(8,128)(2,1)S(1)} collective-permute-done((bf16[64,256]{1,0:T(8,128)(2,1)S(1)}, bf16[64,256]{1,0:T(8,128)(2,1)S(1)}, u32[]{:S(2)}, u32[]{:S(2)}) %collective-permute-start.51) | collective-permute-done | bytes 32800 | tf_op jit(solution)/shard_map/ppermute | solution.py:317
  242.2 3.9 %collective-permute-done.52.rest_1_ = bf16[64,256]{1,0:T(8,128)(2,1)S(1)} collective-permute-done((bf16[64,256]{1,0:T(8,128)(2,1)S(1)}, bf16[64,256]{1,0:T(8,128)(2,1)S(1)}, u32[]{:S(2)}, u32[]{:S(2)}) %collective-permute-start.52) | collective-permute-done | bytes 32800 | tf_op jit(solution)/shard_map/ppermute | solution.py:317
  246.1 4.8 %collective-permute-done.53.rest_2_ = bf16[64,256]{1,0:T(8,128)(2,1)S(1)} collective-permute-done((bf16[64,256]{1,0:T(8,128)(2,1)S(1)}, bf16[64,256]{1,0:T(8,128)(2,1)S(1)}, u32[]{:S(2)}, u32[]{:S(2)}) %collective-permute-start.53) | collective-permute-done | bytes 32800 | tf_op jit(solution)/shard_map/ppermute | solution.py:317
  250.9 1.7 collective-permute-start.54
  252.7 4.0 %collective-permute-done.54.rest_3_ = bf16[64,256]{1,0:T(8,128)(2,1)S(1)} collective-permute-done((bf16[64,256]{1,0:T(8,128)(2,1)S(1)}, bf16[64,256]{1,0:T(8,128)(2,1)S(1)}, u32[]{:S(2)}, u32[]{:S(2)}) %collective-permute-start.54) | collective-permute-done | bytes 32800 | tf_op jit(solution)/shard_map/ppermute | solution.py:317
  258.4 2.5 collective-permute-start.58
  260.9 4.3 %shard_map.116 = bf16[1024,1024]{1,0:T(8,128)(2,1)} custom-call(bf16[1024,1024]{1,0:T(8,128)(2,1)S(1)} %bitcast.20, bf16[1024,128]{1,0:T(8,128)(2,1)S(1)} %get-tuple-element.75.rest_0_, bf16[1024,128]{1,0:T(8,128)(2,1)S(1)} %get-tuple-element.81.rest_2_.rest_1_, bf16[1024,128]{1,0:T(8,128)(2,1)S(1)} %get-tuple-element.87.rest_0_.rest_2_, ...), custom_call_target="tpu_custom_call" | custom-call | flops 2147483648 | bytes 8388608 | tf_op jit(solution)/shard_map/pallas_call | solution.py:26
  265.2 2.3 shard_map.124
  (93 shorter events, 26.1 us)
Async XLA Ops:
  0.6 17.6 %copy-start = (bf16[256,1024]{1,0:T(8,128)(2,1)S(1)}, bf16[256,1024]{1,0:T(8,128)(2,1)}, u32[]{:S(2)}) copy-start(bf16[256,1024]{1,0:T(8,128)(2,1)} %param.11) | copy-start | bytes 1572868
  0.6 29.4 %collective-permute-start.6 = (bf16[1024,1024]{1,0:T(8,128)(2,1)}, bf16[1024,1024]{1,0:T(8,128)(2,1)S(1)}, u32[]{:S(2)}, u32[]{:S(2)}) collective-permute-start(bf16[1024,1024]{1,0:T(8,128)(2,1)} %bitcast.13), channel_id=1, source_target_pairs={{0,4},{4,0},{8,12},{12,8},{16,20},{20,16},{24,28},{28,24},{1,5},{5... | collective-permute-start | bytes 6291464 | tf_op jit(solution)/shard_map/ppermute | solution.py:304
  1.2 81.5 %collective-permute-start.12 = (bf16[1024,1024]{1,0:T(8,128)(2,1)}, bf16[1024,1024]{1,0:T(8,128)(2,1)}, u32[]{:S(2)}, u32[]{:S(2)}) collective-permute-start(bf16[1024,1024]{1,0:T(8,128)(2,1)} %bitcast.17), channel_id=1, source_target_pairs={{0,4},{4,0},{8,12},{12,8},{16,20},{20,16},{24,28},{28,24},{1,5},{5... | collective-permute-start | bytes 6291464 | tf_op jit(solution)/shard_map/ppermute | solution.py:304
  1.3 8.4 %collective-permute-start = (s32[2]{0:T(128)}, s32[2]{0:T(128)S(1)}, u32[]{:S(2)}, u32[]{:S(2)}) collective-permute-start(s32[2]{0:T(128)} %rest_0_.1), channel_id=1, source_target_pairs={{0,8},{4,12},{8,0},{12,4},{16,24},{20,28},{24,16},{28,20},{1,9},{5... | collective-permute-start | bytes 32 | tf_op jit(solution)/shard_map/ppermute | solution.py:317
  4.3 6.8 %collective-permute-start.1 = (s32[2]{0:T(128)}, s32[2]{0:T(128)S(1)}, u32[]{:S(2)}, u32[]{:S(2)}) collective-permute-start(s32[2]{0:T(128)} %rest_0_.1), channel_id=1, source_target_pairs={{0,16},{4,20},{8,24},{12,28},{16,0},{20,4},{24,8},{28,12},{1,17},{... | collective-permute-start | bytes 32 | tf_op jit(solution)/shard_map/ppermute | solution.py:317
  6.9 9.9 %collective-permute-start.3 = (bf16[2,128,128]{2,1,0:T(8,128)(2,1)}, bf16[2,128,128]{2,1,0:T(8,128)(2,1)S(1)}, u32[]{:S(2)}, u32[]{:S(2)}) collective-permute-start(bf16[2,128,128]{2,1,0:T(8,128)(2,1)} %rest_4_.1), channel_id=1, source_target_pairs={{0,8},{4,12},{8,0},{12,4},{16,24},{20,28},{24,16},{28,20},{1,9},{5... | collective-permute-start | bytes 196616 | tf_op jit(solution)/shard_map/ppermute | solution.py:317
  9.7 5.6 %collective-permute-start.2 = (s32[2]{0:T(128)}, s32[2]{0:T(128)S(1)}, u32[]{:S(2)}, u32[]{:S(2)}) collective-permute-start(s32[2]{0:T(128)} %rest_0_.1), channel_id=1, source_target_pairs={{0,24},{4,28},{8,16},{12,20},{16,8},{20,12},{24,0},{28,4},{1,25},{... | collective-permute-start | bytes 32 | tf_op jit(solution)/shard_map/ppermute | solution.py:317
  11.1 8.3 %collective-permute-start.7 = (bf16[256,512]{1,0:T(8,128)(2,1)S(1)}, bf16[256,512]{1,0:T(8,128)(2,1)S(1)}, u32[]{:S(2)}, u32[]{:S(2)}) collective-permute-start(bf16[256,512]{1,0:T(8,128)(2,1)S(1)} %shard_map.103.rest_0_), channel_id=1, source_target_pairs={{0,1},{1,0},{2,3},{3,2},{4,5},{5,4},{6,7},{7,6},{8,9},{9,8},{10,11... | collective-permute-start | bytes 786440 | tf_op jit(solution)/shard_map/ppermute | solution.py:310
  15.3 11.9 %collective-permute-start.8 = (bf16[256,512]{1,0:T(8,128)(2,1)S(1)}, bf16[256,512]{1,0:T(8,128)(2,1)S(1)}, u32[]{:S(2)}, u32[]{:S(2)}) collective-permute-start(bf16[256,512]{1,0:T(8,128)(2,1)S(1)} %shard_map.103.rest_0_), channel_id=1, source_target_pairs={{0,2},{1,3},{2,0},{3,1},{4,6},{5,7},{6,4},{7,5},{8,10},{9,11},{10,... | collective-permute-start | bytes 786440 | tf_op jit(solution)/shard_map/ppermute | solution.py:310
  16.8 11.7 %collective-permute-start.9 = (bf16[256,512]{1,0:T(8,128)(2,1)S(1)}, bf16[256,512]{1,0:T(8,128)(2,1)}, u32[]{:S(2)}, u32[]{:S(2)}) collective-permute-start(bf16[256,512]{1,0:T(8,128)(2,1)S(1)} %shard_map.103.rest_0_), channel_id=1, source_target_pairs={{0,3},{1,2},{2,1},{3,0},{4,7},{5,6},{6,5},{7,4},{8,11},{9,10},{10,... | collective-permute-start | bytes 786440 | tf_op jit(solution)/shard_map/ppermute | solution.py:310
  18.2 62.5 %copy-start.5 = (bf16[2,128,128]{2,1,0:T(8,128)(2,1)S(1)}, bf16[2,128,128]{2,1,0:T(8,128)(2,1)}, u32[]{:S(2)}) copy-start(bf16[2,128,128]{2,1,0:T(8,128)(2,1)} %rest_4_.1) | copy-start | bytes 196612
  18.2 62.5 %copy-start.6 = (s32[2]{0:T(128)S(1)}, s32[2]{0:T(128)}, u32[]{:S(2)}) copy-start(s32[2]{0:T(128)} %rest_0_.1) | copy-start | bytes 28
  19.4 17.7 %collective-permute-start.4 = (bf16[2,128,128]{2,1,0:T(8,128)(2,1)}, bf16[2,128,128]{2,1,0:T(8,128)(2,1)S(1)}, u32[]{:S(2)}, u32[]{:S(2)}) collective-permute-start(bf16[2,128,128]{2,1,0:T(8,128)(2,1)} %rest_4_.1), channel_id=1, source_target_pairs={{0,16},{4,20},{8,24},{12,28},{16,0},{20,4},{24,8},{28,12},{1,17},{... | collective-permute-start | bytes 196616 | tf_op jit(solution)/shard_map/ppermute | solution.py:317
  27.2 11.3 %collective-permute-start.5 = (bf16[2,128,128]{2,1,0:T(8,128)(2,1)}, bf16[2,128,128]{2,1,0:T(8,128)(2,1)S(1)}, u32[]{:S(2)}, u32[]{:S(2)}) collective-permute-start(bf16[2,128,128]{2,1,0:T(8,128)(2,1)} %rest_4_.1), channel_id=1, source_target_pairs={{0,24},{4,28},{8,16},{12,20},{16,8},{20,12},{24,0},{28,4},{1,25},{... | collective-permute-start | bytes 196616 | tf_op jit(solution)/shard_map/ppermute | solution.py:317
  28.5 10.5 %collective-permute-start.13 = (bf16[128,1024]{1,0:T(8,128)(2,1)S(1)}, bf16[128,1024]{1,0:T(8,128)(2,1)S(1)}, u32[]{:S(2)}, u32[]{:S(2)}) collective-permute-start(bf16[128,1024]{1,0:T(8,128)(2,1)S(1)} %dynamic-slice_bitcast_fusion.rest_0_), channel_id=1, source_target_pairs={{0,1},{1,0},{2,3},{3,2},{4,5},{5,4},{6,7},{7,6},{8,9},{9,8},{10,11... | collective-permute-start | bytes 786440 | tf_op jit(solution)/shard_map/ppermute | solution.py:310
  30.0 12.0 %collective-permute-start.14 = (bf16[128,1024]{1,0:T(8,128)(2,1)S(1)}, bf16[128,1024]{1,0:T(8,128)(2,1)S(1)}, u32[]{:S(2)}, u32[]{:S(2)}) collective-permute-start(bf16[128,1024]{1,0:T(8,128)(2,1)S(1)} %dynamic-slice_bitcast_fusion.rest_0_), channel_id=1, source_target_pairs={{0,2},{1,3},{2,0},{3,1},{4,6},{5,7},{6,4},{7,5},{8,10},{9,11},{10,... | collective-permute-start | bytes 786440 | tf_op jit(solution)/shard_map/ppermute | solution.py:310
  33.2 49.6 %copy-start.3 = (bf16[1,1024,1024]{2,1,0:T(8,128)(2,1)S(1)}, bf16[1,1024,1024]{2,1,0:T(8,128)(2,1)}, u32[]{:S(2)}) copy-start(bf16[1,1024,1024]{2,1,0:T(8,128)(2,1)} %param.8) | copy-start | bytes 6291460
  37.2 13.6 %collective-permute-start.10 = (bf16[2,1024,128]{2,1,0:T(8,128)(2,1)S(1)}, bf16[2,1024,128]{2,1,0:T(8,128)(2,1)S(1)}, u32[]{:S(2)}, u32[]{:S(2)}) collective-permute-start(bf16[2,1024,128]{2,1,0:T(8,128)(2,1)S(1)} %get-tuple-element.70.rest_0_), channel_id=1, source_target_pairs={{0,8},{4,12},{8,16},{12,20},{16,24},{20,28},{1,9},{5,13},{9,17},{1... | collective-permute-start | bytes 1572872 | tf_op jit(solution)/shard_map/ppermute | solution.py:321
  38.5 8.6 %collective-permute-start.15 = (bf16[128,1024]{1,0:T(8,128)(2,1)S(1)}, bf16[128,1024]{1,0:T(8,128)(2,1)S(1)}, u32[]{:S(2)}, u32[]{:S(2)}) collective-permute-start(bf16[128,1024]{1,0:T(8,128)(2,1)S(1)} %dynamic-slice_bitcast_fusion.rest_0_), channel_id=1, source_target_pairs={{0,3},{1,2},{2,1},{3,0},{4,7},{5,6},{6,5},{7,4},{8,11},{9,10},{10,... | collective-permute-start | bytes 786440 | tf_op jit(solution)/shard_map/ppermute | solution.py:310
  39.1 22.9 %collective-permute-start.18 = (bf16[2,1024,128]{2,1,0:T(8,128)(2,1)S(1)}, bf16[2,1024,128]{2,1,0:T(8,128)(2,1)S(1)}, u32[]{:S(2)}, u32[]{:S(2)}) collective-permute-start(bf16[2,1024,128]{2,1,0:T(8,128)(2,1)S(1)} %get-tuple-element.76.rest_0_), channel_id=1, source_target_pairs={{0,8},{4,12},{8,16},{12,20},{16,24},{20,28},{1,9},{5,13},{9,17},{1... | collective-permute-start | bytes 1572872 | tf_op jit(solution)/shard_map/ppermute | solution.py:321
  42.1 31.2 %collective-permute-start.22 = (bf16[2,1024,128]{2,1,0:T(8,128)(2,1)S(1)}, bf16[2,1024,128]{2,1,0:T(8,128)(2,1)S(1)}, u32[]{:S(2)}, u32[]{:S(2)}) collective-permute-start(bf16[2,1024,128]{2,1,0:T(8,128)(2,1)S(1)} %get-tuple-element.82.rest_0_), channel_id=1, source_target_pairs={{0,8},{4,12},{8,16},{12,20},{16,24},{20,28},{1,9},{5,13},{9,17},{1... | collective-permute-start | bytes 1572872 | tf_op jit(solution)/shard_map/ppermute | solution.py:321
  47.2 32.9 %collective-permute-start.26 = (bf16[2,1024,128]{2,1,0:T(8,128)(2,1)S(1)}, bf16[2,1024,128]{2,1,0:T(8,128)(2,1)S(1)}, u32[]{:S(2)}, u32[]{:S(2)}) collective-permute-start(bf16[2,1024,128]{2,1,0:T(8,128)(2,1)S(1)} %get-tuple-element.88.rest_0_), channel_id=1, source_target_pairs={{0,8},{4,12},{8,16},{12,20},{16,24},{20,28},{1,9},{5,13},{9,17},{1... | collective-permute-start | bytes 1572872 | tf_op jit(solution)/shard_map/ppermute | solution.py:321
  50.8 36.6 %collective-permute-start.11 = (bf16[2,1024,128]{2,1,0:T(8,128)(2,1)S(1)}, bf16[2,1024,128]{2,1,0:T(8,128)(2,1)S(1)}, u32[]{:S(2)}, u32[]{:S(2)}) collective-permute-start(bf16[2,1024,128]{2,1,0:T(8,128)(2,1)S(1)} %collective-permute-done.10.rest_1_), channel_id=1, source_target_pairs={{8,16},{12,20},{16,24},{20,28},{9,17},{13,21},{17,25},{21,29},{10,... | collective-permute-start | bytes 1572872 | tf_op jit(solution)/shard_map/ppermute | solution.py:321
  62.0 31.2 %collective-permute-start.19 = (bf16[2,1024,128]{2,1,0:T(8,128)(2,1)S(1)}, bf16[2,1024,128]{2,1,0:T(8,128)(2,1)S(1)}, u32[]{:S(2)}, u32[]{:S(2)}) collective-permute-start(bf16[2,1024,128]{2,1,0:T(8,128)(2,1)S(1)} %collective-permute-done.18.rest_1_), channel_id=1, source_target_pairs={{8,16},{12,20},{16,24},{20,28},{9,17},{13,21},{17,25},{21,29},{10,... | collective-permute-start | bytes 1572872 | tf_op jit(solution)/shard_map/ppermute | solution.py:321
  73.3 25.8 %collective-permute-start.23 = (bf16[2,1024,128]{2,1,0:T(8,128)(2,1)S(1)}, bf16[2,1024,128]{2,1,0:T(8,128)(2,1)S(1)}, u32[]{:S(2)}, u32[]{:S(2)}) collective-permute-start(bf16[2,1024,128]{2,1,0:T(8,128)(2,1)S(1)} %collective-permute-done.22.rest_1_), channel_id=1, source_target_pairs={{8,16},{12,20},{16,24},{20,28},{9,17},{13,21},{17,25},{21,29},{10,... | collective-permute-start | bytes 1572872 | tf_op jit(solution)/shard_map/ppermute | solution.py:321
  80.0 24.8 %collective-permute-start.27 = (bf16[2,1024,128]{2,1,0:T(8,128)(2,1)S(1)}, bf16[2,1024,128]{2,1,0:T(8,128)(2,1)S(1)}, u32[]{:S(2)}, u32[]{:S(2)}) collective-permute-start(bf16[2,1024,128]{2,1,0:T(8,128)(2,1)S(1)} %collective-permute-done.26.rest_1_), channel_id=1, source_target_pairs={{8,16},{12,20},{16,24},{20,28},{9,17},{13,21},{17,25},{21,29},{10,... | collective-permute-start | bytes 1572872 | tf_op jit(solution)/shard_map/ppermute | solution.py:321
  91.9 22.2 %collective-permute-start.16 = (bf16[2,1024,128]{2,1,0:T(8,128)(2,1)S(1)}, bf16[2,1024,128]{2,1,0:T(8,128)(2,1)S(1)}, u32[]{:S(2)}, u32[]{:S(2)}) collective-permute-start(bf16[2,1024,128]{2,1,0:T(8,128)(2,1)S(1)} %get-tuple-element.74.rest_0_), channel_id=1, source_target_pairs={{8,0},{12,4},{16,8},{20,12},{24,16},{28,20},{9,1},{13,5},{17,9},{2... | collective-permute-start | bytes 1572872 | tf_op jit(solution)/shard_map/ppermute | solution.py:324
  97.7 27.6 %collective-permute-start.20 = (bf16[2,1024,128]{2,1,0:T(8,128)(2,1)S(1)}, bf16[2,1024,128]{2,1,0:T(8,128)(2,1)S(1)}, u32[]{:S(2)}, u32[]{:S(2)}) collective-permute-start(bf16[2,1024,128]{2,1,0:T(8,128)(2,1)S(1)} %get-tuple-element.80.rest_0_), channel_id=1, source_target_pairs={{8,0},{12,4},{16,8},{20,12},{24,16},{28,20},{9,1},{13,5},{17,9},{2... | collective-permute-start | bytes 1572872 | tf_op jit(solution)/shard_map/ppermute | solution.py:324
  103.6 33.0 %collective-permute-start.24 = (bf16[2,1024,128]{2,1,0:T(8,128)(2,1)S(1)}, bf16[2,1024,128]{2,1,0:T(8,128)(2,1)S(1)}, u32[]{:S(2)}, u32[]{:S(2)}) collective-permute-start(bf16[2,1024,128]{2,1,0:T(8,128)(2,1)S(1)} %get-tuple-element.86.rest_0_), channel_id=1, source_target_pairs={{8,0},{12,4},{16,8},{20,12},{24,16},{28,20},{9,1},{13,5},{17,9},{2... | collective-permute-start | bytes 1572872 | tf_op jit(solution)/shard_map/ppermute | solution.py:324
  109.4 38.4 %collective-permute-start.28 = (bf16[2,1024,128]{2,1,0:T(8,128)(2,1)S(1)}, bf16[2,1024,128]{2,1,0:T(8,128)(2,1)S(1)}, u32[]{:S(2)}, u32[]{:S(2)}) collective-permute-start(bf16[2,1024,128]{2,1,0:T(8,128)(2,1)S(1)} %get-tuple-element.92.rest_0_), channel_id=1, source_target_pairs={{8,0},{12,4},{16,8},{20,12},{24,16},{28,20},{9,1},{13,5},{17,9},{2... | collective-permute-start | bytes 1572872 | tf_op jit(solution)/shard_map/ppermute | solution.py:324
  114.1 44.9 %collective-permute-start.17 = (bf16[2,1024,128]{2,1,0:T(8,128)(2,1)S(1)}, bf16[2,1024,128]{2,1,0:T(8,128)(2,1)S(1)}, u32[]{:S(2)}, u32[]{:S(2)}) collective-permute-start(bf16[2,1024,128]{2,1,0:T(8,128)(2,1)S(1)} %collective-permute-done.16.rest_1_), channel_id=1, source_target_pairs={{8,0},{12,4},{16,8},{20,12},{9,1},{13,5},{17,9},{21,13},{10,2},{14... | collective-permute-start | bytes 1572872 | tf_op jit(solution)/shard_map/ppermute | solution.py:324
  125.3 44.9 %collective-permute-start.21 = (bf16[2,1024,128]{2,1,0:T(8,128)(2,1)S(1)}, bf16[2,1024,128]{2,1,0:T(8,128)(2,1)S(1)}, u32[]{:S(2)}, u32[]{:S(2)}) collective-permute-start(bf16[2,1024,128]{2,1,0:T(8,128)(2,1)S(1)} %collective-permute-done.20.rest_1_), channel_id=1, source_target_pairs={{8,0},{12,4},{16,8},{20,12},{9,1},{13,5},{17,9},{21,13},{10,2},{14... | collective-permute-start | bytes 1572872 | tf_op jit(solution)/shard_map/ppermute | solution.py:324
  131.5 17.8 %collective-permute-start.36 = (bf16[128,1024]{1,0:T(8,128)(2,1)S(1)}, bf16[128,1024]{1,0:T(8,128)(2,1)S(1)}, u32[]{:S(2)}, u32[]{:S(2)}) collective-permute-start(bf16[128,1024]{1,0:T(8,128)(2,1)S(1)} %get-tuple-element.110), channel_id=1, source_target_pairs={{0,1},{1,0},{2,3},{3,2},{4,5},{5,4},{6,7},{7,6},{8,9},{9,8},{10,11... | collective-permute-start | bytes 786440 | tf_op jit(solution)/shard_map/ppermute | solution.py:310
  136.6 44.9 %collective-permute-start.25 = (bf16[2,1024,128]{2,1,0:T(8,128)(2,1)S(1)}, bf16[2,1024,128]{2,1,0:T(8,128)(2,1)S(1)}, u32[]{:S(2)}, u32[]{:S(2)}) collective-permute-start(bf16[2,1024,128]{2,1,0:T(8,128)(2,1)S(1)} %collective-permute-done.24.rest_1_), channel_id=1, source_target_pairs={{8,0},{12,4},{16,8},{20,12},{9,1},{13,5},{17,9},{21,13},{10,2},{14... | collective-permute-start | bytes 1572872 | tf_op jit(solution)/shard_map/ppermute | solution.py:324
  147.8 41.8 %collective-permute-start.29 = (bf16[2,1024,128]{2,1,0:T(8,128)(2,1)S(1)}, bf16[2,1024,128]{2,1,0:T(8,128)(2,1)S(1)}, u32[]{:S(2)}, u32[]{:S(2)}) collective-permute-start(bf16[2,1024,128]{2,1,0:T(8,128)(2,1)S(1)} %collective-permute-done.28.rest_1_), channel_id=1, source_target_pairs={{8,0},{12,4},{16,8},{20,12},{9,1},{13,5},{17,9},{21,13},{10,2},{14... | collective-permute-start | bytes 1572872 | tf_op jit(solution)/shard_map/ppermute | solution.py:324
  149.3 26.4 %collective-permute-start.37 = (bf16[128,1024]{1,0:T(8,128)(2,1)S(1)}, bf16[128,1024]{1,0:T(8,128)(2,1)S(1)}, u32[]{:S(2)}, u32[]{:S(2)}) collective-permute-start(bf16[128,1024]{1,0:T(8,128)(2,1)S(1)} %get-tuple-element.111), channel_id=1, source_target_pairs={{0,2},{1,3},{2,0},{3,1},{4,6},{5,7},{6,4},{7,5},{8,10},{9,11},{10,... | collective-permute-start | bytes 786440 | tf_op jit(solution)/shard_map/ppermute | solution.py:310
  159.0 98.3 %collective-permute-start.32 = (bf16[1024,512]{1,0:T(8,128)(2,1)S(1)}, bf16[1024,512]{1,0:T(8,128)(2,1)S(1)}, u32[]{:S(2)}, u32[]{:S(2)}) collective-permute-start(bf16[1024,512]{1,0:T(8,128)(2,1)S(1)} %get-tuple-element.100.rest_6_), channel_id=1, source_target_pairs={{0,4},{4,0},{8,12},{12,8},{16,20},{20,16},{24,28},{28,24},{1,5},{5... | collective-permute-start | bytes 3145736 | tf_op jit(solution)/shard_map/ppermute | solution.py:304
  170.3 21.8 %collective-permute-start.38 = (bf16[128,1024]{1,0:T(8,128)(2,1)S(1)}, bf16[128,1024]{1,0:T(8,128)(2,1)S(1)}, u32[]{:S(2)}, u32[]{:S(2)}) collective-permute-start(bf16[128,1024]{1,0:T(8,128)(2,1)S(1)} %get-tuple-element.112), channel_id=1, source_target_pairs={{0,3},{1,2},{2,1},{3,0},{4,7},{5,6},{6,5},{7,4},{8,11},{9,10},{10,... | collective-permute-start | bytes 786440 | tf_op jit(solution)/shard_map/ppermute | solution.py:310
  171.1 2.0 copy-start.2
  175.6 16.5 %collective-permute-start.33 = (bf16[256,256]{1,0:T(8,128)(2,1)S(1)}, bf16[256,256]{1,0:T(8,128)(2,1)S(1)}, u32[]{:S(2)}, u32[]{:S(2)}) collective-permute-start(bf16[256,256]{1,0:T(8,128)(2,1)S(1)} %get-tuple-element.102), channel_id=1, source_target_pairs={{0,1},{1,0},{2,3},{3,2},{4,5},{5,4},{6,7},{7,6},{8,9},{9,8},{10,11... | collective-permute-start | bytes 393224 | tf_op jit(solution)/shard_map/ppermute | solution.py:310
  181.5 10.6 %collective-permute-start.34 = (bf16[256,256]{1,0:T(8,128)(2,1)S(1)}, bf16[256,256]{1,0:T(8,128)(2,1)S(1)}, u32[]{:S(2)}, u32[]{:S(2)}) collective-permute-start(bf16[256,256]{1,0:T(8,128)(2,1)S(1)} %get-tuple-element.103), channel_id=1, source_target_pairs={{0,2},{1,3},{2,0},{3,1},{4,6},{5,7},{6,4},{7,5},{8,10},{9,11},{10,... | collective-permute-start | bytes 393224 | tf_op jit(solution)/shard_map/ppermute | solution.py:310
  189.6 5.9 %collective-permute-start.35 = (bf16[256,256]{1,0:T(8,128)(2,1)S(1)}, bf16[256,256]{1,0:T(8,128)(2,1)S(1)}, u32[]{:S(2)}, u32[]{:S(2)}) collective-permute-start(bf16[256,256]{1,0:T(8,128)(2,1)S(1)} %get-tuple-element.104), channel_id=1, source_target_pairs={{0,3},{1,2},{2,1},{3,0},{4,7},{5,6},{6,5},{7,4},{8,11},{9,10},{10,... | collective-permute-start | bytes 393224 | tf_op jit(solution)/shard_map/ppermute | solution.py:310
  196.4 10.2 %collective-permute-start.39 = (bf16[320,256]{1,0:T(8,128)(2,1)S(1)}, bf16[320,256]{1,0:T(8,128)(2,1)S(1)}, u32[]{:S(2)}, u32[]{:S(2)}) collective-permute-start(bf16[320,256]{1,0:T(8,128)(2,1)S(1)} %get-tuple-element.118), channel_id=1, source_target_pairs={{0,8},{4,12},{8,0},{12,4},{16,24},{20,28},{24,16},{28,20},{1,9},{5... | collective-permute-start | bytes 491528 | tf_op jit(solution)/shard_map/ppermute | solution.py:317
  199.0 11.9 %collective-permute-start.40 = (bf16[320,256]{1,0:T(8,128)(2,1)S(1)}, bf16[320,256]{1,0:T(8,128)(2,1)S(1)}, u32[]{:S(2)}, u32[]{:S(2)}) collective-permute-start(bf16[320,256]{1,0:T(8,128)(2,1)S(1)} %get-tuple-element.119), channel_id=1, source_target_pairs={{0,16},{4,20},{8,24},{12,28},{16,0},{20,4},{24,8},{28,12},{1,17},{... | collective-permute-start | bytes 491528 | tf_op jit(solution)/shard_map/ppermute | solution.py:317
  201.6 5.0 %collective-permute-start.46 = (bf16[256,256]{1,0:T(8,128)(2,1)S(1)}, bf16[256,256]{1,0:T(8,128)(2,1)S(1)}, u32[]{:S(2)}, u32[]{:S(2)}) collective-permute-start(bf16[256,256]{1,0:T(8,128)(2,1)S(1)} %get-tuple-element.123), channel_id=1, source_target_pairs={{0,1},{1,0},{2,3},{3,2},{4,5},{5,4},{6,7},{7,6},{8,9},{9,8},{10,11... | collective-permute-start | bytes 393224 | tf_op jit(solution)/shard_map/ppermute | solution.py:310
  202.2 8.8 %collective-permute-start.41 = (bf16[320,256]{1,0:T(8,128)(2,1)S(1)}, bf16[320,256]{1,0:T(8,128)(2,1)S(1)}, u32[]{:S(2)}, u32[]{:S(2)}) collective-permute-start(bf16[320,256]{1,0:T(8,128)(2,1)S(1)} %get-tuple-element.120), channel_id=1, source_target_pairs={{0,24},{4,28},{8,16},{12,20},{16,8},{20,12},{24,0},{28,4},{1,25},{... | collective-permute-start | bytes 491528 | tf_op jit(solution)/shard_map/ppermute | solution.py:317
  206.6 51.7 %collective-permute-start.30 = (bf16[1024,256]{1,0:T(8,128)(2,1)S(1)}, bf16[1024,256]{1,0:T(8,128)(2,1)S(1)}, u32[]{:S(2)}, u32[]{:S(2)}) collective-permute-start(bf16[1024,256]{1,0:T(8,128)(2,1)S(1)} %get-tuple-element.96), channel_id=1, source_target_pairs={{0,4},{4,0},{8,12},{12,8},{16,20},{20,16},{24,28},{28,24},{1,5},{5... | collective-permute-start | bytes 1572872 | tf_op jit(solution)/shard_map/ppermute | solution.py:304
  206.6 51.7 %collective-permute-start.31 = (bf16[1024,256]{1,0:T(8,128)(2,1)S(1)}, bf16[1024,256]{1,0:T(8,128)(2,1)S(1)}, u32[]{:S(2)}, u32[]{:S(2)}) collective-permute-start(bf16[1024,256]{1,0:T(8,128)(2,1)S(1)} %get-tuple-element.99), channel_id=1, source_target_pairs={{0,4},{4,0},{8,12},{12,8},{16,20},{20,16},{24,28},{28,24},{1,5},{5... | collective-permute-start | bytes 1572872 | tf_op jit(solution)/shard_map/ppermute | solution.py:304
  210.9 6.4 %collective-permute-start.47 = (bf16[256,256]{1,0:T(8,128)(2,1)S(1)}, bf16[256,256]{1,0:T(8,128)(2,1)S(1)}, u32[]{:S(2)}, u32[]{:S(2)}) collective-permute-start(bf16[256,256]{1,0:T(8,128)(2,1)S(1)} %get-tuple-element.124), channel_id=1, source_target_pairs={{0,2},{1,3},{2,0},{3,1},{4,6},{5,7},{6,4},{7,5},{8,10},{9,11},{10,... | collective-permute-start | bytes 393224 | tf_op jit(solution)/shard_map/ppermute | solution.py:310
  211.0 6.3 %collective-permute-start.48 = (bf16[256,256]{1,0:T(8,128)(2,1)S(1)}, bf16[256,256]{1,0:T(8,128)(2,1)S(1)}, u32[]{:S(2)}, u32[]{:S(2)}) collective-permute-start(bf16[256,256]{1,0:T(8,128)(2,1)S(1)} %get-tuple-element.125), channel_id=1, source_target_pairs={{0,3},{1,2},{2,1},{3,0},{4,7},{5,6},{6,5},{7,4},{8,11},{9,10},{10,... | collective-permute-start | bytes 393224 | tf_op jit(solution)/shard_map/ppermute | solution.py:310
  217.3 7.1 %collective-permute-start.42 = (bf16[192,256]{1,0:T(8,128)(2,1)S(1)}, bf16[192,256]{1,0:T(8,128)(2,1)S(1)}, u32[]{:S(2)}, u32[]{:S(2)}) collective-permute-start(bf16[192,256]{1,0:T(8,128)(2,1)S(1)} %get-tuple-element.121.rest_0_), channel_id=1, source_target_pairs={{0,8},{4,12},{8,0},{12,4},{16,24},{20,28},{24,16},{28,20},{1,9},{5... | collective-permute-start | bytes 294920 | tf_op jit(solution)/shard_map/ppermute | solution.py:317
  217.3 7.7 %collective-permute-start.43 = (bf16[192,256]{1,0:T(8,128)(2,1)S(1)}, bf16[192,256]{1,0:T(8,128)(2,1)S(1)}, u32[]{:S(2)}, u32[]{:S(2)}) collective-permute-start(bf16[192,256]{1,0:T(8,128)(2,1)S(1)} %get-tuple-element.121.rest_0_), channel_id=1, source_target_pairs={{0,16},{4,20},{8,24},{12,28},{16,0},{20,4},{24,8},{28,12},{1,17},{... | collective-permute-start | bytes 294920 | tf_op jit(solution)/shard_map/ppermute | solution.py:317
  224.4 6.4 %collective-permute-start.44 = (bf16[192,256]{1,0:T(8,128)(2,1)S(1)}, bf16[192,256]{1,0:T(8,128)(2,1)S(1)}, u32[]{:S(2)}, u32[]{:S(2)}) collective-permute-start(bf16[192,256]{1,0:T(8,128)(2,1)S(1)} %get-tuple-element.121.rest_0_), channel_id=1, source_target_pairs={{0,24},{4,28},{8,16},{12,20},{16,8},{20,12},{24,0},{28,4},{1,25},{... | collective-permute-start | bytes 294920 | tf_op jit(solution)/shard_map/ppermute | solution.py:317
  225.1 6.4 %collective-permute-start.49 = (bf16[64,256]{1,0:T(8,128)(2,1)S(1)}, bf16[64,256]{1,0:T(8,128)(2,1)S(1)}, u32[]{:S(2)}, u32[]{:S(2)}) collective-permute-start(bf16[64,256]{1,0:T(8,128)(2,1)S(1)} %get-tuple-element.127), channel_id=1, source_target_pairs={{0,8},{4,12},{8,0},{12,4},{16,24},{20,28},{24,16},{28,20},{1,9},{5... | collective-permute-start | bytes 98312 | tf_op jit(solution)/shard_map/ppermute | solution.py:317
  231.4 33.8 %collective-permute-start.45 = (bf16[4,192,256]{2,1,0:T(8,128)(2,1)S(1)}, bf16[4,192,256]{2,1,0:T(8,128)(2,1)S(1)}, u32[]{:S(2)}, u32[]{:S(2)}) collective-permute-start(bf16[4,192,256]{2,1,0:T(8,128)(2,1)S(1)} %shard_map.120.rest_0_), channel_id=1, source_target_pairs={{0,4},{4,0},{8,12},{12,8},{16,20},{20,16},{24,28},{28,24},{1,5},{5... | collective-permute-start | bytes 1179656 | tf_op jit(solution)/shard_map/ppermute | solution.py:304
  231.5 4.9 %collective-permute-start.50 = (bf16[64,256]{1,0:T(8,128)(2,1)S(1)}, bf16[64,256]{1,0:T(8,128)(2,1)S(1)}, u32[]{:S(2)}, u32[]{:S(2)}) collective-permute-start(bf16[64,256]{1,0:T(8,128)(2,1)S(1)} %get-tuple-element.128), channel_id=1, source_target_pairs={{0,16},{4,20},{8,24},{12,28},{16,0},{20,4},{24,8},{28,12},{1,17},{... | collective-permute-start | bytes 98312 | tf_op jit(solution)/shard_map/ppermute | solution.py:317
  236.3 5.8 %collective-permute-start.51 = (bf16[64,256]{1,0:T(8,128)(2,1)S(1)}, bf16[64,256]{1,0:T(8,128)(2,1)S(1)}, u32[]{:S(2)}, u32[]{:S(2)}) collective-permute-start(bf16[64,256]{1,0:T(8,128)(2,1)S(1)} %get-tuple-element.129), channel_id=1, source_target_pairs={{0,24},{4,28},{8,16},{12,20},{16,8},{20,12},{24,0},{28,4},{1,25},{... | collective-permute-start | bytes 98312 | tf_op jit(solution)/shard_map/ppermute | solution.py:317
  242.1 4.0 %collective-permute-start.52 = (bf16[64,256]{1,0:T(8,128)(2,1)S(1)}, bf16[64,256]{1,0:T(8,128)(2,1)S(1)}, u32[]{:S(2)}, u32[]{:S(2)}) collective-permute-start(bf16[64,256]{1,0:T(8,128)(2,1)S(1)} %shard_map.122.rest_0_), channel_id=1, source_target_pairs={{0,8},{4,12},{8,0},{12,4},{16,24},{20,28},{24,16},{28,20},{1,9},{5... | collective-permute-start | bytes 98312 | tf_op jit(solution)/shard_map/ppermute | solution.py:317
  246.1 4.8 %collective-permute-start.53 = (bf16[64,256]{1,0:T(8,128)(2,1)S(1)}, bf16[64,256]{1,0:T(8,128)(2,1)S(1)}, u32[]{:S(2)}, u32[]{:S(2)}) collective-permute-start(bf16[64,256]{1,0:T(8,128)(2,1)S(1)} %shard_map.122.rest_0_), channel_id=1, source_target_pairs={{0,16},{4,20},{8,24},{12,28},{16,0},{20,4},{24,8},{28,12},{1,17},{... | collective-permute-start | bytes 98312 | tf_op jit(solution)/shard_map/ppermute | solution.py:317
  250.9 5.7 %collective-permute-start.54 = (bf16[64,256]{1,0:T(8,128)(2,1)S(1)}, bf16[64,256]{1,0:T(8,128)(2,1)S(1)}, u32[]{:S(2)}, u32[]{:S(2)}) collective-permute-start(bf16[64,256]{1,0:T(8,128)(2,1)S(1)} %shard_map.122.rest_0_), channel_id=1, source_target_pairs={{0,24},{4,28},{8,16},{12,20},{16,8},{20,12},{24,0},{28,4},{1,25},{... | collective-permute-start | bytes 98312 | tf_op jit(solution)/shard_map/ppermute | solution.py:317
  257.2 7.9 %collective-permute-start.55 = (bf16[4,64,256]{2,1,0:T(8,128)(2,1)S(1)}, bf16[4,64,256]{2,1,0:T(8,128)(2,1)S(1)}, u32[]{:S(2)}, u32[]{:S(2)}) collective-permute-start(bf16[4,64,256]{2,1,0:T(8,128)(2,1)S(1)} %shard_map.123.rest_2_), channel_id=1, source_target_pairs={{0,4},{4,0},{8,12},{12,8},{16,20},{20,16},{24,28},{28,24},{1,5},{5... | collective-permute-start | bytes 393224 | tf_op jit(solution)/shard_map/ppermute | solution.py:304
  257.3 7.9 %collective-permute-start.56 = (bf16[128,256]{1,0:T(8,128)(2,1)S(1)}, bf16[128,256]{1,0:T(8,128)(2,1)S(1)}, u32[]{:S(2)}, u32[]{:S(2)}) collective-permute-start(bf16[128,256]{1,0:T(8,128)(2,1)S(1)} %get-tuple-element.130.rest_4_), channel_id=1, source_target_pairs={{0,1},{1,0},{2,3},{3,2},{4,5},{5,4},{6,7},{7,6},{8,9},{9,8},{10,11... | collective-permute-start | bytes 196616 | tf_op jit(solution)/shard_map/ppermute | solution.py:310
  258.4 6.8 %collective-permute-start.57 = (bf16[128,256]{1,0:T(8,128)(2,1)S(1)}, bf16[128,256]{1,0:T(8,128)(2,1)S(1)}, u32[]{:S(2)}, u32[]{:S(2)}) collective-permute-start(bf16[128,256]{1,0:T(8,128)(2,1)S(1)} %get-tuple-element.130.rest_4_), channel_id=1, source_target_pairs={{0,2},{1,3},{2,0},{3,1},{4,6},{5,7},{6,4},{7,5},{8,10},{9,11},{10,... | collective-permute-start | bytes 196616 | tf_op jit(solution)/shard_map/ppermute | solution.py:310
  258.4 6.8 %collective-permute-start.58 = (bf16[128,256]{1,0:T(8,128)(2,1)S(1)}, bf16[128,256]{1,0:T(8,128)(2,1)S(1)}, u32[]{:S(2)}, u32[]{:S(2)}) collective-permute-start(bf16[128,256]{1,0:T(8,128)(2,1)S(1)} %get-tuple-element.130.rest_4_), channel_id=1, source_target_pairs={{0,3},{1,2},{2,1},{3,0},{4,7},{5,6},{6,5},{7,4},{8,11},{9,10},{10,... | collective-permute-start | bytes 196616 | tf_op jit(solution)/shard_map/ppermute | solution.py:310
  (2 other events, 2.6 us)

commit v3 on v2

--- a/solution.py
+++ b/solution.py
@@ -38,18 +38,22 @@
     return jax.ShapeDtypeStruct(dims, kind)
 
 
-def product_body(parts, tile, turned, meta, own, partner, *rest):
+def product_body(parts, tile, turned, skip, meta, own, partner, *rest):
     weights, outs = rest[:parts], rest[parts:]
+    if skip:
+        outs[-1][:, :skip] = outs[0][...]
+        outs = outs[1:]
     targets, panel = outs[:-1], outs[-1]
     rows = weights[0].shape[0]
     for k in range(parts):
         start = pl.multiple_of((meta[0] ^ k) * rows, rows)
-        panel[pl.ds(start, rows), :] = weights[k][...]
+        panel[pl.ds(start, rows), skip:] = weights[k][...]
     for slot, source in enumerate((own, partner)):
 
         def step(i, carry, slot=slot, source=source):
             at = pl.multiple_of(i * tile, tile)
-            got = dot(source[pl.ds(at, tile), :], panel[...], 1, int(turned)).astype(BF)
+            side = panel[:, skip:]
+            got = dot(source[pl.ds(at, tile), :], side, 1, int(turned)).astype(BF)
             for j, target in enumerate(targets):
                 target[slot, pl.ds(at, tile), :] = got[:, j * LANES : (j + 1) * LANES]
             return carry
@@ -171,8 +175,7 @@
 
 def signal_body(tile, base, *rest):
     side, side_far, target = rest[-3:]
-    count = (len(rest) - 3) // 3 * 2
-    mixes, others = rest[:count], rest[count:-3]
+    mixes, others = rest[:-5], rest[-5:-3]
 
     def step(i, carry):
         at = pl.multiple_of(i * tile, tile)
@@ -244,13 +247,13 @@
 
 def share_body(parts, meta, whole, *outs):
     piece = whole.shape[1] // (2 * parts)
-    each = parts // len(outs)
-    for n, out in enumerate(outs):
-        got = []
-        for f in range(n * each, (n + 1) * each):
-            both = whole[:, 2 * f * piece : 2 * (f + 1) * piece]
-            got.append(jnp.where(meta[2] == 0, both[:, :piece], both[:, piece:]))
-        out[...] = jnp.concatenate(got, axis=1)
+    got = []
+    for f in range(parts):
+        both = whole[:, 2 * f * piece : 2 * (f + 1) * piece]
+        got.append(jnp.where(meta[2] == 0, both[:, :piece], both[:, piece:]))
+    first = outs[0].shape[1] // piece
+    outs[0][...] = jnp.concatenate(got[:first], axis=1)
+    outs[1][...] = jnp.concatenate(got[first:], axis=1)
 
 
 def taps_body(chips, groups, meta, *rest):
@@ -298,7 +301,6 @@
     width = conv_chans // local_groups
     assert 2 * width == LANES and chips == fsdp_size and piece == conv_chans
     chunks = share // LANES
-    per_half = max(chunks // 2, 1)
 
     def to_partner(x):
         return lax.ppermute(x, "seq", [(i, i ^ 1) for i in range(seq_size)])
@@ -324,16 +326,17 @@
         return lax.ppermute(x, "seq", [(i + 2, i) for i in range(seq_size - 2 * hop)])
 
     where = jnp.stack([fsdp_at, chip, core, lengths[0] - chip * block]).astype(jnp.int32)
-    wide = per_half * LANES
-    halves = range(0, chunks, per_half)
-    (in_share,) = call(
-        functools.partial(share_body, fsdp_size), [shape((w_in.shape[0], share), BF)], [where, w_in]
+    wides = [share - LANES, LANES]
+    in_shares = call(
+        functools.partial(share_body, fsdp_size),
+        [shape((w_in.shape[0], x), BF) for x in (LANES, share - LANES)],
+        [where, w_in],
     )
     out_share = lax.dynamic_index_in_dim(
         w_out.reshape(2, piece, channels), core, 0, keepdims=False
     )
     record_far = to_partner(record)
-    in_parts = from_fsdp([in_share] * fsdp_size)
+    in_parts = [from_fsdp([x] * fsdp_size) for x in in_shares]
     upstream_far = to_partner(upstream)
     out_parts = from_fsdp([out_share] * fsdp_size)
     delays = from_chips([dilation] * chips)
@@ -349,15 +352,21 @@
 
     series = shape((2, samples, LANES), BF)
     tile = min(512, samples)
+    first, lead = call(
+        functools.partial(product_body, fsdp_size, tile, False, 0),
+        [series, shape((channels, LANES), BF)],
+        [where, record, record_far] + in_parts[0],
+        flops=2 * block * channels * LANES,
+    )
     got = call(
-        functools.partial(product_body, fsdp_size, tile, False),
-        [series] * chunks + [shape((channels, share), BF)],
-        [where, record, record_far] + in_parts,
-        flops=2 * block * channels * share,
-    )
-    projected, panel = got[:-1], got[-1]
+        functools.partial(product_body, fsdp_size, tile, False, LANES),
+        [series] * (chunks - 1) + [shape((channels, share), BF)],
+        [where, record, record_far] + in_parts[1] + [lead],
+        flops=2 * block * channels * (share - LANES),
+    )
+    projected, panel = (first,) + got[:-1], got[-1]
     grad_gated = call(
-        functools.partial(product_body, fsdp_size, tile, True),
+        functools.partial(product_body, fsdp_size, tile, True, 0),
         [series] * chunks,
         [where, upstream, upstream_far] + out_parts,
         scratch=[pltpu.VMEM((share, channels), BF)],
@@ -420,9 +429,9 @@
         return [packed, to_partner(packed)]
 
     mixed_in, flats = [], []
-    for start in halves:
+    for pick in (range(chunks - 1), range(chunks - 1, chunks)):
         sides = []
-        for j in range(start, start + per_half):
+        for j in pick:
             sides += [own_mixed[j], far_mixed[j]]
         got = outer(sides, (record, record_far), False, True)
         mixed_in.append(to_partner(got[-1]))
@@ -431,7 +440,7 @@
     flat_out = from_fsdp(got)
 
     own_rows = channels // fsdp_size
-    in_part, out_part = wide // chips, piece // chips
+    in_part, out_part = wides[0] // chips, piece // chips
     panel_rows = in_part + out_part * (channels // own_rows)
     kernel_rows = 2 * LANES * conv_chans // own_rows
     whole = (panel_rows + kernel_rows, own_rows)
@@ -440,7 +449,7 @@
         [shape(whole, F32)] + [shape(whole, BF)] * (chips - 1),
         [where] + flats[0] + flat_out + kernel_grads,
         scratch=[
-            pltpu.VMEM((wide, own_rows), F32),
+            pltpu.VMEM((wides[0], own_rows), F32),
             pltpu.VMEM((piece, channels), F32),
             pltpu.VMEM((chips, 2, conv_chans, LANES), BF),
         ],
@@ -454,12 +463,12 @@
     kernel_parts = from_fsdp([mine_kernel] * fsdp_size)
     finals = finish_sum(mine)
 
-    last = (wide // chips, own_rows)
+    last = (wides[1] // chips, own_rows)
     cut = call(
         functools.partial(split_body, fsdp_size, chips),
         [shape(last, F32)] + [shape(last, BF)] * (chips - 1),
         [where] + flats[1],
-        scratch=[pltpu.VMEM((wide, own_rows), F32)],
+        scratch=[pltpu.VMEM((wides[1], own_rows), F32)],
     )
     (mine,) = call(
         functools.partial(sum_body, chips, None), [shape(last, BF)], from_chips(cut), scalars=0
@@ -492,7 +501,8 @@
                     ]
                 at = p * in_part
                 turned[side ^ core_at, at : at + in_part, :] = first[p, :in_part, :]
-                turned[side ^ core_at, wide + at : wide + at + in_part, :] = second[p]
+                at, rows = wides[0] + p * last[0], last[0]
+                turned[side ^ core_at, at : at + rows, :] = second[p]
         for f in range(fsdp_size):
             pair = [turned[c, f * piece : (f + 1) * piece, :] for c in range(2)]
             grad_in[:, 2 * f * piece : 2 * (f + 1) * piece] = jnp.concatenate(pair, axis=0).T

time: 268 us -> 264 us (0.985)
  waiting for transfers between devices: 142 us -> 119 us
  starting transfers between devices: 68.2 us -> 84.4 us
    ppermute x8, waiting for transfers between devices: 28.9 us -> 0.02 us  [up(): lax.ppermute(x, 'seq', [(i, i + 2) for i in range(2 * (hop - 1), seq_size...]
    ppermute x8, waiting for transfers between devices: 59.1 us -> 33.7 us  [down(): lax.ppermute(x, 'seq', [(i + 2, i) for i in range(seq_size - 2 * hop)])]
    ppermute x18, waiting for transfers between devices: 38.7 us -> 60.7 us  [from_chips(): got.append(lax.ppermute(blocks[k], 'seq', pairs))]
    ppermute x18 -> x21, waiting for transfers between devices: 15.5 us -> 25 us  [from_fsdp(): got.append(lax.ppermute(blocks[k], 'fsdp', pairs))]
    ppermute x18 -> x21, starting transfers between devices: 20.3 us -> 29.4 us  [from_fsdp(): got.append(lax.ppermute(blocks[k], 'fsdp', pairs))]
    ppermute x8, starting transfers between devices: 14 us -> 18.2 us  [up(): lax.ppermute(x, 'seq', [(i, i + 2) for i in range(2 * (hop - 1), seq_size...]
    ppermute x18, starting transfers between devices: 22.2 us -> 25 us  [from_chips(): got.append(lax.ppermute(blocks[k], 'seq', pairs))]
    pallas_call x23 -> x24, Pallas kernels: 52.7 us -> 55.1 us  [call(): pl.pallas_call(body, out_shape=tuple(outs), in_specs=[SM] * scalars + [VM...]
  transfers between devices with their start and end apart: 59 -> 62, of which waited for: 26 -> 25; matrix products, arithmetic and copies ran while one was open for 0% -> 0% of each run, Pallas kernels for 19% -> 20%
where the time goes in v3:
time: 264 us; the launch traced here: 263 us
  waiting for transfers between devices  119 us (45%)
  starting transfers between devices  84.4 us (32%)
  Pallas kernels  55.1 us (21%)
  local copies, waits for them, and re-layouts  2.69 us (1%)
    ppermute x18, waiting for transfers between devices, from_chips(): got.append(lax.ppermute(blocks[k], 'seq', pairs))  60.7 us
    pallas_call x24, Pallas kernels, call(): pl.pallas_call(body, out_shape=tuple(outs), in_specs=[SM] * scalars + [VM...  55.1 us
    ppermute x8, waiting for transfers between devices, down(): lax.ppermute(x, 'seq', [(i + 2, i) for i in range(seq_size - 2 * hop)])  33.7 us
    ppermute x21, starting transfers between devices, from_fsdp(): got.append(lax.ppermute(blocks[k], 'fsdp', pairs))  29.4 us
    ppermute x18, starting transfers between devices, from_chips(): got.append(lax.ppermute(blocks[k], 'seq', pairs))  25 us
    ppermute x21, waiting for transfers between devices, from_fsdp(): got.append(lax.ppermute(blocks[k], 'fsdp', pairs))  25 us
    ppermute x8, starting transfers between devices, up(): lax.ppermute(x, 'seq', [(i, i + 2) for i in range(2 * (hop - 1), seq_size...  18.2 us
    ppermute x8, starting transfers between devices, down(): lax.ppermute(x, 'seq', [(i + 2, i) for i in range(seq_size - 2 * hop)])  10.5 us
  transfers between devices with their start and end apart: 62, of which 25 were waited for; matrix products, arithmetic and copies ran while one was open for 0% of the time, Pallas kernels for 20%

profile of v3, /device:TPU:0, one launch (start us, length us, event | category | flops | bytes accessed | tf_op | source)
XLA Modules:
  0.0 263.4 jit_solution(11635581750947960621)
XLA Ops:
  3.7 3.0 %collective-permute-start.7 = (bf16[256,128]{1,0:T(8,128)(2,1)S(1)}, bf16[256,128]{1,0:T(8,128)(2,1)S(1)}, u32[]{:S(2)}, u32[]{:S(2)}) collective-permute-start(bf16[256,128]{1,0:T(8,128)(2,1)S(1)} %get-tuple-element.73.rest_0_), channel_id=1, source_target_pairs={{0,1},{1,0},{2,3},{3,2},{4,5},{5,4},{6,7},{7,6},{8,9},{9,8},{10,11... | collective-permute-start | bytes 196616 | tf_op jit(solution)/shard_map/ppermute | solution.py:312
  6.6 1.5 collective-permute-start.8
  9.0 2.3 collective-permute-start.18
  11.2 1.8 collective-permute-start.19
  14.1 1.9 collective-permute-start
  16.0 1.6 copy-done.1
  17.6 2.3 shard_map.104
  19.9 2.7 %collective-permute-start.1 = (s32[2]{0:T(128)S(1)}, s32[2]{0:T(128)S(1)}, u32[]{:S(2)}, u32[]{:S(2)}) collective-permute-start(s32[2]{0:T(128)S(1)} %copy-done.6), channel_id=1, source_target_pairs={{0,16},{4,20},{8,24},{12,28},{16,0},{20,4},{24,8},{28,12},{1,17},{... | collective-permute-start | bytes 32 | tf_op jit(solution)/shard_map/ppermute | solution.py:319
  22.6 1.9 collective-permute-done.1.rest_2_
  24.4 2.5 collective-permute-start.2
  26.9 2.9 %collective-permute-done.2.rest_3_ = s32[2]{0:T(128)S(1)} collective-permute-done((s32[2]{0:T(128)S(1)}, s32[2]{0:T(128)S(1)}, u32[]{:S(2)}, u32[]{:S(2)}) %collective-permute-start.2) | collective-permute-done | bytes 40 | tf_op jit(solution)/shard_map/ppermute | solution.py:319
  29.8 3.0 %collective-permute-start.4 = (bf16[2,128,128]{2,1,0:T(8,128)(2,1)S(1)}, bf16[2,128,128]{2,1,0:T(8,128)(2,1)S(1)}, u32[]{:S(2)}, u32[]{:S(2)}) collective-permute-start(bf16[2,128,128]{2,1,0:T(8,128)(2,1)S(1)} %copy-done.5), channel_id=1, source_target_pairs={{0,16},{4,20},{8,24},{12,28},{16,0},{20,4},{24,8},{28,12},{1,17},{... | collective-permute-start | bytes 196616 | tf_op jit(solution)/shard_map/ppermute | solution.py:319
  32.9 1.7 collective-permute-start.13
  34.6 2.0 collective-permute-start.10
  36.6 4.1 %shard_map.108 = (bf16[2,1024,128]{2,1,0:T(8,128)(2,1)S(1)}, bf16[2,1024,128]{2,1,0:T(8,128)(2,1)S(1)}, bf16[2,1024,128]{2,1,0:T(8,128)(2,1)S(1)}, bf16[1024,512]{1,0:T(8,128)(2,1)S(1)}) custom-call(s32[4]{0:T(128)S(1)} %pad_add_fusion.meta, bf16[1024,1024]{1,0:T(8,128)(2,1)S(1)} %bitcast.15, ...), custom_call_target="tpu_custom_call" | custom-call | flops 1610612736 | bytes 7864336 | tf_op jit(solution)/shard_map/pallas_call | solution.py:26
  40.7 2.5 collective-permute-start.21
  43.2 14.1 %collective-permute-done.5.rest_7_ = bf16[2,128,128]{2,1,0:T(8,128)(2,1)S(1)} collective-permute-done((bf16[2,128,128]{2,1,0:T(8,128)(2,1)S(1)}, bf16[2,128,128]{2,1,0:T(8,128)(2,1)S(1)}, u32[]{:S(2)}, u32[]{:S(2)}) %collective-permute-start.5) | collective-permute-done | bytes 65568 | tf_op jit(solution)/shard_map/ppermute | solution.py:319
  57.3 3.3 %collective-permute-start.25 = (bf16[2,1024,128]{2,1,0:T(8,128)(2,1)S(1)}, bf16[2,1024,128]{2,1,0:T(8,128)(2,1)S(1)}, u32[]{:S(2)}, u32[]{:S(2)}) collective-permute-start(bf16[2,1024,128]{2,1,0:T(8,128)(2,1)S(1)} %get-tuple-element.88.rest_0_), channel_id=1, source_target_pairs={{0,8},{4,12},{8,16},{12,20},{16,24},{20,28},{1,9},{5,13},{9,17},{1... | collective-permute-start | bytes 1572872 | tf_op jit(solution)/shard_map/ppermute | solution.py:323
  62.5 6.6 %collective-permute-done.14.rest_2_ = bf16[128,1024]{1,0:T(8,128)(2,1)S(1)} collective-permute-done((bf16[128,1024]{1,0:T(8,128)(2,1)S(1)}, bf16[128,1024]{1,0:T(8,128)(2,1)S(1)}, u32[]{:S(2)}, u32[]{:S(2)}) %collective-permute-start.14) | collective-permute-done | bytes 262176 | tf_op jit(solution)/shard_map/ppermute | solution.py:312
  71.8 2.0 shard_map.102
  73.8 2.6 collective-permute-done.15.rest_3_
  76.4 7.7 %collective-permute-start.29 = (bf16[2,1024,128]{2,1,0:T(8,128)(2,1)S(1)}, bf16[2,1024,128]{2,1,0:T(8,128)(2,1)S(1)}, u32[]{:S(2)}, u32[]{:S(2)}) collective-permute-start(bf16[2,1024,128]{2,1,0:T(8,128)(2,1)S(1)} %get-tuple-element.94.rest_0_), channel_id=1, source_target_pairs={{0,8},{4,12},{8,16},{12,20},{16,24},{20,28},{1,9},{5,13},{9,17},{1... | collective-permute-start | bytes 1572872 | tf_op jit(solution)/shard_map/ppermute | solution.py:323
  84.1 4.7 %shard_map.105 = (bf16[2,1024,128]{2,1,0:T(8,128)(2,1)S(1)}, bf16[2,1024,128]{2,1,0:T(8,128)(2,1)S(1)}, bf16[2,1024,128]{2,1,0:T(8,128)(2,1)S(1)}, bf16[2,1024,128]{2,1,0:T(8,128)(2,1)S(1)}) custom-call(s32[4]{0:T(128)S(1)} %pad_add_fusion.meta, bf16[1024,1024]{1,0:T(8,128)(2,1)S(1)} %bitcast.19, bf16[1024,1024]{1,0:T(8,128)(2,1)} %collective-permute-done.12.partner.rest_5_, ...), custom_call_target="tpu_custom_call" | custom-call | flops 2147483648 | bytes 7340048 | tf_op jit(solution)/shard_map/pallas_call | solution.py:26
  88.8 4.5 %shard_map.106 = (bf16[2,1024,128]{2,1,0:T(8,128)(2,1)S(1)}, f32[2,1024,128]{2,1,0:T(8,128)S(1)}, bf16[2,1024,128]{2,1,0:T(8,128)(2,1)S(1)}, bf16[2,128,128]{2,1,0:T(8,128)(2,1)S(1)}) custom-call(s32[4]{0:T(128)S(1)} %pad_add_fusion.meta, s32[8]{0:T(128)S(1)} %get-tuple-element.72.amounts, bf16[2,1024,128]{2,1,0:T(8,128)(2,1)S(1)} %get-tuple-element.74.rest_0_, ...), custom_call_target="tpu_custom_call" | custom-call | flops 805306368 | bytes 4390960 | tf_op jit(solution)/shard_map/pallas_call | solution.py:26
  94.6 4.5 %shard_map.109 = (bf16[2,1024,128]{2,1,0:T(8,128)(2,1)S(1)}, f32[2,1024,128]{2,1,0:T(8,128)S(1)}, bf16[2,1024,128]{2,1,0:T(8,128)(2,1)S(1)}, bf16[2,128,128]{2,1,0:T(8,128)(2,1)S(1)}) custom-call(s32[4]{0:T(128)S(1)} %pad_add_fusion.meta, s32[8]{0:T(128)S(1)} %get-tuple-element.72.amounts, bf16[2,1024,128]{2,1,0:T(8,128)(2,1)S(1)} %get-tuple-element.82.rest_0_, ...), custom_call_target="tpu_custom_call" | custom-call | flops 805306368 | bytes 4390960 | tf_op jit(solution)/shard_map/pallas_call | solution.py:26
  100.4 4.5 %shard_map.111 = (bf16[2,1024,128]{2,1,0:T(8,128)(2,1)S(1)}, f32[2,1024,128]{2,1,0:T(8,128)S(1)}, bf16[2,1024,128]{2,1,0:T(8,128)(2,1)S(1)}, bf16[2,128,128]{2,1,0:T(8,128)(2,1)S(1)}) custom-call(s32[4]{0:T(128)S(1)} %pad_add_fusion.meta, s32[8]{0:T(128)S(1)} %get-tuple-element.72.amounts, bf16[2,1024,128]{2,1,0:T(8,128)(2,1)S(1)} %get-tuple-element.88.rest_0_, ...), custom_call_target="tpu_custom_call" | custom-call | flops 805306368 | bytes 4390960 | tf_op jit(solution)/shard_map/pallas_call | solution.py:26
  108.2 8.5 %collective-permute-done.23.rest_1_ = bf16[2,1024,128]{2,1,0:T(8,128)(2,1)S(1)} collective-permute-done((bf16[2,1024,128]{2,1,0:T(8,128)(2,1)S(1)}, bf16[2,1024,128]{2,1,0:T(8,128)(2,1)S(1)}, u32[]{:S(2)}, u32[]{:S(2)}) %collective-permute-start.23) | collective-permute-done | bytes 524320 | tf_op jit(solution)/shard_map/ppermute | solution.py:326
  118.0 10.4 %collective-permute-done.27.rest_1_ = bf16[2,1024,128]{2,1,0:T(8,128)(2,1)S(1)} collective-permute-done((bf16[2,1024,128]{2,1,0:T(8,128)(2,1)S(1)}, bf16[2,1024,128]{2,1,0:T(8,128)(2,1)S(1)}, u32[]{:S(2)}, u32[]{:S(2)}) %collective-permute-start.27) | collective-permute-done | bytes 524320 | tf_op jit(solution)/shard_map/ppermute | solution.py:326
  129.7 4.5 %shard_map.113 = (bf16[2,1024,128]{2,1,0:T(8,128)(2,1)S(1)}, f32[2,1024,128]{2,1,0:T(8,128)S(1)}, bf16[2,1024,128]{2,1,0:T(8,128)(2,1)S(1)}, bf16[2,128,128]{2,1,0:T(8,128)(2,1)S(1)}) custom-call(s32[4]{0:T(128)S(1)} %pad_add_fusion.meta, s32[8]{0:T(128)S(1)} %get-tuple-element.72.amounts, bf16[2,1024,128]{2,1,0:T(8,128)(2,1)S(1)} %get-tuple-element.94.rest_0_, ...), custom_call_target="tpu_custom_call" | custom-call | flops 805306368 | bytes 4390960 | tf_op jit(solution)/shard_map/pallas_call | solution.py:26
  134.1 1.5 collective-permute-start.31
  135.6 4.8 %shard_map.118 = (f32[128,1024]{1,0:T(8,128)S(1)}, bf16[128,1024]{1,0:T(8,128)(2,1)S(1)}, bf16[128,1024]{1,0:T(8,128)(2,1)S(1)}, bf16[128,1024]{1,0:T(8,128)(2,1)S(1)}) custom-call(s32[4]{0:T(128)S(1)} %pad_add_fusion.meta, bf16[2,1024,128]{2,1,0:T(8,128)(2,1)S(1)} %get-tuple-element.111.rest_0_, bf16[2,1024,128]{2,1,0:T(8,128)(2,1)S(1)} %get-tuple-element.112.rest_1_, ...), custom_call_target="tpu_custom_call" | custom-call | flops 2147483648 | bytes 7602192 | tf_op jit(solution)/shard_map/pallas_call | solution.py:26
  142.7 8.1 %collective-permute-done.24.rest_2_ = bf16[2,1024,128]{2,1,0:T(8,128)(2,1)S(1)} collective-permute-done((bf16[2,1024,128]{2,1,0:T(8,128)(2,1)S(1)}, bf16[2,1024,128]{2,1,0:T(8,128)(2,1)S(1)}, u32[]{:S(2)}, u32[]{:S(2)}) %collective-permute-start.24) | collective-permute-done | bytes 524320 | tf_op jit(solution)/shard_map/ppermute | solution.py:326
  150.8 1.6 collective-permute-start.41
  154.5 6.8 %collective-permute-done.28.rest_2_ = bf16[2,1024,128]{2,1,0:T(8,128)(2,1)S(1)} collective-permute-done((bf16[2,1024,128]{2,1,0:T(8,128)(2,1)S(1)}, bf16[2,1024,128]{2,1,0:T(8,128)(2,1)S(1)}, u32[]{:S(2)}, u32[]{:S(2)}) %collective-permute-start.28) | collective-permute-done | bytes 524320 | tf_op jit(solution)/shard_map/ppermute | solution.py:326
  162.3 3.2 %shard_map.115 = (f32[384,256]{1,0:T(8,128)S(1)}, bf16[384,256]{1,0:T(8,128)(2,1)S(1)}, bf16[384,256]{1,0:T(8,128)(2,1)S(1)}, bf16[384,256]{1,0:T(8,128)(2,1)S(1)}, bf16[1024,384]{1,0:T(8,128)(2,1)S(1)}) custom-call(s32[4]{0:T(128)S(1)} %pad_add_fusion.meta, bf16[1024,128]{1,0:T(8,128)(2,1)S(1)} %get-tuple-element.79.rest_0_, ...), custom_call_target="tpu_custom_call" | custom-call | flops 1610612736 | bytes 7536656 | tf_op jit(solution)/shard_map/pallas_call | solution.py:26
  165.5 1.8 collective-permute-start.36
  170.4 3.0 %collective-permute-done.36.rest_1_ = bf16[384,256]{1,0:T(8,128)(2,1)S(1)} collective-permute-done((bf16[384,256]{1,0:T(8,128)(2,1)S(1)}, bf16[384,256]{1,0:T(8,128)(2,1)S(1)}, u32[]{:S(2)}, u32[]{:S(2)}) %collective-permute-start.36) | collective-permute-done | bytes 196640 | tf_op jit(solution)/shard_map/ppermute | solution.py:312
  173.3 5.2 %collective-permute-done.37.rest_2_ = bf16[384,256]{1,0:T(8,128)(2,1)S(1)} collective-permute-done((bf16[384,256]{1,0:T(8,128)(2,1)S(1)}, bf16[384,256]{1,0:T(8,128)(2,1)S(1)}, u32[]{:S(2)}, u32[]{:S(2)}) %collective-permute-start.37) | collective-permute-done | bytes 196640 | tf_op jit(solution)/shard_map/ppermute | solution.py:312
  179.5 2.5 collective-permute-start.42
  182.1 7.6 %collective-permute-done.42.rest_1_ = bf16[352,256]{1,0:T(8,128)(2,1)S(1)} collective-permute-done((bf16[352,256]{1,0:T(8,128)(2,1)S(1)}, bf16[352,256]{1,0:T(8,128)(2,1)S(1)}, u32[]{:S(2)}, u32[]{:S(2)}) %collective-permute-start.42) | collective-permute-done | bytes 180256 | tf_op jit(solution)/shard_map/ppermute | solution.py:319
  190.4 8.8 %collective-permute-done.43.rest_2_ = bf16[352,256]{1,0:T(8,128)(2,1)S(1)} collective-permute-done((bf16[352,256]{1,0:T(8,128)(2,1)S(1)}, bf16[352,256]{1,0:T(8,128)(2,1)S(1)}, u32[]{:S(2)}, u32[]{:S(2)}) %collective-permute-start.43) | collective-permute-done | bytes 180256 | tf_op jit(solution)/shard_map/ppermute | solution.py:319
  199.4 3.2 %collective-permute-start.45 = (bf16[224,256]{1,0:T(8,128)(2,1)S(1)}, bf16[224,256]{1,0:T(8,128)(2,1)S(1)}, u32[]{:S(2)}, u32[]{:S(2)}) collective-permute-start(bf16[224,256]{1,0:T(8,128)(2,1)S(1)} %get-tuple-element.127.rest_0_), channel_id=1, source_target_pairs={{0,8},{4,12},{8,0},{12,4},{16,24},{20,28},{24,16},{28,20},{1,9},{5... | collective-permute-start | bytes 344072 | tf_op jit(solution)/shard_map/ppermute | solution.py:319
  202.6 2.4 collective-permute-start.47
  206.0 2.0 shard_map.116
  208.0 1.7 collective-permute-start.49
  209.8 3.3 %collective-permute-done.46.rest_2_ = bf16[224,256]{1,0:T(8,128)(2,1)S(1)} collective-permute-done((bf16[224,256]{1,0:T(8,128)(2,1)S(1)}, bf16[224,256]{1,0:T(8,128)(2,1)S(1)}, u32[]{:S(2)}, u32[]{:S(2)}) %collective-permute-start.46) | collective-permute-done | bytes 114720 | tf_op jit(solution)/shard_map/ppermute | solution.py:319
  214.2 1.5 collective-permute-start.50
  215.8 2.7 %collective-permute-done.50.rest_2_ = bf16[128,256]{1,0:T(8,128)(2,1)S(1)} collective-permute-done((bf16[128,256]{1,0:T(8,128)(2,1)S(1)}, bf16[128,256]{1,0:T(8,128)(2,1)S(1)}, u32[]{:S(2)}, u32[]{:S(2)}) %collective-permute-start.50) | collective-permute-done | bytes 65568 | tf_op jit(solution)/shard_map/ppermute | solution.py:312
  218.5 2.4 collective-permute-start.51
  220.9 2.8 %collective-permute-done.51.rest_3_ = bf16[128,256]{1,0:T(8,128)(2,1)S(1)} collective-permute-done((bf16[128,256]{1,0:T(8,128)(2,1)S(1)}, bf16[128,256]{1,0:T(8,128)(2,1)S(1)}, u32[]{:S(2)}, u32[]{:S(2)}) %collective-permute-start.51) | collective-permute-done | bytes 65568 | tf_op jit(solution)/shard_map/ppermute | solution.py:312
  224.3 1.6 collective-permute-start.52
  225.9 2.2 collective-permute-done.52.rest_1_
  228.1 1.4 collective-permute-start.53
  229.5 3.3 %collective-permute-done.53.rest_2_ = bf16[32,256]{1,0:T(8,128)(2,1)S(1)} collective-permute-done((bf16[32,256]{1,0:T(8,128)(2,1)S(1)}, bf16[32,256]{1,0:T(8,128)(2,1)S(1)}, u32[]{:S(2)}, u32[]{:S(2)}) %collective-permute-start.53) | collective-permute-done | bytes 16416 | tf_op jit(solution)/shard_map/ppermute | solution.py:319
  232.8 1.4 collective-permute-start.54
  234.2 4.1 %collective-permute-done.54.rest_3_ = bf16[32,256]{1,0:T(8,128)(2,1)S(1)} collective-permute-done((bf16[32,256]{1,0:T(8,128)(2,1)S(1)}, bf16[32,256]{1,0:T(8,128)(2,1)S(1)}, u32[]{:S(2)}, u32[]{:S(2)}) %collective-permute-start.54) | collective-permute-done | bytes 16416 | tf_op jit(solution)/shard_map/ppermute | solution.py:319
  238.4 3.7 %collective-permute-done.55.rest_1_ = bf16[32,256]{1,0:T(8,128)(2,1)S(1)} collective-permute-done((bf16[32,256]{1,0:T(8,128)(2,1)S(1)}, bf16[32,256]{1,0:T(8,128)(2,1)S(1)}, u32[]{:S(2)}, u32[]{:S(2)}) %collective-permute-start.55) | collective-permute-done | bytes 16416 | tf_op jit(solution)/shard_map/ppermute | solution.py:319
  242.1 4.6 %collective-permute-done.56.rest_2_ = bf16[32,256]{1,0:T(8,128)(2,1)S(1)} collective-permute-done((bf16[32,256]{1,0:T(8,128)(2,1)S(1)}, bf16[32,256]{1,0:T(8,128)(2,1)S(1)}, u32[]{:S(2)}, u32[]{:S(2)}) %collective-permute-start.56) | collective-permute-done | bytes 16416 | tf_op jit(solution)/shard_map/ppermute | solution.py:319
  246.8 1.4 collective-permute-start.57
  248.2 4.1 %collective-permute-done.57.rest_3_ = bf16[32,256]{1,0:T(8,128)(2,1)S(1)} collective-permute-done((bf16[32,256]{1,0:T(8,128)(2,1)S(1)}, bf16[32,256]{1,0:T(8,128)(2,1)S(1)}, u32[]{:S(2)}, u32[]{:S(2)}) %collective-permute-start.57) | collective-permute-done | bytes 16416 | tf_op jit(solution)/shard_map/ppermute | solution.py:319
  252.9 1.6 collective-permute-start.59
  254.6 1.3 collective-permute-start.60
  256.5 4.3 %shard_map.117 = bf16[1024,1024]{1,0:T(8,128)(2,1)} custom-call(bf16[1024,1024]{1,0:T(8,128)(2,1)S(1)} %bitcast.21, bf16[1024,128]{1,0:T(8,128)(2,1)S(1)} %get-tuple-element.79.rest_0_, bf16[1024,128]{1,0:T(8,128)(2,1)S(1)} %get-tuple-element.87.rest_2_.rest_1_, bf16[1024,128]{1,0:T(8,128)(2,1)S(1)} %get-tuple-element.93.rest_4_.rest_2_, ...), custom_call_target="tpu_custom_call" | custom-call | flops 2147483648 | bytes 8388608 | tf_op jit(solution)/shard_map/pallas_call | solution.py:26
  261.1 2.3 shard_map.125
  (100 shorter events, 31.7 us)
Async XLA Ops:
  0.6 13.4 %collective-permute-start.6 = (bf16[1024,1024]{1,0:T(8,128)(2,1)}, bf16[1024,1024]{1,0:T(8,128)(2,1)S(1)}, u32[]{:S(2)}, u32[]{:S(2)}) collective-permute-start(bf16[1024,1024]{1,0:T(8,128)(2,1)} %bitcast.13), channel_id=1, source_target_pairs={{0,4},{4,0},{8,12},{12,8},{16,20},{20,16},{24,28},{28,24},{1,5},{5... | collective-permute-start | bytes 6291464 | tf_op jit(solution)/shard_map/ppermute | solution.py:306
  1.2 82.9 %collective-permute-start.12 = (bf16[1024,1024]{1,0:T(8,128)(2,1)}, bf16[1024,1024]{1,0:T(8,128)(2,1)}, u32[]{:S(2)}, u32[]{:S(2)}) collective-permute-start(bf16[1024,1024]{1,0:T(8,128)(2,1)} %bitcast.18), channel_id=1, source_target_pairs={{0,4},{4,0},{8,12},{12,8},{16,20},{20,16},{24,28},{28,24},{1,5},{5... | collective-permute-start | bytes 6291464 | tf_op jit(solution)/shard_map/ppermute | solution.py:306
  3.7 5.3 %collective-permute-start.7 = (bf16[256,128]{1,0:T(8,128)(2,1)S(1)}, bf16[256,128]{1,0:T(8,128)(2,1)S(1)}, u32[]{:S(2)}, u32[]{:S(2)}) collective-permute-start(bf16[256,128]{1,0:T(8,128)(2,1)S(1)} %get-tuple-element.73.rest_0_), channel_id=1, source_target_pairs={{0,1},{1,0},{2,3},{3,2},{4,5},{5,4},{6,7},{7,6},{8,9},{9,8},{10,11... | collective-permute-start | bytes 196616 | tf_op jit(solution)/shard_map/ppermute | solution.py:312
  6.6 4.6 %collective-permute-start.8 = (bf16[256,128]{1,0:T(8,128)(2,1)S(1)}, bf16[256,128]{1,0:T(8,128)(2,1)S(1)}, u32[]{:S(2)}, u32[]{:S(2)}) collective-permute-start(bf16[256,128]{1,0:T(8,128)(2,1)S(1)} %get-tuple-element.73.rest_0_), channel_id=1, source_target_pairs={{0,2},{1,3},{2,0},{3,1},{4,6},{5,7},{6,4},{7,5},{8,10},{9,11},{10,... | collective-permute-start | bytes 196616 | tf_op jit(solution)/shard_map/ppermute | solution.py:312
  8.2 5.9 %collective-permute-start.9 = (bf16[256,128]{1,0:T(8,128)(2,1)S(1)}, bf16[256,128]{1,0:T(8,128)(2,1)S(1)}, u32[]{:S(2)}, u32[]{:S(2)}) collective-permute-start(bf16[256,128]{1,0:T(8,128)(2,1)S(1)} %get-tuple-element.73.rest_0_), channel_id=1, source_target_pairs={{0,3},{1,2},{2,1},{3,0},{4,7},{5,6},{6,5},{7,4},{8,11},{9,10},{10,... | collective-permute-start | bytes 196616 | tf_op jit(solution)/shard_map/ppermute | solution.py:312
  9.0 20.8 %collective-permute-start.18 = (bf16[256,384]{1,0:T(8,128)(2,1)S(1)}, bf16[256,384]{1,0:T(8,128)(2,1)S(1)}, u32[]{:S(2)}, u32[]{:S(2)}) collective-permute-start(bf16[256,384]{1,0:T(8,128)(2,1)S(1)} %get-tuple-element.80.rest_0_), channel_id=1, source_target_pairs={{0,1},{1,0},{2,3},{3,2},{4,5},{5,4},{6,7},{7,6},{8,9},{9,8},{10,11... | collective-permute-start | bytes 589832 | tf_op jit(solution)/shard_map/ppermute | solution.py:312
  11.2 21.6 %collective-permute-start.19 = (bf16[256,384]{1,0:T(8,128)(2,1)S(1)}, bf16[256,384]{1,0:T(8,128)(2,1)S(1)}, u32[]{:S(2)}, u32[]{:S(2)}) collective-permute-start(bf16[256,384]{1,0:T(8,128)(2,1)S(1)} %get-tuple-element.80.rest_0_), channel_id=1, source_target_pairs={{0,2},{1,3},{2,0},{3,1},{4,6},{5,7},{6,4},{7,5},{8,10},{9,11},{10,... | collective-permute-start | bytes 589832 | tf_op jit(solution)/shard_map/ppermute | solution.py:312
  14.0 20.6 %collective-permute-start.20 = (bf16[256,384]{1,0:T(8,128)(2,1)S(1)}, bf16[256,384]{1,0:T(8,128)(2,1)}, u32[]{:S(2)}, u32[]{:S(2)}) collective-permute-start(bf16[256,384]{1,0:T(8,128)(2,1)S(1)} %get-tuple-element.80.rest_0_), channel_id=1, source_target_pairs={{0,3},{1,2},{2,1},{3,0},{4,7},{5,6},{6,5},{7,4},{8,11},{9,10},{10,... | collective-permute-start | bytes 589832 | tf_op jit(solution)/shard_map/ppermute | solution.py:312
  14.1 5.8 %collective-permute-start = (s32[2]{0:T(128)}, s32[2]{0:T(128)S(1)}, u32[]{:S(2)}, u32[]{:S(2)}) collective-permute-start(s32[2]{0:T(128)} %rest_0_.1), channel_id=1, source_target_pairs={{0,8},{4,12},{8,0},{12,4},{16,24},{20,28},{24,16},{28,20},{1,9},{5... | collective-permute-start | bytes 32 | tf_op jit(solution)/shard_map/ppermute | solution.py:319
  17.5 19.0 %copy-start.2 = (bf16[1,1024,1024]{2,1,0:T(8,128)(2,1)S(1)}, bf16[1,1024,1024]{2,1,0:T(8,128)(2,1)}, u32[]{:S(2)}) copy-start(bf16[1,1024,1024]{2,1,0:T(8,128)(2,1)} %param.7) | copy-start | bytes 6291460
  19.9 4.5 %collective-permute-start.1 = (s32[2]{0:T(128)S(1)}, s32[2]{0:T(128)S(1)}, u32[]{:S(2)}, u32[]{:S(2)}) collective-permute-start(s32[2]{0:T(128)S(1)} %copy-done.6), channel_id=1, source_target_pairs={{0,16},{4,20},{8,24},{12,28},{16,0},{20,4},{24,8},{28,12},{1,17},{... | collective-permute-start | bytes 32 | tf_op jit(solution)/shard_map/ppermute | solution.py:319
  24.4 5.4 %collective-permute-start.2 = (s32[2]{0:T(128)S(1)}, s32[2]{0:T(128)S(1)}, u32[]{:S(2)}, u32[]{:S(2)}) collective-permute-start(s32[2]{0:T(128)S(1)} %copy-done.6), channel_id=1, source_target_pairs={{0,24},{4,28},{8,16},{12,20},{16,8},{20,12},{24,0},{28,4},{1,25},{... | collective-permute-start | bytes 32 | tf_op jit(solution)/shard_map/ppermute | solution.py:319
  29.8 10.9 %collective-permute-start.3 = (bf16[2,128,128]{2,1,0:T(8,128)(2,1)S(1)}, bf16[2,128,128]{2,1,0:T(8,128)(2,1)S(1)}, u32[]{:S(2)}, u32[]{:S(2)}) collective-permute-start(bf16[2,128,128]{2,1,0:T(8,128)(2,1)S(1)} %copy-done.5), channel_id=1, source_target_pairs={{0,8},{4,12},{8,0},{12,4},{16,24},{20,28},{24,16},{28,20},{1,9},{5... | collective-permute-start | bytes 196616 | tf_op jit(solution)/shard_map/ppermute | solution.py:319
  29.8 13.3 %collective-permute-start.4 = (bf16[2,128,128]{2,1,0:T(8,128)(2,1)S(1)}, bf16[2,128,128]{2,1,0:T(8,128)(2,1)S(1)}, u32[]{:S(2)}, u32[]{:S(2)}) collective-permute-start(bf16[2,128,128]{2,1,0:T(8,128)(2,1)S(1)} %copy-done.5), channel_id=1, source_target_pairs={{0,16},{4,20},{8,24},{12,28},{16,0},{20,4},{24,8},{28,12},{1,17},{... | collective-permute-start | bytes 196616 | tf_op jit(solution)/shard_map/ppermute | solution.py:319
  32.9 27.8 %collective-permute-start.13 = (bf16[128,1024]{1,0:T(8,128)(2,1)S(1)}, bf16[128,1024]{1,0:T(8,128)(2,1)S(1)}, u32[]{:S(2)}, u32[]{:S(2)}) collective-permute-start(bf16[128,1024]{1,0:T(8,128)(2,1)S(1)} %dynamic-slice_bitcast_fusion.rest_0_), channel_id=1, source_target_pairs={{0,1},{1,0},{2,3},{3,2},{4,5},{5,4},{6,7},{7,6},{8,9},{9,8},{10,11... | collective-permute-start | bytes 786440 | tf_op jit(solution)/shard_map/ppermute | solution.py:312
  34.6 27.2 %collective-permute-start.10 = (bf16[2,1024,128]{2,1,0:T(8,128)(2,1)S(1)}, bf16[2,1024,128]{2,1,0:T(8,128)(2,1)S(1)}, u32[]{:S(2)}, u32[]{:S(2)}) collective-permute-start(bf16[2,1024,128]{2,1,0:T(8,128)(2,1)S(1)} %get-tuple-element.74.rest_0_), channel_id=1, source_target_pairs={{0,8},{4,12},{8,16},{12,20},{16,24},{20,28},{1,9},{5,13},{9,17},{1... | collective-permute-start | bytes 1572872 | tf_op jit(solution)/shard_map/ppermute | solution.py:323
  36.6 47.5 %copy-start.3 = (bf16[1,1024,1024]{2,1,0:T(8,128)(2,1)S(1)}, bf16[1,1024,1024]{2,1,0:T(8,128)(2,1)}, u32[]{:S(2)}) copy-start(bf16[1,1024,1024]{2,1,0:T(8,128)(2,1)} %param.8) | copy-start | bytes 6291460
  40.7 29.7 %collective-permute-start.21 = (bf16[2,1024,128]{2,1,0:T(8,128)(2,1)S(1)}, bf16[2,1024,128]{2,1,0:T(8,128)(2,1)S(1)}, u32[]{:S(2)}, u32[]{:S(2)}) collective-permute-start(bf16[2,1024,128]{2,1,0:T(8,128)(2,1)S(1)} %get-tuple-element.82.rest_0_), channel_id=1, source_target_pairs={{0,8},{4,12},{8,16},{12,20},{16,24},{20,28},{1,9},{5,13},{9,17},{1... | collective-permute-start | bytes 1572872 | tf_op jit(solution)/shard_map/ppermute | solution.py:323
  43.2 14.2 %collective-permute-start.5 = (bf16[2,128,128]{2,1,0:T(8,128)(2,1)S(1)}, bf16[2,128,128]{2,1,0:T(8,128)(2,1)S(1)}, u32[]{:S(2)}, u32[]{:S(2)}) collective-permute-start(bf16[2,128,128]{2,1,0:T(8,128)(2,1)S(1)} %copy-done.5), channel_id=1, source_target_pairs={{0,24},{4,28},{8,16},{12,20},{16,8},{20,12},{24,0},{28,4},{1,25},{... | collective-permute-start | bytes 196616 | tf_op jit(solution)/shard_map/ppermute | solution.py:319
  57.3 13.8 %collective-permute-start.25 = (bf16[2,1024,128]{2,1,0:T(8,128)(2,1)S(1)}, bf16[2,1024,128]{2,1,0:T(8,128)(2,1)S(1)}, u32[]{:S(2)}, u32[]{:S(2)}) collective-permute-start(bf16[2,1024,128]{2,1,0:T(8,128)(2,1)S(1)} %get-tuple-element.88.rest_0_), channel_id=1, source_target_pairs={{0,8},{4,12},{8,16},{12,20},{16,24},{20,28},{1,9},{5,13},{9,17},{1... | collective-permute-start | bytes 1572872 | tf_op jit(solution)/shard_map/ppermute | solution.py:323
  60.7 8.4 %collective-permute-start.14 = (bf16[128,1024]{1,0:T(8,128)(2,1)S(1)}, bf16[128,1024]{1,0:T(8,128)(2,1)S(1)}, u32[]{:S(2)}, u32[]{:S(2)}) collective-permute-start(bf16[128,1024]{1,0:T(8,128)(2,1)S(1)} %dynamic-slice_bitcast_fusion.rest_0_), channel_id=1, source_target_pairs={{0,2},{1,3},{2,0},{3,1},{4,6},{5,7},{6,4},{7,5},{8,10},{9,11},{10,... | collective-permute-start | bytes 786440 | tf_op jit(solution)/shard_map/ppermute | solution.py:312
  61.8 27.0 %collective-permute-start.11 = (bf16[2,1024,128]{2,1,0:T(8,128)(2,1)S(1)}, bf16[2,1024,128]{2,1,0:T(8,128)(2,1)S(1)}, u32[]{:S(2)}, u32[]{:S(2)}) collective-permute-start(bf16[2,1024,128]{2,1,0:T(8,128)(2,1)S(1)} %collective-permute-done.10.rest_1_), channel_id=1, source_target_pairs={{8,16},{12,20},{16,24},{20,28},{9,17},{13,21},{17,25},{21,29},{10,... | collective-permute-start | bytes 1572872 | tf_op jit(solution)/shard_map/ppermute | solution.py:323
  69.1 7.3 %collective-permute-start.15 = (bf16[128,1024]{1,0:T(8,128)(2,1)S(1)}, bf16[128,1024]{1,0:T(8,128)(2,1)S(1)}, u32[]{:S(2)}, u32[]{:S(2)}) collective-permute-start(bf16[128,1024]{1,0:T(8,128)(2,1)S(1)} %dynamic-slice_bitcast_fusion.rest_0_), channel_id=1, source_target_pairs={{0,3},{1,2},{2,1},{3,0},{4,7},{5,6},{6,5},{7,4},{8,11},{9,10},{10,... | collective-permute-start | bytes 786440 | tf_op jit(solution)/shard_map/ppermute | solution.py:312
  70.4 24.2 %collective-permute-start.22 = (bf16[2,1024,128]{2,1,0:T(8,128)(2,1)S(1)}, bf16[2,1024,128]{2,1,0:T(8,128)(2,1)S(1)}, u32[]{:S(2)}, u32[]{:S(2)}) collective-permute-start(bf16[2,1024,128]{2,1,0:T(8,128)(2,1)S(1)} %collective-permute-done.21.rest_1_), channel_id=1, source_target_pairs={{8,16},{12,20},{16,24},{20,28},{9,17},{13,21},{17,25},{21,29},{10,... | collective-permute-start | bytes 1572872 | tf_op jit(solution)/shard_map/ppermute | solution.py:323
  71.1 29.3 %collective-permute-start.26 = (bf16[2,1024,128]{2,1,0:T(8,128)(2,1)S(1)}, bf16[2,1024,128]{2,1,0:T(8,128)(2,1)S(1)}, u32[]{:S(2)}, u32[]{:S(2)}) collective-permute-start(bf16[2,1024,128]{2,1,0:T(8,128)(2,1)S(1)} %collective-permute-done.25.rest_1_), channel_id=1, source_target_pairs={{8,16},{12,20},{16,24},{20,28},{9,17},{13,21},{17,25},{21,29},{10,... | collective-permute-start | bytes 1572872 | tf_op jit(solution)/shard_map/ppermute | solution.py:323
  76.4 29.8 %collective-permute-start.29 = (bf16[2,1024,128]{2,1,0:T(8,128)(2,1)S(1)}, bf16[2,1024,128]{2,1,0:T(8,128)(2,1)S(1)}, u32[]{:S(2)}, u32[]{:S(2)}) collective-permute-start(bf16[2,1024,128]{2,1,0:T(8,128)(2,1)S(1)} %get-tuple-element.94.rest_0_), channel_id=1, source_target_pairs={{0,8},{4,12},{8,16},{12,20},{16,24},{20,28},{1,9},{5,13},{9,17},{1... | collective-permute-start | bytes 1572872 | tf_op jit(solution)/shard_map/ppermute | solution.py:323
  93.3 13.6 %collective-permute-start.16 = (bf16[2,1024,128]{2,1,0:T(8,128)(2,1)S(1)}, bf16[2,1024,128]{2,1,0:T(8,128)(2,1)S(1)}, u32[]{:S(2)}, u32[]{:S(2)}) collective-permute-start(bf16[2,1024,128]{2,1,0:T(8,128)(2,1)S(1)} %get-tuple-element.78.rest_0_), channel_id=1, source_target_pairs={{8,0},{12,4},{16,8},{20,12},{24,16},{28,20},{9,1},{13,5},{17,9},{2... | collective-permute-start | bytes 1572872 | tf_op jit(solution)/shard_map/ppermute | solution.py:326
  99.1 17.6 %collective-permute-start.23 = (bf16[2,1024,128]{2,1,0:T(8,128)(2,1)S(1)}, bf16[2,1024,128]{2,1,0:T(8,128)(2,1)S(1)}, u32[]{:S(2)}, u32[]{:S(2)}) collective-permute-start(bf16[2,1024,128]{2,1,0:T(8,128)(2,1)S(1)} %get-tuple-element.86.rest_0_), channel_id=1, source_target_pairs={{8,0},{12,4},{16,8},{20,12},{24,16},{28,20},{9,1},{13,5},{17,9},{2... | collective-permute-start | bytes 1572872 | tf_op jit(solution)/shard_map/ppermute | solution.py:326
  104.9 23.5 %collective-permute-start.27 = (bf16[2,1024,128]{2,1,0:T(8,128)(2,1)S(1)}, bf16[2,1024,128]{2,1,0:T(8,128)(2,1)S(1)}, u32[]{:S(2)}, u32[]{:S(2)}) collective-permute-start(bf16[2,1024,128]{2,1,0:T(8,128)(2,1)S(1)} %get-tuple-element.92.rest_0_), channel_id=1, source_target_pairs={{8,0},{12,4},{16,8},{20,12},{24,16},{28,20},{9,1},{13,5},{17,9},{2... | collective-permute-start | bytes 1572872 | tf_op jit(solution)/shard_map/ppermute | solution.py:326
  106.2 23.5 %collective-permute-start.30 = (bf16[2,1024,128]{2,1,0:T(8,128)(2,1)S(1)}, bf16[2,1024,128]{2,1,0:T(8,128)(2,1)S(1)}, u32[]{:S(2)}, u32[]{:S(2)}) collective-permute-start(bf16[2,1024,128]{2,1,0:T(8,128)(2,1)S(1)} %collective-permute-done.29.rest_1_), channel_id=1, source_target_pairs={{8,16},{12,20},{16,24},{20,28},{9,17},{13,21},{17,25},{21,29},{10,... | collective-permute-start | bytes 1572872 | tf_op jit(solution)/shard_map/ppermute | solution.py:323
  106.9 34.5 %collective-permute-start.17 = (bf16[2,1024,128]{2,1,0:T(8,128)(2,1)S(1)}, bf16[2,1024,128]{2,1,0:T(8,128)(2,1)S(1)}, u32[]{:S(2)}, u32[]{:S(2)}) collective-permute-start(bf16[2,1024,128]{2,1,0:T(8,128)(2,1)S(1)} %collective-permute-done.16.rest_1_), channel_id=1, source_target_pairs={{8,0},{12,4},{16,8},{20,12},{9,1},{13,5},{17,9},{21,13},{10,2},{14... | collective-permute-start | bytes 1572872 | tf_op jit(solution)/shard_map/ppermute | solution.py:326
  116.7 34.2 %collective-permute-start.24 = (bf16[2,1024,128]{2,1,0:T(8,128)(2,1)S(1)}, bf16[2,1024,128]{2,1,0:T(8,128)(2,1)S(1)}, u32[]{:S(2)}, u32[]{:S(2)}) collective-permute-start(bf16[2,1024,128]{2,1,0:T(8,128)(2,1)S(1)} %collective-permute-done.23.rest_1_), channel_id=1, source_target_pairs={{8,0},{12,4},{16,8},{20,12},{9,1},{13,5},{17,9},{21,13},{10,2},{14... | collective-permute-start | bytes 1572872 | tf_op jit(solution)/shard_map/ppermute | solution.py:326
  128.4 32.9 %collective-permute-start.28 = (bf16[2,1024,128]{2,1,0:T(8,128)(2,1)S(1)}, bf16[2,1024,128]{2,1,0:T(8,128)(2,1)S(1)}, u32[]{:S(2)}, u32[]{:S(2)}) collective-permute-start(bf16[2,1024,128]{2,1,0:T(8,128)(2,1)S(1)} %collective-permute-done.27.rest_1_), channel_id=1, source_target_pairs={{8,0},{12,4},{16,8},{20,12},{9,1},{13,5},{17,9},{21,13},{10,2},{14... | collective-permute-start | bytes 1572872 | tf_op jit(solution)/shard_map/ppermute | solution.py:326
  134.1 34.9 %collective-permute-start.31 = (bf16[2,1024,128]{2,1,0:T(8,128)(2,1)S(1)}, bf16[2,1024,128]{2,1,0:T(8,128)(2,1)S(1)}, u32[]{:S(2)}, u32[]{:S(2)}) collective-permute-start(bf16[2,1024,128]{2,1,0:T(8,128)(2,1)S(1)} %get-tuple-element.98.rest_0_), channel_id=1, source_target_pairs={{8,0},{12,4},{16,8},{20,12},{24,16},{28,20},{9,1},{13,5},{17,9},{2... | collective-permute-start | bytes 1572872 | tf_op jit(solution)/shard_map/ppermute | solution.py:326
  140.5 25.0 %collective-permute-start.39 = (bf16[128,1024]{1,0:T(8,128)(2,1)S(1)}, bf16[128,1024]{1,0:T(8,128)(2,1)S(1)}, u32[]{:S(2)}, u32[]{:S(2)}) collective-permute-start(bf16[128,1024]{1,0:T(8,128)(2,1)S(1)} %get-tuple-element.116), channel_id=1, source_target_pairs={{0,1},{1,0},{2,3},{3,2},{4,5},{5,4},{6,7},{7,6},{8,9},{9,8},{10,11... | collective-permute-start | bytes 786440 | tf_op jit(solution)/shard_map/ppermute | solution.py:312
  141.5 25.8 %collective-permute-start.40 = (bf16[128,1024]{1,0:T(8,128)(2,1)S(1)}, bf16[128,1024]{1,0:T(8,128)(2,1)S(1)}, u32[]{:S(2)}, u32[]{:S(2)}) collective-permute-start(bf16[128,1024]{1,0:T(8,128)(2,1)S(1)} %get-tuple-element.117), channel_id=1, source_target_pairs={{0,2},{1,3},{2,0},{3,1},{4,6},{5,7},{6,4},{7,5},{8,10},{9,11},{10,... | collective-permute-start | bytes 786440 | tf_op jit(solution)/shard_map/ppermute | solution.py:312
  150.8 17.8 %collective-permute-start.41 = (bf16[128,1024]{1,0:T(8,128)(2,1)S(1)}, bf16[128,1024]{1,0:T(8,128)(2,1)S(1)}, u32[]{:S(2)}, u32[]{:S(2)}) collective-permute-start(bf16[128,1024]{1,0:T(8,128)(2,1)S(1)} %get-tuple-element.118), channel_id=1, source_target_pairs={{0,3},{1,2},{2,1},{3,0},{4,7},{5,6},{6,5},{7,4},{8,11},{9,10},{10,... | collective-permute-start | bytes 786440 | tf_op jit(solution)/shard_map/ppermute | solution.py:312
  161.3 91.7 %collective-permute-start.35 = (bf16[1024,512]{1,0:T(8,128)(2,1)S(1)}, bf16[1024,512]{1,0:T(8,128)(2,1)S(1)}, u32[]{:S(2)}, u32[]{:S(2)}) collective-permute-start(bf16[1024,512]{1,0:T(8,128)(2,1)S(1)} %get-tuple-element.106.rest_6_), channel_id=1, source_target_pairs={{0,4},{4,0},{8,12},{12,8},{16,20},{20,16},{24,28},{28,24},{1,5},{5... | collective-permute-start | bytes 3145736 | tf_op jit(solution)/shard_map/ppermute | solution.py:306
  165.5 7.8 %collective-permute-start.36 = (bf16[384,256]{1,0:T(8,128)(2,1)S(1)}, bf16[384,256]{1,0:T(8,128)(2,1)S(1)}, u32[]{:S(2)}, u32[]{:S(2)}) collective-permute-start(bf16[384,256]{1,0:T(8,128)(2,1)S(1)} %get-tuple-element.108), channel_id=1, source_target_pairs={{0,1},{1,0},{2,3},{3,2},{4,5},{5,4},{6,7},{7,6},{8,9},{9,8},{10,11... | collective-permute-start | bytes 589832 | tf_op jit(solution)/shard_map/ppermute | solution.py:312
  167.3 11.2 %collective-permute-start.37 = (bf16[384,256]{1,0:T(8,128)(2,1)S(1)}, bf16[384,256]{1,0:T(8,128)(2,1)S(1)}, u32[]{:S(2)}, u32[]{:S(2)}) collective-permute-start(bf16[384,256]{1,0:T(8,128)(2,1)S(1)} %get-tuple-element.109), channel_id=1, source_target_pairs={{0,2},{1,3},{2,0},{3,1},{4,6},{5,7},{6,4},{7,5},{8,10},{9,11},{10,... | collective-permute-start | bytes 589832 | tf_op jit(solution)/shard_map/ppermute | solution.py:312
  168.6 9.9 %collective-permute-start.38 = (bf16[384,256]{1,0:T(8,128)(2,1)S(1)}, bf16[384,256]{1,0:T(8,128)(2,1)S(1)}, u32[]{:S(2)}, u32[]{:S(2)}) collective-permute-start(bf16[384,256]{1,0:T(8,128)(2,1)S(1)} %get-tuple-element.110), channel_id=1, source_target_pairs={{0,3},{1,2},{2,1},{3,0},{4,7},{5,6},{6,5},{7,4},{8,11},{9,10},{10,... | collective-permute-start | bytes 589832 | tf_op jit(solution)/shard_map/ppermute | solution.py:312
  169.1 33.5 %collective-permute-start.32 = (bf16[2,1024,128]{2,1,0:T(8,128)(2,1)S(1)}, bf16[2,1024,128]{2,1,0:T(8,128)(2,1)S(1)}, u32[]{:S(2)}, u32[]{:S(2)}) collective-permute-start(bf16[2,1024,128]{2,1,0:T(8,128)(2,1)S(1)} %collective-permute-done.31.rest_1_), channel_id=1, source_target_pairs={{8,0},{12,4},{16,8},{20,12},{9,1},{13,5},{17,9},{21,13},{10,2},{14... | collective-permute-start | bytes 1572872 | tf_op jit(solution)/shard_map/ppermute | solution.py:326
  173.3 82.6 %collective-permute-start.33 = (bf16[1024,384]{1,0:T(8,128)(2,1)S(1)}, bf16[1024,384]{1,0:T(8,128)(2,1)S(1)}, u32[]{:S(2)}, u32[]{:S(2)}) collective-permute-start(bf16[1024,384]{1,0:T(8,128)(2,1)S(1)} %get-tuple-element.103), channel_id=1, source_target_pairs={{0,4},{4,0},{8,12},{12,8},{16,20},{20,16},{24,28},{28,24},{1,5},{5... | collective-permute-start | bytes 2359304 | tf_op jit(solution)/shard_map/ppermute | solution.py:306
  179.5 10.2 %collective-permute-start.42 = (bf16[352,256]{1,0:T(8,128)(2,1)S(1)}, bf16[352,256]{1,0:T(8,128)(2,1)S(1)}, u32[]{:S(2)}, u32[]{:S(2)}) collective-permute-start(bf16[352,256]{1,0:T(8,128)(2,1)S(1)} %get-tuple-element.124), channel_id=1, source_target_pairs={{0,8},{4,12},{8,0},{12,4},{16,24},{20,28},{24,16},{28,20},{1,9},{5... | collective-permute-start | bytes 540680 | tf_op jit(solution)/shard_map/ppermute | solution.py:319
  182.1 17.2 %collective-permute-start.43 = (bf16[352,256]{1,0:T(8,128)(2,1)S(1)}, bf16[352,256]{1,0:T(8,128)(2,1)S(1)}, u32[]{:S(2)}, u32[]{:S(2)}) collective-permute-start(bf16[352,256]{1,0:T(8,128)(2,1)S(1)} %get-tuple-element.125), channel_id=1, source_target_pairs={{0,16},{4,20},{8,24},{12,28},{16,0},{20,4},{24,8},{28,12},{1,17},{... | collective-permute-start | bytes 540680 | tf_op jit(solution)/shard_map/ppermute | solution.py:319
  189.7 9.5 %collective-permute-start.44 = (bf16[352,256]{1,0:T(8,128)(2,1)S(1)}, bf16[352,256]{1,0:T(8,128)(2,1)S(1)}, u32[]{:S(2)}, u32[]{:S(2)}) collective-permute-start(bf16[352,256]{1,0:T(8,128)(2,1)S(1)} %get-tuple-element.126), channel_id=1, source_target_pairs={{0,24},{4,28},{8,16},{12,20},{16,8},{20,12},{24,0},{28,4},{1,25},{... | collective-permute-start | bytes 540680 | tf_op jit(solution)/shard_map/ppermute | solution.py:319
  199.4 8.7 %collective-permute-start.45 = (bf16[224,256]{1,0:T(8,128)(2,1)S(1)}, bf16[224,256]{1,0:T(8,128)(2,1)S(1)}, u32[]{:S(2)}, u32[]{:S(2)}) collective-permute-start(bf16[224,256]{1,0:T(8,128)(2,1)S(1)} %get-tuple-element.127.rest_0_), channel_id=1, source_target_pairs={{0,8},{4,12},{8,0},{12,4},{16,24},{20,28},{24,16},{28,20},{1,9},{5... | collective-permute-start | bytes 344072 | tf_op jit(solution)/shard_map/ppermute | solution.py:319
  202.6 10.5 %collective-permute-start.46 = (bf16[224,256]{1,0:T(8,128)(2,1)S(1)}, bf16[224,256]{1,0:T(8,128)(2,1)S(1)}, u32[]{:S(2)}, u32[]{:S(2)}) collective-permute-start(bf16[224,256]{1,0:T(8,128)(2,1)S(1)} %get-tuple-element.127.rest_0_), channel_id=1, source_target_pairs={{0,16},{4,20},{8,24},{12,28},{16,0},{20,4},{24,8},{28,12},{1,17},{... | collective-permute-start | bytes 344072 | tf_op jit(solution)/shard_map/ppermute | solution.py:319
  202.6 10.5 %collective-permute-start.47 = (bf16[224,256]{1,0:T(8,128)(2,1)S(1)}, bf16[224,256]{1,0:T(8,128)(2,1)S(1)}, u32[]{:S(2)}, u32[]{:S(2)}) collective-permute-start(bf16[224,256]{1,0:T(8,128)(2,1)S(1)} %get-tuple-element.127.rest_0_), channel_id=1, source_target_pairs={{0,24},{4,28},{8,16},{12,20},{16,8},{20,12},{24,0},{28,4},{1,25},{... | collective-permute-start | bytes 344072 | tf_op jit(solution)/shard_map/ppermute | solution.py:319
  208.0 6.2 %collective-permute-start.49 = (bf16[128,256]{1,0:T(8,128)(2,1)S(1)}, bf16[128,256]{1,0:T(8,128)(2,1)S(1)}, u32[]{:S(2)}, u32[]{:S(2)}) collective-permute-start(bf16[128,256]{1,0:T(8,128)(2,1)S(1)} %get-tuple-element.129), channel_id=1, source_target_pairs={{0,1},{1,0},{2,3},{3,2},{4,5},{5,4},{6,7},{7,6},{8,9},{9,8},{10,11... | collective-permute-start | bytes 196616 | tf_op jit(solution)/shard_map/ppermute | solution.py:312
  213.1 41.5 %collective-permute-start.34 = (bf16[1024,128]{1,0:T(8,128)(2,1)S(1)}, bf16[1024,128]{1,0:T(8,128)(2,1)S(1)}, u32[]{:S(2)}, u32[]{:S(2)}) collective-permute-start(bf16[1024,128]{1,0:T(8,128)(2,1)S(1)} %get-tuple-element.105), channel_id=1, source_target_pairs={{0,4},{4,0},{8,12},{12,8},{16,20},{20,16},{24,28},{28,24},{1,5},{5... | collective-permute-start | bytes 786440 | tf_op jit(solution)/shard_map/ppermute | solution.py:306
  213.7 47.4 %collective-permute-start.48 = (bf16[4,224,256]{2,1,0:T(8,128)(2,1)S(1)}, bf16[4,224,256]{2,1,0:T(8,128)(2,1)S(1)}, u32[]{:S(2)}, u32[]{:S(2)}) collective-permute-start(bf16[4,224,256]{2,1,0:T(8,128)(2,1)S(1)} %shard_map.121.rest_0_), channel_id=1, source_target_pairs={{0,4},{4,0},{8,12},{12,8},{16,20},{20,16},{24,28},{28,24},{1,5},{5... | collective-permute-start | bytes 1376264 | tf_op jit(solution)/shard_map/ppermute | solution.py:306
  214.2 4.3 %collective-permute-start.50 = (bf16[128,256]{1,0:T(8,128)(2,1)S(1)}, bf16[128,256]{1,0:T(8,128)(2,1)S(1)}, u32[]{:S(2)}, u32[]{:S(2)}) collective-permute-start(bf16[128,256]{1,0:T(8,128)(2,1)S(1)} %get-tuple-element.130), channel_id=1, source_target_pairs={{0,2},{1,3},{2,0},{3,1},{4,6},{5,7},{6,4},{7,5},{8,10},{9,11},{10,... | collective-permute-start | bytes 196616 | tf_op jit(solution)/shard_map/ppermute | solution.py:312
  218.5 5.2 %collective-permute-start.51 = (bf16[128,256]{1,0:T(8,128)(2,1)S(1)}, bf16[128,256]{1,0:T(8,128)(2,1)S(1)}, u32[]{:S(2)}, u32[]{:S(2)}) collective-permute-start(bf16[128,256]{1,0:T(8,128)(2,1)S(1)} %get-tuple-element.131), channel_id=1, source_target_pairs={{0,3},{1,2},{2,1},{3,0},{4,7},{5,6},{6,5},{7,4},{8,11},{9,10},{10,... | collective-permute-start | bytes 196616 | tf_op jit(solution)/shard_map/ppermute | solution.py:312
  224.3 3.8 %collective-permute-start.52 = (bf16[32,256]{1,0:T(8,128)(2,1)S(1)}, bf16[32,256]{1,0:T(8,128)(2,1)S(1)}, u32[]{:S(2)}, u32[]{:S(2)}) collective-permute-start(bf16[32,256]{1,0:T(8,128)(2,1)S(1)} %get-tuple-element.133), channel_id=1, source_target_pairs={{0,8},{4,12},{8,0},{12,4},{16,24},{20,28},{24,16},{28,20},{1,9},{5... | collective-permute-start | bytes 49160 | tf_op jit(solution)/shard_map/ppermute | solution.py:319
  228.1 4.7 %collective-permute-start.53 = (bf16[32,256]{1,0:T(8,128)(2,1)S(1)}, bf16[32,256]{1,0:T(8,128)(2,1)S(1)}, u32[]{:S(2)}, u32[]{:S(2)}) collective-permute-start(bf16[32,256]{1,0:T(8,128)(2,1)S(1)} %get-tuple-element.134), channel_id=1, source_target_pairs={{0,16},{4,20},{8,24},{12,28},{16,0},{20,4},{24,8},{28,12},{1,17},{... | collective-permute-start | bytes 49160 | tf_op jit(solution)/shard_map/ppermute | solution.py:319
  232.8 5.5 %collective-permute-start.54 = (bf16[32,256]{1,0:T(8,128)(2,1)S(1)}, bf16[32,256]{1,0:T(8,128)(2,1)S(1)}, u32[]{:S(2)}, u32[]{:S(2)}) collective-permute-start(bf16[32,256]{1,0:T(8,128)(2,1)S(1)} %get-tuple-element.135), channel_id=1, source_target_pairs={{0,24},{4,28},{8,16},{12,20},{16,8},{20,12},{24,0},{28,4},{1,25},{... | collective-permute-start | bytes 49160 | tf_op jit(solution)/shard_map/ppermute | solution.py:319
  238.3 3.8 %collective-permute-start.55 = (bf16[32,256]{1,0:T(8,128)(2,1)S(1)}, bf16[32,256]{1,0:T(8,128)(2,1)S(1)}, u32[]{:S(2)}, u32[]{:S(2)}) collective-permute-start(bf16[32,256]{1,0:T(8,128)(2,1)S(1)} %shard_map.123.rest_0_), channel_id=1, source_target_pairs={{0,8},{4,12},{8,0},{12,4},{16,24},{20,28},{24,16},{28,20},{1,9},{5... | collective-permute-start | bytes 49160 | tf_op jit(solution)/shard_map/ppermute | solution.py:319
  242.1 4.6 %collective-permute-start.56 = (bf16[32,256]{1,0:T(8,128)(2,1)S(1)}, bf16[32,256]{1,0:T(8,128)(2,1)S(1)}, u32[]{:S(2)}, u32[]{:S(2)}) collective-permute-start(bf16[32,256]{1,0:T(8,128)(2,1)S(1)} %shard_map.123.rest_0_), channel_id=1, source_target_pairs={{0,16},{4,20},{8,24},{12,28},{16,0},{20,4},{24,8},{28,12},{1,17},{... | collective-permute-start | bytes 49160 | tf_op jit(solution)/shard_map/ppermute | solution.py:319
  246.8 5.5 %collective-permute-start.57 = (bf16[32,256]{1,0:T(8,128)(2,1)S(1)}, bf16[32,256]{1,0:T(8,128)(2,1)S(1)}, u32[]{:S(2)}, u32[]{:S(2)}) collective-permute-start(bf16[32,256]{1,0:T(8,128)(2,1)S(1)} %shard_map.123.rest_0_), channel_id=1, source_target_pairs={{0,24},{4,28},{8,16},{12,20},{16,8},{20,12},{24,0},{28,4},{1,25},{... | collective-permute-start | bytes 49160 | tf_op jit(solution)/shard_map/ppermute | solution.py:319
  252.9 7.9 %collective-permute-start.58 = (bf16[4,32,256]{2,1,0:T(8,128)(2,1)S(1)}, bf16[4,32,256]{2,1,0:T(8,128)(2,1)S(1)}, u32[]{:S(2)}, u32[]{:S(2)}) collective-permute-start(bf16[4,32,256]{2,1,0:T(8,128)(2,1)S(1)} %shard_map.124.rest_2_), channel_id=1, source_target_pairs={{0,4},{4,0},{8,12},{12,8},{16,20},{20,16},{24,28},{28,24},{1,5},{5... | collective-permute-start | bytes 196616 | tf_op jit(solution)/shard_map/ppermute | solution.py:306
  252.9 7.9 %collective-permute-start.59 = (bf16[128,256]{1,0:T(8,128)(2,1)S(1)}, bf16[128,256]{1,0:T(8,128)(2,1)S(1)}, u32[]{:S(2)}, u32[]{:S(2)}) collective-permute-start(bf16[128,256]{1,0:T(8,128)(2,1)S(1)} %get-tuple-element.136.rest_4_), channel_id=1, source_target_pairs={{0,1},{1,0},{2,3},{3,2},{4,5},{5,4},{6,7},{7,6},{8,9},{9,8},{10,11... | collective-permute-start | bytes 196616 | tf_op jit(solution)/shard_map/ppermute | solution.py:312
  254.6 6.2 %collective-permute-start.60 = (bf16[128,256]{1,0:T(8,128)(2,1)S(1)}, bf16[128,256]{1,0:T(8,128)(2,1)S(1)}, u32[]{:S(2)}, u32[]{:S(2)}) collective-permute-start(bf16[128,256]{1,0:T(8,128)(2,1)S(1)} %get-tuple-element.136.rest_4_), channel_id=1, source_target_pairs={{0,2},{1,3},{2,0},{3,1},{4,6},{5,7},{6,4},{7,5},{8,10},{9,11},{10,... | collective-permute-start | bytes 196616 | tf_op jit(solution)/shard_map/ppermute | solution.py:312
  255.9 5.2 %collective-permute-start.61 = (bf16[128,256]{1,0:T(8,128)(2,1)S(1)}, bf16[128,256]{1,0:T(8,128)(2,1)S(1)}, u32[]{:S(2)}, u32[]{:S(2)}) collective-permute-start(bf16[128,256]{1,0:T(8,128)(2,1)S(1)} %get-tuple-element.136.rest_4_), channel_id=1, source_target_pairs={{0,3},{1,2},{2,1},{3,0},{4,7},{5,6},{6,5},{7,4},{8,11},{9,10},{10,... | collective-permute-start | bytes 196616 | tf_op jit(solution)/shard_map/ppermute | solution.py:312
  (5 other events, 37.7 us)

commit v4 on v3

--- a/solution.py
+++ b/solution.py
@@ -115,7 +115,7 @@
                 right = pltpu.roll(right, width, 1)
             else:
                 left = pltpu.roll(left, width, 1)
-            grad_kernel[tap, g * width : (g + 1) * width, :] = select_lanes(left, right).astype(BF)
+            grad_kernel[tap, g * width : (g + 1) * width, :] = select_lanes(left, right)
 
 
 def mixed_body(hops, tile, pair, meta, amounts, tap_zero, *rest):
@@ -142,10 +142,11 @@
         lax.fori_loop(0, half // tile, step, 0)
 
 
-def outer_body(chunks, parts, tile, by_rows, split, meta, *rest):
+def outer_body(chunks, parts, tile, split, taps, meta, *rest):
     count = chunks * (2 if split else 1)
     lefts, rest = rest[:count], rest[count:]
-    rights, outs, total = rest[:2], rest[2:-1], rest[-1]
+    rights, rest = rest[:2], rest[2:]
+    kernels, outs, total = rest[: -1 - parts - split], rest[-1 - parts - split : -1], rest[-1]
     total[...] = jnp.zeros_like(total)
     for slot in range(2):
 
@@ -162,15 +163,26 @@
             return carry
 
         lax.fori_loop(0, rights[slot].shape[0] // tile, step, 0)
-    rows, columns = outs[0].shape
+    columns = outs[0].shape[1]
     for k in range(parts):
-        if by_rows:
-            start = pl.multiple_of((meta[0] ^ k) * rows, rows)
-            got = total[pl.ds(start, rows), :]
-        else:
+        if split:
             start = pl.multiple_of((meta[0] ^ k) * columns, columns)
-            got = total[:, pl.ds(start, columns)]
-        outs[k][...] = got.astype(outs[k].dtype)
+            outs[k][...] = total[:, pl.ds(start, columns)].astype(outs[k].dtype)
+            continue
+        rows = total.shape[0] // parts
+        start = pl.multiple_of((meta[0] ^ k) * rows, rows)
+        outs[k][:rows, :] = total[pl.ds(start, rows), :].astype(outs[k].dtype)
+        few = taps // parts
+        spot = 0
+        for kernel in kernels:
+            for low in range(0, LANES, taps):
+                for tap in range(2):
+                    start = pl.multiple_of(low + (meta[0] ^ k) * few, 8)
+                    top, left = rows + spot // columns * few, spot % columns
+                    outs[k][top : top + few, left : left + LANES] = kernel[
+                        tap, pl.ds(start, few), :
+                    ].astype(outs[k].dtype)
+                    spot += LANES
 
 
 def signal_body(tile, base, *rest):
@@ -203,29 +215,30 @@
         outs[k][...] = total[pl.ds(at, rows), :].astype(outs[k].dtype)
 
 
-def gather_body(count, chips, pairs, meta, *rest):
+def gather_body(count, chips, few, meta, *rest):
     first, second = rest[:count], rest[count : 2 * count]
-    kernels, rest = rest[2 * count : 2 * count + pairs], rest[2 * count + pairs :]
-    outs, (sum_one, sum_two, held) = rest[:-3], rest[-3:]
+    outs, (sum_one, sum_two) = rest[2 * count : -2], rest[-2:]
     sum_one[...] = tree([x[...].astype(F32) for x in first])
     sum_two[...] = tree([x[...].astype(F32) for x in second])
-    width = sum_one.shape[1]
-    one, two, taps = sum_one.shape[0] // chips, sum_two.shape[0] // chips, held.shape[2]
-    for j in range(pairs):
-        for n in range(LANES // taps):
-            held[j * (LANES // taps) + n] = kernels[j][:, n * taps : (n + 1) * taps, :]
+    width, wide = sum_one.shape[1], sum_two.shape[1]
+    one = sum_one.shape[0] // chips
+    flat = sum_two.shape[0] - 2 * LANES * chips * few // wide
+    two = flat // chips
     for k in range(chips):
         at, kind = meta[1] ^ k, outs[k].dtype
         outs[k][:one, :] = sum_one[pl.ds(pl.multiple_of(at * one, 8), one), :].astype(kind)
         block = sum_two[pl.ds(pl.multiple_of(at * two, 8), two), :].astype(kind)
         top = one
-        for n in range(block.shape[1] // width):
+        for n in range(wide // width):
             outs[k][top : top + two, :] = block[:, n * width : (n + 1) * width]
             top += two
-        for tap in range(2):
-            column = (tap * LANES) % width
-            row = top + (tap * LANES) // width * taps
-            outs[k][row : row + taps, column : column + LANES] = held[at, tap].astype(kind)
+        each = wide // (2 * LANES)
+        row = pl.multiple_of(flat + at // each * few, 8)
+        lane = pl.multiple_of(at % each * (2 * LANES), 2 * LANES)
+        block = sum_two[pl.ds(row, few), pl.ds(lane, 2 * LANES)].astype(kind)
+        for n in range(2 * LANES // width):
+            outs[k][top : top + few, :] = block[:, n * width : (n + 1) * width]
+            top += few
 
 
 def divide_body(count, *rest):
@@ -326,7 +339,7 @@
         return lax.ppermute(x, "seq", [(i + 2, i) for i in range(seq_size - 2 * hop)])
 
     where = jnp.stack([fsdp_at, chip, core, lengths[0] - chip * block]).astype(jnp.int32)
-    wides = [share - LANES, LANES]
+    wides = [share // 2, share // 2]
     in_shares = call(
         functools.partial(share_body, fsdp_size),
         [shape((w_in.shape[0], x), BF) for x in (LANES, share - LANES)],
@@ -383,7 +396,7 @@
             chain.append(up(chain[-1], hop))
         out, tap_zero, tap_one, grad_kernel = call(
             functools.partial(conv_body, hops, tile, j),
-            [series, shape((2, samples, LANES), F32), series, shape((2, LANES, LANES), BF)],
+            [series, shape((2, samples, LANES), F32), series, shape((2, LANES, LANES), F32)],
             [where, amounts] + chain + [grad_gated[j], kernels[j]],
             scratch=[long, pltpu.VMEM((2 * LANES, 2 * LANES), F32)],
             flops=6 * block * 4 * LANES * LANES,
@@ -406,16 +419,20 @@
 
     tile = min(512, samples)
 
-    def outer(lefts, rights, by_rows, split):
+    few = conv_chans // fsdp_size
+
+    def outer(lefts, rights, split):
         count = len(lefts) // 2 if split else len(lefts)
         rows, columns = LANES * count, channels
-        one = (piece, columns) if by_rows else (rows, columns // fsdp_size)
+        more = [] if split else kernel_grads
+        tall = piece + 2 * LANES * chips * few // channels
+        one = (rows, columns // fsdp_size) if split else (tall, columns)
         return call(
-            functools.partial(outer_body, count, fsdp_size, tile, by_rows, split),
+            functools.partial(outer_body, count, fsdp_size, tile, split, conv_chans),
             [shape(one, F32)]
             + [shape(one, BF)] * (fsdp_size - 1)
             + ([shape((samples, rows), BF)] if split else []),
-            [where] + list(lefts) + list(rights),
+            [where] + list(lefts) + list(rights) + more,
             scratch=[pltpu.VMEM((rows, columns), F32)],
             flops=2 * block * rows * columns,
         )
@@ -429,30 +446,26 @@
         return [packed, to_partner(packed)]
 
     mixed_in, flats = [], []
-    for pick in (range(chunks - 1), range(chunks - 1, chunks)):
+    for pick in (range(chunks // 2), range(chunks // 2, chunks)):
         sides = []
         for j in pick:
             sides += [own_mixed[j], far_mixed[j]]
-        got = outer(sides, (record, record_far), False, True)
+        got = outer(sides, (record, record_far), True)
         mixed_in.append(to_partner(got[-1]))
         flats.append(from_fsdp(got[:fsdp_size]))
-    got = outer(gated, (upstream, upstream_far), True, False)
+    got = outer(gated, (upstream, upstream_far), False)
     flat_out = from_fsdp(got)
 
     own_rows = channels // fsdp_size
     in_part, out_part = wides[0] // chips, piece // chips
     panel_rows = in_part + out_part * (channels // own_rows)
-    kernel_rows = 2 * LANES * conv_chans // own_rows
+    kernel_rows = 2 * LANES * few // own_rows
     whole = (panel_rows + kernel_rows, own_rows)
     cut = call(
-        functools.partial(gather_body, fsdp_size, chips, chunks),
+        functools.partial(gather_body, fsdp_size, chips, few),
         [shape(whole, F32)] + [shape(whole, BF)] * (chips - 1),
-        [where] + flats[0] + flat_out + kernel_grads,
-        scratch=[
-            pltpu.VMEM((wides[0], own_rows), F32),
-            pltpu.VMEM((piece, channels), F32),
-            pltpu.VMEM((chips, 2, conv_chans, LANES), BF),
-        ],
+        [where] + flats[0] + flat_out,
+        scratch=[pltpu.VMEM((wides[0], own_rows), F32), pltpu.VMEM(flat_out[0].shape, F32)],
     )
     mine, mine_kernel = call(
         functools.partial(divide_body, chips),
@@ -506,11 +519,12 @@
         for f in range(fsdp_size):
             pair = [turned[c, f * piece : (f + 1) * piece, :] for c in range(2)]
             grad_in[:, 2 * f * piece : 2 * (f + 1) * piece] = jnp.concatenate(pair, axis=0).T
-        total = tree([x[...].astype(F32) for x in parts]) * factor
-        for tap in range(2):
-            column = (tap * LANES) % own_rows
-            row = (tap * LANES) // own_rows * conv_chans
-            grad_conv[tap] = total[row : row + conv_chans, column : column + LANES]
+        for k, x in enumerate(parts):
+            total = x[...].astype(F32) * factor
+            at = pl.multiple_of((meta[0] ^ k) * few, 8)
+            for tap in range(2):
+                left, top = (tap * LANES) % own_rows, (tap * LANES) // own_rows * few
+                grad_conv[tap, pl.ds(at, few), :] = total[top : top + few, left : left + LANES]
 
     grad_in, grad_out, grad_conv = call(
         finish_body,

time: 264 us -> 259 us (0.981)
  starting transfers between devices: 84.4 us -> 67.6 us
  waiting for transfers between devices: 119 us -> 131 us
    ppermute x8, waiting for transfers between devices: 33.7 us -> 64.7 us  [down(): lax.ppermute(x, 'seq', [(i + 2, i) for i in range(seq_size - 2 * hop)])]
    ppermute x8, waiting for transfers between devices: 0.02 us -> 23.6 us  [up(): lax.ppermute(x, 'seq', [(i, i + 2) for i in range(2 * (hop - 1), seq_size...]
    ppermute x18, waiting for transfers between devices: 60.7 us -> 37.7 us  [from_chips(): got.append(lax.ppermute(blocks[k], 'seq', pairs))]
    ppermute x21, waiting for transfers between devices: 25 us -> 5.33 us  [from_fsdp(): got.append(lax.ppermute(blocks[k], 'fsdp', pairs))]
    ppermute x21, starting transfers between devices: 29.4 us -> 23.7 us  [from_fsdp(): got.append(lax.ppermute(blocks[k], 'fsdp', pairs))]
    ppermute x18, starting transfers between devices: 25 us -> 19.4 us  [from_chips(): got.append(lax.ppermute(blocks[k], 'seq', pairs))]
    ppermute x8, starting transfers between devices: 18.2 us -> 13.1 us  [up(): lax.ppermute(x, 'seq', [(i, i + 2) for i in range(2 * (hop - 1), seq_size...]
  transfers between devices with their start and end apart: 62 -> 62, of which waited for: 25 -> 29; matrix products, arithmetic and copies ran while one was open for 0% -> 0% of each run, Pallas kernels for 20% -> 20%
where the time goes in v4:
time: 259 us; the launch traced here: 258 us
  waiting for transfers between devices  131 us (51%)
  starting transfers between devices  67.6 us (26%)
  Pallas kernels  54.4 us (21%)
  local copies, waits for them, and re-layouts  2.68 us (1%)
    ppermute x8, waiting for transfers between devices, down(): lax.ppermute(x, 'seq', [(i + 2, i) for i in range(seq_size - 2 * hop)])  64.7 us
    pallas_call x24, Pallas kernels, call(): pl.pallas_call(body, out_shape=tuple(outs), in_specs=[SM] * scalars + [VM...  54.4 us
    ppermute x18, waiting for transfers between devices, from_chips(): got.append(lax.ppermute(blocks[k], 'seq', pairs))  37.7 us
    ppermute x21, starting transfers between devices, from_fsdp(): got.append(lax.ppermute(blocks[k], 'fsdp', pairs))  23.7 us
    ppermute x8, waiting for transfers between devices, up(): lax.ppermute(x, 'seq', [(i, i + 2) for i in range(2 * (hop - 1), seq_size...  23.6 us
    ppermute x18, starting transfers between devices, from_chips(): got.append(lax.ppermute(blocks[k], 'seq', pairs))  19.4 us
    ppermute x8, starting transfers between devices, up(): lax.ppermute(x, 'seq', [(i, i + 2) for i in range(2 * (hop - 1), seq_size...  13.1 us
    ppermute x8, starting transfers between devices, down(): lax.ppermute(x, 'seq', [(i + 2, i) for i in range(seq_size - 2 * hop)])  10.5 us
  transfers between devices with their start and end apart: 62, of which 29 were waited for; matrix products, arithmetic and copies ran while one was open for 0% of the time, Pallas kernels for 20%

profile of v4, /device:TPU:0, one launch (start us, length us, event | category | flops | bytes accessed | tf_op | source)
XLA Modules:
  0.0 258.0 jit_solution(15531464312601663648)
XLA Ops:
  1.3 3.0 %collective-permute-start = (s32[2]{0:T(128)}, s32[2]{0:T(128)S(1)}, u32[]{:S(2)}, u32[]{:S(2)}) collective-permute-start(s32[2]{0:T(128)} %rest_0_.1), channel_id=1, source_target_pairs={{0,8},{4,12},{8,0},{12,4},{16,24},{20,28},{24,16},{28,20},{1,9},{5... | collective-permute-start | bytes 32 | tf_op jit(solution)/shard_map/ppermute | solution.py:332
  4.3 2.6 %collective-permute-start.1 = (s32[2]{0:T(128)}, s32[2]{0:T(128)S(1)}, u32[]{:S(2)}, u32[]{:S(2)}) collective-permute-start(s32[2]{0:T(128)} %rest_0_.1), channel_id=1, source_target_pairs={{0,16},{4,20},{8,24},{12,28},{16,0},{20,4},{24,8},{28,12},{1,17},{... | collective-permute-start | bytes 32 | tf_op jit(solution)/shard_map/ppermute | solution.py:332
  8.9 3.1 %collective-permute-start.4 = (bf16[2,128,128]{2,1,0:T(8,128)(2,1)}, bf16[2,128,128]{2,1,0:T(8,128)(2,1)S(1)}, u32[]{:S(2)}, u32[]{:S(2)}) collective-permute-start(bf16[2,128,128]{2,1,0:T(8,128)(2,1)} %rest_4_.1), channel_id=1, source_target_pairs={{0,16},{4,20},{8,24},{12,28},{16,0},{20,4},{24,8},{28,12},{1,17},{... | collective-permute-start | bytes 196616 | tf_op jit(solution)/shard_map/ppermute | solution.py:332
  14.1 1.7 collective-permute-start.7
  16.3 1.5 collective-permute-start.8
  18.7 2.5 collective-permute-start.9
  21.7 1.3 collective-permute-start.19
  24.0 2.7 %collective-permute-start.20 = (bf16[256,384]{1,0:T(8,128)(2,1)S(1)}, bf16[256,384]{1,0:T(8,128)(2,1)S(1)}, u32[]{:S(2)}, u32[]{:S(2)}) collective-permute-start(bf16[256,384]{1,0:T(8,128)(2,1)S(1)} %get-tuple-element.80.rest_0_), channel_id=1, source_target_pairs={{0,3},{1,2},{2,1},{3,0},{4,7},{5,6},{6,5},{7,4},{8,11},{9,10},{10,... | collective-permute-start | bytes 589832 | tf_op jit(solution)/shard_map/ppermute | solution.py:325
  27.4 1.6 copy-done.1
  29.0 2.3 shard_map.104
  31.6 2.7 %collective-permute-start.15 = (bf16[128,1024]{1,0:T(8,128)(2,1)S(1)}, bf16[128,1024]{1,0:T(8,128)(2,1)S(1)}, u32[]{:S(2)}, u32[]{:S(2)}) collective-permute-start(bf16[128,1024]{1,0:T(8,128)(2,1)S(1)} %dynamic-slice_bitcast_fusion.rest_0_), channel_id=1, source_target_pairs={{0,3},{1,2},{2,1},{3,0},{4,7},{5,6},{6,5},{7,4},{8,11},{9,10},{10,... | collective-permute-start | bytes 786440 | tf_op jit(solution)/shard_map/ppermute | solution.py:325
  34.4 1.3 collective-permute-start.10
  35.7 3.5 %shard_map.108 = (bf16[2,1024,128]{2,1,0:T(8,128)(2,1)S(1)}, bf16[2,1024,128]{2,1,0:T(8,128)(2,1)S(1)}, bf16[2,1024,128]{2,1,0:T(8,128)(2,1)S(1)}, bf16[1024,512]{1,0:T(8,128)(2,1)S(1)}) custom-call(s32[4]{0:T(128)S(1)} %pad_add_fusion.meta, bf16[1024,1024]{1,0:T(8,128)(2,1)S(1)} %bitcast.15, bf16[1024,1024]{1,0:T(8,128)(2,1)S(1)} %collective-permute-done.6.partner.rest_5_, ...), custom_call_target="tpu_custom_call" | custom-call | flops 1610612736 | bytes 7864336 | tf_op jit(solution)/shard_map/pallas_call | solution.py:26
  39.3 3.7 %collective-permute-start.21 = (bf16[2,1024,128]{2,1,0:T(8,128)(2,1)S(1)}, bf16[2,1024,128]{2,1,0:T(8,128)(2,1)S(1)}, u32[]{:S(2)}, u32[]{:S(2)}) collective-permute-start(bf16[2,1024,128]{2,1,0:T(8,128)(2,1)S(1)} %get-tuple-element.82.rest_0_), channel_id=1, source_target_pairs={{0,8},{4,12},{8,16},{12,20},{16,24},{20,28},{1,9},{5,13},{9,17},{1... | collective-permute-start | bytes 1572872 | tf_op jit(solution)/shard_map/ppermute | solution.py:336
  42.9 3.5 %collective-permute-start.25 = (bf16[2,1024,128]{2,1,0:T(8,128)(2,1)S(1)}, bf16[2,1024,128]{2,1,0:T(8,128)(2,1)S(1)}, u32[]{:S(2)}, u32[]{:S(2)}) collective-permute-start(bf16[2,1024,128]{2,1,0:T(8,128)(2,1)S(1)} %get-tuple-element.88.rest_0_), channel_id=1, source_target_pairs={{0,8},{4,12},{8,16},{12,20},{16,24},{20,28},{1,9},{5,13},{9,17},{1... | collective-permute-start | bytes 1572872 | tf_op jit(solution)/shard_map/ppermute | solution.py:336
  46.4 1.9 collective-permute-start.29
  49.0 9.7 %collective-permute-done.21.rest_1_ = bf16[2,1024,128]{2,1,0:T(8,128)(2,1)S(1)} collective-permute-done((bf16[2,1024,128]{2,1,0:T(8,128)(2,1)S(1)}, bf16[2,1024,128]{2,1,0:T(8,128)(2,1)S(1)}, u32[]{:S(2)}, u32[]{:S(2)}) %collective-permute-start.21) | collective-permute-done | bytes 524320 | tf_op jit(solution)/shard_map/ppermute | solution.py:336
  59.5 2.0 shard_map.102
  61.5 8.5 %collective-permute-done.25.rest_1_ = bf16[2,1024,128]{2,1,0:T(8,128)(2,1)S(1)} collective-permute-done((bf16[2,1024,128]{2,1,0:T(8,128)(2,1)S(1)}, bf16[2,1024,128]{2,1,0:T(8,128)(2,1)S(1)}, u32[]{:S(2)}, u32[]{:S(2)}) %collective-permute-start.25) | collective-permute-done | bytes 524320 | tf_op jit(solution)/shard_map/ppermute | solution.py:336
  70.7 5.3 %collective-permute-done.29.rest_1_ = bf16[2,1024,128]{2,1,0:T(8,128)(2,1)S(1)} collective-permute-done((bf16[2,1024,128]{2,1,0:T(8,128)(2,1)S(1)}, bf16[2,1024,128]{2,1,0:T(8,128)(2,1)S(1)}, u32[]{:S(2)}, u32[]{:S(2)}) %collective-permute-start.29) | collective-permute-done | bytes 524320 | tf_op jit(solution)/shard_map/ppermute | solution.py:336
  76.7 4.7 %shard_map.105 = (bf16[2,1024,128]{2,1,0:T(8,128)(2,1)S(1)}, bf16[2,1024,128]{2,1,0:T(8,128)(2,1)S(1)}, bf16[2,1024,128]{2,1,0:T(8,128)(2,1)S(1)}, bf16[2,1024,128]{2,1,0:T(8,128)(2,1)S(1)}) custom-call(s32[4]{0:T(128)S(1)} %pad_add_fusion.meta, bf16[1024,1024]{1,0:T(8,128)(2,1)S(1)} %bitcast.19, bf16[1024,1024]{1,0:T(8,128)(2,1)} %collective-permute-done.12.partner.rest_5_, ...), custom_call_target="tpu_custom_call" | custom-call | flops 2147483648 | bytes 7340048 | tf_op jit(solution)/shard_map/pallas_call | solution.py:26
  81.4 4.5 %shard_map.106 = (bf16[2,1024,128]{2,1,0:T(8,128)(2,1)S(1)}, f32[2,1024,128]{2,1,0:T(8,128)S(1)}, bf16[2,1024,128]{2,1,0:T(8,128)(2,1)S(1)}, f32[2,128,128]{2,1,0:T(8,128)S(1)}) custom-call(s32[4]{0:T(128)S(1)} %pad_add_fusion.meta, s32[8]{0:T(128)S(1)} %get-tuple-element.72.amounts, bf16[2,1024,128]{2,1,0:T(8,128)(2,1)S(1)} %get-tuple-element.74.rest_0_, ...), custom_call_target="tpu_custom_call" | custom-call | flops 805306368 | bytes 4456496 | tf_op jit(solution)/shard_map/pallas_call | solution.py:26
  85.9 1.3 collective-permute-start.16
  87.2 4.5 %shard_map.109 = (bf16[2,1024,128]{2,1,0:T(8,128)(2,1)S(1)}, f32[2,1024,128]{2,1,0:T(8,128)S(1)}, bf16[2,1024,128]{2,1,0:T(8,128)(2,1)S(1)}, f32[2,128,128]{2,1,0:T(8,128)S(1)}) custom-call(s32[4]{0:T(128)S(1)} %pad_add_fusion.meta, s32[8]{0:T(128)S(1)} %get-tuple-element.72.amounts, bf16[2,1024,128]{2,1,0:T(8,128)(2,1)S(1)} %get-tuple-element.82.rest_0_, ...), custom_call_target="tpu_custom_call" | custom-call | flops 805306368 | bytes 4456496 | tf_op jit(solution)/shard_map/pallas_call | solution.py:26
  91.7 1.3 collective-permute-start.23
  93.0 4.5 %shard_map.111 = (bf16[2,1024,128]{2,1,0:T(8,128)(2,1)S(1)}, f32[2,1024,128]{2,1,0:T(8,128)S(1)}, bf16[2,1024,128]{2,1,0:T(8,128)(2,1)S(1)}, f32[2,128,128]{2,1,0:T(8,128)S(1)}) custom-call(s32[4]{0:T(128)S(1)} %pad_add_fusion.meta, s32[8]{0:T(128)S(1)} %get-tuple-element.72.amounts, bf16[2,1024,128]{2,1,0:T(8,128)(2,1)S(1)} %get-tuple-element.88.rest_0_, ...), custom_call_target="tpu_custom_call" | custom-call | flops 805306368 | bytes 4456496 | tf_op jit(solution)/shard_map/pallas_call | solution.py:26
  97.5 1.3 collective-permute-start.27
  98.8 4.5 %shard_map.113 = (bf16[2,1024,128]{2,1,0:T(8,128)(2,1)S(1)}, f32[2,1024,128]{2,1,0:T(8,128)S(1)}, bf16[2,1024,128]{2,1,0:T(8,128)(2,1)S(1)}, f32[2,128,128]{2,1,0:T(8,128)S(1)}) custom-call(s32[4]{0:T(128)S(1)} %pad_add_fusion.meta, s32[8]{0:T(128)S(1)} %get-tuple-element.72.amounts, bf16[2,1024,128]{2,1,0:T(8,128)(2,1)S(1)} %get-tuple-element.94.rest_0_, ...), custom_call_target="tpu_custom_call" | custom-call | flops 805306368 | bytes 4456496 | tf_op jit(solution)/shard_map/pallas_call | solution.py:26
  103.2 1.3 collective-permute-start.31
  104.5 8.0 %collective-permute-done.16.rest_1_ = bf16[2,1024,128]{2,1,0:T(8,128)(2,1)S(1)} collective-permute-done((bf16[2,1024,128]{2,1,0:T(8,128)(2,1)S(1)}, bf16[2,1024,128]{2,1,0:T(8,128)(2,1)S(1)}, u32[]{:S(2)}, u32[]{:S(2)}) %collective-permute-start.16) | collective-permute-done | bytes 524320 | tf_op jit(solution)/shard_map/ppermute | solution.py:339
  112.6 1.3 collective-permute-start.17
  113.9 10.0 %collective-permute-done.23.rest_1_ = bf16[2,1024,128]{2,1,0:T(8,128)(2,1)S(1)} collective-permute-done((bf16[2,1024,128]{2,1,0:T(8,128)(2,1)S(1)}, bf16[2,1024,128]{2,1,0:T(8,128)(2,1)S(1)}, u32[]{:S(2)}, u32[]{:S(2)}) %collective-permute-start.23) | collective-permute-done | bytes 524320 | tf_op jit(solution)/shard_map/ppermute | solution.py:339
  123.8 1.3 collective-permute-start.24
  125.1 4.9 %shard_map.118 = (f32[160,1024]{1,0:T(8,128)S(1)}, bf16[160,1024]{1,0:T(8,128)(2,1)S(1)}, bf16[160,1024]{1,0:T(8,128)(2,1)S(1)}, bf16[160,1024]{1,0:T(8,128)(2,1)S(1)}) custom-call(s32[4]{0:T(128)S(1)} %pad_add_fusion.meta, bf16[2,1024,128]{2,1,0:T(8,128)(2,1)S(1)} %get-tuple-element.111.rest_0_, bf16[2,1024,128]{2,1,0:T(8,128)(2,1)S(1)} %get-tuple-element.112.rest_1_, ...), custom_call_target="tpu_custom_call" | custom-call | flops 2147483648 | bytes 8454160 | tf_op jit(solution)/shard_map/pallas_call | solution.py:26
  130.1 5.9 %collective-permute-done.27.rest_1_ = bf16[2,1024,128]{2,1,0:T(8,128)(2,1)S(1)} collective-permute-done((bf16[2,1024,128]{2,1,0:T(8,128)(2,1)S(1)}, bf16[2,1024,128]{2,1,0:T(8,128)(2,1)S(1)}, u32[]{:S(2)}, u32[]{:S(2)}) %collective-permute-start.27) | collective-permute-done | bytes 524320 | tf_op jit(solution)/shard_map/ppermute | solution.py:339
  136.0 1.3 collective-permute-start.28
  137.2 9.9 %collective-permute-done.31.rest_1_ = bf16[2,1024,128]{2,1,0:T(8,128)(2,1)S(1)} collective-permute-done((bf16[2,1024,128]{2,1,0:T(8,128)(2,1)S(1)}, bf16[2,1024,128]{2,1,0:T(8,128)(2,1)S(1)}, u32[]{:S(2)}, u32[]{:S(2)}) %collective-permute-start.31) | collective-permute-done | bytes 524320 | tf_op jit(solution)/shard_map/ppermute | solution.py:339
  147.2 1.5 collective-permute-start.32
  148.7 9.7 %collective-permute-done.17.rest_2_ = bf16[2,1024,128]{2,1,0:T(8,128)(2,1)S(1)} collective-permute-done((bf16[2,1024,128]{2,1,0:T(8,128)(2,1)S(1)}, bf16[2,1024,128]{2,1,0:T(8,128)(2,1)S(1)}, u32[]{:S(2)}, u32[]{:S(2)}) %collective-permute-start.17) | collective-permute-done | bytes 524320 | tf_op jit(solution)/shard_map/ppermute | solution.py:339
  158.4 11.2 %collective-permute-done.24.rest_2_ = bf16[2,1024,128]{2,1,0:T(8,128)(2,1)S(1)} collective-permute-done((bf16[2,1024,128]{2,1,0:T(8,128)(2,1)S(1)}, bf16[2,1024,128]{2,1,0:T(8,128)(2,1)S(1)}, u32[]{:S(2)}, u32[]{:S(2)}) %collective-permute-start.24) | collective-permute-done | bytes 524320 | tf_op jit(solution)/shard_map/ppermute | solution.py:339
  171.7 2.5 shard_map.115
  175.3 4.7 %collective-permute-done.28.rest_2_ = bf16[2,1024,128]{2,1,0:T(8,128)(2,1)S(1)} collective-permute-done((bf16[2,1024,128]{2,1,0:T(8,128)(2,1)S(1)}, bf16[2,1024,128]{2,1,0:T(8,128)(2,1)S(1)}, u32[]{:S(2)}, u32[]{:S(2)}) %collective-permute-start.28) | collective-permute-done | bytes 524320 | tf_op jit(solution)/shard_map/ppermute | solution.py:339
  180.4 5.2 %collective-permute-done.32.rest_2_ = bf16[2,1024,128]{2,1,0:T(8,128)(2,1)S(1)} collective-permute-done((bf16[2,1024,128]{2,1,0:T(8,128)(2,1)S(1)}, bf16[2,1024,128]{2,1,0:T(8,128)(2,1)S(1)}, u32[]{:S(2)}, u32[]{:S(2)}) %collective-permute-start.32) | collective-permute-done | bytes 524320 | tf_op jit(solution)/shard_map/ppermute | solution.py:339
  185.6 1.6 collective-permute-start.38
  189.3 2.6 shard_map.116
  193.7 3.1 %collective-permute-start.42 = (bf16[224,256]{1,0:T(8,128)(2,1)S(1)}, bf16[224,256]{1,0:T(8,128)(2,1)S(1)}, u32[]{:S(2)}, u32[]{:S(2)}) collective-permute-start(bf16[224,256]{1,0:T(8,128)(2,1)S(1)} %get-tuple-element.124), channel_id=1, source_target_pairs={{0,8},{4,12},{8,0},{12,4},{16,24},{20,28},{24,16},{28,20},{1,9},{5... | collective-permute-start | bytes 344072 | tf_op jit(solution)/shard_map/ppermute | solution.py:332
  196.8 2.4 collective-permute-start.44
  199.8 4.7 %collective-permute-done.43.rest_2_ = bf16[224,256]{1,0:T(8,128)(2,1)S(1)} collective-permute-done((bf16[224,256]{1,0:T(8,128)(2,1)S(1)}, bf16[224,256]{1,0:T(8,128)(2,1)S(1)}, u32[]{:S(2)}, u32[]{:S(2)}) %collective-permute-start.43) | collective-permute-done | bytes 114720 | tf_op jit(solution)/shard_map/ppermute | solution.py:332
  205.1 1.5 collective-permute-start.51
  206.6 2.8 %collective-permute-done.50.rest_2_ = bf16[256,256]{1,0:T(8,128)(2,1)S(1)} collective-permute-done((bf16[256,256]{1,0:T(8,128)(2,1)S(1)}, bf16[256,256]{1,0:T(8,128)(2,1)S(1)}, u32[]{:S(2)}, u32[]{:S(2)}) %collective-permute-start.50) | collective-permute-done | bytes 131104 | tf_op jit(solution)/shard_map/ppermute | solution.py:325
  209.5 1.5 collective-permute-done.51.rest_3_
  212.1 2.0 collective-permute-done.45.rest_1_
  215.2 2.5 collective-permute-done.46.rest_2_
  217.8 2.7 %collective-permute-done.47.rest_3_ = bf16[192,256]{1,0:T(8,128)(2,1)S(1)} collective-permute-done((bf16[192,256]{1,0:T(8,128)(2,1)S(1)}, bf16[192,256]{1,0:T(8,128)(2,1)S(1)}, u32[]{:S(2)}, u32[]{:S(2)}) %collective-permute-start.47) | collective-permute-done | bytes 98336 | tf_op jit(solution)/shard_map/ppermute | solution.py:332
  221.7 4.8 %collective-permute-done.53.rest_2_ = bf16[64,256]{1,0:T(8,128)(2,1)S(1)} collective-permute-done((bf16[64,256]{1,0:T(8,128)(2,1)S(1)}, bf16[64,256]{1,0:T(8,128)(2,1)S(1)}, u32[]{:S(2)}, u32[]{:S(2)}) %collective-permute-start.53) | collective-permute-done | bytes 32800 | tf_op jit(solution)/shard_map/ppermute | solution.py:332
  226.4 1.3 collective-permute-start.54
  227.7 4.4 %collective-permute-done.54.rest_3_ = bf16[64,256]{1,0:T(8,128)(2,1)S(1)} collective-permute-done((bf16[64,256]{1,0:T(8,128)(2,1)S(1)}, bf16[64,256]{1,0:T(8,128)(2,1)S(1)}, u32[]{:S(2)}, u32[]{:S(2)}) %collective-permute-start.54) | collective-permute-done | bytes 32800 | tf_op jit(solution)/shard_map/ppermute | solution.py:332
  232.2 3.9 %collective-permute-done.55.rest_1_ = bf16[64,256]{1,0:T(8,128)(2,1)S(1)} collective-permute-done((bf16[64,256]{1,0:T(8,128)(2,1)S(1)}, bf16[64,256]{1,0:T(8,128)(2,1)S(1)}, u32[]{:S(2)}, u32[]{:S(2)}) %collective-permute-start.55) | collective-permute-done | bytes 32800 | tf_op jit(solution)/shard_map/ppermute | solution.py:332
  236.1 5.2 %collective-permute-done.56.rest_2_ = bf16[64,256]{1,0:T(8,128)(2,1)S(1)} collective-permute-done((bf16[64,256]{1,0:T(8,128)(2,1)S(1)}, bf16[64,256]{1,0:T(8,128)(2,1)S(1)}, u32[]{:S(2)}, u32[]{:S(2)}) %collective-permute-start.56) | collective-permute-done | bytes 32800 | tf_op jit(solution)/shard_map/ppermute | solution.py:332
  241.4 1.2 collective-permute-start.57
  242.6 4.5 %collective-permute-done.57.rest_3_ = bf16[64,256]{1,0:T(8,128)(2,1)S(1)} collective-permute-done((bf16[64,256]{1,0:T(8,128)(2,1)S(1)}, bf16[64,256]{1,0:T(8,128)(2,1)S(1)}, u32[]{:S(2)}, u32[]{:S(2)}) %collective-permute-start.57) | collective-permute-done | bytes 32800 | tf_op jit(solution)/shard_map/ppermute | solution.py:332
  248.9 1.2 collective-permute-start.60
  251.3 4.3 %shard_map.117 = bf16[1024,1024]{1,0:T(8,128)(2,1)} custom-call(bf16[1024,1024]{1,0:T(8,128)(2,1)S(1)} %bitcast.21, bf16[1024,128]{1,0:T(8,128)(2,1)S(1)} %get-tuple-element.79.rest_0_, bf16[1024,128]{1,0:T(8,128)(2,1)S(1)} %get-tuple-element.87.rest_2_.rest_1_, bf16[1024,128]{1,0:T(8,128)(2,1)S(1)} %get-tuple-element.93.rest_0_.rest_2_, ...), custom_call_target="tpu_custom_call" | custom-call | flops 2147483648 | bytes 8388608 | tf_op jit(solution)/shard_map/pallas_call | solution.py:26
  255.6 2.3 shard_map.125
  (100 shorter events, 25.8 us)
Async XLA Ops:
  0.6 26.1 %copy-start = (bf16[256,1024]{1,0:T(8,128)(2,1)S(1)}, bf16[256,1024]{1,0:T(8,128)(2,1)}, u32[]{:S(2)}) copy-start(bf16[256,1024]{1,0:T(8,128)(2,1)} %param.11) | copy-start | bytes 1572868
  0.6 26.1 %collective-permute-start.6 = (bf16[1024,1024]{1,0:T(8,128)(2,1)}, bf16[1024,1024]{1,0:T(8,128)(2,1)S(1)}, u32[]{:S(2)}, u32[]{:S(2)}) collective-permute-start(bf16[1024,1024]{1,0:T(8,128)(2,1)} %bitcast.13), channel_id=1, source_target_pairs={{0,4},{4,0},{8,12},{12,8},{16,20},{20,16},{24,28},{28,24},{1,5},{5... | collective-permute-start | bytes 6291464 | tf_op jit(solution)/shard_map/ppermute | solution.py:319
  1.2 75.5 %collective-permute-start.12 = (bf16[1024,1024]{1,0:T(8,128)(2,1)}, bf16[1024,1024]{1,0:T(8,128)(2,1)}, u32[]{:S(2)}, u32[]{:S(2)}) collective-permute-start(bf16[1024,1024]{1,0:T(8,128)(2,1)} %bitcast.18), channel_id=1, source_target_pairs={{0,4},{4,0},{8,12},{12,8},{16,20},{20,16},{24,28},{28,24},{1,5},{5... | collective-permute-start | bytes 6291464 | tf_op jit(solution)/shard_map/ppermute | solution.py:319
  1.3 6.2 %collective-permute-start = (s32[2]{0:T(128)}, s32[2]{0:T(128)S(1)}, u32[]{:S(2)}, u32[]{:S(2)}) collective-permute-start(s32[2]{0:T(128)} %rest_0_.1), channel_id=1, source_target_pairs={{0,8},{4,12},{8,0},{12,4},{16,24},{20,28},{24,16},{28,20},{1,9},{5... | collective-permute-start | bytes 32 | tf_op jit(solution)/shard_map/ppermute | solution.py:332
  4.3 4.6 %collective-permute-start.1 = (s32[2]{0:T(128)}, s32[2]{0:T(128)S(1)}, u32[]{:S(2)}, u32[]{:S(2)}) collective-permute-start(s32[2]{0:T(128)} %rest_0_.1), channel_id=1, source_target_pairs={{0,16},{4,20},{8,24},{12,28},{16,0},{20,4},{24,8},{28,12},{1,17},{... | collective-permute-start | bytes 32 | tf_op jit(solution)/shard_map/ppermute | solution.py:332
  6.9 5.5 %collective-permute-start.2 = (s32[2]{0:T(128)}, s32[2]{0:T(128)S(1)}, u32[]{:S(2)}, u32[]{:S(2)}) collective-permute-start(s32[2]{0:T(128)} %rest_0_.1), channel_id=1, source_target_pairs={{0,24},{4,28},{8,16},{12,20},{16,8},{20,12},{24,0},{28,4},{1,25},{... | collective-permute-start | bytes 32 | tf_op jit(solution)/shard_map/ppermute | solution.py:332
  7.5 6.6 %collective-permute-start.3 = (bf16[2,128,128]{2,1,0:T(8,128)(2,1)}, bf16[2,128,128]{2,1,0:T(8,128)(2,1)S(1)}, u32[]{:S(2)}, u32[]{:S(2)}) collective-permute-start(bf16[2,128,128]{2,1,0:T(8,128)(2,1)} %rest_4_.1), channel_id=1, source_target_pairs={{0,8},{4,12},{8,0},{12,4},{16,24},{20,28},{24,16},{28,20},{1,9},{5... | collective-permute-start | bytes 196616 | tf_op jit(solution)/shard_map/ppermute | solution.py:332
  8.9 7.4 %collective-permute-start.4 = (bf16[2,128,128]{2,1,0:T(8,128)(2,1)}, bf16[2,128,128]{2,1,0:T(8,128)(2,1)S(1)}, u32[]{:S(2)}, u32[]{:S(2)}) collective-permute-start(bf16[2,128,128]{2,1,0:T(8,128)(2,1)} %rest_4_.1), channel_id=1, source_target_pairs={{0,16},{4,20},{8,24},{12,28},{16,0},{20,4},{24,8},{28,12},{1,17},{... | collective-permute-start | bytes 196616 | tf_op jit(solution)/shard_map/ppermute | solution.py:332
  12.4 6.3 %collective-permute-start.5 = (bf16[2,128,128]{2,1,0:T(8,128)(2,1)}, bf16[2,128,128]{2,1,0:T(8,128)(2,1)S(1)}, u32[]{:S(2)}, u32[]{:S(2)}) collective-permute-start(bf16[2,128,128]{2,1,0:T(8,128)(2,1)} %rest_4_.1), channel_id=1, source_target_pairs={{0,24},{4,28},{8,16},{12,20},{16,8},{20,12},{24,0},{28,4},{1,25},{... | collective-permute-start | bytes 196616 | tf_op jit(solution)/shard_map/ppermute | solution.py:332
  14.1 7.1 %collective-permute-start.7 = (bf16[256,128]{1,0:T(8,128)(2,1)S(1)}, bf16[256,128]{1,0:T(8,128)(2,1)S(1)}, u32[]{:S(2)}, u32[]{:S(2)}) collective-permute-start(bf16[256,128]{1,0:T(8,128)(2,1)S(1)} %get-tuple-element.73.rest_0_), channel_id=1, source_target_pairs={{0,1},{1,0},{2,3},{3,2},{4,5},{5,4},{6,7},{7,6},{8,9},{9,8},{10,11... | collective-permute-start | bytes 196616 | tf_op jit(solution)/shard_map/ppermute | solution.py:325
  16.3 5.5 %collective-permute-start.8 = (bf16[256,128]{1,0:T(8,128)(2,1)S(1)}, bf16[256,128]{1,0:T(8,128)(2,1)S(1)}, u32[]{:S(2)}, u32[]{:S(2)}) collective-permute-start(bf16[256,128]{1,0:T(8,128)(2,1)S(1)} %get-tuple-element.73.rest_0_), channel_id=1, source_target_pairs={{0,2},{1,3},{2,0},{3,1},{4,6},{5,7},{6,4},{7,5},{8,10},{9,11},{10,... | collective-permute-start | bytes 196616 | tf_op jit(solution)/shard_map/ppermute | solution.py:325
  18.7 5.3 %collective-permute-start.9 = (bf16[256,128]{1,0:T(8,128)(2,1)S(1)}, bf16[256,128]{1,0:T(8,128)(2,1)S(1)}, u32[]{:S(2)}, u32[]{:S(2)}) collective-permute-start(bf16[256,128]{1,0:T(8,128)(2,1)S(1)} %get-tuple-element.73.rest_0_), channel_id=1, source_target_pairs={{0,3},{1,2},{2,1},{3,0},{4,7},{5,6},{6,5},{7,4},{8,11},{9,10},{10,... | collective-permute-start | bytes 196616 | tf_op jit(solution)/shard_map/ppermute | solution.py:325
  21.2 10.1 %collective-permute-start.18 = (bf16[256,384]{1,0:T(8,128)(2,1)S(1)}, bf16[256,384]{1,0:T(8,128)(2,1)S(1)}, u32[]{:S(2)}, u32[]{:S(2)}) collective-permute-start(bf16[256,384]{1,0:T(8,128)(2,1)S(1)} %get-tuple-element.80.rest_0_), channel_id=1, source_target_pairs={{0,1},{1,0},{2,3},{3,2},{4,5},{5,4},{6,7},{7,6},{8,9},{9,8},{10,11... | collective-permute-start | bytes 589832 | tf_op jit(solution)/shard_map/ppermute | solution.py:325
  21.7 9.9 %collective-permute-start.19 = (bf16[256,384]{1,0:T(8,128)(2,1)S(1)}, bf16[256,384]{1,0:T(8,128)(2,1)S(1)}, u32[]{:S(2)}, u32[]{:S(2)}) collective-permute-start(bf16[256,384]{1,0:T(8,128)(2,1)S(1)} %get-tuple-element.80.rest_0_), channel_id=1, source_target_pairs={{0,2},{1,3},{2,0},{3,1},{4,6},{5,7},{6,4},{7,5},{8,10},{9,11},{10,... | collective-permute-start | bytes 589832 | tf_op jit(solution)/shard_map/ppermute | solution.py:325
  24.0 10.3 %collective-permute-start.20 = (bf16[256,384]{1,0:T(8,128)(2,1)S(1)}, bf16[256,384]{1,0:T(8,128)(2,1)S(1)}, u32[]{:S(2)}, u32[]{:S(2)}) collective-permute-start(bf16[256,384]{1,0:T(8,128)(2,1)S(1)} %get-tuple-element.80.rest_0_), channel_id=1, source_target_pairs={{0,3},{1,2},{2,1},{3,0},{4,7},{5,6},{6,5},{7,4},{8,11},{9,10},{10,... | collective-permute-start | bytes 589832 | tf_op jit(solution)/shard_map/ppermute | solution.py:325
  26.8 12.4 %collective-permute-start.13 = (bf16[128,1024]{1,0:T(8,128)(2,1)S(1)}, bf16[128,1024]{1,0:T(8,128)(2,1)S(1)}, u32[]{:S(2)}, u32[]{:S(2)}) collective-permute-start(bf16[128,1024]{1,0:T(8,128)(2,1)S(1)} %dynamic-slice_bitcast_fusion.rest_0_), channel_id=1, source_target_pairs={{0,1},{1,0},{2,3},{3,2},{4,5},{5,4},{6,7},{7,6},{8,9},{9,8},{10,11... | collective-permute-start | bytes 786440 | tf_op jit(solution)/shard_map/ppermute | solution.py:325
  31.3 11.6 %collective-permute-start.14 = (bf16[128,1024]{1,0:T(8,128)(2,1)S(1)}, bf16[128,1024]{1,0:T(8,128)(2,1)S(1)}, u32[]{:S(2)}, u32[]{:S(2)}) collective-permute-start(bf16[128,1024]{1,0:T(8,128)(2,1)S(1)} %dynamic-slice_bitcast_fusion.rest_0_), channel_id=1, source_target_pairs={{0,2},{1,3},{2,0},{3,1},{4,6},{5,7},{6,4},{7,5},{8,10},{9,11},{10,... | collective-permute-start | bytes 786440 | tf_op jit(solution)/shard_map/ppermute | solution.py:325
  31.6 14.8 %collective-permute-start.15 = (bf16[128,1024]{1,0:T(8,128)(2,1)S(1)}, bf16[128,1024]{1,0:T(8,128)(2,1)S(1)}, u32[]{:S(2)}, u32[]{:S(2)}) collective-permute-start(bf16[128,1024]{1,0:T(8,128)(2,1)S(1)} %dynamic-slice_bitcast_fusion.rest_0_), channel_id=1, source_target_pairs={{0,3},{1,2},{2,1},{3,0},{4,7},{5,6},{6,5},{7,4},{8,11},{9,10},{10,... | collective-permute-start | bytes 786440 | tf_op jit(solution)/shard_map/ppermute | solution.py:325
  34.4 14.0 %collective-permute-start.10 = (bf16[2,1024,128]{2,1,0:T(8,128)(2,1)S(1)}, bf16[2,1024,128]{2,1,0:T(8,128)(2,1)S(1)}, u32[]{:S(2)}, u32[]{:S(2)}) collective-permute-start(bf16[2,1024,128]{2,1,0:T(8,128)(2,1)S(1)} %get-tuple-element.74.rest_0_), channel_id=1, source_target_pairs={{0,8},{4,12},{8,16},{12,20},{16,24},{20,28},{1,9},{5,13},{9,17},{1... | collective-permute-start | bytes 1572872 | tf_op jit(solution)/shard_map/ppermute | solution.py:336
  35.7 41.0 %copy-start.3 = (bf16[1,1024,1024]{2,1,0:T(8,128)(2,1)S(1)}, bf16[1,1024,1024]{2,1,0:T(8,128)(2,1)}, u32[]{:S(2)}) copy-start(bf16[1,1024,1024]{2,1,0:T(8,128)(2,1)} %param.8) | copy-start | bytes 6291460
  39.3 19.5 %collective-permute-start.21 = (bf16[2,1024,128]{2,1,0:T(8,128)(2,1)S(1)}, bf16[2,1024,128]{2,1,0:T(8,128)(2,1)S(1)}, u32[]{:S(2)}, u32[]{:S(2)}) collective-permute-start(bf16[2,1024,128]{2,1,0:T(8,128)(2,1)S(1)} %get-tuple-element.82.rest_0_), channel_id=1, source_target_pairs={{0,8},{4,12},{8,16},{12,20},{16,24},{20,28},{1,9},{5,13},{9,17},{1... | collective-permute-start | bytes 1572872 | tf_op jit(solution)/shard_map/ppermute | solution.py:336
  42.9 27.1 %collective-permute-start.25 = (bf16[2,1024,128]{2,1,0:T(8,128)(2,1)S(1)}, bf16[2,1024,128]{2,1,0:T(8,128)(2,1)S(1)}, u32[]{:S(2)}, u32[]{:S(2)}) collective-permute-start(bf16[2,1024,128]{2,1,0:T(8,128)(2,1)S(1)} %get-tuple-element.88.rest_0_), channel_id=1, source_target_pairs={{0,8},{4,12},{8,16},{12,20},{16,24},{20,28},{1,9},{5,13},{9,17},{1... | collective-permute-start | bytes 1572872 | tf_op jit(solution)/shard_map/ppermute | solution.py:336
  46.4 29.6 %collective-permute-start.29 = (bf16[2,1024,128]{2,1,0:T(8,128)(2,1)S(1)}, bf16[2,1024,128]{2,1,0:T(8,128)(2,1)S(1)}, u32[]{:S(2)}, u32[]{:S(2)}) collective-permute-start(bf16[2,1024,128]{2,1,0:T(8,128)(2,1)S(1)} %get-tuple-element.94.rest_0_), channel_id=1, source_target_pairs={{0,8},{4,12},{8,16},{12,20},{16,24},{20,28},{1,9},{5,13},{9,17},{1... | collective-permute-start | bytes 1572872 | tf_op jit(solution)/shard_map/ppermute | solution.py:336
  48.3 33.1 %collective-permute-start.11 = (bf16[2,1024,128]{2,1,0:T(8,128)(2,1)S(1)}, bf16[2,1024,128]{2,1,0:T(8,128)(2,1)S(1)}, u32[]{:S(2)}, u32[]{:S(2)}) collective-permute-start(bf16[2,1024,128]{2,1,0:T(8,128)(2,1)S(1)} %collective-permute-done.10.rest_1_), channel_id=1, source_target_pairs={{8,16},{12,20},{16,24},{20,28},{9,17},{13,21},{17,25},{21,29},{10,... | collective-permute-start | bytes 1572872 | tf_op jit(solution)/shard_map/ppermute | solution.py:336
  58.8 28.4 %collective-permute-start.22 = (bf16[2,1024,128]{2,1,0:T(8,128)(2,1)S(1)}, bf16[2,1024,128]{2,1,0:T(8,128)(2,1)S(1)}, u32[]{:S(2)}, u32[]{:S(2)}) collective-permute-start(bf16[2,1024,128]{2,1,0:T(8,128)(2,1)S(1)} %collective-permute-done.21.rest_1_), channel_id=1, source_target_pairs={{8,16},{12,20},{16,24},{20,28},{9,17},{13,21},{17,25},{21,29},{10,... | collective-permute-start | bytes 1572872 | tf_op jit(solution)/shard_map/ppermute | solution.py:336
  70.0 23.0 %collective-permute-start.26 = (bf16[2,1024,128]{2,1,0:T(8,128)(2,1)S(1)}, bf16[2,1024,128]{2,1,0:T(8,128)(2,1)S(1)}, u32[]{:S(2)}, u32[]{:S(2)}) collective-permute-start(bf16[2,1024,128]{2,1,0:T(8,128)(2,1)S(1)} %collective-permute-done.25.rest_1_), channel_id=1, source_target_pairs={{8,16},{12,20},{16,24},{20,28},{9,17},{13,21},{17,25},{21,29},{10,... | collective-permute-start | bytes 1572872 | tf_op jit(solution)/shard_map/ppermute | solution.py:336
  76.0 22.7 %collective-permute-start.30 = (bf16[2,1024,128]{2,1,0:T(8,128)(2,1)S(1)}, bf16[2,1024,128]{2,1,0:T(8,128)(2,1)S(1)}, u32[]{:S(2)}, u32[]{:S(2)}) collective-permute-start(bf16[2,1024,128]{2,1,0:T(8,128)(2,1)S(1)} %collective-permute-done.29.rest_1_), channel_id=1, source_target_pairs={{8,16},{12,20},{16,24},{20,28},{9,17},{13,21},{17,25},{21,29},{10,... | collective-permute-start | bytes 1572872 | tf_op jit(solution)/shard_map/ppermute | solution.py:336
  85.9 26.7 %collective-permute-start.16 = (bf16[2,1024,128]{2,1,0:T(8,128)(2,1)S(1)}, bf16[2,1024,128]{2,1,0:T(8,128)(2,1)S(1)}, u32[]{:S(2)}, u32[]{:S(2)}) collective-permute-start(bf16[2,1024,128]{2,1,0:T(8,128)(2,1)S(1)} %get-tuple-element.78.rest_0_), channel_id=1, source_target_pairs={{8,0},{12,4},{16,8},{20,12},{24,16},{28,20},{9,1},{13,5},{17,9},{2... | collective-permute-start | bytes 1572872 | tf_op jit(solution)/shard_map/ppermute | solution.py:339
  91.7 32.2 %collective-permute-start.23 = (bf16[2,1024,128]{2,1,0:T(8,128)(2,1)S(1)}, bf16[2,1024,128]{2,1,0:T(8,128)(2,1)S(1)}, u32[]{:S(2)}, u32[]{:S(2)}) collective-permute-start(bf16[2,1024,128]{2,1,0:T(8,128)(2,1)S(1)} %get-tuple-element.86.rest_0_), channel_id=1, source_target_pairs={{8,0},{12,4},{16,8},{20,12},{24,16},{28,20},{9,1},{13,5},{17,9},{2... | collective-permute-start | bytes 1572872 | tf_op jit(solution)/shard_map/ppermute | solution.py:339
  97.5 38.5 %collective-permute-start.27 = (bf16[2,1024,128]{2,1,0:T(8,128)(2,1)S(1)}, bf16[2,1024,128]{2,1,0:T(8,128)(2,1)S(1)}, u32[]{:S(2)}, u32[]{:S(2)}) collective-permute-start(bf16[2,1024,128]{2,1,0:T(8,128)(2,1)S(1)} %get-tuple-element.92.rest_0_), channel_id=1, source_target_pairs={{8,0},{12,4},{16,8},{20,12},{24,16},{28,20},{9,1},{13,5},{17,9},{2... | collective-permute-start | bytes 1572872 | tf_op jit(solution)/shard_map/ppermute | solution.py:339
  103.2 43.9 %collective-permute-start.31 = (bf16[2,1024,128]{2,1,0:T(8,128)(2,1)S(1)}, bf16[2,1024,128]{2,1,0:T(8,128)(2,1)S(1)}, u32[]{:S(2)}, u32[]{:S(2)}) collective-permute-start(bf16[2,1024,128]{2,1,0:T(8,128)(2,1)S(1)} %get-tuple-element.98.rest_0_), channel_id=1, source_target_pairs={{8,0},{12,4},{16,8},{20,12},{24,16},{28,20},{9,1},{13,5},{17,9},{2... | collective-permute-start | bytes 1572872 | tf_op jit(solution)/shard_map/ppermute | solution.py:339
  112.6 45.8 %collective-permute-start.17 = (bf16[2,1024,128]{2,1,0:T(8,128)(2,1)S(1)}, bf16[2,1024,128]{2,1,0:T(8,128)(2,1)S(1)}, u32[]{:S(2)}, u32[]{:S(2)}) collective-permute-start(bf16[2,1024,128]{2,1,0:T(8,128)(2,1)S(1)} %collective-permute-done.16.rest_1_), channel_id=1, source_target_pairs={{8,0},{12,4},{16,8},{20,12},{9,1},{13,5},{17,9},{21,13},{10,2},{14... | collective-permute-start | bytes 1572872 | tf_op jit(solution)/shard_map/ppermute | solution.py:339
  123.8 45.8 %collective-permute-start.24 = (bf16[2,1024,128]{2,1,0:T(8,128)(2,1)S(1)}, bf16[2,1024,128]{2,1,0:T(8,128)(2,1)S(1)}, u32[]{:S(2)}, u32[]{:S(2)}) collective-permute-start(bf16[2,1024,128]{2,1,0:T(8,128)(2,1)S(1)} %collective-permute-done.23.rest_1_), channel_id=1, source_target_pairs={{8,0},{12,4},{16,8},{20,12},{9,1},{13,5},{17,9},{21,13},{10,2},{14... | collective-permute-start | bytes 1572872 | tf_op jit(solution)/shard_map/ppermute | solution.py:339
  130.0 18.7 %collective-permute-start.39 = (bf16[160,1024]{1,0:T(8,128)(2,1)S(1)}, bf16[160,1024]{1,0:T(8,128)(2,1)S(1)}, u32[]{:S(2)}, u32[]{:S(2)}) collective-permute-start(bf16[160,1024]{1,0:T(8,128)(2,1)S(1)} %get-tuple-element.120), channel_id=1, source_target_pairs={{0,1},{1,0},{2,3},{3,2},{4,5},{5,4},{6,7},{7,6},{8,9},{9,8},{10,11... | collective-permute-start | bytes 983048 | tf_op jit(solution)/shard_map/ppermute | solution.py:325
  136.0 44.1 %collective-permute-start.28 = (bf16[2,1024,128]{2,1,0:T(8,128)(2,1)S(1)}, bf16[2,1024,128]{2,1,0:T(8,128)(2,1)S(1)}, u32[]{:S(2)}, u32[]{:S(2)}) collective-permute-start(bf16[2,1024,128]{2,1,0:T(8,128)(2,1)S(1)} %collective-permute-done.27.rest_1_), channel_id=1, source_target_pairs={{8,0},{12,4},{16,8},{20,12},{9,1},{13,5},{17,9},{21,13},{10,2},{14... | collective-permute-start | bytes 1572872 | tf_op jit(solution)/shard_map/ppermute | solution.py:339
  147.2 38.5 %collective-permute-start.32 = (bf16[2,1024,128]{2,1,0:T(8,128)(2,1)S(1)}, bf16[2,1024,128]{2,1,0:T(8,128)(2,1)S(1)}, u32[]{:S(2)}, u32[]{:S(2)}) collective-permute-start(bf16[2,1024,128]{2,1,0:T(8,128)(2,1)S(1)} %collective-permute-done.31.rest_1_), channel_id=1, source_target_pairs={{8,0},{12,4},{16,8},{20,12},{9,1},{13,5},{17,9},{21,13},{10,2},{14... | collective-permute-start | bytes 1572872 | tf_op jit(solution)/shard_map/ppermute | solution.py:339
  148.7 25.6 %collective-permute-start.40 = (bf16[160,1024]{1,0:T(8,128)(2,1)S(1)}, bf16[160,1024]{1,0:T(8,128)(2,1)S(1)}, u32[]{:S(2)}, u32[]{:S(2)}) collective-permute-start(bf16[160,1024]{1,0:T(8,128)(2,1)S(1)} %get-tuple-element.121), channel_id=1, source_target_pairs={{0,2},{1,3},{2,0},{3,1},{4,6},{5,7},{6,4},{7,5},{8,10},{9,11},{10,... | collective-permute-start | bytes 983048 | tf_op jit(solution)/shard_map/ppermute | solution.py:325
  158.4 89.3 %collective-permute-start.35 = (bf16[1024,512]{1,0:T(8,128)(2,1)S(1)}, bf16[1024,512]{1,0:T(8,128)(2,1)S(1)}, u32[]{:S(2)}, u32[]{:S(2)}) collective-permute-start(bf16[1024,512]{1,0:T(8,128)(2,1)S(1)} %get-tuple-element.106.rest_6_), channel_id=1, source_target_pairs={{0,4},{4,0},{8,12},{12,8},{16,20},{20,16},{24,28},{28,24},{1,5},{5... | collective-permute-start | bytes 3145736 | tf_op jit(solution)/shard_map/ppermute | solution.py:319
  169.7 22.2 %collective-permute-start.41 = (bf16[160,1024]{1,0:T(8,128)(2,1)S(1)}, bf16[160,1024]{1,0:T(8,128)(2,1)S(1)}, u32[]{:S(2)}, u32[]{:S(2)}) collective-permute-start(bf16[160,1024]{1,0:T(8,128)(2,1)S(1)} %get-tuple-element.122), channel_id=1, source_target_pairs={{0,3},{1,2},{2,1},{3,0},{4,7},{5,6},{6,5},{7,4},{8,11},{9,10},{10,... | collective-permute-start | bytes 983048 | tf_op jit(solution)/shard_map/ppermute | solution.py:325
  174.2 18.5 %collective-permute-start.36 = (bf16[256,256]{1,0:T(8,128)(2,1)S(1)}, bf16[256,256]{1,0:T(8,128)(2,1)S(1)}, u32[]{:S(2)}, u32[]{:S(2)}) collective-permute-start(bf16[256,256]{1,0:T(8,128)(2,1)S(1)} %get-tuple-element.108), channel_id=1, source_target_pairs={{0,1},{1,0},{2,3},{3,2},{4,5},{5,4},{6,7},{7,6},{8,9},{9,8},{10,11... | collective-permute-start | bytes 393224 | tf_op jit(solution)/shard_map/ppermute | solution.py:325
  180.0 12.7 %collective-permute-start.37 = (bf16[256,256]{1,0:T(8,128)(2,1)S(1)}, bf16[256,256]{1,0:T(8,128)(2,1)S(1)}, u32[]{:S(2)}, u32[]{:S(2)}) collective-permute-start(bf16[256,256]{1,0:T(8,128)(2,1)S(1)} %get-tuple-element.109), channel_id=1, source_target_pairs={{0,2},{1,3},{2,0},{3,1},{4,6},{5,7},{6,4},{7,5},{8,10},{9,11},{10,... | collective-permute-start | bytes 393224 | tf_op jit(solution)/shard_map/ppermute | solution.py:325
  185.6 7.1 %collective-permute-start.38 = (bf16[256,256]{1,0:T(8,128)(2,1)S(1)}, bf16[256,256]{1,0:T(8,128)(2,1)S(1)}, u32[]{:S(2)}, u32[]{:S(2)}) collective-permute-start(bf16[256,256]{1,0:T(8,128)(2,1)S(1)} %get-tuple-element.110), channel_id=1, source_target_pairs={{0,3},{1,2},{2,1},{3,0},{4,7},{5,6},{6,5},{7,4},{8,11},{9,10},{10,... | collective-permute-start | bytes 393224 | tf_op jit(solution)/shard_map/ppermute | solution.py:325
  191.8 7.4 %collective-permute-start.49 = (bf16[256,256]{1,0:T(8,128)(2,1)S(1)}, bf16[256,256]{1,0:T(8,128)(2,1)S(1)}, u32[]{:S(2)}, u32[]{:S(2)}) collective-permute-start(bf16[256,256]{1,0:T(8,128)(2,1)S(1)} %get-tuple-element.129), channel_id=1, source_target_pairs={{0,1},{1,0},{2,3},{3,2},{4,5},{5,4},{6,7},{7,6},{8,9},{9,8},{10,11... | collective-permute-start | bytes 393224 | tf_op jit(solution)/shard_map/ppermute | solution.py:325
  193.7 5.9 %collective-permute-start.42 = (bf16[224,256]{1,0:T(8,128)(2,1)S(1)}, bf16[224,256]{1,0:T(8,128)(2,1)S(1)}, u32[]{:S(2)}, u32[]{:S(2)}) collective-permute-start(bf16[224,256]{1,0:T(8,128)(2,1)S(1)} %get-tuple-element.124), channel_id=1, source_target_pairs={{0,8},{4,12},{8,0},{12,4},{16,24},{20,28},{24,16},{28,20},{1,9},{5... | collective-permute-start | bytes 344072 | tf_op jit(solution)/shard_map/ppermute | solution.py:332
  196.8 7.7 %collective-permute-start.43 = (bf16[224,256]{1,0:T(8,128)(2,1)S(1)}, bf16[224,256]{1,0:T(8,128)(2,1)S(1)}, u32[]{:S(2)}, u32[]{:S(2)}) collective-permute-start(bf16[224,256]{1,0:T(8,128)(2,1)S(1)} %get-tuple-element.125), channel_id=1, source_target_pairs={{0,16},{4,20},{8,24},{12,28},{16,0},{20,4},{24,8},{28,12},{1,17},{... | collective-permute-start | bytes 344072 | tf_op jit(solution)/shard_map/ppermute | solution.py:332
  196.8 8.3 %collective-permute-start.44 = (bf16[224,256]{1,0:T(8,128)(2,1)S(1)}, bf16[224,256]{1,0:T(8,128)(2,1)S(1)}, u32[]{:S(2)}, u32[]{:S(2)}) collective-permute-start(bf16[224,256]{1,0:T(8,128)(2,1)S(1)} %get-tuple-element.126), channel_id=1, source_target_pairs={{0,24},{4,28},{8,16},{12,20},{16,8},{20,12},{24,0},{28,4},{1,25},{... | collective-permute-start | bytes 344072 | tf_op jit(solution)/shard_map/ppermute | solution.py:332
  199.3 49.6 %collective-permute-start.33 = (bf16[1024,256]{1,0:T(8,128)(2,1)S(1)}, bf16[1024,256]{1,0:T(8,128)(2,1)S(1)}, u32[]{:S(2)}, u32[]{:S(2)}) collective-permute-start(bf16[1024,256]{1,0:T(8,128)(2,1)S(1)} %get-tuple-element.102), channel_id=1, source_target_pairs={{0,4},{4,0},{8,12},{12,8},{16,20},{20,16},{24,28},{28,24},{1,5},{5... | collective-permute-start | bytes 1572872 | tf_op jit(solution)/shard_map/ppermute | solution.py:319
  199.6 50.6 %collective-permute-start.34 = (bf16[1024,256]{1,0:T(8,128)(2,1)S(1)}, bf16[1024,256]{1,0:T(8,128)(2,1)S(1)}, u32[]{:S(2)}, u32[]{:S(2)}) collective-permute-start(bf16[1024,256]{1,0:T(8,128)(2,1)S(1)} %get-tuple-element.105), channel_id=1, source_target_pairs={{0,4},{4,0},{8,12},{12,8},{16,20},{20,16},{24,28},{28,24},{1,5},{5... | collective-permute-start | bytes 1572872 | tf_op jit(solution)/shard_map/ppermute | solution.py:319
  204.5 5.0 %collective-permute-start.50 = (bf16[256,256]{1,0:T(8,128)(2,1)S(1)}, bf16[256,256]{1,0:T(8,128)(2,1)S(1)}, u32[]{:S(2)}, u32[]{:S(2)}) collective-permute-start(bf16[256,256]{1,0:T(8,128)(2,1)S(1)} %get-tuple-element.130), channel_id=1, source_target_pairs={{0,2},{1,3},{2,0},{3,1},{4,6},{5,7},{6,4},{7,5},{8,10},{9,11},{10,... | collective-permute-start | bytes 393224 | tf_op jit(solution)/shard_map/ppermute | solution.py:325
  205.1 5.9 %collective-permute-start.51 = (bf16[256,256]{1,0:T(8,128)(2,1)S(1)}, bf16[256,256]{1,0:T(8,128)(2,1)S(1)}, u32[]{:S(2)}, u32[]{:S(2)}) collective-permute-start(bf16[256,256]{1,0:T(8,128)(2,1)S(1)} %get-tuple-element.131), channel_id=1, source_target_pairs={{0,3},{1,2},{2,1},{3,0},{4,7},{5,6},{6,5},{7,4},{8,11},{9,10},{10,... | collective-permute-start | bytes 393224 | tf_op jit(solution)/shard_map/ppermute | solution.py:325
  209.4 4.6 %collective-permute-start.45 = (bf16[192,256]{1,0:T(8,128)(2,1)S(1)}, bf16[192,256]{1,0:T(8,128)(2,1)S(1)}, u32[]{:S(2)}, u32[]{:S(2)}) collective-permute-start(bf16[192,256]{1,0:T(8,128)(2,1)S(1)} %get-tuple-element.127.rest_0_), channel_id=1, source_target_pairs={{0,8},{4,12},{8,0},{12,4},{16,24},{20,28},{24,16},{28,20},{1,9},{5... | collective-permute-start | bytes 294920 | tf_op jit(solution)/shard_map/ppermute | solution.py:332
  211.0 6.7 %collective-permute-start.46 = (bf16[192,256]{1,0:T(8,128)(2,1)S(1)}, bf16[192,256]{1,0:T(8,128)(2,1)S(1)}, u32[]{:S(2)}, u32[]{:S(2)}) collective-permute-start(bf16[192,256]{1,0:T(8,128)(2,1)S(1)} %get-tuple-element.127.rest_0_), channel_id=1, source_target_pairs={{0,16},{4,20},{8,24},{12,28},{16,0},{20,4},{24,8},{28,12},{1,17},{... | collective-permute-start | bytes 294920 | tf_op jit(solution)/shard_map/ppermute | solution.py:332
  214.1 6.4 %collective-permute-start.47 = (bf16[192,256]{1,0:T(8,128)(2,1)S(1)}, bf16[192,256]{1,0:T(8,128)(2,1)S(1)}, u32[]{:S(2)}, u32[]{:S(2)}) collective-permute-start(bf16[192,256]{1,0:T(8,128)(2,1)S(1)} %get-tuple-element.127.rest_0_), channel_id=1, source_target_pairs={{0,24},{4,28},{8,16},{12,20},{16,8},{20,12},{24,0},{28,4},{1,25},{... | collective-permute-start | bytes 294920 | tf_op jit(solution)/shard_map/ppermute | solution.py:332
  217.7 3.9 %collective-permute-start.52 = (bf16[64,256]{1,0:T(8,128)(2,1)S(1)}, bf16[64,256]{1,0:T(8,128)(2,1)S(1)}, u32[]{:S(2)}, u32[]{:S(2)}) collective-permute-start(bf16[64,256]{1,0:T(8,128)(2,1)S(1)} %get-tuple-element.133), channel_id=1, source_target_pairs={{0,8},{4,12},{8,0},{12,4},{16,24},{20,28},{24,16},{28,20},{1,9},{5... | collective-permute-start | bytes 98312 | tf_op jit(solution)/shard_map/ppermute | solution.py:332
  221.1 34.6 %collective-permute-start.48 = (bf16[4,192,256]{2,1,0:T(8,128)(2,1)S(1)}, bf16[4,192,256]{2,1,0:T(8,128)(2,1)S(1)}, u32[]{:S(2)}, u32[]{:S(2)}) collective-permute-start(bf16[4,192,256]{2,1,0:T(8,128)(2,1)S(1)} %shard_map.121.rest_0_), channel_id=1, source_target_pairs={{0,4},{4,0},{8,12},{12,8},{16,20},{20,16},{24,28},{28,24},{1,5},{5... | collective-permute-start | bytes 1179656 | tf_op jit(solution)/shard_map/ppermute | solution.py:319
  221.6 4.8 %collective-permute-start.53 = (bf16[64,256]{1,0:T(8,128)(2,1)S(1)}, bf16[64,256]{1,0:T(8,128)(2,1)S(1)}, u32[]{:S(2)}, u32[]{:S(2)}) collective-permute-start(bf16[64,256]{1,0:T(8,128)(2,1)S(1)} %get-tuple-element.134), channel_id=1, source_target_pairs={{0,16},{4,20},{8,24},{12,28},{16,0},{20,4},{24,8},{28,12},{1,17},{... | collective-permute-start | bytes 98312 | tf_op jit(solution)/shard_map/ppermute | solution.py:332
  226.4 5.7 %collective-permute-start.54 = (bf16[64,256]{1,0:T(8,128)(2,1)S(1)}, bf16[64,256]{1,0:T(8,128)(2,1)S(1)}, u32[]{:S(2)}, u32[]{:S(2)}) collective-permute-start(bf16[64,256]{1,0:T(8,128)(2,1)S(1)} %get-tuple-element.135), channel_id=1, source_target_pairs={{0,24},{4,28},{8,16},{12,20},{16,8},{20,12},{24,0},{28,4},{1,25},{... | collective-permute-start | bytes 98312 | tf_op jit(solution)/shard_map/ppermute | solution.py:332
  232.2 4.0 %collective-permute-start.55 = (bf16[64,256]{1,0:T(8,128)(2,1)S(1)}, bf16[64,256]{1,0:T(8,128)(2,1)S(1)}, u32[]{:S(2)}, u32[]{:S(2)}) collective-permute-start(bf16[64,256]{1,0:T(8,128)(2,1)S(1)} %shard_map.123.rest_0_), channel_id=1, source_target_pairs={{0,8},{4,12},{8,0},{12,4},{16,24},{20,28},{24,16},{28,20},{1,9},{5... | collective-permute-start | bytes 98312 | tf_op jit(solution)/shard_map/ppermute | solution.py:332
  236.1 5.2 %collective-permute-start.56 = (bf16[64,256]{1,0:T(8,128)(2,1)S(1)}, bf16[64,256]{1,0:T(8,128)(2,1)S(1)}, u32[]{:S(2)}, u32[]{:S(2)}) collective-permute-start(bf16[64,256]{1,0:T(8,128)(2,1)S(1)} %shard_map.123.rest_0_), channel_id=1, source_target_pairs={{0,16},{4,20},{8,24},{12,28},{16,0},{20,4},{24,8},{28,12},{1,17},{... | collective-permute-start | bytes 98312 | tf_op jit(solution)/shard_map/ppermute | solution.py:332
  241.4 5.7 %collective-permute-start.57 = (bf16[64,256]{1,0:T(8,128)(2,1)S(1)}, bf16[64,256]{1,0:T(8,128)(2,1)S(1)}, u32[]{:S(2)}, u32[]{:S(2)}) collective-permute-start(bf16[64,256]{1,0:T(8,128)(2,1)S(1)} %shard_map.123.rest_0_), channel_id=1, source_target_pairs={{0,24},{4,28},{8,16},{12,20},{16,8},{20,12},{24,0},{28,4},{1,25},{... | collective-permute-start | bytes 98312 | tf_op jit(solution)/shard_map/ppermute | solution.py:332
  247.6 8.0 %collective-permute-start.58 = (bf16[4,64,256]{2,1,0:T(8,128)(2,1)S(1)}, bf16[4,64,256]{2,1,0:T(8,128)(2,1)S(1)}, u32[]{:S(2)}, u32[]{:S(2)}) collective-permute-start(bf16[4,64,256]{2,1,0:T(8,128)(2,1)S(1)} %shard_map.124.rest_2_), channel_id=1, source_target_pairs={{0,4},{4,0},{8,12},{12,8},{16,20},{20,16},{24,28},{28,24},{1,5},{5... | collective-permute-start | bytes 393224 | tf_op jit(solution)/shard_map/ppermute | solution.py:319
  247.7 7.9 %collective-permute-start.59 = (bf16[32,256]{1,0:T(8,128)(2,1)S(1)}, bf16[32,256]{1,0:T(8,128)(2,1)S(1)}, u32[]{:S(2)}, u32[]{:S(2)}) collective-permute-start(bf16[32,256]{1,0:T(8,128)(2,1)S(1)} %get-tuple-element.136.rest_4_), channel_id=1, source_target_pairs={{0,1},{1,0},{2,3},{3,2},{4,5},{5,4},{6,7},{7,6},{8,9},{9,8},{10,11... | collective-permute-start | bytes 49160 | tf_op jit(solution)/shard_map/ppermute | solution.py:325
  248.9 6.7 %collective-permute-start.60 = (bf16[32,256]{1,0:T(8,128)(2,1)S(1)}, bf16[32,256]{1,0:T(8,128)(2,1)S(1)}, u32[]{:S(2)}, u32[]{:S(2)}) collective-permute-start(bf16[32,256]{1,0:T(8,128)(2,1)S(1)} %get-tuple-element.136.rest_4_), channel_id=1, source_target_pairs={{0,2},{1,3},{2,0},{3,1},{4,6},{5,7},{6,4},{7,5},{8,10},{9,11},{10,... | collective-permute-start | bytes 49160 | tf_op jit(solution)/shard_map/ppermute | solution.py:325
  250.1 5.5 %collective-permute-start.61 = (bf16[32,256]{1,0:T(8,128)(2,1)S(1)}, bf16[32,256]{1,0:T(8,128)(2,1)S(1)}, u32[]{:S(2)}, u32[]{:S(2)}) collective-permute-start(bf16[32,256]{1,0:T(8,128)(2,1)S(1)} %get-tuple-element.136.rest_4_), channel_id=1, source_target_pairs={{0,3},{1,2},{2,1},{3,0},{4,7},{5,6},{6,5},{7,4},{8,11},{9,10},{10,... | collective-permute-start | bytes 49160 | tf_op jit(solution)/shard_map/ppermute | solution.py:325
  (5 other events, 56.9 us)

commit v5 on v4

--- a/solution.py
+++ b/solution.py
@@ -15,18 +15,19 @@
 F32 = jnp.float32
 VM = pl.BlockSpec(memory_space=pltpu.VMEM)
 SM = pl.BlockSpec(memory_space=pltpu.SMEM)
+ANY = pl.BlockSpec(memory_space=pl.ANY)
 
 
 def dot(a, b, ca, cb):
     return lax.dot_general(a, b, (((ca,), (cb,)), ((), ())), preferred_element_type=F32)
 
 
-def call(body, outs, ins, scratch=(), flops=0, scalars=1, small=0):
+def call(body, outs, ins, scratch=(), flops=0, scalars=1, small=0, stay=()):
     moved = sum(math.prod(x.shape) * x.dtype.itemsize for x in list(ins) + list(outs))
     return pl.pallas_call(
         body,
         out_shape=tuple(outs),
-        in_specs=[SM] * scalars + [VM] * (len(ins) - scalars),
+        in_specs=[SM if n < scalars else ANY if n in stay else VM for n in range(len(ins))],
         out_specs=tuple([SM] * small + [VM] * (len(outs) - small)),
         scratch_shapes=list(scratch),
         cost_estimate=pl.CostEstimate(flops=flops, bytes_accessed=moved, transcendentals=0),
@@ -56,6 +57,28 @@
             got = dot(source[pl.ds(at, tile), :], side, 1, int(turned)).astype(BF)
             for j, target in enumerate(targets):
                 target[slot, pl.ds(at, tile), :] = got[:, j * LANES : (j + 1) * LANES]
+            return carry
+
+        lax.fori_loop(0, source.shape[0] // tile, step, 0)
+
+
+def first_body(parts, tile, meta, own, partner, *rest):
+    held, sem = rest[-2:]
+    copy = pltpu.make_async_copy(own, held, sem)
+    copy.start()
+    weights, (target, panel) = rest[:parts], rest[parts:-2]
+    rows = weights[0].shape[0]
+    for k in range(parts):
+        start = pl.multiple_of((meta[0] ^ k) * rows, rows)
+        panel[pl.ds(start, rows), :] = weights[k][...]
+    for slot, source in ((1, partner), (0, held)):
+        if slot == 0:
+            copy.wait()
+
+        def step(i, carry, slot=slot, source=source):
+            at = pl.multiple_of(i * tile, tile)
+            got = dot(source[pl.ds(at, tile), :], panel[...], 1, 0).astype(BF)
+            target[slot, pl.ds(at, tile), :] = got
             return carry
 
         lax.fori_loop(0, source.shape[0] // tile, step, 0)
@@ -186,15 +209,17 @@
 
 
 def signal_body(tile, base, *rest):
-    side, side_far, target = rest[-3:]
-    mixes, others = rest[:-5], rest[-5:-3]
+    target, lanes = rest[-1], rest[-2].shape[1] // 2
+    low = 0 if target.dtype == F32 else lanes
+    side, side_far = (x[:, low : low + lanes] for x in rest[-3:-1])
+    mixes, other = rest[:-4], rest[-4]
 
     def step(i, carry):
         at = pl.multiple_of(i * tile, tile)
         mix = jnp.concatenate([x[pl.ds(at, tile), :] for x in mixes], axis=1)
-        other = jnp.concatenate([x[pl.ds(at, tile), :] for x in others], axis=1)
-        acc = base[pl.ds(at, tile), :].astype(F32) + dot(mix, side[...], 1, 1)
-        target[pl.ds(at, tile), :] = (acc + dot(other, side_far[...], 1, 1)).astype(BF)
+        acc = base[pl.ds(at, tile), :].astype(F32) + dot(mix, side, 1, 1)
+        acc = acc + dot(other[pl.ds(at, tile), :], side_far, 1, 1)
+        target[pl.ds(at, tile), :] = acc.astype(target.dtype)
         return carry
 
     lax.fori_loop(0, base.shape[0] // tile, step, 0)
@@ -254,19 +279,20 @@
 
 
 def pack_body(count, meta, *rest):
+    out = rest[-1]
+    rows = rest[0].shape[0]
     for k in range(count):
-        rest[count][meta[1] ^ k] = rest[k][...]
-
-
-def share_body(parts, meta, whole, *outs):
+        out[meta[1] ^ k, :rows, :] = rest[k][...]
+        out[meta[1] ^ k, rows:, :] = rest[count + k][...]
+
+
+def share_body(parts, skip, meta, whole, out):
     piece = whole.shape[1] // (2 * parts)
     got = []
-    for f in range(parts):
+    for f in range(skip // piece, parts):
         both = whole[:, 2 * f * piece : 2 * (f + 1) * piece]
         got.append(jnp.where(meta[2] == 0, both[:, :piece], both[:, piece:]))
-    first = outs[0].shape[1] // piece
-    outs[0][...] = jnp.concatenate(got[:first], axis=1)
-    outs[1][...] = jnp.concatenate(got[first:], axis=1)
+    out[...] = jnp.concatenate(got, axis=1)
 
 
 def taps_body(chips, groups, meta, *rest):
@@ -340,11 +366,19 @@
 
     where = jnp.stack([fsdp_at, chip, core, lengths[0] - chip * block]).astype(jnp.int32)
     wides = [share // 2, share // 2]
-    in_shares = call(
-        functools.partial(share_body, fsdp_size),
-        [shape((w_in.shape[0], x), BF) for x in (LANES, share - LANES)],
+    lead_share = jnp.concatenate(
+        [
+            lax.dynamic_slice_in_dim(w_in, (2 * f + core) * piece, piece, 1)
+            for f in range(LANES // piece)
+        ],
+        axis=1,
+    )
+    (rest_share,) = call(
+        functools.partial(share_body, fsdp_size, LANES),
+        [shape((w_in.shape[0], share - LANES), BF)],
         [where, w_in],
     )
+    in_shares = [lead_share, rest_share]
     out_share = lax.dynamic_index_in_dim(
         w_out.reshape(2, piece, channels), core, 0, keepdims=False
     )
@@ -366,10 +400,12 @@
     series = shape((2, samples, LANES), BF)
     tile = min(512, samples)
     first, lead = call(
-        functools.partial(product_body, fsdp_size, tile, False, 0),
+        functools.partial(first_body, fsdp_size, tile),
         [series, shape((channels, LANES), BF)],
         [where, record, record_far] + in_parts[0],
+        scratch=[pltpu.VMEM((samples, channels), BF), pltpu.SemaphoreType.DMA],
         flops=2 * block * channels * LANES,
+        stay=(1,),
     )
     got = call(
         functools.partial(product_body, fsdp_size, tile, False, LANES),
@@ -437,14 +473,6 @@
             flops=2 * block * rows * columns,
         )
 
-    def finish_sum(mine):
-        rows, columns = mine.shape
-        got = from_chips([mine] * chips)
-        (packed,) = call(
-            functools.partial(pack_body, chips), [shape((chips, rows, columns), BF)], [where] + got
-        )
-        return [packed, to_partner(packed)]
-
     mixed_in, flats = [], []
     for pick in (range(chunks // 2), range(chunks // 2, chunks)):
         sides = []
@@ -474,7 +502,7 @@
         scalars=0,
     )
     kernel_parts = from_fsdp([mine_kernel] * fsdp_size)
-    finals = finish_sum(mine)
+    gathered = from_chips([mine] * chips)
 
     last = (wides[1] // chips, own_rows)
     cut = call(
@@ -486,25 +514,33 @@
     (mine,) = call(
         functools.partial(sum_body, chips, None), [shape(last, BF)], from_chips(cut), scalars=0
     )
-    finals += finish_sum(mine)
+    gathered += from_chips([mine] * chips)
+    (packed,) = call(
+        functools.partial(pack_body, chips),
+        [shape((chips, panel_rows + last[0], own_rows), BF)],
+        [where] + gathered,
+    )
+    finals = [packed, to_partner(packed)]
 
     tile = min(256, samples)
 
-    (grad_signal,) = call(
-        functools.partial(signal_body, tile),
-        [shape((samples, channels), BF)],
-        [upstream] + own_mixed + mixed_in + [panel, panel_far],
-        scalars=0,
-        flops=2 * samples * channels * channels,
-    )
+    total = upstream
+    for n in range(2):
+        (total,) = call(
+            functools.partial(signal_body, tile),
+            [shape((samples, channels), BF if n else F32)],
+            [total] + own_mixed[n * chunks // 2 :][: chunks // 2] + [mixed_in[n], panel, panel_far],
+            scalars=0,
+            flops=samples * channels * channels,
+        )
+    grad_signal = total
 
     def finish_body(meta, *rest):
-        packs, parts = rest[:4], rest[4 : 4 + fsdp_size]
-        grad_in, grad_out, grad_conv, turned = rest[4 + fsdp_size :]
+        packs, parts = rest[:2], rest[2 : 2 + fsdp_size]
+        grad_in, grad_out, grad_conv, turned = rest[2 + fsdp_size :]
         core_at = meta[2]
         for side in range(2):
             first = packs[side][...].astype(F32) * factor
-            second = packs[2 + side][...].astype(F32) * factor
             for p in range(chips):
                 at = pl.multiple_of((side ^ core_at) * piece + p * out_part, 8)
                 for n in range(channels // own_rows):
@@ -515,7 +551,7 @@
                 at = p * in_part
                 turned[side ^ core_at, at : at + in_part, :] = first[p, :in_part, :]
                 at, rows = wides[0] + p * last[0], last[0]
-                turned[side ^ core_at, at : at + rows, :] = second[p]
+                turned[side ^ core_at, at : at + rows, :] = first[p, panel_rows:, :]
         for f in range(fsdp_size):
             pair = [turned[c, f * piece : (f + 1) * piece, :] for c in range(2)]
             grad_in[:, 2 * f * piece : 2 * (f + 1) * piece] = jnp.concatenate(pair, axis=0).T

time: 259 us -> 257 us (level)
  waiting for transfers between devices: 131 us -> 120 us
  starting transfers between devices: 67.6 us -> 74.8 us
    ppermute x18, waiting for transfers between devices: 37.7 us -> 26 us  [from_chips(): got.append(lax.ppermute(blocks[k], 'seq', pairs))]
    ppermute x18, starting transfers between devices: 19.4 us -> 24.7 us  [from_chips(): got.append(lax.ppermute(blocks[k], 'seq', pairs))]
    ppermute x8, starting transfers between devices: 13.1 us -> 15.9 us  [up(): lax.ppermute(x, 'seq', [(i, i + 2) for i in range(2 * (hop - 1), seq_size...]
  transfers between devices with their start and end apart: 62 -> 61, of which waited for: 29 -> 27; matrix products, arithmetic and copies ran while one was open for 0% -> 0% of each run, Pallas kernels for 20% -> 21%
where the time goes in v5:
time: 257 us; the launch traced here: 256 us
  waiting for transfers between devices  120 us (47%)
  starting transfers between devices  74.8 us (29%)
  Pallas kernels  55.5 us (22%)
  local copies, waits for them, and re-layouts  3.52 us (1%)
    ppermute x8, waiting for transfers between devices, down(): lax.ppermute(x, 'seq', [(i + 2, i) for i in range(seq_size - 2 * hop)])  63.8 us
    pallas_call x24, Pallas kernels, call(): pl.pallas_call(body, out_shape=tuple(outs), in_specs=[SM if n < scalars e...  55.5 us
    ppermute x18, waiting for transfers between devices, from_chips(): got.append(lax.ppermute(blocks[k], 'seq', pairs))  26 us
    ppermute x8, waiting for transfers between devices, up(): lax.ppermute(x, 'seq', [(i, i + 2) for i in range(2 * (hop - 1), seq_size...  25.4 us
    ppermute x18, starting transfers between devices, from_chips(): got.append(lax.ppermute(blocks[k], 'seq', pairs))  24.7 us
    ppermute x21, starting transfers between devices, from_fsdp(): got.append(lax.ppermute(blocks[k], 'fsdp', pairs))  23 us
    ppermute x8, starting transfers between devices, up(): lax.ppermute(x, 'seq', [(i, i + 2) for i in range(2 * (hop - 1), seq_size...  15.9 us
    ppermute x8, starting transfers between devices, down(): lax.ppermute(x, 'seq', [(i + 2, i) for i in range(seq_size - 2 * hop)])  10.5 us
  transfers between devices with their start and end apart: 61, of which 27 were waited for; matrix products, arithmetic and copies ran while one was open for 0% of the time, Pallas kernels for 21%

profile of v5, /device:TPU:0, one launch (start us, length us, event | category | flops | bytes accessed | tf_op | source)
XLA Modules:
  0.0 256.1 jit_solution(4556459985980429900)
XLA Ops:
  2.1 2.9 %collective-permute-start.7 = (bf16[256,128]{1,0:T(8,128)(2,1)S(1)}, bf16[256,128]{1,0:T(8,128)(2,1)S(1)}, u32[]{:S(2)}, u32[]{:S(2)}) collective-permute-start(bf16[256,128]{1,0:T(8,128)(2,1)S(1)} %constant_dynamic-slice_fusion.rest_0_), channel_id=1, source_target_pairs={{0,1},{1,0},{2,3},{3,2},{4,5},{5,4},{6,7},{7,6},{8,9},{9,8},{10,11... | collective-permute-start | bytes 196616 | tf_op jit(solution)/shard_map/ppermute | solution.py:351
  5.0 1.5 collective-permute-start.8
  6.6 1.6 collective-permute-start
  8.8 1.5 collective-permute-done.rest_1_
  10.3 2.6 %collective-permute-start.1 = (s32[2]{0:T(128)}, s32[2]{0:T(128)S(1)}, u32[]{:S(2)}, u32[]{:S(2)}) collective-permute-start(s32[2]{0:T(128)} %rest_0_.1), channel_id=1, source_target_pairs={{0,16},{4,20},{8,24},{12,28},{16,0},{20,4},{24,8},{28,12},{1,17},{... | collective-permute-start | bytes 32 | tf_op jit(solution)/shard_map/ppermute | solution.py:358
  12.8 2.0 collective-permute-done.1.rest_2_
  14.9 3.6 %collective-permute-start.2 = (s32[2]{0:T(128)}, s32[2]{0:T(128)S(1)}, u32[]{:S(2)}, u32[]{:S(2)}) collective-permute-start(s32[2]{0:T(128)} %rest_0_.1), channel_id=1, source_target_pairs={{0,24},{4,28},{8,16},{12,20},{16,8},{20,12},{24,0},{28,4},{1,25},{... | collective-permute-start | bytes 32 | tf_op jit(solution)/shard_map/ppermute | solution.py:358
  18.5 1.9 collective-permute-done.2.rest_3_
  22.3 1.8 collective-permute-start.18
  24.1 2.2 collective-permute-done.9.rest_3_
  26.3 2.0 collective-permute-start.20
  28.4 1.6 collective-permute-start.13
  29.9 1.6 copy-done.1
  31.5 2.5 shard_map.103
  34.1 1.7 collective-permute-done.19.rest_2_
  35.8 1.8 collective-permute-start.4
  37.6 1.9 collective-permute-start.5
  39.5 4.0 %shard_map.108 = (bf16[2,1024,128]{2,1,0:T(8,128)(2,1)S(1)}, bf16[2,1024,128]{2,1,0:T(8,128)(2,1)S(1)}, bf16[2,1024,128]{2,1,0:T(8,128)(2,1)S(1)}, bf16[1024,512]{1,0:T(8,128)(2,1)S(1)}) custom-call(s32[4]{0:T(128)S(1)} %pad_add_fusion.meta, bf16[1024,1024]{1,0:T(8,128)(2,1)S(1)} %bitcast.15, bf16[1024,1024]{1,0:T(8,128)(2,1)S(1)} %collective-permute-done.6.partner.rest_5_, ...), custom_call_target="tpu_custom_call" | custom-call | flops 1610612736 | bytes 7864336 | tf_op jit(solution)/shard_map/pallas_call | solution.py:27
  43.6 2.5 collective-permute-start.31
  46.4 3.9 %collective-permute-start.21 = (bf16[2,1024,128]{2,1,0:T(8,128)(2,1)S(1)}, bf16[2,1024,128]{2,1,0:T(8,128)(2,1)S(1)}, u32[]{:S(2)}, u32[]{:S(2)}) collective-permute-start(bf16[2,1024,128]{2,1,0:T(8,128)(2,1)S(1)} %get-tuple-element.78.rest_0_), channel_id=1, source_target_pairs={{0,8},{4,12},{8,16},{12,20},{16,24},{20,28},{1,9},{5,13},{9,17},{1... | collective-permute-start | bytes 1572872 | tf_op jit(solution)/shard_map/ppermute | solution.py:362
  50.3 2.9 %collective-permute-start.10 = (bf16[2,1024,128]{2,1,0:T(8,128)(2,1)S(1)}, bf16[2,1024,128]{2,1,0:T(8,128)(2,1)S(1)}, u32[]{:S(2)}, u32[]{:S(2)}) collective-permute-start(bf16[2,1024,128]{2,1,0:T(8,128)(2,1)S(1)} %get-tuple-element.71.rest_0_), channel_id=1, source_target_pairs={{0,8},{4,12},{8,16},{12,20},{16,24},{20,28},{1,9},{5,13},{9,17},{1... | collective-permute-start | bytes 1572872 | tf_op jit(solution)/shard_map/ppermute | solution.py:362
  53.4 3.9 %collective-permute-start.27 = (bf16[2,1024,128]{2,1,0:T(8,128)(2,1)S(1)}, bf16[2,1024,128]{2,1,0:T(8,128)(2,1)S(1)}, u32[]{:S(2)}, u32[]{:S(2)}) collective-permute-start(bf16[2,1024,128]{2,1,0:T(8,128)(2,1)S(1)} %get-tuple-element.88.rest_0_), channel_id=1, source_target_pairs={{0,8},{4,12},{8,16},{12,20},{16,24},{20,28},{1,9},{5,13},{9,17},{1... | collective-permute-start | bytes 1572872 | tf_op jit(solution)/shard_map/ppermute | solution.py:362
  59.0 10.5 %collective-permute-done.21.rest_1_ = bf16[2,1024,128]{2,1,0:T(8,128)(2,1)S(1)} collective-permute-done((bf16[2,1024,128]{2,1,0:T(8,128)(2,1)S(1)}, bf16[2,1024,128]{2,1,0:T(8,128)(2,1)S(1)}, u32[]{:S(2)}, u32[]{:S(2)}) %collective-permute-start.21) | collective-permute-done | bytes 524320 | tf_op jit(solution)/shard_map/ppermute | solution.py:362
  70.2 8.9 %collective-permute-done.10.rest_1_ = bf16[2,1024,128]{2,1,0:T(8,128)(2,1)S(1)} collective-permute-done((bf16[2,1024,128]{2,1,0:T(8,128)(2,1)S(1)}, bf16[2,1024,128]{2,1,0:T(8,128)(2,1)S(1)}, u32[]{:S(2)}, u32[]{:S(2)}) %collective-permute-start.10) | collective-permute-done | bytes 524320 | tf_op jit(solution)/shard_map/ppermute | solution.py:362
  79.8 4.9 %collective-permute-done.27.rest_1_ = bf16[2,1024,128]{2,1,0:T(8,128)(2,1)S(1)} collective-permute-done((bf16[2,1024,128]{2,1,0:T(8,128)(2,1)S(1)}, bf16[2,1024,128]{2,1,0:T(8,128)(2,1)S(1)}, u32[]{:S(2)}, u32[]{:S(2)}) %collective-permute-start.27) | collective-permute-done | bytes 524320 | tf_op jit(solution)/shard_map/ppermute | solution.py:362
  85.5 2.0 shard_map.102
  87.5 4.7 %shard_map.104 = (bf16[2,1024,128]{2,1,0:T(8,128)(2,1)S(1)}, bf16[2,1024,128]{2,1,0:T(8,128)(2,1)S(1)}, bf16[2,1024,128]{2,1,0:T(8,128)(2,1)S(1)}, bf16[2,1024,128]{2,1,0:T(8,128)(2,1)S(1)}) custom-call(s32[4]{0:T(128)S(1)} %pad_add_fusion.meta, bf16[1024,1024]{1,0:T(8,128)(2,1)S(1)} %bitcast.19, bf16[1024,1024]{1,0:T(8,128)(2,1)} %collective-permute-done.12.partner.rest_5_, ...), custom_call_target="tpu_custom_call" | custom-call | flops 2147483648 | bytes 7340048 | tf_op jit(solution)/shard_map/pallas_call | solution.py:27
  92.2 4.5 %shard_map.115 = (bf16[2,1024,128]{2,1,0:T(8,128)(2,1)S(1)}, f32[2,1024,128]{2,1,0:T(8,128)S(1)}, bf16[2,1024,128]{2,1,0:T(8,128)(2,1)S(1)}, f32[2,128,128]{2,1,0:T(8,128)S(1)}) custom-call(s32[4]{0:T(128)S(1)} %pad_add_fusion.meta, s32[8]{0:T(128)S(1)} %get-tuple-element.70.amounts, bf16[2,1024,128]{2,1,0:T(8,128)(2,1)S(1)} %get-tuple-element.94.rest_0_, ...), custom_call_target="tpu_custom_call" | custom-call | flops 805306368 | bytes 4456496 | tf_op jit(solution)/shard_map/pallas_call | solution.py:27
  96.6 1.3 collective-permute-start.33
  97.9 4.5 %shard_map.109 = (bf16[2,1024,128]{2,1,0:T(8,128)(2,1)S(1)}, f32[2,1024,128]{2,1,0:T(8,128)S(1)}, bf16[2,1024,128]{2,1,0:T(8,128)(2,1)S(1)}, f32[2,128,128]{2,1,0:T(8,128)S(1)}) custom-call(s32[4]{0:T(128)S(1)} %pad_add_fusion.meta, s32[8]{0:T(128)S(1)} %get-tuple-element.70.amounts, bf16[2,1024,128]{2,1,0:T(8,128)(2,1)S(1)} %get-tuple-element.78.rest_0_, ...), custom_call_target="tpu_custom_call" | custom-call | flops 805306368 | bytes 4456496 | tf_op jit(solution)/shard_map/pallas_call | solution.py:27
  102.4 1.3 collective-permute-start.23
  103.7 4.5 %shard_map.105 = (bf16[2,1024,128]{2,1,0:T(8,128)(2,1)S(1)}, f32[2,1024,128]{2,1,0:T(8,128)S(1)}, bf16[2,1024,128]{2,1,0:T(8,128)(2,1)S(1)}, f32[2,128,128]{2,1,0:T(8,128)S(1)}) custom-call(s32[4]{0:T(128)S(1)} %pad_add_fusion.meta, s32[8]{0:T(128)S(1)} %get-tuple-element.70.amounts, bf16[2,1024,128]{2,1,0:T(8,128)(2,1)S(1)} %get-tuple-element.71.rest_0_, ...), custom_call_target="tpu_custom_call" | custom-call | flops 805306368 | bytes 4456496 | tf_op jit(solution)/shard_map/pallas_call | solution.py:27
  108.2 1.3 collective-permute-start.16
  109.5 4.5 %shard_map.113 = (bf16[2,1024,128]{2,1,0:T(8,128)(2,1)S(1)}, f32[2,1024,128]{2,1,0:T(8,128)S(1)}, bf16[2,1024,128]{2,1,0:T(8,128)(2,1)S(1)}, f32[2,128,128]{2,1,0:T(8,128)S(1)}) custom-call(s32[4]{0:T(128)S(1)} %pad_add_fusion.meta, s32[8]{0:T(128)S(1)} %get-tuple-element.70.amounts, bf16[2,1024,128]{2,1,0:T(8,128)(2,1)S(1)} %get-tuple-element.88.rest_0_, ...), custom_call_target="tpu_custom_call" | custom-call | flops 805306368 | bytes 4456496 | tf_op jit(solution)/shard_map/pallas_call | solution.py:27
  114.0 1.3 collective-permute-start.29
  115.3 7.4 %collective-permute-done.33.rest_1_ = bf16[2,1024,128]{2,1,0:T(8,128)(2,1)S(1)} collective-permute-done((bf16[2,1024,128]{2,1,0:T(8,128)(2,1)S(1)}, bf16[2,1024,128]{2,1,0:T(8,128)(2,1)S(1)}, u32[]{:S(2)}, u32[]{:S(2)}) %collective-permute-start.33) | collective-permute-done | bytes 524320 | tf_op jit(solution)/shard_map/ppermute | solution.py:365
  122.7 1.3 collective-permute-start.34
  123.9 10.0 %collective-permute-done.23.rest_1_ = bf16[2,1024,128]{2,1,0:T(8,128)(2,1)S(1)} collective-permute-done((bf16[2,1024,128]{2,1,0:T(8,128)(2,1)S(1)}, bf16[2,1024,128]{2,1,0:T(8,128)(2,1)S(1)}, u32[]{:S(2)}, u32[]{:S(2)}) %collective-permute-start.23) | collective-permute-done | bytes 524320 | tf_op jit(solution)/shard_map/ppermute | solution.py:365
  133.9 1.3 collective-permute-start.24
  135.2 11.1 %collective-permute-done.16.rest_1_ = bf16[2,1024,128]{2,1,0:T(8,128)(2,1)S(1)} collective-permute-done((bf16[2,1024,128]{2,1,0:T(8,128)(2,1)S(1)}, bf16[2,1024,128]{2,1,0:T(8,128)(2,1)S(1)}, u32[]{:S(2)}, u32[]{:S(2)}) %collective-permute-start.16) | collective-permute-done | bytes 524320 | tf_op jit(solution)/shard_map/ppermute | solution.py:365
  146.3 1.3 collective-permute-start.17
  147.6 9.9 %collective-permute-done.29.rest_1_ = bf16[2,1024,128]{2,1,0:T(8,128)(2,1)S(1)} collective-permute-done((bf16[2,1024,128]{2,1,0:T(8,128)(2,1)S(1)}, bf16[2,1024,128]{2,1,0:T(8,128)(2,1)S(1)}, u32[]{:S(2)}, u32[]{:S(2)}) %collective-permute-start.29) | collective-permute-done | bytes 524320 | tf_op jit(solution)/shard_map/ppermute | solution.py:365
  157.5 1.5 collective-permute-start.30
  159.0 4.9 %shard_map.119 = (f32[160,1024]{1,0:T(8,128)S(1)}, bf16[160,1024]{1,0:T(8,128)(2,1)S(1)}, bf16[160,1024]{1,0:T(8,128)(2,1)S(1)}, bf16[160,1024]{1,0:T(8,128)(2,1)S(1)}) custom-call(s32[4]{0:T(128)S(1)} %pad_add_fusion.meta, bf16[2,1024,128]{2,1,0:T(8,128)(2,1)S(1)} %get-tuple-element.107.rest_0_, bf16[2,1024,128]{2,1,0:T(8,128)(2,1)S(1)} %get-tuple-element.108.rest_1_, ...), custom_call_target="tpu_custom_call" | custom-call | flops 2147483648 | bytes 8454160 | tf_op jit(solution)/shard_map/pallas_call | solution.py:27
  164.5 4.3 %collective-permute-done.34.rest_2_ = bf16[2,1024,128]{2,1,0:T(8,128)(2,1)S(1)} collective-permute-done((bf16[2,1024,128]{2,1,0:T(8,128)(2,1)S(1)}, bf16[2,1024,128]{2,1,0:T(8,128)(2,1)S(1)}, u32[]{:S(2)}, u32[]{:S(2)}) %collective-permute-start.34) | collective-permute-done | bytes 524320 | tf_op jit(solution)/shard_map/ppermute | solution.py:365
  169.4 10.6 %collective-permute-done.24.rest_2_ = bf16[2,1024,128]{2,1,0:T(8,128)(2,1)S(1)} collective-permute-done((bf16[2,1024,128]{2,1,0:T(8,128)(2,1)S(1)}, bf16[2,1024,128]{2,1,0:T(8,128)(2,1)S(1)}, u32[]{:S(2)}, u32[]{:S(2)}) %collective-permute-start.24) | collective-permute-done | bytes 524320 | tf_op jit(solution)/shard_map/ppermute | solution.py:365
  180.6 9.4 %collective-permute-done.17.rest_2_ = bf16[2,1024,128]{2,1,0:T(8,128)(2,1)S(1)} collective-permute-done((bf16[2,1024,128]{2,1,0:T(8,128)(2,1)S(1)}, bf16[2,1024,128]{2,1,0:T(8,128)(2,1)S(1)}, u32[]{:S(2)}, u32[]{:S(2)}) %collective-permute-start.17) | collective-permute-done | bytes 524320 | tf_op jit(solution)/shard_map/ppermute | solution.py:365
  192.0 2.6 shard_map.111
  199.4 1.9 collective-permute-start.38
  201.3 2.5 shard_map.117
  206.6 1.9 collective-permute-start.50
  209.5 2.5 collective-permute-start.42
  212.1 2.5 collective-permute-start.44
  217.4 3.4 %collective-permute-done.43.rest_2_ = bf16[224,256]{1,0:T(8,128)(2,1)S(1)} collective-permute-done((bf16[224,256]{1,0:T(8,128)(2,1)S(1)}, bf16[224,256]{1,0:T(8,128)(2,1)S(1)}, u32[]{:S(2)}, u32[]{:S(2)}) %collective-permute-start.43) | collective-permute-done | bytes 114720 | tf_op jit(solution)/shard_map/ppermute | solution.py:358
  220.7 1.2 collective-permute-start.53
  222.0 2.3 collective-permute-start.45
  228.4 2.6 %collective-permute-done.54.rest_5_ = bf16[64,256]{1,0:T(8,128)(2,1)S(1)} collective-permute-done((bf16[64,256]{1,0:T(8,128)(2,1)S(1)}, bf16[64,256]{1,0:T(8,128)(2,1)S(1)}, u32[]{:S(2)}, u32[]{:S(2)}) %collective-permute-start.54) | collective-permute-done | bytes 32800 | tf_op jit(solution)/shard_map/ppermute | solution.py:358
  232.6 4.2 %collective-permute-done.56.rest_7_ = bf16[64,256]{1,0:T(8,128)(2,1)S(1)} collective-permute-done((bf16[64,256]{1,0:T(8,128)(2,1)S(1)}, bf16[64,256]{1,0:T(8,128)(2,1)S(1)}, u32[]{:S(2)}, u32[]{:S(2)}) %collective-permute-start.56) | collective-permute-done | bytes 32800 | tf_op jit(solution)/shard_map/ppermute | solution.py:358
  236.8 1.2 collective-permute-start.47
  238.0 6.2 %collective-permute-done.46.rest_2_ = bf16[192,256]{1,0:T(8,128)(2,1)S(1)} collective-permute-done((bf16[192,256]{1,0:T(8,128)(2,1)S(1)}, bf16[192,256]{1,0:T(8,128)(2,1)S(1)}, u32[]{:S(2)}, u32[]{:S(2)}) %collective-permute-start.46) | collective-permute-done | bytes 98336 | tf_op jit(solution)/shard_map/ppermute | solution.py:358
  246.8 1.6 collective-permute-start.60
  248.4 2.0 shard_map.112.base
  250.4 3.3 %shard_map.118 = bf16[1024,1024]{1,0:T(8,128)(2,1)} custom-call(f32[1024,1024]{1,0:T(8,128)S(1)} %shard_map.112.base, bf16[1024,128]{1,0:T(8,128)(2,1)S(1)} %get-tuple-element.93.rest_0_, bf16[1024,128]{1,0:T(8,128)(2,1)S(1)} %get-tuple-element.99.rest_2_.rest_1_, bf16[1024,256]{1,0:T(8,128)(2,1)S(1)} %collective-permute-done.35.rest_2_, ...), custom_call_target="tpu_custom_call" | custom-call | flops 1073741824 | bytes 9437184 | tf_op jit(solution)/shard_map/pallas_call | solution.py:27
  253.7 2.3 shard_map.125
  (99 shorter events, 31.3 us)
Async XLA Ops:
  0.6 27.7 %copy-start = (bf16[256,1024]{1,0:T(8,128)(2,1)S(1)}, bf16[256,1024]{1,0:T(8,128)(2,1)}, u32[]{:S(2)}) copy-start(bf16[256,1024]{1,0:T(8,128)(2,1)} %param.11) | copy-start | bytes 1572868
  0.6 27.7 %collective-permute-start.6 = (bf16[1024,1024]{1,0:T(8,128)(2,1)}, bf16[1024,1024]{1,0:T(8,128)(2,1)S(1)}, u32[]{:S(2)}, u32[]{:S(2)}) collective-permute-start(bf16[1024,1024]{1,0:T(8,128)(2,1)} %bitcast.13), channel_id=1, source_target_pairs={{0,4},{4,0},{8,12},{12,8},{16,20},{20,16},{24,28},{28,24},{1,5},{5... | collective-permute-start | bytes 6291464 | tf_op jit(solution)/shard_map/ppermute | solution.py:345
  1.2 86.3 %collective-permute-start.12 = (bf16[1024,1024]{1,0:T(8,128)(2,1)}, bf16[1024,1024]{1,0:T(8,128)(2,1)}, u32[]{:S(2)}, u32[]{:S(2)}) collective-permute-start(bf16[1024,1024]{1,0:T(8,128)(2,1)} %bitcast.18), channel_id=1, source_target_pairs={{0,4},{4,0},{8,12},{12,8},{16,20},{20,16},{24,28},{28,24},{1,5},{5... | collective-permute-start | bytes 6291464 | tf_op jit(solution)/shard_map/ppermute | solution.py:345
  2.1 18.5 %collective-permute-start.7 = (bf16[256,128]{1,0:T(8,128)(2,1)S(1)}, bf16[256,128]{1,0:T(8,128)(2,1)S(1)}, u32[]{:S(2)}, u32[]{:S(2)}) collective-permute-start(bf16[256,128]{1,0:T(8,128)(2,1)S(1)} %constant_dynamic-slice_fusion.rest_0_), channel_id=1, source_target_pairs={{0,1},{1,0},{2,3},{3,2},{4,5},{5,4},{6,7},{7,6},{8,9},{9,8},{10,11... | collective-permute-start | bytes 196616 | tf_op jit(solution)/shard_map/ppermute | solution.py:351
  5.0 17.3 %collective-permute-start.8 = (bf16[256,128]{1,0:T(8,128)(2,1)S(1)}, bf16[256,128]{1,0:T(8,128)(2,1)S(1)}, u32[]{:S(2)}, u32[]{:S(2)}) collective-permute-start(bf16[256,128]{1,0:T(8,128)(2,1)S(1)} %constant_dynamic-slice_fusion.rest_0_), channel_id=1, source_target_pairs={{0,2},{1,3},{2,0},{3,1},{4,6},{5,7},{6,4},{7,5},{8,10},{9,11},{10,... | collective-permute-start | bytes 196616 | tf_op jit(solution)/shard_map/ppermute | solution.py:351
  6.6 3.7 %collective-permute-start = (s32[2]{0:T(128)}, s32[2]{0:T(128)S(1)}, u32[]{:S(2)}, u32[]{:S(2)}) collective-permute-start(s32[2]{0:T(128)} %rest_0_.1), channel_id=1, source_target_pairs={{0,8},{4,12},{8,0},{12,4},{16,24},{20,28},{24,16},{28,20},{1,9},{5... | collective-permute-start | bytes 32 | tf_op jit(solution)/shard_map/ppermute | solution.py:358
  10.3 4.6 %collective-permute-start.1 = (s32[2]{0:T(128)}, s32[2]{0:T(128)S(1)}, u32[]{:S(2)}, u32[]{:S(2)}) collective-permute-start(s32[2]{0:T(128)} %rest_0_.1), channel_id=1, source_target_pairs={{0,16},{4,20},{8,24},{12,28},{16,0},{20,4},{24,8},{28,12},{1,17},{... | collective-permute-start | bytes 32 | tf_op jit(solution)/shard_map/ppermute | solution.py:358
  14.9 5.5 %collective-permute-start.2 = (s32[2]{0:T(128)}, s32[2]{0:T(128)S(1)}, u32[]{:S(2)}, u32[]{:S(2)}) collective-permute-start(s32[2]{0:T(128)} %rest_0_.1), channel_id=1, source_target_pairs={{0,24},{4,28},{8,16},{12,20},{16,8},{20,12},{24,0},{28,4},{1,25},{... | collective-permute-start | bytes 32 | tf_op jit(solution)/shard_map/ppermute | solution.py:358
  20.4 6.0 %collective-permute-start.9 = (bf16[256,128]{1,0:T(8,128)(2,1)S(1)}, bf16[256,128]{1,0:T(8,128)(2,1)S(1)}, u32[]{:S(2)}, u32[]{:S(2)}) collective-permute-start(bf16[256,128]{1,0:T(8,128)(2,1)S(1)} %constant_dynamic-slice_fusion.rest_0_), channel_id=1, source_target_pairs={{0,3},{1,2},{2,1},{3,0},{4,7},{5,6},{6,5},{7,4},{8,11},{9,10},{10,... | collective-permute-start | bytes 196616 | tf_op jit(solution)/shard_map/ppermute | solution.py:351
  20.6 5.7 %collective-permute-start.3 = (bf16[2,128,128]{2,1,0:T(8,128)(2,1)}, bf16[2,128,128]{2,1,0:T(8,128)(2,1)S(1)}, u32[]{:S(2)}, u32[]{:S(2)}) collective-permute-start(bf16[2,128,128]{2,1,0:T(8,128)(2,1)} %rest_4_.1), channel_id=1, source_target_pairs={{0,8},{4,12},{8,0},{12,4},{16,24},{20,28},{24,16},{28,20},{1,9},{5... | collective-permute-start | bytes 196616 | tf_op jit(solution)/shard_map/ppermute | solution.py:358
  22.3 11.7 %collective-permute-start.18 = (bf16[256,384]{1,0:T(8,128)(2,1)S(1)}, bf16[256,384]{1,0:T(8,128)(2,1)S(1)}, u32[]{:S(2)}, u32[]{:S(2)}) collective-permute-start(bf16[256,384]{1,0:T(8,128)(2,1)S(1)} %shard_map.107.rest_0_), channel_id=1, source_target_pairs={{0,1},{1,0},{2,3},{3,2},{4,5},{5,4},{6,7},{7,6},{8,9},{9,8},{10,11... | collective-permute-start | bytes 589832 | tf_op jit(solution)/shard_map/ppermute | solution.py:351
  26.3 9.5 %collective-permute-start.19 = (bf16[256,384]{1,0:T(8,128)(2,1)S(1)}, bf16[256,384]{1,0:T(8,128)(2,1)S(1)}, u32[]{:S(2)}, u32[]{:S(2)}) collective-permute-start(bf16[256,384]{1,0:T(8,128)(2,1)S(1)} %shard_map.107.rest_0_), channel_id=1, source_target_pairs={{0,2},{1,3},{2,0},{3,1},{4,6},{5,7},{6,4},{7,5},{8,10},{9,11},{10,... | collective-permute-start | bytes 589832 | tf_op jit(solution)/shard_map/ppermute | solution.py:351
  26.3 11.2 %collective-permute-start.20 = (bf16[256,384]{1,0:T(8,128)(2,1)S(1)}, bf16[256,384]{1,0:T(8,128)(2,1)}, u32[]{:S(2)}, u32[]{:S(2)}) collective-permute-start(bf16[256,384]{1,0:T(8,128)(2,1)S(1)} %shard_map.107.rest_0_), channel_id=1, source_target_pairs={{0,3},{1,2},{2,1},{3,0},{4,7},{5,6},{6,5},{7,4},{8,11},{9,10},{10,... | collective-permute-start | bytes 589832 | tf_op jit(solution)/shard_map/ppermute | solution.py:351
  28.4 18.0 %collective-permute-start.13 = (bf16[128,1024]{1,0:T(8,128)(2,1)S(1)}, bf16[128,1024]{1,0:T(8,128)(2,1)S(1)}, u32[]{:S(2)}, u32[]{:S(2)}) collective-permute-start(bf16[128,1024]{1,0:T(8,128)(2,1)S(1)} %dynamic-slice_bitcast_fusion.rest_0_), channel_id=1, source_target_pairs={{0,1},{1,0},{2,3},{3,2},{4,5},{5,4},{6,7},{7,6},{8,9},{9,8},{10,11... | collective-permute-start | bytes 786440 | tf_op jit(solution)/shard_map/ppermute | solution.py:351
  34.0 16.3 %collective-permute-start.14 = (bf16[128,1024]{1,0:T(8,128)(2,1)S(1)}, bf16[128,1024]{1,0:T(8,128)(2,1)S(1)}, u32[]{:S(2)}, u32[]{:S(2)}) collective-permute-start(bf16[128,1024]{1,0:T(8,128)(2,1)S(1)} %dynamic-slice_bitcast_fusion.rest_0_), channel_id=1, source_target_pairs={{0,2},{1,3},{2,0},{3,1},{4,6},{5,7},{6,4},{7,5},{8,10},{9,11},{10,... | collective-permute-start | bytes 786440 | tf_op jit(solution)/shard_map/ppermute | solution.py:351
  35.8 7.8 %collective-permute-start.4 = (bf16[2,128,128]{2,1,0:T(8,128)(2,1)S(1)}, bf16[2,128,128]{2,1,0:T(8,128)(2,1)S(1)}, u32[]{:S(2)}, u32[]{:S(2)}) collective-permute-start(bf16[2,128,128]{2,1,0:T(8,128)(2,1)S(1)} %copy-done.5), channel_id=1, source_target_pairs={{0,16},{4,20},{8,24},{12,28},{16,0},{20,4},{24,8},{28,12},{1,17},{... | collective-permute-start | bytes 196616 | tf_op jit(solution)/shard_map/ppermute | solution.py:358
  37.6 8.5 %collective-permute-start.5 = (bf16[2,128,128]{2,1,0:T(8,128)(2,1)S(1)}, bf16[2,128,128]{2,1,0:T(8,128)(2,1)S(1)}, u32[]{:S(2)}, u32[]{:S(2)}) collective-permute-start(bf16[2,128,128]{2,1,0:T(8,128)(2,1)S(1)} %copy-done.5), channel_id=1, source_target_pairs={{0,24},{4,28},{8,16},{12,20},{16,8},{20,12},{24,0},{28,4},{1,25},{... | collective-permute-start | bytes 196616 | tf_op jit(solution)/shard_map/ppermute | solution.py:358
  39.5 45.9 %copy-start.6 = (s32[2]{0:T(128)S(1)}, s32[2]{0:T(128)}, u32[]{:S(2)}) copy-start(s32[2]{0:T(128)} %rest_0_.1) | copy-start | bytes 28
  39.5 48.0 %copy-start.3 = (bf16[1,1024,1024]{2,1,0:T(8,128)(2,1)S(1)}, bf16[1,1024,1024]{2,1,0:T(8,128)(2,1)}, u32[]{:S(2)}) copy-start(bf16[1,1024,1024]{2,1,0:T(8,128)(2,1)} %param.8) | copy-start | bytes 6291460
  43.6 14.7 %collective-permute-start.31 = (bf16[2,1024,128]{2,1,0:T(8,128)(2,1)S(1)}, bf16[2,1024,128]{2,1,0:T(8,128)(2,1)S(1)}, u32[]{:S(2)}, u32[]{:S(2)}) collective-permute-start(bf16[2,1024,128]{2,1,0:T(8,128)(2,1)S(1)} %get-tuple-element.94.rest_0_), channel_id=1, source_target_pairs={{0,8},{4,12},{8,16},{12,20},{16,24},{20,28},{1,9},{5,13},{9,17},{1... | collective-permute-start | bytes 1572872 | tf_op jit(solution)/shard_map/ppermute | solution.py:362
  46.1 7.3 %collective-permute-start.15 = (bf16[128,1024]{1,0:T(8,128)(2,1)S(1)}, bf16[128,1024]{1,0:T(8,128)(2,1)S(1)}, u32[]{:S(2)}, u32[]{:S(2)}) collective-permute-start(bf16[128,1024]{1,0:T(8,128)(2,1)S(1)} %dynamic-slice_bitcast_fusion.rest_0_), channel_id=1, source_target_pairs={{0,3},{1,2},{2,1},{3,0},{4,7},{5,6},{6,5},{7,4},{8,11},{9,10},{10,... | collective-permute-start | bytes 786440 | tf_op jit(solution)/shard_map/ppermute | solution.py:351
  46.4 23.2 %collective-permute-start.21 = (bf16[2,1024,128]{2,1,0:T(8,128)(2,1)S(1)}, bf16[2,1024,128]{2,1,0:T(8,128)(2,1)S(1)}, u32[]{:S(2)}, u32[]{:S(2)}) collective-permute-start(bf16[2,1024,128]{2,1,0:T(8,128)(2,1)S(1)} %get-tuple-element.78.rest_0_), channel_id=1, source_target_pairs={{0,8},{4,12},{8,16},{12,20},{16,24},{20,28},{1,9},{5,13},{9,17},{1... | collective-permute-start | bytes 1572872 | tf_op jit(solution)/shard_map/ppermute | solution.py:362
  50.3 28.9 %collective-permute-start.10 = (bf16[2,1024,128]{2,1,0:T(8,128)(2,1)S(1)}, bf16[2,1024,128]{2,1,0:T(8,128)(2,1)S(1)}, u32[]{:S(2)}, u32[]{:S(2)}) collective-permute-start(bf16[2,1024,128]{2,1,0:T(8,128)(2,1)S(1)} %get-tuple-element.71.rest_0_), channel_id=1, source_target_pairs={{0,8},{4,12},{8,16},{12,20},{16,24},{20,28},{1,9},{5,13},{9,17},{1... | collective-permute-start | bytes 1572872 | tf_op jit(solution)/shard_map/ppermute | solution.py:362
  53.4 31.4 %collective-permute-start.27 = (bf16[2,1024,128]{2,1,0:T(8,128)(2,1)S(1)}, bf16[2,1024,128]{2,1,0:T(8,128)(2,1)S(1)}, u32[]{:S(2)}, u32[]{:S(2)}) collective-permute-start(bf16[2,1024,128]{2,1,0:T(8,128)(2,1)S(1)} %get-tuple-element.88.rest_0_), channel_id=1, source_target_pairs={{0,8},{4,12},{8,16},{12,20},{16,24},{20,28},{1,9},{5,13},{9,17},{1... | collective-permute-start | bytes 1572872 | tf_op jit(solution)/shard_map/ppermute | solution.py:362
  58.3 33.8 %collective-permute-start.32 = (bf16[2,1024,128]{2,1,0:T(8,128)(2,1)S(1)}, bf16[2,1024,128]{2,1,0:T(8,128)(2,1)S(1)}, u32[]{:S(2)}, u32[]{:S(2)}) collective-permute-start(bf16[2,1024,128]{2,1,0:T(8,128)(2,1)S(1)} %collective-permute-done.31.rest_1_), channel_id=1, source_target_pairs={{8,16},{12,20},{16,24},{20,28},{9,17},{13,21},{17,25},{21,29},{10,... | collective-permute-start | bytes 1572872 | tf_op jit(solution)/shard_map/ppermute | solution.py:362
  69.5 28.4 %collective-permute-start.22 = (bf16[2,1024,128]{2,1,0:T(8,128)(2,1)S(1)}, bf16[2,1024,128]{2,1,0:T(8,128)(2,1)S(1)}, u32[]{:S(2)}, u32[]{:S(2)}) collective-permute-start(bf16[2,1024,128]{2,1,0:T(8,128)(2,1)S(1)} %collective-permute-done.21.rest_1_), channel_id=1, source_target_pairs={{8,16},{12,20},{16,24},{20,28},{9,17},{13,21},{17,25},{21,29},{10,... | collective-permute-start | bytes 1572872 | tf_op jit(solution)/shard_map/ppermute | solution.py:362
  79.1 24.6 %collective-permute-start.11 = (bf16[2,1024,128]{2,1,0:T(8,128)(2,1)S(1)}, bf16[2,1024,128]{2,1,0:T(8,128)(2,1)S(1)}, u32[]{:S(2)}, u32[]{:S(2)}) collective-permute-start(bf16[2,1024,128]{2,1,0:T(8,128)(2,1)S(1)} %collective-permute-done.10.rest_1_), channel_id=1, source_target_pairs={{8,16},{12,20},{16,24},{20,28},{9,17},{13,21},{17,25},{21,29},{10,... | collective-permute-start | bytes 1572872 | tf_op jit(solution)/shard_map/ppermute | solution.py:362
  84.8 24.7 %collective-permute-start.28 = (bf16[2,1024,128]{2,1,0:T(8,128)(2,1)S(1)}, bf16[2,1024,128]{2,1,0:T(8,128)(2,1)S(1)}, u32[]{:S(2)}, u32[]{:S(2)}) collective-permute-start(bf16[2,1024,128]{2,1,0:T(8,128)(2,1)S(1)} %collective-permute-done.27.rest_1_), channel_id=1, source_target_pairs={{8,16},{12,20},{16,24},{20,28},{9,17},{13,21},{17,25},{21,29},{10,... | collective-permute-start | bytes 1572872 | tf_op jit(solution)/shard_map/ppermute | solution.py:362
  96.6 26.0 %collective-permute-start.33 = (bf16[2,1024,128]{2,1,0:T(8,128)(2,1)S(1)}, bf16[2,1024,128]{2,1,0:T(8,128)(2,1)S(1)}, u32[]{:S(2)}, u32[]{:S(2)}) collective-permute-start(bf16[2,1024,128]{2,1,0:T(8,128)(2,1)S(1)} %get-tuple-element.98.rest_0_), channel_id=1, source_target_pairs={{8,0},{12,4},{16,8},{20,12},{24,16},{28,20},{9,1},{13,5},{17,9},{2... | collective-permute-start | bytes 1572872 | tf_op jit(solution)/shard_map/ppermute | solution.py:365
  102.4 31.5 %collective-permute-start.23 = (bf16[2,1024,128]{2,1,0:T(8,128)(2,1)S(1)}, bf16[2,1024,128]{2,1,0:T(8,128)(2,1)S(1)}, u32[]{:S(2)}, u32[]{:S(2)}) collective-permute-start(bf16[2,1024,128]{2,1,0:T(8,128)(2,1)S(1)} %get-tuple-element.82.rest_0_), channel_id=1, source_target_pairs={{8,0},{12,4},{16,8},{20,12},{24,16},{28,20},{9,1},{13,5},{17,9},{2... | collective-permute-start | bytes 1572872 | tf_op jit(solution)/shard_map/ppermute | solution.py:365
  108.2 38.1 %collective-permute-start.16 = (bf16[2,1024,128]{2,1,0:T(8,128)(2,1)S(1)}, bf16[2,1024,128]{2,1,0:T(8,128)(2,1)S(1)}, u32[]{:S(2)}, u32[]{:S(2)}) collective-permute-start(bf16[2,1024,128]{2,1,0:T(8,128)(2,1)S(1)} %get-tuple-element.75.rest_0_), channel_id=1, source_target_pairs={{8,0},{12,4},{16,8},{20,12},{24,16},{28,20},{9,1},{13,5},{17,9},{2... | collective-permute-start | bytes 1572872 | tf_op jit(solution)/shard_map/ppermute | solution.py:365
  114.0 43.6 %collective-permute-start.29 = (bf16[2,1024,128]{2,1,0:T(8,128)(2,1)S(1)}, bf16[2,1024,128]{2,1,0:T(8,128)(2,1)S(1)}, u32[]{:S(2)}, u32[]{:S(2)}) collective-permute-start(bf16[2,1024,128]{2,1,0:T(8,128)(2,1)S(1)} %get-tuple-element.92.rest_0_), channel_id=1, source_target_pairs={{8,0},{12,4},{16,8},{20,12},{24,16},{28,20},{9,1},{13,5},{17,9},{2... | collective-permute-start | bytes 1572872 | tf_op jit(solution)/shard_map/ppermute | solution.py:365
  122.7 46.1 %collective-permute-start.34 = (bf16[2,1024,128]{2,1,0:T(8,128)(2,1)S(1)}, bf16[2,1024,128]{2,1,0:T(8,128)(2,1)S(1)}, u32[]{:S(2)}, u32[]{:S(2)}) collective-permute-start(bf16[2,1024,128]{2,1,0:T(8,128)(2,1)S(1)} %collective-permute-done.33.rest_1_), channel_id=1, source_target_pairs={{8,0},{12,4},{16,8},{20,12},{9,1},{13,5},{17,9},{21,13},{10,2},{14... | collective-permute-start | bytes 1572872 | tf_op jit(solution)/shard_map/ppermute | solution.py:365
  133.9 46.1 %collective-permute-start.24 = (bf16[2,1024,128]{2,1,0:T(8,128)(2,1)S(1)}, bf16[2,1024,128]{2,1,0:T(8,128)(2,1)S(1)}, u32[]{:S(2)}, u32[]{:S(2)}) collective-permute-start(bf16[2,1024,128]{2,1,0:T(8,128)(2,1)S(1)} %collective-permute-done.23.rest_1_), channel_id=1, source_target_pairs={{8,0},{12,4},{16,8},{20,12},{9,1},{13,5},{17,9},{21,13},{10,2},{14... | collective-permute-start | bytes 1572872 | tf_op jit(solution)/shard_map/ppermute | solution.py:365
  146.3 43.8 %collective-permute-start.17 = (bf16[2,1024,128]{2,1,0:T(8,128)(2,1)S(1)}, bf16[2,1024,128]{2,1,0:T(8,128)(2,1)S(1)}, u32[]{:S(2)}, u32[]{:S(2)}) collective-permute-start(bf16[2,1024,128]{2,1,0:T(8,128)(2,1)S(1)} %collective-permute-done.16.rest_1_), channel_id=1, source_target_pairs={{8,0},{12,4},{16,8},{20,12},{9,1},{13,5},{17,9},{21,13},{10,2},{14... | collective-permute-start | bytes 1572872 | tf_op jit(solution)/shard_map/ppermute | solution.py:365
  157.5 38.2 %collective-permute-start.30 = (bf16[2,1024,128]{2,1,0:T(8,128)(2,1)S(1)}, bf16[2,1024,128]{2,1,0:T(8,128)(2,1)S(1)}, u32[]{:S(2)}, u32[]{:S(2)}) collective-permute-start(bf16[2,1024,128]{2,1,0:T(8,128)(2,1)S(1)} %collective-permute-done.29.rest_1_), channel_id=1, source_target_pairs={{8,0},{12,4},{16,8},{20,12},{9,1},{13,5},{17,9},{21,13},{10,2},{14... | collective-permute-start | bytes 1572872 | tf_op jit(solution)/shard_map/ppermute | solution.py:365
  163.9 34.6 %collective-permute-start.39 = (bf16[160,1024]{1,0:T(8,128)(2,1)S(1)}, bf16[160,1024]{1,0:T(8,128)(2,1)S(1)}, u32[]{:S(2)}, u32[]{:S(2)}) collective-permute-start(bf16[160,1024]{1,0:T(8,128)(2,1)S(1)} %get-tuple-element.116), channel_id=1, source_target_pairs={{0,1},{1,0},{2,3},{3,2},{4,5},{5,4},{6,7},{7,6},{8,9},{9,8},{10,11... | collective-permute-start | bytes 983048 | tf_op jit(solution)/shard_map/ppermute | solution.py:351
  168.8 30.7 %collective-permute-start.40 = (bf16[160,1024]{1,0:T(8,128)(2,1)S(1)}, bf16[160,1024]{1,0:T(8,128)(2,1)S(1)}, u32[]{:S(2)}, u32[]{:S(2)}) collective-permute-start(bf16[160,1024]{1,0:T(8,128)(2,1)S(1)} %get-tuple-element.117), channel_id=1, source_target_pairs={{0,2},{1,3},{2,0},{3,1},{4,6},{5,7},{6,4},{7,5},{8,10},{9,11},{10,... | collective-permute-start | bytes 983048 | tf_op jit(solution)/shard_map/ppermute | solution.py:351
  180.0 23.9 %collective-permute-start.41 = (bf16[160,1024]{1,0:T(8,128)(2,1)S(1)}, bf16[160,1024]{1,0:T(8,128)(2,1)S(1)}, u32[]{:S(2)}, u32[]{:S(2)}) collective-permute-start(bf16[160,1024]{1,0:T(8,128)(2,1)S(1)} %get-tuple-element.118), channel_id=1, source_target_pairs={{0,3},{1,2},{2,1},{3,0},{4,7},{5,6},{6,5},{7,4},{8,11},{9,10},{10,... | collective-permute-start | bytes 983048 | tf_op jit(solution)/shard_map/ppermute | solution.py:351
  190.1 55.6 %collective-permute-start.26 = (bf16[1024,512]{1,0:T(8,128)(2,1)S(1)}, bf16[1024,512]{1,0:T(8,128)(2,1)S(1)}, u32[]{:S(2)}, u32[]{:S(2)}) collective-permute-start(bf16[1024,512]{1,0:T(8,128)(2,1)S(1)} %get-tuple-element.87.rest_3_), channel_id=1, source_target_pairs={{0,4},{4,0},{8,12},{12,8},{16,20},{20,16},{24,28},{28,24},{1,5},{5... | collective-permute-start | bytes 3145736 | tf_op jit(solution)/shard_map/ppermute | solution.py:345
  195.7 9.0 %collective-permute-start.36 = (bf16[256,256]{1,0:T(8,128)(2,1)S(1)}, bf16[256,256]{1,0:T(8,128)(2,1)S(1)}, u32[]{:S(2)}, u32[]{:S(2)}) collective-permute-start(bf16[256,256]{1,0:T(8,128)(2,1)S(1)} %get-tuple-element.104), channel_id=1, source_target_pairs={{0,1},{1,0},{2,3},{3,2},{4,5},{5,4},{6,7},{7,6},{8,9},{9,8},{10,11... | collective-permute-start | bytes 393224 | tf_op jit(solution)/shard_map/ppermute | solution.py:351
  198.5 8.1 %collective-permute-start.37 = (bf16[256,256]{1,0:T(8,128)(2,1)S(1)}, bf16[256,256]{1,0:T(8,128)(2,1)S(1)}, u32[]{:S(2)}, u32[]{:S(2)}) collective-permute-start(bf16[256,256]{1,0:T(8,128)(2,1)S(1)} %get-tuple-element.105), channel_id=1, source_target_pairs={{0,2},{1,3},{2,0},{3,1},{4,6},{5,7},{6,4},{7,5},{8,10},{9,11},{10,... | collective-permute-start | bytes 393224 | tf_op jit(solution)/shard_map/ppermute | solution.py:351
  199.4 9.1 %collective-permute-start.38 = (bf16[256,256]{1,0:T(8,128)(2,1)S(1)}, bf16[256,256]{1,0:T(8,128)(2,1)S(1)}, u32[]{:S(2)}, u32[]{:S(2)}) collective-permute-start(bf16[256,256]{1,0:T(8,128)(2,1)S(1)} %get-tuple-element.106), channel_id=1, source_target_pairs={{0,3},{1,2},{2,1},{3,0},{4,7},{5,6},{6,5},{7,4},{8,11},{9,10},{10,... | collective-permute-start | bytes 393224 | tf_op jit(solution)/shard_map/ppermute | solution.py:351
  203.9 8.2 %collective-permute-start.48 = (bf16[256,256]{1,0:T(8,128)(2,1)S(1)}, bf16[256,256]{1,0:T(8,128)(2,1)S(1)}, u32[]{:S(2)}, u32[]{:S(2)}) collective-permute-start(bf16[256,256]{1,0:T(8,128)(2,1)S(1)} %get-tuple-element.125), channel_id=1, source_target_pairs={{0,1},{1,0},{2,3},{3,2},{4,5},{5,4},{6,7},{7,6},{8,9},{9,8},{10,11... | collective-permute-start | bytes 393224 | tf_op jit(solution)/shard_map/ppermute | solution.py:351
  204.7 7.4 %collective-permute-start.49 = (bf16[256,256]{1,0:T(8,128)(2,1)S(1)}, bf16[256,256]{1,0:T(8,128)(2,1)S(1)}, u32[]{:S(2)}, u32[]{:S(2)}) collective-permute-start(bf16[256,256]{1,0:T(8,128)(2,1)S(1)} %get-tuple-element.126), channel_id=1, source_target_pairs={{0,2},{1,3},{2,0},{3,1},{4,6},{5,7},{6,4},{7,5},{8,10},{9,11},{10,... | collective-permute-start | bytes 393224 | tf_op jit(solution)/shard_map/ppermute | solution.py:351
  206.6 8.0 %collective-permute-start.50 = (bf16[256,256]{1,0:T(8,128)(2,1)S(1)}, bf16[256,256]{1,0:T(8,128)(2,1)S(1)}, u32[]{:S(2)}, u32[]{:S(2)}) collective-permute-start(bf16[256,256]{1,0:T(8,128)(2,1)S(1)} %get-tuple-element.127), channel_id=1, source_target_pairs={{0,3},{1,2},{2,1},{3,0},{4,7},{5,6},{6,5},{7,4},{8,11},{9,10},{10,... | collective-permute-start | bytes 393224 | tf_op jit(solution)/shard_map/ppermute | solution.py:351
  209.5 7.8 %collective-permute-start.42 = (bf16[224,256]{1,0:T(8,128)(2,1)S(1)}, bf16[224,256]{1,0:T(8,128)(2,1)S(1)}, u32[]{:S(2)}, u32[]{:S(2)}) collective-permute-start(bf16[224,256]{1,0:T(8,128)(2,1)S(1)} %get-tuple-element.120), channel_id=1, source_target_pairs={{0,8},{4,12},{8,0},{12,4},{16,24},{20,28},{24,16},{28,20},{1,9},{5... | collective-permute-start | bytes 344072 | tf_op jit(solution)/shard_map/ppermute | solution.py:358
  212.1 8.7 %collective-permute-start.43 = (bf16[224,256]{1,0:T(8,128)(2,1)S(1)}, bf16[224,256]{1,0:T(8,128)(2,1)S(1)}, u32[]{:S(2)}, u32[]{:S(2)}) collective-permute-start(bf16[224,256]{1,0:T(8,128)(2,1)S(1)} %get-tuple-element.121), channel_id=1, source_target_pairs={{0,16},{4,20},{8,24},{12,28},{16,0},{20,4},{24,8},{28,12},{1,17},{... | collective-permute-start | bytes 344072 | tf_op jit(solution)/shard_map/ppermute | solution.py:358
  212.1 8.7 %collective-permute-start.44 = (bf16[224,256]{1,0:T(8,128)(2,1)S(1)}, bf16[224,256]{1,0:T(8,128)(2,1)S(1)}, u32[]{:S(2)}, u32[]{:S(2)}) collective-permute-start(bf16[224,256]{1,0:T(8,128)(2,1)S(1)} %get-tuple-element.122), channel_id=1, source_target_pairs={{0,24},{4,28},{8,16},{12,20},{16,8},{20,12},{24,0},{28,4},{1,25},{... | collective-permute-start | bytes 344072 | tf_op jit(solution)/shard_map/ppermute | solution.py:358
  215.3 6.8 %collective-permute-start.51 = (bf16[64,256]{1,0:T(8,128)(2,1)S(1)}, bf16[64,256]{1,0:T(8,128)(2,1)S(1)}, u32[]{:S(2)}, u32[]{:S(2)}) collective-permute-start(bf16[64,256]{1,0:T(8,128)(2,1)S(1)} %get-tuple-element.129), channel_id=1, source_target_pairs={{0,8},{4,12},{8,0},{12,4},{16,24},{20,28},{24,16},{28,20},{1,9},{5... | collective-permute-start | bytes 98312 | tf_op jit(solution)/shard_map/ppermute | solution.py:358
  217.4 29.4 %collective-permute-start.25 = (bf16[1024,256]{1,0:T(8,128)(2,1)S(1)}, bf16[1024,256]{1,0:T(8,128)(2,1)S(1)}, u32[]{:S(2)}, u32[]{:S(2)}) collective-permute-start(bf16[1024,256]{1,0:T(8,128)(2,1)S(1)} %get-tuple-element.86), channel_id=1, source_target_pairs={{0,4},{4,0},{8,12},{12,8},{16,20},{20,16},{24,28},{28,24},{1,5},{5... | collective-permute-start | bytes 1572872 | tf_op jit(solution)/shard_map/ppermute | solution.py:345
  220.7 4.8 %collective-permute-start.52 = (bf16[64,256]{1,0:T(8,128)(2,1)S(1)}, bf16[64,256]{1,0:T(8,128)(2,1)S(1)}, u32[]{:S(2)}, u32[]{:S(2)}) collective-permute-start(bf16[64,256]{1,0:T(8,128)(2,1)S(1)} %get-tuple-element.130), channel_id=1, source_target_pairs={{0,16},{4,20},{8,24},{12,28},{16,0},{20,4},{24,8},{28,12},{1,17},{... | collective-permute-start | bytes 98312 | tf_op jit(solution)/shard_map/ppermute | solution.py:358
  220.7 6.0 %collective-permute-start.53 = (bf16[64,256]{1,0:T(8,128)(2,1)S(1)}, bf16[64,256]{1,0:T(8,128)(2,1)S(1)}, u32[]{:S(2)}, u32[]{:S(2)}) collective-permute-start(bf16[64,256]{1,0:T(8,128)(2,1)S(1)} %get-tuple-element.131), channel_id=1, source_target_pairs={{0,24},{4,28},{8,16},{12,20},{16,8},{20,12},{24,0},{28,4},{1,25},{... | collective-permute-start | bytes 98312 | tf_op jit(solution)/shard_map/ppermute | solution.py:358
  222.0 14.8 %collective-permute-start.45 = (bf16[192,256]{1,0:T(8,128)(2,1)S(1)}, bf16[192,256]{1,0:T(8,128)(2,1)S(1)}, u32[]{:S(2)}, u32[]{:S(2)}) collective-permute-start(bf16[192,256]{1,0:T(8,128)(2,1)S(1)} %get-tuple-element.123.rest_0_), channel_id=1, source_target_pairs={{0,8},{4,12},{8,0},{12,4},{16,24},{20,28},{24,16},{28,20},{1,9},{5... | collective-permute-start | bytes 294920 | tf_op jit(solution)/shard_map/ppermute | solution.py:358
  226.8 4.3 %collective-permute-start.54 = (bf16[64,256]{1,0:T(8,128)(2,1)S(1)}, bf16[64,256]{1,0:T(8,128)(2,1)S(1)}, u32[]{:S(2)}, u32[]{:S(2)}) collective-permute-start(bf16[64,256]{1,0:T(8,128)(2,1)S(1)} %shard_map.123.rest_4_), channel_id=1, source_target_pairs={{0,8},{4,12},{8,0},{12,4},{16,24},{20,28},{24,16},{28,20},{1,9},{5... | collective-permute-start | bytes 98312 | tf_op jit(solution)/shard_map/ppermute | solution.py:358
  227.8 4.8 %collective-permute-start.55 = (bf16[64,256]{1,0:T(8,128)(2,1)S(1)}, bf16[64,256]{1,0:T(8,128)(2,1)S(1)}, u32[]{:S(2)}, u32[]{:S(2)}) collective-permute-start(bf16[64,256]{1,0:T(8,128)(2,1)S(1)} %shard_map.123.rest_4_), channel_id=1, source_target_pairs={{0,16},{4,20},{8,24},{12,28},{16,0},{20,4},{24,8},{28,12},{1,17},{... | collective-permute-start | bytes 98312 | tf_op jit(solution)/shard_map/ppermute | solution.py:358
  231.1 5.7 %collective-permute-start.56 = (bf16[64,256]{1,0:T(8,128)(2,1)S(1)}, bf16[64,256]{1,0:T(8,128)(2,1)S(1)}, u32[]{:S(2)}, u32[]{:S(2)}) collective-permute-start(bf16[64,256]{1,0:T(8,128)(2,1)S(1)} %shard_map.123.rest_4_), channel_id=1, source_target_pairs={{0,24},{4,28},{8,16},{12,20},{16,8},{20,12},{24,0},{28,4},{1,25},{... | collective-permute-start | bytes 98312 | tf_op jit(solution)/shard_map/ppermute | solution.py:358
  232.6 17.8 %collective-permute-start.35 = (bf16[1024,256]{1,0:T(8,128)(2,1)S(1)}, bf16[1024,256]{1,0:T(8,128)(2,1)S(1)}, u32[]{:S(2)}, u32[]{:S(2)}) collective-permute-start(bf16[1024,256]{1,0:T(8,128)(2,1)S(1)} %get-tuple-element.102), channel_id=1, source_target_pairs={{0,4},{4,0},{8,12},{12,8},{16,20},{20,16},{24,28},{28,24},{1,5},{5... | collective-permute-start | bytes 1572872 | tf_op jit(solution)/shard_map/ppermute | solution.py:345
  236.8 7.4 %collective-permute-start.46 = (bf16[192,256]{1,0:T(8,128)(2,1)S(1)}, bf16[192,256]{1,0:T(8,128)(2,1)S(1)}, u32[]{:S(2)}, u32[]{:S(2)}) collective-permute-start(bf16[192,256]{1,0:T(8,128)(2,1)S(1)} %get-tuple-element.123.rest_0_), channel_id=1, source_target_pairs={{0,16},{4,20},{8,24},{12,28},{16,0},{20,4},{24,8},{28,12},{1,17},{... | collective-permute-start | bytes 294920 | tf_op jit(solution)/shard_map/ppermute | solution.py:358
  236.8 7.4 %collective-permute-start.47 = (bf16[192,256]{1,0:T(8,128)(2,1)S(1)}, bf16[192,256]{1,0:T(8,128)(2,1)S(1)}, u32[]{:S(2)}, u32[]{:S(2)}) collective-permute-start(bf16[192,256]{1,0:T(8,128)(2,1)S(1)} %get-tuple-element.123.rest_0_), channel_id=1, source_target_pairs={{0,24},{4,28},{8,16},{12,20},{16,8},{20,12},{24,0},{28,4},{1,25},{... | collective-permute-start | bytes 294920 | tf_op jit(solution)/shard_map/ppermute | solution.py:358
  244.8 9.0 %collective-permute-start.57 = (bf16[4,256,256]{2,1,0:T(8,128)(2,1)S(1)}, bf16[4,256,256]{2,1,0:T(8,128)(2,1)S(1)}, u32[]{:S(2)}, u32[]{:S(2)}) collective-permute-start(bf16[4,256,256]{2,1,0:T(8,128)(2,1)S(1)} %shard_map.124.rest_0_), channel_id=1, source_target_pairs={{0,4},{4,0},{8,12},{12,8},{16,20},{20,16},{24,28},{28,24},{1,5},{5... | collective-permute-start | bytes 1572872 | tf_op jit(solution)/shard_map/ppermute | solution.py:345
  244.8 8.9 %collective-permute-start.58 = (bf16[32,256]{1,0:T(8,128)(2,1)S(1)}, bf16[32,256]{1,0:T(8,128)(2,1)S(1)}, u32[]{:S(2)}, u32[]{:S(2)}) collective-permute-start(bf16[32,256]{1,0:T(8,128)(2,1)S(1)} %get-tuple-element.132.rest_2_), channel_id=1, source_target_pairs={{0,1},{1,0},{2,3},{3,2},{4,5},{5,4},{6,7},{7,6},{8,9},{9,8},{10,11... | collective-permute-start | bytes 49160 | tf_op jit(solution)/shard_map/ppermute | solution.py:351
  245.7 8.0 %collective-permute-start.59 = (bf16[32,256]{1,0:T(8,128)(2,1)S(1)}, bf16[32,256]{1,0:T(8,128)(2,1)S(1)}, u32[]{:S(2)}, u32[]{:S(2)}) collective-permute-start(bf16[32,256]{1,0:T(8,128)(2,1)S(1)} %get-tuple-element.132.rest_2_), channel_id=1, source_target_pairs={{0,2},{1,3},{2,0},{3,1},{4,6},{5,7},{6,4},{7,5},{8,10},{9,11},{10,... | collective-permute-start | bytes 49160 | tf_op jit(solution)/shard_map/ppermute | solution.py:351
  246.8 7.0 %collective-permute-start.60 = (bf16[32,256]{1,0:T(8,128)(2,1)S(1)}, bf16[32,256]{1,0:T(8,128)(2,1)S(1)}, u32[]{:S(2)}, u32[]{:S(2)}) collective-permute-start(bf16[32,256]{1,0:T(8,128)(2,1)S(1)} %get-tuple-element.132.rest_2_), channel_id=1, source_target_pairs={{0,3},{1,2},{2,1},{3,0},{4,7},{5,6},{6,5},{7,4},{8,11},{9,10},{10,... | collective-permute-start | bytes 49160 | tf_op jit(solution)/shard_map/ppermute | solution.py:351
  (4 other events, 12.0 us)

commit v6 on v5

--- a/solution.py
+++ b/solution.py
@@ -15,7 +15,7 @@
 F32 = jnp.float32
 VM = pl.BlockSpec(memory_space=pltpu.VMEM)
 SM = pl.BlockSpec(memory_space=pltpu.SMEM)
-ANY = pl.BlockSpec(memory_space=pl.ANY)
+FAR = pl.BlockSpec(memory_space=pltpu.HBM)
 
 
 def dot(a, b, ca, cb):
@@ -27,7 +27,7 @@
     return pl.pallas_call(
         body,
         out_shape=tuple(outs),
-        in_specs=[SM if n < scalars else ANY if n in stay else VM for n in range(len(ins))],
+        in_specs=[SM if n < scalars else FAR if n in stay else VM for n in range(len(ins))],
         out_specs=tuple([SM] * small + [VM] * (len(outs) - small)),
         scratch_shapes=list(scratch),
         cost_estimate=pl.CostEstimate(flops=flops, bytes_accessed=moved, transcendentals=0),
@@ -91,7 +91,7 @@
 
 def conv_body(hops, tile, pair, meta, amounts, *rest):
     sources, rest = rest[: hops + 1], rest[hops + 1 :]
-    upstream, kernel, gated, tap_zero, tap_one, grad_kernel, series, total = rest
+    upstream, kernel, gated, acts, late, tap_one, series = rest
     half = sources[0].shape[1]
     core, alive = meta[2], meta[3]
     late_a, late_b = amounts[2 * pair], amounts[2 * pair + 1]
@@ -100,17 +100,17 @@
             series[(2 * (hops - n) + h) * half : (2 * (hops - n) + h + 1) * half, :] = (
                 sources[n][h ^ core].astype(F32)
             )
-    total[...] = jnp.zeros_like(total)
     per_half = half // tile
 
     def step(i, carry):
         slot = (i // per_half) ^ core
         row = pl.multiple_of((i % per_half) * tile, tile)
         start = 2 * hops * half + i * tile
-        late = select_lanes(
+        before = select_lanes(
             series[pl.ds(start - late_a, tile), :], series[pl.ds(start - late_b, tile), :]
         ).astype(BF)
-        stacked = jnp.concatenate([sources[0][slot, pl.ds(row, tile), :], late], axis=1)
+        late[slot, pl.ds(row, tile), :] = before
+        stacked = jnp.concatenate([sources[0][slot, pl.ds(row, tile), :], before], axis=1)
         pre = dot(stacked, kernel[...], 1, 0)
         tanh_act = jnp.tanh(pre[:, :LANES])
         sig_act = jax.nn.sigmoid(pre[:, LANES:])
@@ -120,14 +120,29 @@
         masked = upstream[slot, pl.ds(row, tile), :].astype(F32) * mask
         grad_filter = masked * sig_act * (1.0 - tanh_act * tanh_act)
         grad_gate = masked * tanh_act * sig_act * (1.0 - sig_act)
-        acts = jnp.concatenate([grad_filter.astype(BF), grad_gate.astype(BF)], axis=1)
-        total[...] += dot(stacked, acts, 0, 0)
-        back = dot(acts, kernel[...], 1, 1)
-        tap_zero[slot, pl.ds(row, tile), :] = back[:, :LANES]
-        tap_one[slot, pl.ds(row, tile), :] = back[:, LANES:].astype(BF)
+        both = jnp.concatenate([grad_filter.astype(BF), grad_gate.astype(BF)], axis=1)
+        acts[slot, pl.ds(row, tile), :] = both
+        tap_one[slot, pl.ds(row, tile), :] = dot(both, kernel[LANES:, :], 1, 1).astype(BF)
         return carry
 
     lax.fori_loop(0, 2 * per_half, step, 0)
+
+
+def taps_grad_body(tile, own, late, acts, kernel, tap_zero, grad_kernel, total):
+    total[...] = jnp.zeros_like(total)
+    for slot in range(2):
+
+        def step(i, carry, slot=slot):
+            row = pl.multiple_of(i * tile, tile)
+            both = acts[slot, pl.ds(row, tile), :]
+            stacked = jnp.concatenate(
+                [own[slot, pl.ds(row, tile), :], late[slot, pl.ds(row, tile), :]], axis=1
+            )
+            total[...] += dot(stacked, both, 0, 0)
+            tap_zero[slot, pl.ds(row, tile), :] = dot(both, kernel[:LANES, :], 1, 1)
+            return carry
+
+        lax.fori_loop(0, own.shape[1] // tile, step, 0)
     width = LANES // 2
     for tap in range(2):
         for g in range(2):
@@ -430,13 +445,21 @@
         chain = [projected[j]]
         for hop in range(1, hops + 1):
             chain.append(up(chain[-1], hop))
-        out, tap_zero, tap_one, grad_kernel = call(
+        out, acts, late, tap_one = call(
             functools.partial(conv_body, hops, tile, j),
-            [series, shape((2, samples, LANES), F32), series, shape((2, LANES, LANES), F32)],
+            [series, shape((2, samples, 2 * LANES), BF), series, series],
             [where, amounts] + chain + [grad_gated[j], kernels[j]],
-            scratch=[long, pltpu.VMEM((2 * LANES, 2 * LANES), F32)],
-            flops=6 * block * 4 * LANES * LANES,
+            scratch=[long],
+            flops=4 * block * 4 * LANES * LANES,
             scalars=2,
+        )
+        tap_zero, grad_kernel = call(
+            functools.partial(taps_grad_body, 512 if samples % 512 == 0 else samples),
+            [shape((2, samples, LANES), F32), shape((2, LANES, LANES), F32)],
+            [projected[j], late, acts, kernels[j]],
+            scratch=[pltpu.VMEM((2 * LANES, 2 * LANES), F32)],
+            flops=4 * block * 4 * LANES * LANES,
+            scalars=0,
         )
         gated.append(out)
         kernel_grads.append(grad_kernel)

time: 257 us -> 256 us (level)
    ppermute x8, waiting for transfers between devices: 63.8 us -> 61 us  [down(): lax.ppermute(x, 'seq', [(i + 2, i) for i in range(seq_size - 2 * hop)])]
    pallas_call x24 -> x28, Pallas kernels: 55.5 us -> 57.3 us  [call(): pl.pallas_call(body, out_shape=tuple(outs), in_specs=[SM if n < scalars e...]
  transfers between devices with their start and end apart: 61 -> 61, of which waited for: 27 -> 27; matrix products, arithmetic and copies ran while one was open for 0% -> 0% of each run, Pallas kernels for 21% -> 22%
where the time goes in v6:
time: 256 us; the launch traced here: 255 us
  waiting for transfers between devices  118 us (46%)
  starting transfers between devices  74.8 us (29%)
  Pallas kernels  57.3 us (22%)
  local copies, waits for them, and re-layouts  3.52 us (1%)
    ppermute x8, waiting for transfers between devices, down(): lax.ppermute(x, 'seq', [(i + 2, i) for i in range(seq_size - 2 * hop)])  61 us
    pallas_call x28, Pallas kernels, call(): pl.pallas_call(body, out_shape=tuple(outs), in_specs=[SM if n < scalars e...  57.3 us
    ppermute x18, waiting for transfers between devices, from_chips(): got.append(lax.ppermute(blocks[k], 'seq', pairs))  26 us
    ppermute x8, waiting for transfers between devices, up(): lax.ppermute(x, 'seq', [(i, i + 2) for i in range(2 * (hop - 1), seq_size...  25.4 us
    ppermute x18, starting transfers between devices, from_chips(): got.append(lax.ppermute(blocks[k], 'seq', pairs))  24.7 us
    ppermute x21, starting transfers between devices, from_fsdp(): got.append(lax.ppermute(blocks[k], 'fsdp', pairs))  23.1 us
    ppermute x8, starting transfers between devices, up(): lax.ppermute(x, 'seq', [(i, i + 2) for i in range(2 * (hop - 1), seq_size...  15.8 us
    ppermute x8, starting transfers between devices, down(): lax.ppermute(x, 'seq', [(i + 2, i) for i in range(seq_size - 2 * hop)])  10.5 us
  transfers between devices with their start and end apart: 61, of which 27 were waited for; matrix products, arithmetic and copies ran while one was open for 0% of the time, Pallas kernels for 22%

profile of v6, /device:TPU:0, one launch (start us, length us, event | category | flops | bytes accessed | tf_op | source)
XLA Modules:
  0.0 255.2 jit_solution(7999031658635657409)
XLA Ops:
  2.1 2.9 %collective-permute-start.7 = (bf16[256,128]{1,0:T(8,128)(2,1)S(1)}, bf16[256,128]{1,0:T(8,128)(2,1)S(1)}, u32[]{:S(2)}, u32[]{:S(2)}) collective-permute-start(bf16[256,128]{1,0:T(8,128)(2,1)S(1)} %constant_dynamic-slice_fusion.rest_0_), channel_id=1, source_target_pairs={{0,1},{1,0},{2,3},{3,2},{4,5},{5,4},{6,7},{7,6},{8,9},{9,8},{10,11... | collective-permute-start | bytes 196616 | tf_op jit(solution)/shard_map/ppermute | solution.py:366
  5.0 1.5 collective-permute-start.8
  6.6 1.6 collective-permute-start
  8.8 1.5 collective-permute-done.rest_1_
  10.3 2.6 %collective-permute-start.1 = (s32[2]{0:T(128)}, s32[2]{0:T(128)S(1)}, u32[]{:S(2)}, u32[]{:S(2)}) collective-permute-start(s32[2]{0:T(128)} %rest_0_.1), channel_id=1, source_target_pairs={{0,16},{4,20},{8,24},{12,28},{16,0},{20,4},{24,8},{28,12},{1,17},{... | collective-permute-start | bytes 32 | tf_op jit(solution)/shard_map/ppermute | solution.py:373
  12.8 2.0 collective-permute-done.1.rest_2_
  14.9 3.6 %collective-permute-start.2 = (s32[2]{0:T(128)}, s32[2]{0:T(128)S(1)}, u32[]{:S(2)}, u32[]{:S(2)}) collective-permute-start(s32[2]{0:T(128)} %rest_0_.1), channel_id=1, source_target_pairs={{0,24},{4,28},{8,16},{12,20},{16,8},{20,12},{24,0},{28,4},{1,25},{... | collective-permute-start | bytes 32 | tf_op jit(solution)/shard_map/ppermute | solution.py:373
  18.5 1.9 collective-permute-done.2.rest_3_
  22.3 1.8 collective-permute-start.18
  24.1 2.2 collective-permute-done.9.rest_3_
  26.3 2.0 collective-permute-start.20
  28.4 1.6 collective-permute-start.13
  29.9 1.6 copy-done.1
  31.5 2.5 shard_map.103
  34.1 1.7 collective-permute-done.19.rest_2_
  35.8 1.8 collective-permute-start.4
  37.6 2.0 collective-permute-start.5
  39.5 4.0 %shard_map.109 = (bf16[2,1024,128]{2,1,0:T(8,128)(2,1)S(1)}, bf16[2,1024,128]{2,1,0:T(8,128)(2,1)S(1)}, bf16[2,1024,128]{2,1,0:T(8,128)(2,1)S(1)}, bf16[1024,512]{1,0:T(8,128)(2,1)S(1)}) custom-call(s32[4]{0:T(128)S(1)} %pad_add_fusion.meta, bf16[1024,1024]{1,0:T(8,128)(2,1)S(1)} %bitcast.15, bf16[1024,1024]{1,0:T(8,128)(2,1)S(1)} %collective-permute-done.6.partner.rest_5_, ...), custom_call_target="tpu_custom_call" | custom-call | flops 1610612736 | bytes 7864336 | tf_op jit(solution)/shard_map/pallas_call | solution.py:27
  43.6 2.4 collective-permute-start.31
  46.4 3.9 %collective-permute-start.21 = (bf16[2,1024,128]{2,1,0:T(8,128)(2,1)S(1)}, bf16[2,1024,128]{2,1,0:T(8,128)(2,1)S(1)}, u32[]{:S(2)}, u32[]{:S(2)}) collective-permute-start(bf16[2,1024,128]{2,1,0:T(8,128)(2,1)S(1)} %get-tuple-element.88.rest_0_.own), channel_id=1, source_target_pairs={{0,8},{4,12},{8,16},{12,20},{16,24},{20,28},{1,9},{5,13},{9,17},{1... | collective-permute-start | bytes 1572872 | tf_op jit(solution)/shard_map/ppermute | solution.py:377
  50.3 2.8 %collective-permute-start.10 = (bf16[2,1024,128]{2,1,0:T(8,128)(2,1)S(1)}, bf16[2,1024,128]{2,1,0:T(8,128)(2,1)S(1)}, u32[]{:S(2)}, u32[]{:S(2)}) collective-permute-start(bf16[2,1024,128]{2,1,0:T(8,128)(2,1)S(1)} %get-tuple-element.79.rest_0_.own), channel_id=1, source_target_pairs={{0,8},{4,12},{8,16},{12,20},{16,24},{20,28},{1,9},{5,13},{9,17},{1... | collective-permute-start | bytes 1572872 | tf_op jit(solution)/shard_map/ppermute | solution.py:377
  53.4 3.9 %collective-permute-start.27 = (bf16[2,1024,128]{2,1,0:T(8,128)(2,1)S(1)}, bf16[2,1024,128]{2,1,0:T(8,128)(2,1)S(1)}, u32[]{:S(2)}, u32[]{:S(2)}) collective-permute-start(bf16[2,1024,128]{2,1,0:T(8,128)(2,1)S(1)} %get-tuple-element.100.rest_0_.own), channel_id=1, source_target_pairs={{0,8},{4,12},{8,16},{12,20},{16,24},{20,28},{1,9},{5,13},{9,17},{1... | collective-permute-start | bytes 1572872 | tf_op jit(solution)/shard_map/ppermute | solution.py:377
  59.0 10.5 %collective-permute-done.21.rest_1_ = bf16[2,1024,128]{2,1,0:T(8,128)(2,1)S(1)} collective-permute-done((bf16[2,1024,128]{2,1,0:T(8,128)(2,1)S(1)}, bf16[2,1024,128]{2,1,0:T(8,128)(2,1)S(1)}, u32[]{:S(2)}, u32[]{:S(2)}) %collective-permute-start.21) | collective-permute-done | bytes 524320 | tf_op jit(solution)/shard_map/ppermute | solution.py:377
  70.2 8.9 %collective-permute-done.10.rest_1_ = bf16[2,1024,128]{2,1,0:T(8,128)(2,1)S(1)} collective-permute-done((bf16[2,1024,128]{2,1,0:T(8,128)(2,1)S(1)}, bf16[2,1024,128]{2,1,0:T(8,128)(2,1)S(1)}, u32[]{:S(2)}, u32[]{:S(2)}) %collective-permute-start.10) | collective-permute-done | bytes 524320 | tf_op jit(solution)/shard_map/ppermute | solution.py:377
  79.8 4.9 %collective-permute-done.27.rest_1_ = bf16[2,1024,128]{2,1,0:T(8,128)(2,1)S(1)} collective-permute-done((bf16[2,1024,128]{2,1,0:T(8,128)(2,1)S(1)}, bf16[2,1024,128]{2,1,0:T(8,128)(2,1)S(1)}, u32[]{:S(2)}, u32[]{:S(2)}) %collective-permute-start.27) | collective-permute-done | bytes 524320 | tf_op jit(solution)/shard_map/ppermute | solution.py:377
  85.5 2.0 shard_map.102
  87.5 4.7 %shard_map.104 = (bf16[2,1024,128]{2,1,0:T(8,128)(2,1)S(1)}, bf16[2,1024,128]{2,1,0:T(8,128)(2,1)S(1)}, bf16[2,1024,128]{2,1,0:T(8,128)(2,1)S(1)}, bf16[2,1024,128]{2,1,0:T(8,128)(2,1)S(1)}) custom-call(s32[4]{0:T(128)S(1)} %pad_add_fusion.meta, bf16[1024,1024]{1,0:T(8,128)(2,1)S(1)} %bitcast.19, bf16[1024,1024]{1,0:T(8,128)(2,1)} %collective-permute-done.12.partner.rest_5_, ...), custom_call_target="tpu_custom_call" | custom-call | flops 2147483648 | bytes 7340048 | tf_op jit(solution)/shard_map/pallas_call | solution.py:27
  92.1 3.6 %shard_map.118 = (bf16[2,1024,128]{2,1,0:T(8,128)(2,1)S(1)}, bf16[2,1024,256]{2,1,0:T(8,128)(2,1)S(1)}, bf16[2,1024,128]{2,1,0:T(8,128)(2,1)S(1)}, bf16[2,1024,128]{2,1,0:T(8,128)(2,1)S(1)}) custom-call(s32[4]{0:T(128)S(1)} %pad_add_fusion.meta, s32[8]{0:T(128)S(1)} %get-tuple-element.78.amounts, bf16[2,1024,128]{2,1,0:T(8,128)(2,1)S(1)} %get-tuple-element.108.rest_0_.own, ...), custom_call_target="tpu_custom_call" | custom-call | flops 536870912 | bytes 4849712 | tf_op jit(solution)/shard_map/pallas_call | solution.py:27
  95.7 1.3 collective-permute-start.33
  97.0 3.6 %shard_map.110 = (bf16[2,1024,128]{2,1,0:T(8,128)(2,1)S(1)}, bf16[2,1024,256]{2,1,0:T(8,128)(2,1)S(1)}, bf16[2,1024,128]{2,1,0:T(8,128)(2,1)S(1)}, bf16[2,1024,128]{2,1,0:T(8,128)(2,1)S(1)}) custom-call(s32[4]{0:T(128)S(1)} %pad_add_fusion.meta, s32[8]{0:T(128)S(1)} %get-tuple-element.78.amounts, bf16[2,1024,128]{2,1,0:T(8,128)(2,1)S(1)} %get-tuple-element.88.rest_0_.own, ...), custom_call_target="tpu_custom_call" | custom-call | flops 536870912 | bytes 4849712 | tf_op jit(solution)/shard_map/pallas_call | solution.py:27
  100.6 1.3 collective-permute-start.23
  101.9 3.5 %shard_map.105 = (bf16[2,1024,128]{2,1,0:T(8,128)(2,1)S(1)}, bf16[2,1024,256]{2,1,0:T(8,128)(2,1)S(1)}, bf16[2,1024,128]{2,1,0:T(8,128)(2,1)S(1)}, bf16[2,1024,128]{2,1,0:T(8,128)(2,1)S(1)}) custom-call(s32[4]{0:T(128)S(1)} %pad_add_fusion.meta, s32[8]{0:T(128)S(1)} %get-tuple-element.78.amounts, bf16[2,1024,128]{2,1,0:T(8,128)(2,1)S(1)} %get-tuple-element.79.rest_0_.own, ...), custom_call_target="tpu_custom_call" | custom-call | flops 536870912 | bytes 4849712 | tf_op jit(solution)/shard_map/pallas_call | solution.py:27
  105.4 1.3 collective-permute-start.16
  106.7 3.6 %shard_map.115 = (bf16[2,1024,128]{2,1,0:T(8,128)(2,1)S(1)}, bf16[2,1024,256]{2,1,0:T(8,128)(2,1)S(1)}, bf16[2,1024,128]{2,1,0:T(8,128)(2,1)S(1)}, bf16[2,1024,128]{2,1,0:T(8,128)(2,1)S(1)}) custom-call(s32[4]{0:T(128)S(1)} %pad_add_fusion.meta, s32[8]{0:T(128)S(1)} %get-tuple-element.78.amounts, bf16[2,1024,128]{2,1,0:T(8,128)(2,1)S(1)} %get-tuple-element.100.rest_0_.own, ...), custom_call_target="tpu_custom_call" | custom-call | flops 536870912 | bytes 4849712 | tf_op jit(solution)/shard_map/pallas_call | solution.py:27
  110.3 1.3 collective-permute-start.29
  111.6 10.1 %collective-permute-done.33.rest_1_ = bf16[2,1024,128]{2,1,0:T(8,128)(2,1)S(1)} collective-permute-done((bf16[2,1024,128]{2,1,0:T(8,128)(2,1)S(1)}, bf16[2,1024,128]{2,1,0:T(8,128)(2,1)S(1)}, u32[]{:S(2)}, u32[]{:S(2)}) %collective-permute-start.33) | collective-permute-done | bytes 524320 | tf_op jit(solution)/shard_map/ppermute | solution.py:380
  121.7 1.3 collective-permute-start.34
  123.0 10.0 %collective-permute-done.23.rest_1_ = bf16[2,1024,128]{2,1,0:T(8,128)(2,1)S(1)} collective-permute-done((bf16[2,1024,128]{2,1,0:T(8,128)(2,1)S(1)}, bf16[2,1024,128]{2,1,0:T(8,128)(2,1)S(1)}, u32[]{:S(2)}, u32[]{:S(2)}) %collective-permute-start.23) | collective-permute-done | bytes 524320 | tf_op jit(solution)/shard_map/ppermute | solution.py:380
  134.3 11.1 %collective-permute-done.16.rest_1_ = bf16[2,1024,128]{2,1,0:T(8,128)(2,1)S(1)} collective-permute-done((bf16[2,1024,128]{2,1,0:T(8,128)(2,1)S(1)}, bf16[2,1024,128]{2,1,0:T(8,128)(2,1)S(1)}, u32[]{:S(2)}, u32[]{:S(2)}) %collective-permute-start.16) | collective-permute-done | bytes 524320 | tf_op jit(solution)/shard_map/ppermute | solution.py:380
  146.7 1.4 shard_map.119
  148.1 1.4 shard_map.116
  149.4 1.4 shard_map.111
  150.8 5.8 %collective-permute-done.29.rest_1_ = bf16[2,1024,128]{2,1,0:T(8,128)(2,1)S(1)} collective-permute-done((bf16[2,1024,128]{2,1,0:T(8,128)(2,1)S(1)}, bf16[2,1024,128]{2,1,0:T(8,128)(2,1)S(1)}, u32[]{:S(2)}, u32[]{:S(2)}) %collective-permute-start.29) | collective-permute-done | bytes 524320 | tf_op jit(solution)/shard_map/ppermute | solution.py:380
  156.6 1.5 collective-permute-start.30
  158.1 1.4 shard_map.106
  159.5 4.8 %shard_map.123 = (f32[160,1024]{1,0:T(8,128)S(1)}, bf16[160,1024]{1,0:T(8,128)(2,1)S(1)}, bf16[160,1024]{1,0:T(8,128)(2,1)S(1)}, bf16[160,1024]{1,0:T(8,128)(2,1)S(1)}) custom-call(s32[4]{0:T(128)S(1)} %pad_add_fusion.meta, bf16[2,1024,128]{2,1,0:T(8,128)(2,1)S(1)} %get-tuple-element.123.rest_0_, bf16[2,1024,128]{2,1,0:T(8,128)(2,1)S(1)} %get-tuple-element.124.rest_1_, ...), custom_call_target="tpu_custom_call" | custom-call | flops 2147483648 | bytes 8454160 | tf_op jit(solution)/shard_map/pallas_call | solution.py:27
  164.9 2.9 %collective-permute-done.34.rest_2_ = bf16[2,1024,128]{2,1,0:T(8,128)(2,1)S(1)} collective-permute-done((bf16[2,1024,128]{2,1,0:T(8,128)(2,1)S(1)}, bf16[2,1024,128]{2,1,0:T(8,128)(2,1)S(1)}, u32[]{:S(2)}, u32[]{:S(2)}) %collective-permute-start.34) | collective-permute-done | bytes 524320 | tf_op jit(solution)/shard_map/ppermute | solution.py:380
  168.5 10.6 %collective-permute-done.24.rest_2_ = bf16[2,1024,128]{2,1,0:T(8,128)(2,1)S(1)} collective-permute-done((bf16[2,1024,128]{2,1,0:T(8,128)(2,1)S(1)}, bf16[2,1024,128]{2,1,0:T(8,128)(2,1)S(1)}, u32[]{:S(2)}, u32[]{:S(2)}) %collective-permute-start.24) | collective-permute-done | bytes 524320 | tf_op jit(solution)/shard_map/ppermute | solution.py:380
  179.7 9.5 %collective-permute-done.17.rest_2_ = bf16[2,1024,128]{2,1,0:T(8,128)(2,1)S(1)} collective-permute-done((bf16[2,1024,128]{2,1,0:T(8,128)(2,1)S(1)}, bf16[2,1024,128]{2,1,0:T(8,128)(2,1)S(1)}, u32[]{:S(2)}, u32[]{:S(2)}) %collective-permute-start.17) | collective-permute-done | bytes 524320 | tf_op jit(solution)/shard_map/ppermute | solution.py:380
  191.1 2.6 %shard_map.113 = (f32[256,256]{1,0:T(8,128)S(1)}, bf16[256,256]{1,0:T(8,128)(2,1)S(1)}, bf16[256,256]{1,0:T(8,128)(2,1)S(1)}, bf16[256,256]{1,0:T(8,128)(2,1)S(1)}, bf16[1024,256]{1,0:T(8,128)(2,1)S(1)}) custom-call(s32[4]{0:T(128)S(1)} %pad_add_fusion.meta, bf16[1024,128]{1,0:T(8,128)(2,1)S(1)} %get-tuple-element.86.rest_0_, ...), custom_call_target="tpu_custom_call" | custom-call | flops 1073741824 | bytes 6422544 | tf_op jit(solution)/shard_map/pallas_call | solution.py:27
  198.5 1.9 collective-permute-start.38
  200.4 2.5 shard_map.121
  205.7 2.0 collective-permute-start.50
  208.6 2.5 collective-permute-start.42
  211.2 2.5 collective-permute-start.44
  216.5 3.4 %collective-permute-done.43.rest_2_ = bf16[224,256]{1,0:T(8,128)(2,1)S(1)} collective-permute-done((bf16[224,256]{1,0:T(8,128)(2,1)S(1)}, bf16[224,256]{1,0:T(8,128)(2,1)S(1)}, u32[]{:S(2)}, u32[]{:S(2)}) %collective-permute-start.43) | collective-permute-done | bytes 114720 | tf_op jit(solution)/shard_map/ppermute | solution.py:373
  221.2 2.3 collective-permute-start.45
  227.5 2.7 %collective-permute-done.54.rest_5_ = bf16[64,256]{1,0:T(8,128)(2,1)S(1)} collective-permute-done((bf16[64,256]{1,0:T(8,128)(2,1)S(1)}, bf16[64,256]{1,0:T(8,128)(2,1)S(1)}, u32[]{:S(2)}, u32[]{:S(2)}) %collective-permute-start.54) | collective-permute-done | bytes 32800 | tf_op jit(solution)/shard_map/ppermute | solution.py:373
  231.7 4.2 %collective-permute-done.56.rest_7_ = bf16[64,256]{1,0:T(8,128)(2,1)S(1)} collective-permute-done((bf16[64,256]{1,0:T(8,128)(2,1)S(1)}, bf16[64,256]{1,0:T(8,128)(2,1)S(1)}, u32[]{:S(2)}, u32[]{:S(2)}) %collective-permute-start.56) | collective-permute-done | bytes 32800 | tf_op jit(solution)/shard_map/ppermute | solution.py:373
  237.1 6.2 %collective-permute-done.46.rest_2_ = bf16[192,256]{1,0:T(8,128)(2,1)S(1)} collective-permute-done((bf16[192,256]{1,0:T(8,128)(2,1)S(1)}, bf16[192,256]{1,0:T(8,128)(2,1)S(1)}, u32[]{:S(2)}, u32[]{:S(2)}) %collective-permute-start.46) | collective-permute-done | bytes 98336 | tf_op jit(solution)/shard_map/ppermute | solution.py:373
  245.8 1.8 collective-permute-start.60
  247.5 2.0 shard_map.114.base
  249.5 3.3 %shard_map.122 = bf16[1024,1024]{1,0:T(8,128)(2,1)} custom-call(f32[1024,1024]{1,0:T(8,128)S(1)} %shard_map.114.base, bf16[1024,128]{1,0:T(8,128)(2,1)S(1)} %get-tuple-element.107.rest_0_, bf16[1024,128]{1,0:T(8,128)(2,1)S(1)} %get-tuple-element.115.rest_2_.rest_1_, bf16[1024,256]{1,0:T(8,128)(2,1)S(1)} %collective-permute-done.35.rest_2_, ...), custom_call_target="tpu_custom_call" | custom-call | flops 1073741824 | bytes 9437184 | tf_op jit(solution)/shard_map/pallas_call | solution.py:27
  252.9 2.3 shard_map.129
  (103 shorter events, 36.1 us)
Async XLA Ops:
  0.6 27.7 %copy-start = (bf16[256,1024]{1,0:T(8,128)(2,1)S(1)}, bf16[256,1024]{1,0:T(8,128)(2,1)}, u32[]{:S(2)}) copy-start(bf16[256,1024]{1,0:T(8,128)(2,1)} %param.11) | copy-start | bytes 1572868
  0.6 27.7 %collective-permute-start.6 = (bf16[1024,1024]{1,0:T(8,128)(2,1)}, bf16[1024,1024]{1,0:T(8,128)(2,1)S(1)}, u32[]{:S(2)}, u32[]{:S(2)}) collective-permute-start(bf16[1024,1024]{1,0:T(8,128)(2,1)} %bitcast.13), channel_id=1, source_target_pairs={{0,4},{4,0},{8,12},{12,8},{16,20},{20,16},{24,28},{28,24},{1,5},{5... | collective-permute-start | bytes 6291464 | tf_op jit(solution)/shard_map/ppermute | solution.py:360
  1.2 86.2 %collective-permute-start.12 = (bf16[1024,1024]{1,0:T(8,128)(2,1)}, bf16[1024,1024]{1,0:T(8,128)(2,1)}, u32[]{:S(2)}, u32[]{:S(2)}) collective-permute-start(bf16[1024,1024]{1,0:T(8,128)(2,1)} %bitcast.18), channel_id=1, source_target_pairs={{0,4},{4,0},{8,12},{12,8},{16,20},{20,16},{24,28},{28,24},{1,5},{5... | collective-permute-start | bytes 6291464 | tf_op jit(solution)/shard_map/ppermute | solution.py:360
  2.1 18.5 %collective-permute-start.7 = (bf16[256,128]{1,0:T(8,128)(2,1)S(1)}, bf16[256,128]{1,0:T(8,128)(2,1)S(1)}, u32[]{:S(2)}, u32[]{:S(2)}) collective-permute-start(bf16[256,128]{1,0:T(8,128)(2,1)S(1)} %constant_dynamic-slice_fusion.rest_0_), channel_id=1, source_target_pairs={{0,1},{1,0},{2,3},{3,2},{4,5},{5,4},{6,7},{7,6},{8,9},{9,8},{10,11... | collective-permute-start | bytes 196616 | tf_op jit(solution)/shard_map/ppermute | solution.py:366
  5.0 17.3 %collective-permute-start.8 = (bf16[256,128]{1,0:T(8,128)(2,1)S(1)}, bf16[256,128]{1,0:T(8,128)(2,1)S(1)}, u32[]{:S(2)}, u32[]{:S(2)}) collective-permute-start(bf16[256,128]{1,0:T(8,128)(2,1)S(1)} %constant_dynamic-slice_fusion.rest_0_), channel_id=1, source_target_pairs={{0,2},{1,3},{2,0},{3,1},{4,6},{5,7},{6,4},{7,5},{8,10},{9,11},{10,... | collective-permute-start | bytes 196616 | tf_op jit(solution)/shard_map/ppermute | solution.py:366
  6.6 3.7 %collective-permute-start = (s32[2]{0:T(128)}, s32[2]{0:T(128)S(1)}, u32[]{:S(2)}, u32[]{:S(2)}) collective-permute-start(s32[2]{0:T(128)} %rest_0_.1), channel_id=1, source_target_pairs={{0,8},{4,12},{8,0},{12,4},{16,24},{20,28},{24,16},{28,20},{1,9},{5... | collective-permute-start | bytes 32 | tf_op jit(solution)/shard_map/ppermute | solution.py:373
  10.3 4.6 %collective-permute-start.1 = (s32[2]{0:T(128)}, s32[2]{0:T(128)S(1)}, u32[]{:S(2)}, u32[]{:S(2)}) collective-permute-start(s32[2]{0:T(128)} %rest_0_.1), channel_id=1, source_target_pairs={{0,16},{4,20},{8,24},{12,28},{16,0},{20,4},{24,8},{28,12},{1,17},{... | collective-permute-start | bytes 32 | tf_op jit(solution)/shard_map/ppermute | solution.py:373
  14.9 5.5 %collective-permute-start.2 = (s32[2]{0:T(128)}, s32[2]{0:T(128)S(1)}, u32[]{:S(2)}, u32[]{:S(2)}) collective-permute-start(s32[2]{0:T(128)} %rest_0_.1), channel_id=1, source_target_pairs={{0,24},{4,28},{8,16},{12,20},{16,8},{20,12},{24,0},{28,4},{1,25},{... | collective-permute-start | bytes 32 | tf_op jit(solution)/shard_map/ppermute | solution.py:373
  20.4 6.0 %collective-permute-start.9 = (bf16[256,128]{1,0:T(8,128)(2,1)S(1)}, bf16[256,128]{1,0:T(8,128)(2,1)S(1)}, u32[]{:S(2)}, u32[]{:S(2)}) collective-permute-start(bf16[256,128]{1,0:T(8,128)(2,1)S(1)} %constant_dynamic-slice_fusion.rest_0_), channel_id=1, source_target_pairs={{0,3},{1,2},{2,1},{3,0},{4,7},{5,6},{6,5},{7,4},{8,11},{9,10},{10,... | collective-permute-start | bytes 196616 | tf_op jit(solution)/shard_map/ppermute | solution.py:366
  20.6 5.7 %collective-permute-start.3 = (bf16[2,128,128]{2,1,0:T(8,128)(2,1)}, bf16[2,128,128]{2,1,0:T(8,128)(2,1)S(1)}, u32[]{:S(2)}, u32[]{:S(2)}) collective-permute-start(bf16[2,128,128]{2,1,0:T(8,128)(2,1)} %rest_4_.1), channel_id=1, source_target_pairs={{0,8},{4,12},{8,0},{12,4},{16,24},{20,28},{24,16},{28,20},{1,9},{5... | collective-permute-start | bytes 196616 | tf_op jit(solution)/shard_map/ppermute | solution.py:373
  22.3 11.7 %collective-permute-start.18 = (bf16[256,384]{1,0:T(8,128)(2,1)S(1)}, bf16[256,384]{1,0:T(8,128)(2,1)S(1)}, u32[]{:S(2)}, u32[]{:S(2)}) collective-permute-start(bf16[256,384]{1,0:T(8,128)(2,1)S(1)} %shard_map.108.rest_0_), channel_id=1, source_target_pairs={{0,1},{1,0},{2,3},{3,2},{4,5},{5,4},{6,7},{7,6},{8,9},{9,8},{10,11... | collective-permute-start | bytes 589832 | tf_op jit(solution)/shard_map/ppermute | solution.py:366
  26.3 9.5 %collective-permute-start.19 = (bf16[256,384]{1,0:T(8,128)(2,1)S(1)}, bf16[256,384]{1,0:T(8,128)(2,1)S(1)}, u32[]{:S(2)}, u32[]{:S(2)}) collective-permute-start(bf16[256,384]{1,0:T(8,128)(2,1)S(1)} %shard_map.108.rest_0_), channel_id=1, source_target_pairs={{0,2},{1,3},{2,0},{3,1},{4,6},{5,7},{6,4},{7,5},{8,10},{9,11},{10,... | collective-permute-start | bytes 589832 | tf_op jit(solution)/shard_map/ppermute | solution.py:366
  26.3 11.2 %collective-permute-start.20 = (bf16[256,384]{1,0:T(8,128)(2,1)S(1)}, bf16[256,384]{1,0:T(8,128)(2,1)}, u32[]{:S(2)}, u32[]{:S(2)}) collective-permute-start(bf16[256,384]{1,0:T(8,128)(2,1)S(1)} %shard_map.108.rest_0_), channel_id=1, source_target_pairs={{0,3},{1,2},{2,1},{3,0},{4,7},{5,6},{6,5},{7,4},{8,11},{9,10},{10,... | collective-permute-start | bytes 589832 | tf_op jit(solution)/shard_map/ppermute | solution.py:366
  28.4 18.0 %collective-permute-start.13 = (bf16[128,1024]{1,0:T(8,128)(2,1)S(1)}, bf16[128,1024]{1,0:T(8,128)(2,1)S(1)}, u32[]{:S(2)}, u32[]{:S(2)}) collective-permute-start(bf16[128,1024]{1,0:T(8,128)(2,1)S(1)} %dynamic-slice_bitcast_fusion.rest_0_), channel_id=1, source_target_pairs={{0,1},{1,0},{2,3},{3,2},{4,5},{5,4},{6,7},{7,6},{8,9},{9,8},{10,11... | collective-permute-start | bytes 786440 | tf_op jit(solution)/shard_map/ppermute | solution.py:366
  34.0 16.3 %collective-permute-start.14 = (bf16[128,1024]{1,0:T(8,128)(2,1)S(1)}, bf16[128,1024]{1,0:T(8,128)(2,1)S(1)}, u32[]{:S(2)}, u32[]{:S(2)}) collective-permute-start(bf16[128,1024]{1,0:T(8,128)(2,1)S(1)} %dynamic-slice_bitcast_fusion.rest_0_), channel_id=1, source_target_pairs={{0,2},{1,3},{2,0},{3,1},{4,6},{5,7},{6,4},{7,5},{8,10},{9,11},{10,... | collective-permute-start | bytes 786440 | tf_op jit(solution)/shard_map/ppermute | solution.py:366
  35.8 7.8 %collective-permute-start.4 = (bf16[2,128,128]{2,1,0:T(8,128)(2,1)S(1)}, bf16[2,128,128]{2,1,0:T(8,128)(2,1)S(1)}, u32[]{:S(2)}, u32[]{:S(2)}) collective-permute-start(bf16[2,128,128]{2,1,0:T(8,128)(2,1)S(1)} %copy-done.5), channel_id=1, source_target_pairs={{0,16},{4,20},{8,24},{12,28},{16,0},{20,4},{24,8},{28,12},{1,17},{... | collective-permute-start | bytes 196616 | tf_op jit(solution)/shard_map/ppermute | solution.py:373
  37.6 8.5 %collective-permute-start.5 = (bf16[2,128,128]{2,1,0:T(8,128)(2,1)S(1)}, bf16[2,128,128]{2,1,0:T(8,128)(2,1)S(1)}, u32[]{:S(2)}, u32[]{:S(2)}) collective-permute-start(bf16[2,128,128]{2,1,0:T(8,128)(2,1)S(1)} %copy-done.5), channel_id=1, source_target_pairs={{0,24},{4,28},{8,16},{12,20},{16,8},{20,12},{24,0},{28,4},{1,25},{... | collective-permute-start | bytes 196616 | tf_op jit(solution)/shard_map/ppermute | solution.py:373
  39.5 45.9 %copy-start.6 = (s32[2]{0:T(128)S(1)}, s32[2]{0:T(128)}, u32[]{:S(2)}) copy-start(s32[2]{0:T(128)} %rest_0_.1) | copy-start | bytes 28
  39.5 47.9 %copy-start.3 = (bf16[1,1024,1024]{2,1,0:T(8,128)(2,1)S(1)}, bf16[1,1024,1024]{2,1,0:T(8,128)(2,1)}, u32[]{:S(2)}) copy-start(bf16[1,1024,1024]{2,1,0:T(8,128)(2,1)} %param.8) | copy-start | bytes 6291460
  43.6 14.7 %collective-permute-start.31 = (bf16[2,1024,128]{2,1,0:T(8,128)(2,1)S(1)}, bf16[2,1024,128]{2,1,0:T(8,128)(2,1)S(1)}, u32[]{:S(2)}, u32[]{:S(2)}) collective-permute-start(bf16[2,1024,128]{2,1,0:T(8,128)(2,1)S(1)} %get-tuple-element.108.rest_0_.own), channel_id=1, source_target_pairs={{0,8},{4,12},{8,16},{12,20},{16,24},{20,28},{1,9},{5,13},{9,17},{1... | collective-permute-start | bytes 1572872 | tf_op jit(solution)/shard_map/ppermute | solution.py:377
  46.1 7.3 %collective-permute-start.15 = (bf16[128,1024]{1,0:T(8,128)(2,1)S(1)}, bf16[128,1024]{1,0:T(8,128)(2,1)S(1)}, u32[]{:S(2)}, u32[]{:S(2)}) collective-permute-start(bf16[128,1024]{1,0:T(8,128)(2,1)S(1)} %dynamic-slice_bitcast_fusion.rest_0_), channel_id=1, source_target_pairs={{0,3},{1,2},{2,1},{3,0},{4,7},{5,6},{6,5},{7,4},{8,11},{9,10},{10,... | collective-permute-start | bytes 786440 | tf_op jit(solution)/shard_map/ppermute | solution.py:366
  46.4 23.2 %collective-permute-start.21 = (bf16[2,1024,128]{2,1,0:T(8,128)(2,1)S(1)}, bf16[2,1024,128]{2,1,0:T(8,128)(2,1)S(1)}, u32[]{:S(2)}, u32[]{:S(2)}) collective-permute-start(bf16[2,1024,128]{2,1,0:T(8,128)(2,1)S(1)} %get-tuple-element.88.rest_0_.own), channel_id=1, source_target_pairs={{0,8},{4,12},{8,16},{12,20},{16,24},{20,28},{1,9},{5,13},{9,17},{1... | collective-permute-start | bytes 1572872 | tf_op jit(solution)/shard_map/ppermute | solution.py:377
  50.3 28.8 %collective-permute-start.10 = (bf16[2,1024,128]{2,1,0:T(8,128)(2,1)S(1)}, bf16[2,1024,128]{2,1,0:T(8,128)(2,1)S(1)}, u32[]{:S(2)}, u32[]{:S(2)}) collective-permute-start(bf16[2,1024,128]{2,1,0:T(8,128)(2,1)S(1)} %get-tuple-element.79.rest_0_.own), channel_id=1, source_target_pairs={{0,8},{4,12},{8,16},{12,20},{16,24},{20,28},{1,9},{5,13},{9,17},{1... | collective-permute-start | bytes 1572872 | tf_op jit(solution)/shard_map/ppermute | solution.py:377
  53.4 31.3 %collective-permute-start.27 = (bf16[2,1024,128]{2,1,0:T(8,128)(2,1)S(1)}, bf16[2,1024,128]{2,1,0:T(8,128)(2,1)S(1)}, u32[]{:S(2)}, u32[]{:S(2)}) collective-permute-start(bf16[2,1024,128]{2,1,0:T(8,128)(2,1)S(1)} %get-tuple-element.100.rest_0_.own), channel_id=1, source_target_pairs={{0,8},{4,12},{8,16},{12,20},{16,24},{20,28},{1,9},{5,13},{9,17},{1... | collective-permute-start | bytes 1572872 | tf_op jit(solution)/shard_map/ppermute | solution.py:377
  58.3 33.8 %collective-permute-start.32 = (bf16[2,1024,128]{2,1,0:T(8,128)(2,1)S(1)}, bf16[2,1024,128]{2,1,0:T(8,128)(2,1)S(1)}, u32[]{:S(2)}, u32[]{:S(2)}) collective-permute-start(bf16[2,1024,128]{2,1,0:T(8,128)(2,1)S(1)} %collective-permute-done.31.rest_1_), channel_id=1, source_target_pairs={{8,16},{12,20},{16,24},{20,28},{9,17},{13,21},{17,25},{21,29},{10,... | collective-permute-start | bytes 1572872 | tf_op jit(solution)/shard_map/ppermute | solution.py:377
  69.6 27.4 %collective-permute-start.22 = (bf16[2,1024,128]{2,1,0:T(8,128)(2,1)S(1)}, bf16[2,1024,128]{2,1,0:T(8,128)(2,1)S(1)}, u32[]{:S(2)}, u32[]{:S(2)}) collective-permute-start(bf16[2,1024,128]{2,1,0:T(8,128)(2,1)S(1)} %collective-permute-done.21.rest_1_), channel_id=1, source_target_pairs={{8,16},{12,20},{16,24},{20,28},{9,17},{13,21},{17,25},{21,29},{10,... | collective-permute-start | bytes 1572872 | tf_op jit(solution)/shard_map/ppermute | solution.py:377
  79.1 22.7 %collective-permute-start.11 = (bf16[2,1024,128]{2,1,0:T(8,128)(2,1)S(1)}, bf16[2,1024,128]{2,1,0:T(8,128)(2,1)S(1)}, u32[]{:S(2)}, u32[]{:S(2)}) collective-permute-start(bf16[2,1024,128]{2,1,0:T(8,128)(2,1)S(1)} %collective-permute-done.10.rest_1_), channel_id=1, source_target_pairs={{8,16},{12,20},{16,24},{20,28},{9,17},{13,21},{17,25},{21,29},{10,... | collective-permute-start | bytes 1572872 | tf_op jit(solution)/shard_map/ppermute | solution.py:377
  84.8 22.0 %collective-permute-start.28 = (bf16[2,1024,128]{2,1,0:T(8,128)(2,1)S(1)}, bf16[2,1024,128]{2,1,0:T(8,128)(2,1)S(1)}, u32[]{:S(2)}, u32[]{:S(2)}) collective-permute-start(bf16[2,1024,128]{2,1,0:T(8,128)(2,1)S(1)} %collective-permute-done.27.rest_1_), channel_id=1, source_target_pairs={{8,16},{12,20},{16,24},{20,28},{9,17},{13,21},{17,25},{21,29},{10,... | collective-permute-start | bytes 1572872 | tf_op jit(solution)/shard_map/ppermute | solution.py:377
  95.7 26.0 %collective-permute-start.33 = (bf16[2,1024,128]{2,1,0:T(8,128)(2,1)S(1)}, bf16[2,1024,128]{2,1,0:T(8,128)(2,1)S(1)}, u32[]{:S(2)}, u32[]{:S(2)}) collective-permute-start(bf16[2,1024,128]{2,1,0:T(8,128)(2,1)S(1)} %get-tuple-element.114.rest_0_), channel_id=1, source_target_pairs={{8,0},{12,4},{16,8},{20,12},{24,16},{28,20},{9,1},{13,5},{17,9},{2... | collective-permute-start | bytes 1572872 | tf_op jit(solution)/shard_map/ppermute | solution.py:380
  100.6 32.4 %collective-permute-start.23 = (bf16[2,1024,128]{2,1,0:T(8,128)(2,1)S(1)}, bf16[2,1024,128]{2,1,0:T(8,128)(2,1)S(1)}, u32[]{:S(2)}, u32[]{:S(2)}) collective-permute-start(bf16[2,1024,128]{2,1,0:T(8,128)(2,1)S(1)} %get-tuple-element.94.rest_0_), channel_id=1, source_target_pairs={{8,0},{12,4},{16,8},{20,12},{24,16},{28,20},{9,1},{13,5},{17,9},{2... | collective-permute-start | bytes 1572872 | tf_op jit(solution)/shard_map/ppermute | solution.py:380
  105.4 39.9 %collective-permute-start.16 = (bf16[2,1024,128]{2,1,0:T(8,128)(2,1)S(1)}, bf16[2,1024,128]{2,1,0:T(8,128)(2,1)S(1)}, u32[]{:S(2)}, u32[]{:S(2)}) collective-permute-start(bf16[2,1024,128]{2,1,0:T(8,128)(2,1)S(1)} %get-tuple-element.85.rest_0_), channel_id=1, source_target_pairs={{8,0},{12,4},{16,8},{20,12},{24,16},{28,20},{9,1},{13,5},{17,9},{2... | collective-permute-start | bytes 1572872 | tf_op jit(solution)/shard_map/ppermute | solution.py:380
  110.3 46.3 %collective-permute-start.29 = (bf16[2,1024,128]{2,1,0:T(8,128)(2,1)S(1)}, bf16[2,1024,128]{2,1,0:T(8,128)(2,1)S(1)}, u32[]{:S(2)}, u32[]{:S(2)}) collective-permute-start(bf16[2,1024,128]{2,1,0:T(8,128)(2,1)S(1)} %get-tuple-element.106.rest_0_), channel_id=1, source_target_pairs={{8,0},{12,4},{16,8},{20,12},{24,16},{28,20},{9,1},{13,5},{17,9},{2... | collective-permute-start | bytes 1572872 | tf_op jit(solution)/shard_map/ppermute | solution.py:380
  121.7 46.1 %collective-permute-start.34 = (bf16[2,1024,128]{2,1,0:T(8,128)(2,1)S(1)}, bf16[2,1024,128]{2,1,0:T(8,128)(2,1)S(1)}, u32[]{:S(2)}, u32[]{:S(2)}) collective-permute-start(bf16[2,1024,128]{2,1,0:T(8,128)(2,1)S(1)} %collective-permute-done.33.rest_1_), channel_id=1, source_target_pairs={{8,0},{12,4},{16,8},{20,12},{9,1},{13,5},{17,9},{21,13},{10,2},{14... | collective-permute-start | bytes 1572872 | tf_op jit(solution)/shard_map/ppermute | solution.py:380
  133.0 46.1 %collective-permute-start.24 = (bf16[2,1024,128]{2,1,0:T(8,128)(2,1)S(1)}, bf16[2,1024,128]{2,1,0:T(8,128)(2,1)S(1)}, u32[]{:S(2)}, u32[]{:S(2)}) collective-permute-start(bf16[2,1024,128]{2,1,0:T(8,128)(2,1)S(1)} %collective-permute-done.23.rest_1_), channel_id=1, source_target_pairs={{8,0},{12,4},{16,8},{20,12},{9,1},{13,5},{17,9},{21,13},{10,2},{14... | collective-permute-start | bytes 1572872 | tf_op jit(solution)/shard_map/ppermute | solution.py:380
  145.4 43.8 %collective-permute-start.17 = (bf16[2,1024,128]{2,1,0:T(8,128)(2,1)S(1)}, bf16[2,1024,128]{2,1,0:T(8,128)(2,1)S(1)}, u32[]{:S(2)}, u32[]{:S(2)}) collective-permute-start(bf16[2,1024,128]{2,1,0:T(8,128)(2,1)S(1)} %collective-permute-done.16.rest_1_), channel_id=1, source_target_pairs={{8,0},{12,4},{16,8},{20,12},{9,1},{13,5},{17,9},{21,13},{10,2},{14... | collective-permute-start | bytes 1572872 | tf_op jit(solution)/shard_map/ppermute | solution.py:380
  156.6 38.2 %collective-permute-start.30 = (bf16[2,1024,128]{2,1,0:T(8,128)(2,1)S(1)}, bf16[2,1024,128]{2,1,0:T(8,128)(2,1)S(1)}, u32[]{:S(2)}, u32[]{:S(2)}) collective-permute-start(bf16[2,1024,128]{2,1,0:T(8,128)(2,1)S(1)} %collective-permute-done.29.rest_1_), channel_id=1, source_target_pairs={{8,0},{12,4},{16,8},{20,12},{9,1},{13,5},{17,9},{21,13},{10,2},{14... | collective-permute-start | bytes 1572872 | tf_op jit(solution)/shard_map/ppermute | solution.py:380
  164.3 33.3 %collective-permute-start.39 = (bf16[160,1024]{1,0:T(8,128)(2,1)S(1)}, bf16[160,1024]{1,0:T(8,128)(2,1)S(1)}, u32[]{:S(2)}, u32[]{:S(2)}) collective-permute-start(bf16[160,1024]{1,0:T(8,128)(2,1)S(1)} %get-tuple-element.132), channel_id=1, source_target_pairs={{0,1},{1,0},{2,3},{3,2},{4,5},{5,4},{6,7},{7,6},{8,9},{9,8},{10,11... | collective-permute-start | bytes 983048 | tf_op jit(solution)/shard_map/ppermute | solution.py:366
  167.8 30.7 %collective-permute-start.40 = (bf16[160,1024]{1,0:T(8,128)(2,1)S(1)}, bf16[160,1024]{1,0:T(8,128)(2,1)S(1)}, u32[]{:S(2)}, u32[]{:S(2)}) collective-permute-start(bf16[160,1024]{1,0:T(8,128)(2,1)S(1)} %get-tuple-element.133), channel_id=1, source_target_pairs={{0,2},{1,3},{2,0},{3,1},{4,6},{5,7},{6,4},{7,5},{8,10},{9,11},{10,... | collective-permute-start | bytes 983048 | tf_op jit(solution)/shard_map/ppermute | solution.py:366
  179.1 23.9 %collective-permute-start.41 = (bf16[160,1024]{1,0:T(8,128)(2,1)S(1)}, bf16[160,1024]{1,0:T(8,128)(2,1)S(1)}, u32[]{:S(2)}, u32[]{:S(2)}) collective-permute-start(bf16[160,1024]{1,0:T(8,128)(2,1)S(1)} %get-tuple-element.134), channel_id=1, source_target_pairs={{0,3},{1,2},{2,1},{3,0},{4,7},{5,6},{6,5},{7,4},{8,11},{9,10},{10,... | collective-permute-start | bytes 983048 | tf_op jit(solution)/shard_map/ppermute | solution.py:366
  189.2 55.6 %collective-permute-start.26 = (bf16[1024,512]{1,0:T(8,128)(2,1)S(1)}, bf16[1024,512]{1,0:T(8,128)(2,1)S(1)}, u32[]{:S(2)}, u32[]{:S(2)}) collective-permute-start(bf16[1024,512]{1,0:T(8,128)(2,1)S(1)} %get-tuple-element.99.rest_3_), channel_id=1, source_target_pairs={{0,4},{4,0},{8,12},{12,8},{16,20},{20,16},{24,28},{28,24},{1,5},{5... | collective-permute-start | bytes 3145736 | tf_op jit(solution)/shard_map/ppermute | solution.py:360
  194.8 9.0 %collective-permute-start.36 = (bf16[256,256]{1,0:T(8,128)(2,1)S(1)}, bf16[256,256]{1,0:T(8,128)(2,1)S(1)}, u32[]{:S(2)}, u32[]{:S(2)}) collective-permute-start(bf16[256,256]{1,0:T(8,128)(2,1)S(1)} %get-tuple-element.120), channel_id=1, source_target_pairs={{0,1},{1,0},{2,3},{3,2},{4,5},{5,4},{6,7},{7,6},{8,9},{9,8},{10,11... | collective-permute-start | bytes 393224 | tf_op jit(solution)/shard_map/ppermute | solution.py:366
  197.6 8.1 %collective-permute-start.37 = (bf16[256,256]{1,0:T(8,128)(2,1)S(1)}, bf16[256,256]{1,0:T(8,128)(2,1)S(1)}, u32[]{:S(2)}, u32[]{:S(2)}) collective-permute-start(bf16[256,256]{1,0:T(8,128)(2,1)S(1)} %get-tuple-element.121), channel_id=1, source_target_pairs={{0,2},{1,3},{2,0},{3,1},{4,6},{5,7},{6,4},{7,5},{8,10},{9,11},{10,... | collective-permute-start | bytes 393224 | tf_op jit(solution)/shard_map/ppermute | solution.py:366
  198.5 9.1 %collective-permute-start.38 = (bf16[256,256]{1,0:T(8,128)(2,1)S(1)}, bf16[256,256]{1,0:T(8,128)(2,1)S(1)}, u32[]{:S(2)}, u32[]{:S(2)}) collective-permute-start(bf16[256,256]{1,0:T(8,128)(2,1)S(1)} %get-tuple-element.122), channel_id=1, source_target_pairs={{0,3},{1,2},{2,1},{3,0},{4,7},{5,6},{6,5},{7,4},{8,11},{9,10},{10,... | collective-permute-start | bytes 393224 | tf_op jit(solution)/shard_map/ppermute | solution.py:366
  203.0 8.2 %collective-permute-start.48 = (bf16[256,256]{1,0:T(8,128)(2,1)S(1)}, bf16[256,256]{1,0:T(8,128)(2,1)S(1)}, u32[]{:S(2)}, u32[]{:S(2)}) collective-permute-start(bf16[256,256]{1,0:T(8,128)(2,1)S(1)} %get-tuple-element.141), channel_id=1, source_target_pairs={{0,1},{1,0},{2,3},{3,2},{4,5},{5,4},{6,7},{7,6},{8,9},{9,8},{10,11... | collective-permute-start | bytes 393224 | tf_op jit(solution)/shard_map/ppermute | solution.py:366
  203.8 7.4 %collective-permute-start.49 = (bf16[256,256]{1,0:T(8,128)(2,1)S(1)}, bf16[256,256]{1,0:T(8,128)(2,1)S(1)}, u32[]{:S(2)}, u32[]{:S(2)}) collective-permute-start(bf16[256,256]{1,0:T(8,128)(2,1)S(1)} %get-tuple-element.142), channel_id=1, source_target_pairs={{0,2},{1,3},{2,0},{3,1},{4,6},{5,7},{6,4},{7,5},{8,10},{9,11},{10,... | collective-permute-start | bytes 393224 | tf_op jit(solution)/shard_map/ppermute | solution.py:366
  205.7 8.0 %collective-permute-start.50 = (bf16[256,256]{1,0:T(8,128)(2,1)S(1)}, bf16[256,256]{1,0:T(8,128)(2,1)S(1)}, u32[]{:S(2)}, u32[]{:S(2)}) collective-permute-start(bf16[256,256]{1,0:T(8,128)(2,1)S(1)} %get-tuple-element.143), channel_id=1, source_target_pairs={{0,3},{1,2},{2,1},{3,0},{4,7},{5,6},{6,5},{7,4},{8,11},{9,10},{10,... | collective-permute-start | bytes 393224 | tf_op jit(solution)/shard_map/ppermute | solution.py:366
  208.6 7.8 %collective-permute-start.42 = (bf16[224,256]{1,0:T(8,128)(2,1)S(1)}, bf16[224,256]{1,0:T(8,128)(2,1)S(1)}, u32[]{:S(2)}, u32[]{:S(2)}) collective-permute-start(bf16[224,256]{1,0:T(8,128)(2,1)S(1)} %get-tuple-element.136), channel_id=1, source_target_pairs={{0,8},{4,12},{8,0},{12,4},{16,24},{20,28},{24,16},{28,20},{1,9},{5... | collective-permute-start | bytes 344072 | tf_op jit(solution)/shard_map/ppermute | solution.py:373
  211.2 8.7 %collective-permute-start.43 = (bf16[224,256]{1,0:T(8,128)(2,1)S(1)}, bf16[224,256]{1,0:T(8,128)(2,1)S(1)}, u32[]{:S(2)}, u32[]{:S(2)}) collective-permute-start(bf16[224,256]{1,0:T(8,128)(2,1)S(1)} %get-tuple-element.137), channel_id=1, source_target_pairs={{0,16},{4,20},{8,24},{12,28},{16,0},{20,4},{24,8},{28,12},{1,17},{... | collective-permute-start | bytes 344072 | tf_op jit(solution)/shard_map/ppermute | solution.py:373
  211.2 8.7 %collective-permute-start.44 = (bf16[224,256]{1,0:T(8,128)(2,1)S(1)}, bf16[224,256]{1,0:T(8,128)(2,1)S(1)}, u32[]{:S(2)}, u32[]{:S(2)}) collective-permute-start(bf16[224,256]{1,0:T(8,128)(2,1)S(1)} %get-tuple-element.138), channel_id=1, source_target_pairs={{0,24},{4,28},{8,16},{12,20},{16,8},{20,12},{24,0},{28,4},{1,25},{... | collective-permute-start | bytes 344072 | tf_op jit(solution)/shard_map/ppermute | solution.py:373
  214.4 6.8 %collective-permute-start.51 = (bf16[64,256]{1,0:T(8,128)(2,1)S(1)}, bf16[64,256]{1,0:T(8,128)(2,1)S(1)}, u32[]{:S(2)}, u32[]{:S(2)}) collective-permute-start(bf16[64,256]{1,0:T(8,128)(2,1)S(1)} %get-tuple-element.145), channel_id=1, source_target_pairs={{0,8},{4,12},{8,0},{12,4},{16,24},{20,28},{24,16},{28,20},{1,9},{5... | collective-permute-start | bytes 98312 | tf_op jit(solution)/shard_map/ppermute | solution.py:373
  216.5 29.3 %collective-permute-start.25 = (bf16[1024,256]{1,0:T(8,128)(2,1)S(1)}, bf16[1024,256]{1,0:T(8,128)(2,1)S(1)}, u32[]{:S(2)}, u32[]{:S(2)}) collective-permute-start(bf16[1024,256]{1,0:T(8,128)(2,1)S(1)} %get-tuple-element.98), channel_id=1, source_target_pairs={{0,4},{4,0},{8,12},{12,8},{16,20},{20,16},{24,28},{28,24},{1,5},{5... | collective-permute-start | bytes 1572872 | tf_op jit(solution)/shard_map/ppermute | solution.py:360
  219.8 4.8 %collective-permute-start.52 = (bf16[64,256]{1,0:T(8,128)(2,1)S(1)}, bf16[64,256]{1,0:T(8,128)(2,1)S(1)}, u32[]{:S(2)}, u32[]{:S(2)}) collective-permute-start(bf16[64,256]{1,0:T(8,128)(2,1)S(1)} %get-tuple-element.146), channel_id=1, source_target_pairs={{0,16},{4,20},{8,24},{12,28},{16,0},{20,4},{24,8},{28,12},{1,17},{... | collective-permute-start | bytes 98312 | tf_op jit(solution)/shard_map/ppermute | solution.py:373
  219.8 6.0 %collective-permute-start.53 = (bf16[64,256]{1,0:T(8,128)(2,1)S(1)}, bf16[64,256]{1,0:T(8,128)(2,1)S(1)}, u32[]{:S(2)}, u32[]{:S(2)}) collective-permute-start(bf16[64,256]{1,0:T(8,128)(2,1)S(1)} %get-tuple-element.147), channel_id=1, source_target_pairs={{0,24},{4,28},{8,16},{12,20},{16,8},{20,12},{24,0},{28,4},{1,25},{... | collective-permute-start | bytes 98312 | tf_op jit(solution)/shard_map/ppermute | solution.py:373
  221.2 14.8 %collective-permute-start.45 = (bf16[192,256]{1,0:T(8,128)(2,1)S(1)}, bf16[192,256]{1,0:T(8,128)(2,1)S(1)}, u32[]{:S(2)}, u32[]{:S(2)}) collective-permute-start(bf16[192,256]{1,0:T(8,128)(2,1)S(1)} %get-tuple-element.139.rest_0_), channel_id=1, source_target_pairs={{0,8},{4,12},{8,0},{12,4},{16,24},{20,28},{24,16},{28,20},{1,9},{5... | collective-permute-start | bytes 294920 | tf_op jit(solution)/shard_map/ppermute | solution.py:373
  225.9 4.3 %collective-permute-start.54 = (bf16[64,256]{1,0:T(8,128)(2,1)S(1)}, bf16[64,256]{1,0:T(8,128)(2,1)S(1)}, u32[]{:S(2)}, u32[]{:S(2)}) collective-permute-start(bf16[64,256]{1,0:T(8,128)(2,1)S(1)} %shard_map.127.rest_4_), channel_id=1, source_target_pairs={{0,8},{4,12},{8,0},{12,4},{16,24},{20,28},{24,16},{28,20},{1,9},{5... | collective-permute-start | bytes 98312 | tf_op jit(solution)/shard_map/ppermute | solution.py:373
  226.9 4.8 %collective-permute-start.55 = (bf16[64,256]{1,0:T(8,128)(2,1)S(1)}, bf16[64,256]{1,0:T(8,128)(2,1)S(1)}, u32[]{:S(2)}, u32[]{:S(2)}) collective-permute-start(bf16[64,256]{1,0:T(8,128)(2,1)S(1)} %shard_map.127.rest_4_), channel_id=1, source_target_pairs={{0,16},{4,20},{8,24},{12,28},{16,0},{20,4},{24,8},{28,12},{1,17},{... | collective-permute-start | bytes 98312 | tf_op jit(solution)/shard_map/ppermute | solution.py:373
  230.2 5.7 %collective-permute-start.56 = (bf16[64,256]{1,0:T(8,128)(2,1)S(1)}, bf16[64,256]{1,0:T(8,128)(2,1)S(1)}, u32[]{:S(2)}, u32[]{:S(2)}) collective-permute-start(bf16[64,256]{1,0:T(8,128)(2,1)S(1)} %shard_map.127.rest_4_), channel_id=1, source_target_pairs={{0,24},{4,28},{8,16},{12,20},{16,8},{20,12},{24,0},{28,4},{1,25},{... | collective-permute-start | bytes 98312 | tf_op jit(solution)/shard_map/ppermute | solution.py:373
  231.7 17.8 %collective-permute-start.35 = (bf16[1024,256]{1,0:T(8,128)(2,1)S(1)}, bf16[1024,256]{1,0:T(8,128)(2,1)S(1)}, u32[]{:S(2)}, u32[]{:S(2)}) collective-permute-start(bf16[1024,256]{1,0:T(8,128)(2,1)S(1)} %get-tuple-element.118), channel_id=1, source_target_pairs={{0,4},{4,0},{8,12},{12,8},{16,20},{20,16},{24,28},{28,24},{1,5},{5... | collective-permute-start | bytes 1572872 | tf_op jit(solution)/shard_map/ppermute | solution.py:360
  235.9 7.4 %collective-permute-start.46 = (bf16[192,256]{1,0:T(8,128)(2,1)S(1)}, bf16[192,256]{1,0:T(8,128)(2,1)S(1)}, u32[]{:S(2)}, u32[]{:S(2)}) collective-permute-start(bf16[192,256]{1,0:T(8,128)(2,1)S(1)} %get-tuple-element.139.rest_0_), channel_id=1, source_target_pairs={{0,16},{4,20},{8,24},{12,28},{16,0},{20,4},{24,8},{28,12},{1,17},{... | collective-permute-start | bytes 294920 | tf_op jit(solution)/shard_map/ppermute | solution.py:373
  235.9 7.4 %collective-permute-start.47 = (bf16[192,256]{1,0:T(8,128)(2,1)S(1)}, bf16[192,256]{1,0:T(8,128)(2,1)S(1)}, u32[]{:S(2)}, u32[]{:S(2)}) collective-permute-start(bf16[192,256]{1,0:T(8,128)(2,1)S(1)} %get-tuple-element.139.rest_0_), channel_id=1, source_target_pairs={{0,24},{4,28},{8,16},{12,20},{16,8},{20,12},{24,0},{28,4},{1,25},{... | collective-permute-start | bytes 294920 | tf_op jit(solution)/shard_map/ppermute | solution.py:373
  243.9 9.0 %collective-permute-start.57 = (bf16[4,256,256]{2,1,0:T(8,128)(2,1)S(1)}, bf16[4,256,256]{2,1,0:T(8,128)(2,1)S(1)}, u32[]{:S(2)}, u32[]{:S(2)}) collective-permute-start(bf16[4,256,256]{2,1,0:T(8,128)(2,1)S(1)} %shard_map.128.rest_0_), channel_id=1, source_target_pairs={{0,4},{4,0},{8,12},{12,8},{16,20},{20,16},{24,28},{28,24},{1,5},{5... | collective-permute-start | bytes 1572872 | tf_op jit(solution)/shard_map/ppermute | solution.py:360
  243.9 8.9 %collective-permute-start.58 = (bf16[32,256]{1,0:T(8,128)(2,1)S(1)}, bf16[32,256]{1,0:T(8,128)(2,1)S(1)}, u32[]{:S(2)}, u32[]{:S(2)}) collective-permute-start(bf16[32,256]{1,0:T(8,128)(2,1)S(1)} %get-tuple-element.148.rest_2_), channel_id=1, source_target_pairs={{0,1},{1,0},{2,3},{3,2},{4,5},{5,4},{6,7},{7,6},{8,9},{9,8},{10,11... | collective-permute-start | bytes 49160 | tf_op jit(solution)/shard_map/ppermute | solution.py:366
  244.8 8.0 %collective-permute-start.59 = (bf16[32,256]{1,0:T(8,128)(2,1)S(1)}, bf16[32,256]{1,0:T(8,128)(2,1)S(1)}, u32[]{:S(2)}, u32[]{:S(2)}) collective-permute-start(bf16[32,256]{1,0:T(8,128)(2,1)S(1)} %get-tuple-element.148.rest_2_), channel_id=1, source_target_pairs={{0,2},{1,3},{2,0},{3,1},{4,6},{5,7},{6,4},{7,5},{8,10},{9,11},{10,... | collective-permute-start | bytes 49160 | tf_op jit(solution)/shard_map/ppermute | solution.py:366
  245.8 7.1 %collective-permute-start.60 = (bf16[32,256]{1,0:T(8,128)(2,1)S(1)}, bf16[32,256]{1,0:T(8,128)(2,1)S(1)}, u32[]{:S(2)}, u32[]{:S(2)}) collective-permute-start(bf16[32,256]{1,0:T(8,128)(2,1)S(1)} %get-tuple-element.148.rest_2_), channel_id=1, source_target_pairs={{0,3},{1,2},{2,1},{3,0},{4,7},{5,6},{6,5},{7,4},{8,11},{9,10},{10,... | collective-permute-start | bytes 49160 | tf_op jit(solution)/shard_map/ppermute | solution.py:366
  (4 other events, 12.0 us)

commit v7 on v6

--- a/solution.py
+++ b/solution.py
@@ -11,6 +11,7 @@
 
 MAX_DILATION = 4095
 LANES = 128
+NOTE = 16
 BF = jnp.bfloat16
 F32 = jnp.float32
 VM = pl.BlockSpec(memory_space=pltpu.VMEM)
@@ -311,16 +312,18 @@
 
 
 def taps_body(chips, groups, meta, *rest):
-    delays, blocks = rest[:chips], rest[chips : 2 * chips]
-    amounts, outs = rest[2 * chips], rest[2 * chips + 1 :]
+    blocks, amounts, outs = rest[:chips], rest[chips], rest[chips + 1 :]
+    rows = blocks[0].shape[0] - NOTE
     width = LANES // 2
     for out in outs:
         out[...] = jnp.zeros_like(out)
     for k in range(chips):
         at = meta[1] ^ k
+        notes = blocks[k][rows:, :].astype(F32)
         for n in range(groups):
             group = at * groups + n
-            amounts[group] = delays[k][n]
+            both = notes[2 * n : 2 * n + 1, :] * 64.0 + notes[2 * n + 1 : 2 * n + 2, :]
+            amounts[group] = jnp.max(both).astype(jnp.int32)
             for spot in range(2 * len(outs)):
 
                 @pl.when(group == spot)
@@ -328,7 +331,8 @@
                     out, g = outs[spot // 2], spot % 2
                     for tap in range(2):
                         top = tap * LANES + g * width
-                        block = blocks[k][tap, n * width : (n + 1) * width, :].astype(F32)
+                        low = tap * rows // 2 + n * width
+                        block = blocks[k][low : low + width, :].astype(F32)
                         lane = lax.broadcasted_iota(jnp.int32, block.shape, 1)
                         here = (lane < width) == (g == 0)
                         other = pltpu.roll(block, width, 1)
@@ -401,13 +405,14 @@
     in_parts = [from_fsdp([x] * fsdp_size) for x in in_shares]
     upstream_far = to_partner(upstream)
     out_parts = from_fsdp([out_share] * fsdp_size)
-    delays = from_chips([dilation] * chips)
-    conv_parts = from_chips([w_conv] * chips)
+    noted = jnp.concatenate([dilation // 64, dilation % 64]).reshape(2, -1).T.reshape(-1, 1)
+    noted = jnp.pad(jnp.broadcast_to(noted, (2 * local_groups, LANES)), ((0, NOTE - 2 * local_groups), (0, 0)))
+    noted = jnp.concatenate([w_conv.reshape(-1, LANES), noted.astype(BF)])
+    conv_parts = from_chips([noted] * chips)
     taps = call(
         functools.partial(taps_body, chips, local_groups),
         [shape((2 * chunks,), jnp.int32)] + [shape((2 * LANES, 2 * LANES), BF)] * chunks,
-        [where] + delays + conv_parts,
-        scalars=1 + chips,
+        [where] + conv_parts,
         small=1,
     )
     amounts, kernels = taps[0], taps[1:]
@@ -417,7 +422,7 @@
     first, lead = call(
         functools.partial(first_body, fsdp_size, tile),
         [series, shape((channels, LANES), BF)],
-        [where, record, record_far] + in_parts[0],
+        [where, pltpu.with_memory_space_constraint(record, pltpu.HBM), record_far] + in_parts[0],
         scratch=[pltpu.VMEM((samples, channels), BF), pltpu.SemaphoreType.DMA],
         flops=2 * block * channels * LANES,
         stay=(1,),

time: 256 us -> 248 us (0.969)
  waiting for transfers between devices: 118 us -> 109 us
    ppermute x8, waiting for transfers between devices: 61 us -> 54.3 us  [down(): lax.ppermute(x, 'seq', [(i + 2, i) for i in range(seq_size - 2 * hop)])]
    ppermute x21, starting transfers between devices: 23.1 us -> 29.7 us  [from_fsdp(): got.append(lax.ppermute(blocks[k], 'fsdp', pairs))]
    ppermute x18 -> x15, starting transfers between devices: 24.7 us -> 19.8 us  [from_chips(): got.append(lax.ppermute(blocks[k], 'seq', pairs))]
    ppermute x8, waiting for transfers between devices: 25.4 us -> 29.7 us  [up(): lax.ppermute(x, 'seq', [(i, i + 2) for i in range(2 * (hop - 1), seq_size...]
    ppermute x18 -> x15, waiting for transfers between devices: 26 us -> 21.9 us  [from_chips(): got.append(lax.ppermute(blocks[k], 'seq', pairs))]
    ppermute x8, starting transfers between devices: 15.8 us -> 13 us  [up(): lax.ppermute(x, 'seq', [(i, i + 2) for i in range(2 * (hop - 1), seq_size...]
  transfers between devices with their start and end apart: 61 -> 58, of which waited for: 27 -> 22; matrix products, arithmetic and copies ran while one was open for 0% -> 1% of each run, Pallas kernels for 22% -> 23%
where the time goes in v7:
time: 248 us; the launch traced here: 247 us
  waiting for transfers between devices  109 us (44%)
  starting transfers between devices  73.8 us (30%)
  Pallas kernels  58.8 us (24%)
    pallas_call x28, Pallas kernels, call(): pl.pallas_call(body, out_shape=tuple(outs), in_specs=[SM if n < scalars e...  58.8 us
    ppermute x8, waiting for transfers between devices, down(): lax.ppermute(x, 'seq', [(i + 2, i) for i in range(seq_size - 2 * hop)])  54.3 us
    ppermute x21, starting transfers between devices, from_fsdp(): got.append(lax.ppermute(blocks[k], 'fsdp', pairs))  29.7 us
    ppermute x8, waiting for transfers between devices, up(): lax.ppermute(x, 'seq', [(i, i + 2) for i in range(2 * (hop - 1), seq_size...  29.7 us
    ppermute x15, waiting for transfers between devices, from_chips(): got.append(lax.ppermute(blocks[k], 'seq', pairs))  21.9 us
    ppermute x15, starting transfers between devices, from_chips(): got.append(lax.ppermute(blocks[k], 'seq', pairs))  19.8 us
    ppermute x8, starting transfers between devices, up(): lax.ppermute(x, 'seq', [(i, i + 2) for i in range(2 * (hop - 1), seq_size...  13 us
    ppermute x8, starting transfers between devices, down(): lax.ppermute(x, 'seq', [(i + 2, i) for i in range(seq_size - 2 * hop)])  10.5 us
  transfers between devices with their start and end apart: 58, of which 22 were waited for; matrix products, arithmetic and copies ran while one was open for 1% of the time, Pallas kernels for 23%

profile of v7, /device:TPU:0, one launch (start us, length us, event | category | flops | bytes accessed | tf_op | source)
XLA Modules:
  0.0 247.4 jit_solution(11410681288938364747)
XLA Ops:
  2.1 2.9 %collective-permute-start.4 = (bf16[256,128]{1,0:T(8,128)(2,1)S(1)}, bf16[256,128]{1,0:T(8,128)(2,1)S(1)}, u32[]{:S(2)}, u32[]{:S(2)}) collective-permute-start(bf16[256,128]{1,0:T(8,128)(2,1)S(1)} %constant_dynamic-slice_fusion.rest_0_), channel_id=1, source_target_pairs={{0,1},{1,0},{2,3},{3,2},{4,5},{5,4},{6,7},{7,6},{8,9},{9,8},{10,11... | collective-permute-start | bytes 196616 | tf_op jit(solution)/shard_map/ppermute | solution.py:370
  5.0 1.5 collective-permute-start.5
  9.2 2.1 collective-permute-start
  13.1 1.6 collective-permute-start.15
  14.6 1.5 collective-permute-start.16
  16.7 1.6 collective-permute-start.10
  18.2 3.0 %shard_map.103 = (bf16[2,1024,128]{2,1,0:T(8,128)(2,1)S(1)}, bf16[1024,128]{1,0:T(8,128)(2,1)S(1)}) custom-call(s32[4]{0:T(128)S(1)} %pad_add_fusion.meta, bf16[1024,1024]{1,0:T(8,128)(2,1)} %bitcast.16, bf16[1024,1024]{1,0:T(8,128)(2,1)S(1)} %collective-permute-done.3.partner.rest_5_, bf16[256,128]{1,0:T(8,128)(2,1)S(1)} %constant_dynamic-slice_fusion.rest_0_, ...), custom_call_target="tpu_custom_call" | custom-call | flops 536870912 | bytes 5242896 | tf_op jit(solution)/shard_map/pallas_call | solution.py:28
  21.3 1.6 collective-permute-start.11
  22.8 1.4 collective-permute-done.16.rest_2_
  24.2 2.6 %collective-permute-start.1 = (bf16[272,128]{1,0:T(8,128)(2,1)S(1)}, bf16[272,128]{1,0:T(8,128)(2,1)S(1)}, u32[]{:S(2)}, u32[]{:S(2)}) collective-permute-start(bf16[272,128]{1,0:T(8,128)(2,1)S(1)} %pad_maximum_fusion.rest_0_), channel_id=1, source_target_pairs={{0,16},{4,20},{8,24},{12,28},{16,0},{20,4},{24,8},{28,12},{1,17},{... | collective-permute-start | bytes 208904 | tf_op jit(solution)/shard_map/ppermute | solution.py:377
  26.8 1.6 collective-permute-start.2
  28.4 4.1 %shard_map.109 = (bf16[2,1024,128]{2,1,0:T(8,128)(2,1)S(1)}, bf16[2,1024,128]{2,1,0:T(8,128)(2,1)S(1)}, bf16[2,1024,128]{2,1,0:T(8,128)(2,1)S(1)}, bf16[1024,512]{1,0:T(8,128)(2,1)S(1)}) custom-call(s32[4]{0:T(128)S(1)} %pad_add_fusion.meta, bf16[1024,1024]{1,0:T(8,128)(2,1)S(1)} %bitcast.17, bf16[1024,1024]{1,0:T(8,128)(2,1)S(1)} %collective-permute-done.3.partner.rest_5_, ...), custom_call_target="tpu_custom_call" | custom-call | flops 1610612736 | bytes 7864336 | tf_op jit(solution)/shard_map/pallas_call | solution.py:28
  32.6 2.6 %collective-permute-start.28 = (bf16[2,1024,128]{2,1,0:T(8,128)(2,1)S(1)}, bf16[2,1024,128]{2,1,0:T(8,128)(2,1)S(1)}, u32[]{:S(2)}, u32[]{:S(2)}) collective-permute-start(bf16[2,1024,128]{2,1,0:T(8,128)(2,1)S(1)} %get-tuple-element.108.rest_0_.own), channel_id=1, source_target_pairs={{0,8},{4,12},{8,16},{12,20},{16,24},{20,28},{1,9},{5,13},{9,17},{1... | collective-permute-start | bytes 1572872 | tf_op jit(solution)/shard_map/ppermute | solution.py:381
  35.2 1.7 collective-permute-start.12
  36.9 1.9 collective-permute-start.18
  38.9 3.7 %collective-permute-start.7 = (bf16[2,1024,128]{2,1,0:T(8,128)(2,1)S(1)}, bf16[2,1024,128]{2,1,0:T(8,128)(2,1)S(1)}, u32[]{:S(2)}, u32[]{:S(2)}) collective-permute-start(bf16[2,1024,128]{2,1,0:T(8,128)(2,1)S(1)} %get-tuple-element.79.rest_0_.own), channel_id=1, source_target_pairs={{0,8},{4,12},{8,16},{12,20},{16,24},{20,28},{1,9},{5,13},{9,17},{1... | collective-permute-start | bytes 1572872 | tf_op jit(solution)/shard_map/ppermute | solution.py:381
  42.6 2.0 collective-permute-start.24
  44.6 2.9 %collective-permute-done.28.rest_1_ = bf16[2,1024,128]{2,1,0:T(8,128)(2,1)S(1)} collective-permute-done((bf16[2,1024,128]{2,1,0:T(8,128)(2,1)S(1)}, bf16[2,1024,128]{2,1,0:T(8,128)(2,1)S(1)}, u32[]{:S(2)}, u32[]{:S(2)}) %collective-permute-start.28) | collective-permute-done | bytes 524320 | tf_op jit(solution)/shard_map/ppermute | solution.py:381
  48.2 10.5 %collective-permute-done.18.rest_1_ = bf16[2,1024,128]{2,1,0:T(8,128)(2,1)S(1)} collective-permute-done((bf16[2,1024,128]{2,1,0:T(8,128)(2,1)S(1)}, bf16[2,1024,128]{2,1,0:T(8,128)(2,1)S(1)}, u32[]{:S(2)}, u32[]{:S(2)}) %collective-permute-start.18) | collective-permute-done | bytes 524320 | tf_op jit(solution)/shard_map/ppermute | solution.py:381
  59.4 10.5 %collective-permute-done.7.rest_1_ = bf16[2,1024,128]{2,1,0:T(8,128)(2,1)S(1)} collective-permute-done((bf16[2,1024,128]{2,1,0:T(8,128)(2,1)S(1)}, bf16[2,1024,128]{2,1,0:T(8,128)(2,1)S(1)}, u32[]{:S(2)}, u32[]{:S(2)}) %collective-permute-start.7) | collective-permute-done | bytes 524320 | tf_op jit(solution)/shard_map/ppermute | solution.py:381
  70.7 5.8 %collective-permute-done.24.rest_1_ = bf16[2,1024,128]{2,1,0:T(8,128)(2,1)S(1)} collective-permute-done((bf16[2,1024,128]{2,1,0:T(8,128)(2,1)S(1)}, bf16[2,1024,128]{2,1,0:T(8,128)(2,1)S(1)}, u32[]{:S(2)}, u32[]{:S(2)}) %collective-permute-start.24) | collective-permute-done | bytes 524320 | tf_op jit(solution)/shard_map/ppermute | solution.py:381
  77.1 2.8 %shard_map.102 = (s32[8]{0:T(128)S(1)}, bf16[256,256]{1,0:T(8,128)(2,1)S(1)}, bf16[256,256]{1,0:T(8,128)(2,1)S(1)}, bf16[256,256]{1,0:T(8,128)(2,1)S(1)}, bf16[256,256]{1,0:T(8,128)(2,1)S(1)}) custom-call(s32[4]{0:T(128)S(1)} %pad_add_fusion.meta, bf16[272,128]{1,0:T(8,128)(2,1)S(1)} %pad_maximum_fusion.rest_0_, ...), custom_call_target="tpu_custom_call" | custom-call | bytes 802864 | tf_op jit(solution)/shard_map/pallas_call | solution.py:28
  80.0 4.6 %shard_map.104 = (bf16[2,1024,128]{2,1,0:T(8,128)(2,1)S(1)}, bf16[2,1024,128]{2,1,0:T(8,128)(2,1)S(1)}, bf16[2,1024,128]{2,1,0:T(8,128)(2,1)S(1)}, bf16[2,1024,128]{2,1,0:T(8,128)(2,1)S(1)}) custom-call(s32[4]{0:T(128)S(1)} %pad_add_fusion.meta, bf16[1024,1024]{1,0:T(8,128)(2,1)S(1)} %bitcast.21, bf16[1024,1024]{1,0:T(8,128)(2,1)} %collective-permute-done.9.partner.rest_5_, ...), custom_call_target="tpu_custom_call" | custom-call | flops 2147483648 | bytes 7340048 | tf_op jit(solution)/shard_map/pallas_call | solution.py:28
  84.7 3.6 %shard_map.118 = (bf16[2,1024,128]{2,1,0:T(8,128)(2,1)S(1)}, bf16[2,1024,256]{2,1,0:T(8,128)(2,1)S(1)}, bf16[2,1024,128]{2,1,0:T(8,128)(2,1)S(1)}, bf16[2,1024,128]{2,1,0:T(8,128)(2,1)S(1)}) custom-call(s32[4]{0:T(128)S(1)} %pad_add_fusion.meta, s32[8]{0:T(128)S(1)} %get-tuple-element.78.amounts, bf16[2,1024,128]{2,1,0:T(8,128)(2,1)S(1)} %get-tuple-element.108.rest_0_.own, ...), custom_call_target="tpu_custom_call" | custom-call | flops 536870912 | bytes 4849712 | tf_op jit(solution)/shard_map/pallas_call | solution.py:28
  88.2 1.3 collective-permute-start.30
  89.5 3.6 %shard_map.110 = (bf16[2,1024,128]{2,1,0:T(8,128)(2,1)S(1)}, bf16[2,1024,256]{2,1,0:T(8,128)(2,1)S(1)}, bf16[2,1024,128]{2,1,0:T(8,128)(2,1)S(1)}, bf16[2,1024,128]{2,1,0:T(8,128)(2,1)S(1)}) custom-call(s32[4]{0:T(128)S(1)} %pad_add_fusion.meta, s32[8]{0:T(128)S(1)} %get-tuple-element.78.amounts, bf16[2,1024,128]{2,1,0:T(8,128)(2,1)S(1)} %get-tuple-element.88.rest_0_.own, ...), custom_call_target="tpu_custom_call" | custom-call | flops 536870912 | bytes 4849712 | tf_op jit(solution)/shard_map/pallas_call | solution.py:28
  93.1 1.3 collective-permute-start.20
  94.4 3.6 %shard_map.105 = (bf16[2,1024,128]{2,1,0:T(8,128)(2,1)S(1)}, bf16[2,1024,256]{2,1,0:T(8,128)(2,1)S(1)}, bf16[2,1024,128]{2,1,0:T(8,128)(2,1)S(1)}, bf16[2,1024,128]{2,1,0:T(8,128)(2,1)S(1)}) custom-call(s32[4]{0:T(128)S(1)} %pad_add_fusion.meta, s32[8]{0:T(128)S(1)} %get-tuple-element.78.amounts, bf16[2,1024,128]{2,1,0:T(8,128)(2,1)S(1)} %get-tuple-element.79.rest_0_.own, ...), custom_call_target="tpu_custom_call" | custom-call | flops 536870912 | bytes 4849712 | tf_op jit(solution)/shard_map/pallas_call | solution.py:28
  99.3 3.6 %shard_map.115 = (bf16[2,1024,128]{2,1,0:T(8,128)(2,1)S(1)}, bf16[2,1024,256]{2,1,0:T(8,128)(2,1)S(1)}, bf16[2,1024,128]{2,1,0:T(8,128)(2,1)S(1)}, bf16[2,1024,128]{2,1,0:T(8,128)(2,1)S(1)}) custom-call(s32[4]{0:T(128)S(1)} %pad_add_fusion.meta, s32[8]{0:T(128)S(1)} %get-tuple-element.78.amounts, bf16[2,1024,128]{2,1,0:T(8,128)(2,1)S(1)} %get-tuple-element.100.rest_0_.own, ...), custom_call_target="tpu_custom_call" | custom-call | flops 536870912 | bytes 4849712 | tf_op jit(solution)/shard_map/pallas_call | solution.py:28
  104.2 6.7 %collective-permute-done.30.rest_1_ = bf16[2,1024,128]{2,1,0:T(8,128)(2,1)S(1)} collective-permute-done((bf16[2,1024,128]{2,1,0:T(8,128)(2,1)S(1)}, bf16[2,1024,128]{2,1,0:T(8,128)(2,1)S(1)}, u32[]{:S(2)}, u32[]{:S(2)}) %collective-permute-start.30) | collective-permute-done | bytes 524320 | tf_op jit(solution)/shard_map/ppermute | solution.py:384
  112.2 9.9 %collective-permute-done.20.rest_1_ = bf16[2,1024,128]{2,1,0:T(8,128)(2,1)S(1)} collective-permute-done((bf16[2,1024,128]{2,1,0:T(8,128)(2,1)S(1)}, bf16[2,1024,128]{2,1,0:T(8,128)(2,1)S(1)}, u32[]{:S(2)}, u32[]{:S(2)}) %collective-permute-start.20) | collective-permute-done | bytes 524320 | tf_op jit(solution)/shard_map/ppermute | solution.py:384
  123.4 9.9 %collective-permute-done.13.rest_1_ = bf16[2,1024,128]{2,1,0:T(8,128)(2,1)S(1)} collective-permute-done((bf16[2,1024,128]{2,1,0:T(8,128)(2,1)S(1)}, bf16[2,1024,128]{2,1,0:T(8,128)(2,1)S(1)}, u32[]{:S(2)}, u32[]{:S(2)}) %collective-permute-start.13) | collective-permute-done | bytes 524320 | tf_op jit(solution)/shard_map/ppermute | solution.py:384
  134.6 1.4 shard_map.119
  136.0 1.4 shard_map.116
  137.4 1.4 shard_map.111
  138.8 5.8 %collective-permute-done.26.rest_1_ = bf16[2,1024,128]{2,1,0:T(8,128)(2,1)S(1)} collective-permute-done((bf16[2,1024,128]{2,1,0:T(8,128)(2,1)S(1)}, bf16[2,1024,128]{2,1,0:T(8,128)(2,1)S(1)}, u32[]{:S(2)}, u32[]{:S(2)}) %collective-permute-start.26) | collective-permute-done | bytes 524320 | tf_op jit(solution)/shard_map/ppermute | solution.py:384
  144.6 1.5 collective-permute-start.27
  146.0 1.4 shard_map.106
  147.4 4.8 %shard_map.123 = (f32[160,1024]{1,0:T(8,128)S(1)}, bf16[160,1024]{1,0:T(8,128)(2,1)S(1)}, bf16[160,1024]{1,0:T(8,128)(2,1)S(1)}, bf16[160,1024]{1,0:T(8,128)(2,1)S(1)}) custom-call(s32[4]{0:T(128)S(1)} %pad_add_fusion.meta, bf16[2,1024,128]{2,1,0:T(8,128)(2,1)S(1)} %get-tuple-element.123.rest_0_, bf16[2,1024,128]{2,1,0:T(8,128)(2,1)S(1)} %get-tuple-element.124.rest_1_, ...), custom_call_target="tpu_custom_call" | custom-call | flops 2147483648 | bytes 8454160 | tf_op jit(solution)/shard_map/pallas_call | solution.py:28
  152.3 1.4 collective-permute-start.36
  153.7 2.1 collective-permute-done.31.rest_2_
  155.8 3.1 %collective-permute-start.37 = (bf16[160,1024]{1,0:T(8,128)(2,1)S(1)}, bf16[160,1024]{1,0:T(8,128)(2,1)S(1)}, u32[]{:S(2)}, u32[]{:S(2)}) collective-permute-start(bf16[160,1024]{1,0:T(8,128)(2,1)S(1)} %get-tuple-element.133), channel_id=1, source_target_pairs={{0,2},{1,3},{2,0},{3,1},{4,6},{5,7},{6,4},{7,5},{8,10},{9,11},{10,... | collective-permute-start | bytes 983048 | tf_op jit(solution)/shard_map/ppermute | solution.py:370
  158.9 8.1 %collective-permute-done.21.rest_2_ = bf16[2,1024,128]{2,1,0:T(8,128)(2,1)S(1)} collective-permute-done((bf16[2,1024,128]{2,1,0:T(8,128)(2,1)S(1)}, bf16[2,1024,128]{2,1,0:T(8,128)(2,1)S(1)}, u32[]{:S(2)}, u32[]{:S(2)}) %collective-permute-start.21) | collective-permute-done | bytes 524320 | tf_op jit(solution)/shard_map/ppermute | solution.py:384
  167.0 1.3 collective-permute-start.38
  168.4 9.9 %collective-permute-done.14.rest_2_ = bf16[2,1024,128]{2,1,0:T(8,128)(2,1)S(1)} collective-permute-done((bf16[2,1024,128]{2,1,0:T(8,128)(2,1)S(1)}, bf16[2,1024,128]{2,1,0:T(8,128)(2,1)S(1)}, u32[]{:S(2)}, u32[]{:S(2)}) %collective-permute-start.14) | collective-permute-done | bytes 524320 | tf_op jit(solution)/shard_map/ppermute | solution.py:384
  180.2 2.5 %shard_map.113 = (f32[256,256]{1,0:T(8,128)S(1)}, bf16[256,256]{1,0:T(8,128)(2,1)S(1)}, bf16[256,256]{1,0:T(8,128)(2,1)S(1)}, bf16[256,256]{1,0:T(8,128)(2,1)S(1)}, bf16[1024,256]{1,0:T(8,128)(2,1)S(1)}) custom-call(s32[4]{0:T(128)S(1)} %pad_add_fusion.meta, bf16[1024,128]{1,0:T(8,128)(2,1)S(1)} %get-tuple-element.86.rest_0_, ...), custom_call_target="tpu_custom_call" | custom-call | flops 1073741824 | bytes 6422544 | tf_op jit(solution)/shard_map/pallas_call | solution.py:28
  182.8 1.8 collective-permute-done.27.rest_2_
  184.6 1.6 collective-permute-start.33
  189.2 1.5 collective-permute-start.35
  190.7 2.5 %shard_map.121 = (f32[256,256]{1,0:T(8,128)S(1)}, bf16[256,256]{1,0:T(8,128)(2,1)S(1)}, bf16[256,256]{1,0:T(8,128)(2,1)S(1)}, bf16[256,256]{1,0:T(8,128)(2,1)S(1)}, bf16[1024,256]{1,0:T(8,128)(2,1)S(1)}) custom-call(s32[4]{0:T(128)S(1)} %pad_add_fusion.meta, bf16[1024,128]{1,0:T(8,128)(2,1)S(1)} %get-tuple-element.107.rest_0_, ...), custom_call_target="tpu_custom_call" | custom-call | flops 1073741824 | bytes 6422544 | tf_op jit(solution)/shard_map/pallas_call | solution.py:28
  195.4 1.7 collective-permute-done.34.rest_2_
  197.0 1.3 collective-permute-start.47
  199.3 2.5 %collective-permute-start.39 = (bf16[224,256]{1,0:T(8,128)(2,1)S(1)}, bf16[224,256]{1,0:T(8,128)(2,1)S(1)}, u32[]{:S(2)}, u32[]{:S(2)}) collective-permute-start(bf16[224,256]{1,0:T(8,128)(2,1)S(1)} %get-tuple-element.136), channel_id=1, source_target_pairs={{0,8},{4,12},{8,0},{12,4},{16,24},{20,28},{24,16},{28,20},{1,9},{5... | collective-permute-start | bytes 344072 | tf_op jit(solution)/shard_map/ppermute | solution.py:377
  201.9 2.4 collective-permute-start.41
  206.6 5.6 %collective-permute-done.40.rest_2_ = bf16[224,256]{1,0:T(8,128)(2,1)S(1)} collective-permute-done((bf16[224,256]{1,0:T(8,128)(2,1)S(1)}, bf16[224,256]{1,0:T(8,128)(2,1)S(1)}, u32[]{:S(2)}, u32[]{:S(2)}) %collective-permute-start.40) | collective-permute-done | bytes 114720 | tf_op jit(solution)/shard_map/ppermute | solution.py:377
  212.2 1.4 collective-permute-start.50
  213.8 2.1 collective-permute-start.42
  220.0 2.3 collective-permute-done.51.rest_5_
  223.9 4.3 %collective-permute-done.53.rest_7_ = bf16[64,256]{1,0:T(8,128)(2,1)S(1)} collective-permute-done((bf16[64,256]{1,0:T(8,128)(2,1)S(1)}, bf16[64,256]{1,0:T(8,128)(2,1)S(1)}, u32[]{:S(2)}, u32[]{:S(2)}) %collective-permute-start.53) | collective-permute-done | bytes 32800 | tf_op jit(solution)/shard_map/ppermute | solution.py:377
  229.2 6.2 %collective-permute-done.43.rest_2_ = bf16[192,256]{1,0:T(8,128)(2,1)S(1)} collective-permute-done((bf16[192,256]{1,0:T(8,128)(2,1)S(1)}, bf16[192,256]{1,0:T(8,128)(2,1)S(1)}, u32[]{:S(2)}, u32[]{:S(2)}) %collective-permute-start.43) | collective-permute-done | bytes 98336 | tf_op jit(solution)/shard_map/ppermute | solution.py:377
  237.1 2.6 %collective-permute-start.57 = (bf16[32,256]{1,0:T(8,128)(2,1)S(1)}, bf16[32,256]{1,0:T(8,128)(2,1)S(1)}, u32[]{:S(2)}, u32[]{:S(2)}) collective-permute-start(bf16[32,256]{1,0:T(8,128)(2,1)S(1)} %get-tuple-element.148.rest_2_), channel_id=1, source_target_pairs={{0,3},{1,2},{2,1},{3,0},{4,7},{5,6},{6,5},{7,4},{8,11},{9,10},{10,... | collective-permute-start | bytes 49160 | tf_op jit(solution)/shard_map/ppermute | solution.py:370
  239.7 2.0 shard_map.114.base
  241.7 3.3 %shard_map.122 = bf16[1024,1024]{1,0:T(8,128)(2,1)} custom-call(f32[1024,1024]{1,0:T(8,128)S(1)} %shard_map.114.base, bf16[1024,128]{1,0:T(8,128)(2,1)S(1)} %get-tuple-element.107.rest_0_, bf16[1024,128]{1,0:T(8,128)(2,1)S(1)} %get-tuple-element.115.rest_2_.rest_1_, bf16[1024,256]{1,0:T(8,128)(2,1)S(1)} %collective-permute-done.32.rest_2_, ...), custom_call_target="tpu_custom_call" | custom-call | flops 1073741824 | bytes 9437184 | tf_op jit(solution)/shard_map/pallas_call | solution.py:28
  245.1 2.3 shard_map.129
  (98 shorter events, 33.6 us)
Async XLA Ops:
  0.6 16.0 %copy-start = (bf16[256,1024]{1,0:T(8,128)(2,1)S(1)}, bf16[256,1024]{1,0:T(8,128)(2,1)}, u32[]{:S(2)}) copy-start(bf16[256,1024]{1,0:T(8,128)(2,1)} %param.11) | copy-start | bytes 1572868
  0.6 16.0 %collective-permute-start.3 = (bf16[1024,1024]{1,0:T(8,128)(2,1)}, bf16[1024,1024]{1,0:T(8,128)(2,1)S(1)}, u32[]{:S(2)}, u32[]{:S(2)}) collective-permute-start(bf16[1024,1024]{1,0:T(8,128)(2,1)} %bitcast.15), channel_id=1, source_target_pairs={{0,4},{4,0},{8,12},{12,8},{16,20},{20,16},{24,28},{28,24},{1,5},{5... | collective-permute-start | bytes 6291464 | tf_op jit(solution)/shard_map/ppermute | solution.py:364
  1.2 78.8 %collective-permute-start.9 = (bf16[1024,1024]{1,0:T(8,128)(2,1)}, bf16[1024,1024]{1,0:T(8,128)(2,1)}, u32[]{:S(2)}, u32[]{:S(2)}) collective-permute-start(bf16[1024,1024]{1,0:T(8,128)(2,1)} %bitcast.20), channel_id=1, source_target_pairs={{0,4},{4,0},{8,12},{12,8},{16,20},{20,16},{24,28},{28,24},{1,5},{5... | collective-permute-start | bytes 6291464 | tf_op jit(solution)/shard_map/ppermute | solution.py:364
  2.1 7.1 %collective-permute-start.4 = (bf16[256,128]{1,0:T(8,128)(2,1)S(1)}, bf16[256,128]{1,0:T(8,128)(2,1)S(1)}, u32[]{:S(2)}, u32[]{:S(2)}) collective-permute-start(bf16[256,128]{1,0:T(8,128)(2,1)S(1)} %constant_dynamic-slice_fusion.rest_0_), channel_id=1, source_target_pairs={{0,1},{1,0},{2,3},{3,2},{4,5},{5,4},{6,7},{7,6},{8,9},{9,8},{10,11... | collective-permute-start | bytes 196616 | tf_op jit(solution)/shard_map/ppermute | solution.py:370
  5.0 8.0 %collective-permute-start.5 = (bf16[256,128]{1,0:T(8,128)(2,1)S(1)}, bf16[256,128]{1,0:T(8,128)(2,1)S(1)}, u32[]{:S(2)}, u32[]{:S(2)}) collective-permute-start(bf16[256,128]{1,0:T(8,128)(2,1)S(1)} %constant_dynamic-slice_fusion.rest_0_), channel_id=1, source_target_pairs={{0,2},{1,3},{2,0},{3,1},{4,6},{5,7},{6,4},{7,5},{8,10},{9,11},{10,... | collective-permute-start | bytes 196616 | tf_op jit(solution)/shard_map/ppermute | solution.py:370
  6.6 8.1 %collective-permute-start.6 = (bf16[256,128]{1,0:T(8,128)(2,1)S(1)}, bf16[256,128]{1,0:T(8,128)(2,1)S(1)}, u32[]{:S(2)}, u32[]{:S(2)}) collective-permute-start(bf16[256,128]{1,0:T(8,128)(2,1)S(1)} %constant_dynamic-slice_fusion.rest_0_), channel_id=1, source_target_pairs={{0,3},{1,2},{2,1},{3,0},{4,7},{5,6},{6,5},{7,4},{8,11},{9,10},{10,... | collective-permute-start | bytes 196616 | tf_op jit(solution)/shard_map/ppermute | solution.py:370
  9.2 6.9 %collective-permute-start = (bf16[272,128]{1,0:T(8,128)(2,1)S(1)}, bf16[272,128]{1,0:T(8,128)(2,1)S(1)}, u32[]{:S(2)}, u32[]{:S(2)}) collective-permute-start(bf16[272,128]{1,0:T(8,128)(2,1)S(1)} %pad_maximum_fusion.rest_0_), channel_id=1, source_target_pairs={{0,8},{4,12},{8,0},{12,4},{16,24},{20,28},{24,16},{28,20},{1,9},{5... | collective-permute-start | bytes 208904 | tf_op jit(solution)/shard_map/ppermute | solution.py:377
  11.4 1.0 copy-start.3
  13.1 8.2 %collective-permute-start.15 = (bf16[256,384]{1,0:T(8,128)(2,1)S(1)}, bf16[256,384]{1,0:T(8,128)(2,1)S(1)}, u32[]{:S(2)}, u32[]{:S(2)}) collective-permute-start(bf16[256,384]{1,0:T(8,128)(2,1)S(1)} %shard_map.108.rest_0_), channel_id=1, source_target_pairs={{0,1},{1,0},{2,3},{3,2},{4,5},{5,4},{6,7},{7,6},{8,9},{9,8},{10,11... | collective-permute-start | bytes 589832 | tf_op jit(solution)/shard_map/ppermute | solution.py:370
  14.6 9.6 %collective-permute-start.16 = (bf16[256,384]{1,0:T(8,128)(2,1)S(1)}, bf16[256,384]{1,0:T(8,128)(2,1)}, u32[]{:S(2)}, u32[]{:S(2)}) collective-permute-start(bf16[256,384]{1,0:T(8,128)(2,1)S(1)} %shard_map.108.rest_0_), channel_id=1, source_target_pairs={{0,2},{1,3},{2,0},{3,1},{4,6},{5,7},{6,4},{7,5},{8,10},{9,11},{10,... | collective-permute-start | bytes 589832 | tf_op jit(solution)/shard_map/ppermute | solution.py:370
  16.1 10.7 %collective-permute-start.17 = (bf16[256,384]{1,0:T(8,128)(2,1)S(1)}, bf16[256,384]{1,0:T(8,128)(2,1)}, u32[]{:S(2)}, u32[]{:S(2)}) collective-permute-start(bf16[256,384]{1,0:T(8,128)(2,1)S(1)} %shard_map.108.rest_0_), channel_id=1, source_target_pairs={{0,3},{1,2},{2,1},{3,0},{4,7},{5,6},{6,5},{7,4},{8,11},{9,10},{10,... | collective-permute-start | bytes 589832 | tf_op jit(solution)/shard_map/ppermute | solution.py:370
  16.6 11.8 %copy-start.1 = (bf16[1,1024,1024]{2,1,0:T(8,128)(2,1)S(1)}, bf16[1,1024,1024]{2,1,0:T(8,128)(2,1)}, u32[]{:S(2)}) copy-start(bf16[1,1024,1024]{2,1,0:T(8,128)(2,1)} %param.7) | copy-start | bytes 6291460
  16.7 20.3 %collective-permute-start.10 = (bf16[128,1024]{1,0:T(8,128)(2,1)S(1)}, bf16[128,1024]{1,0:T(8,128)(2,1)S(1)}, u32[]{:S(2)}, u32[]{:S(2)}) collective-permute-start(bf16[128,1024]{1,0:T(8,128)(2,1)S(1)} %dynamic-slice_bitcast_fusion.rest_0_), channel_id=1, source_target_pairs={{0,1},{1,0},{2,3},{3,2},{4,5},{5,4},{6,7},{7,6},{8,9},{9,8},{10,11... | collective-permute-start | bytes 786440 | tf_op jit(solution)/shard_map/ppermute | solution.py:370
  21.3 17.6 %collective-permute-start.11 = (bf16[128,1024]{1,0:T(8,128)(2,1)S(1)}, bf16[128,1024]{1,0:T(8,128)(2,1)S(1)}, u32[]{:S(2)}, u32[]{:S(2)}) collective-permute-start(bf16[128,1024]{1,0:T(8,128)(2,1)S(1)} %dynamic-slice_bitcast_fusion.rest_0_), channel_id=1, source_target_pairs={{0,2},{1,3},{2,0},{3,1},{4,6},{5,7},{6,4},{7,5},{8,10},{9,11},{10,... | collective-permute-start | bytes 786440 | tf_op jit(solution)/shard_map/ppermute | solution.py:370
  24.2 8.4 %collective-permute-start.1 = (bf16[272,128]{1,0:T(8,128)(2,1)S(1)}, bf16[272,128]{1,0:T(8,128)(2,1)S(1)}, u32[]{:S(2)}, u32[]{:S(2)}) collective-permute-start(bf16[272,128]{1,0:T(8,128)(2,1)S(1)} %pad_maximum_fusion.rest_0_), channel_id=1, source_target_pairs={{0,16},{4,20},{8,24},{12,28},{16,0},{20,4},{24,8},{28,12},{1,17},{... | collective-permute-start | bytes 208904 | tf_op jit(solution)/shard_map/ppermute | solution.py:377
  26.8 8.4 %collective-permute-start.2 = (bf16[272,128]{1,0:T(8,128)(2,1)S(1)}, bf16[272,128]{1,0:T(8,128)(2,1)S(1)}, u32[]{:S(2)}, u32[]{:S(2)}) collective-permute-start(bf16[272,128]{1,0:T(8,128)(2,1)S(1)} %pad_maximum_fusion.rest_0_), channel_id=1, source_target_pairs={{0,24},{4,28},{8,16},{12,20},{16,8},{20,12},{24,0},{28,4},{1,25},{... | collective-permute-start | bytes 208904 | tf_op jit(solution)/shard_map/ppermute | solution.py:377
  28.4 51.5 %copy-start.2 = (bf16[1,1024,1024]{2,1,0:T(8,128)(2,1)S(1)}, bf16[1,1024,1024]{2,1,0:T(8,128)(2,1)}, u32[]{:S(2)}) copy-start(bf16[1,1024,1024]{2,1,0:T(8,128)(2,1)} %param.8) | copy-start | bytes 6291460
  32.6 14.9 %collective-permute-start.28 = (bf16[2,1024,128]{2,1,0:T(8,128)(2,1)S(1)}, bf16[2,1024,128]{2,1,0:T(8,128)(2,1)S(1)}, u32[]{:S(2)}, u32[]{:S(2)}) collective-permute-start(bf16[2,1024,128]{2,1,0:T(8,128)(2,1)S(1)} %get-tuple-element.108.rest_0_.own), channel_id=1, source_target_pairs={{0,8},{4,12},{8,16},{12,20},{16,24},{20,28},{1,9},{5,13},{9,17},{1... | collective-permute-start | bytes 1572872 | tf_op jit(solution)/shard_map/ppermute | solution.py:381
  35.2 7.3 %collective-permute-start.12 = (bf16[128,1024]{1,0:T(8,128)(2,1)S(1)}, bf16[128,1024]{1,0:T(8,128)(2,1)S(1)}, u32[]{:S(2)}, u32[]{:S(2)}) collective-permute-start(bf16[128,1024]{1,0:T(8,128)(2,1)S(1)} %dynamic-slice_bitcast_fusion.rest_0_), channel_id=1, source_target_pairs={{0,3},{1,2},{2,1},{3,0},{4,7},{5,6},{6,5},{7,4},{8,11},{9,10},{10,... | collective-permute-start | bytes 786440 | tf_op jit(solution)/shard_map/ppermute | solution.py:370
  36.9 21.8 %collective-permute-start.18 = (bf16[2,1024,128]{2,1,0:T(8,128)(2,1)S(1)}, bf16[2,1024,128]{2,1,0:T(8,128)(2,1)S(1)}, u32[]{:S(2)}, u32[]{:S(2)}) collective-permute-start(bf16[2,1024,128]{2,1,0:T(8,128)(2,1)S(1)} %get-tuple-element.88.rest_0_.own), channel_id=1, source_target_pairs={{0,8},{4,12},{8,16},{12,20},{16,24},{20,28},{1,9},{5,13},{9,17},{1... | collective-permute-start | bytes 1572872 | tf_op jit(solution)/shard_map/ppermute | solution.py:381
  38.9 31.1 %collective-permute-start.7 = (bf16[2,1024,128]{2,1,0:T(8,128)(2,1)S(1)}, bf16[2,1024,128]{2,1,0:T(8,128)(2,1)S(1)}, u32[]{:S(2)}, u32[]{:S(2)}) collective-permute-start(bf16[2,1024,128]{2,1,0:T(8,128)(2,1)S(1)} %get-tuple-element.79.rest_0_.own), channel_id=1, source_target_pairs={{0,8},{4,12},{8,16},{12,20},{16,24},{20,28},{1,9},{5,13},{9,17},{1... | collective-permute-start | bytes 1572872 | tf_op jit(solution)/shard_map/ppermute | solution.py:381
  42.6 33.9 %collective-permute-start.24 = (bf16[2,1024,128]{2,1,0:T(8,128)(2,1)S(1)}, bf16[2,1024,128]{2,1,0:T(8,128)(2,1)S(1)}, u32[]{:S(2)}, u32[]{:S(2)}) collective-permute-start(bf16[2,1024,128]{2,1,0:T(8,128)(2,1)S(1)} %get-tuple-element.100.rest_0_.own), channel_id=1, source_target_pairs={{0,8},{4,12},{8,16},{12,20},{16,24},{20,28},{1,9},{5,13},{9,17},{1... | collective-permute-start | bytes 1572872 | tf_op jit(solution)/shard_map/ppermute | solution.py:381
  47.5 37.2 %collective-permute-start.29 = (bf16[2,1024,128]{2,1,0:T(8,128)(2,1)S(1)}, bf16[2,1024,128]{2,1,0:T(8,128)(2,1)S(1)}, u32[]{:S(2)}, u32[]{:S(2)}) collective-permute-start(bf16[2,1024,128]{2,1,0:T(8,128)(2,1)S(1)} %collective-permute-done.28.rest_1_), channel_id=1, source_target_pairs={{8,16},{12,20},{16,24},{20,28},{9,17},{13,21},{17,25},{21,29},{10,... | collective-permute-start | bytes 1572872 | tf_op jit(solution)/shard_map/ppermute | solution.py:381
  58.7 30.8 %collective-permute-start.19 = (bf16[2,1024,128]{2,1,0:T(8,128)(2,1)S(1)}, bf16[2,1024,128]{2,1,0:T(8,128)(2,1)S(1)}, u32[]{:S(2)}, u32[]{:S(2)}) collective-permute-start(bf16[2,1024,128]{2,1,0:T(8,128)(2,1)S(1)} %collective-permute-done.18.rest_1_), channel_id=1, source_target_pairs={{8,16},{12,20},{16,24},{20,28},{9,17},{13,21},{17,25},{21,29},{10,... | collective-permute-start | bytes 1572872 | tf_op jit(solution)/shard_map/ppermute | solution.py:381
  70.0 24.5 %collective-permute-start.8 = (bf16[2,1024,128]{2,1,0:T(8,128)(2,1)S(1)}, bf16[2,1024,128]{2,1,0:T(8,128)(2,1)S(1)}, u32[]{:S(2)}, u32[]{:S(2)}) collective-permute-start(bf16[2,1024,128]{2,1,0:T(8,128)(2,1)S(1)} %collective-permute-done.7.rest_1_), channel_id=1, source_target_pairs={{8,16},{12,20},{16,24},{20,28},{9,17},{13,21},{17,25},{21,29},{10,... | collective-permute-start | bytes 1572872 | tf_op jit(solution)/shard_map/ppermute | solution.py:381
  76.4 22.9 %collective-permute-start.25 = (bf16[2,1024,128]{2,1,0:T(8,128)(2,1)S(1)}, bf16[2,1024,128]{2,1,0:T(8,128)(2,1)S(1)}, u32[]{:S(2)}, u32[]{:S(2)}) collective-permute-start(bf16[2,1024,128]{2,1,0:T(8,128)(2,1)S(1)} %collective-permute-done.24.rest_1_), channel_id=1, source_target_pairs={{8,16},{12,20},{16,24},{20,28},{9,17},{13,21},{17,25},{21,29},{10,... | collective-permute-start | bytes 1572872 | tf_op jit(solution)/shard_map/ppermute | solution.py:381
  88.2 22.6 %collective-permute-start.30 = (bf16[2,1024,128]{2,1,0:T(8,128)(2,1)S(1)}, bf16[2,1024,128]{2,1,0:T(8,128)(2,1)S(1)}, u32[]{:S(2)}, u32[]{:S(2)}) collective-permute-start(bf16[2,1024,128]{2,1,0:T(8,128)(2,1)S(1)} %get-tuple-element.114.rest_0_), channel_id=1, source_target_pairs={{8,0},{12,4},{16,8},{20,12},{24,16},{28,20},{9,1},{13,5},{17,9},{2... | collective-permute-start | bytes 1572872 | tf_op jit(solution)/shard_map/ppermute | solution.py:384
  93.1 29.0 %collective-permute-start.20 = (bf16[2,1024,128]{2,1,0:T(8,128)(2,1)S(1)}, bf16[2,1024,128]{2,1,0:T(8,128)(2,1)S(1)}, u32[]{:S(2)}, u32[]{:S(2)}) collective-permute-start(bf16[2,1024,128]{2,1,0:T(8,128)(2,1)S(1)} %get-tuple-element.94.rest_0_), channel_id=1, source_target_pairs={{8,0},{12,4},{16,8},{20,12},{24,16},{28,20},{9,1},{13,5},{17,9},{2... | collective-permute-start | bytes 1572872 | tf_op jit(solution)/shard_map/ppermute | solution.py:384
  98.0 35.3 %collective-permute-start.13 = (bf16[2,1024,128]{2,1,0:T(8,128)(2,1)S(1)}, bf16[2,1024,128]{2,1,0:T(8,128)(2,1)S(1)}, u32[]{:S(2)}, u32[]{:S(2)}) collective-permute-start(bf16[2,1024,128]{2,1,0:T(8,128)(2,1)S(1)} %get-tuple-element.85.rest_0_), channel_id=1, source_target_pairs={{8,0},{12,4},{16,8},{20,12},{24,16},{28,20},{9,1},{13,5},{17,9},{2... | collective-permute-start | bytes 1572872 | tf_op jit(solution)/shard_map/ppermute | solution.py:384
  102.9 41.7 %collective-permute-start.26 = (bf16[2,1024,128]{2,1,0:T(8,128)(2,1)S(1)}, bf16[2,1024,128]{2,1,0:T(8,128)(2,1)S(1)}, u32[]{:S(2)}, u32[]{:S(2)}) collective-permute-start(bf16[2,1024,128]{2,1,0:T(8,128)(2,1)S(1)} %get-tuple-element.106.rest_0_), channel_id=1, source_target_pairs={{8,0},{12,4},{16,8},{20,12},{24,16},{28,20},{9,1},{13,5},{17,9},{2... | collective-permute-start | bytes 1572872 | tf_op jit(solution)/shard_map/ppermute | solution.py:384
  110.9 44.9 %collective-permute-start.31 = (bf16[2,1024,128]{2,1,0:T(8,128)(2,1)S(1)}, bf16[2,1024,128]{2,1,0:T(8,128)(2,1)S(1)}, u32[]{:S(2)}, u32[]{:S(2)}) collective-permute-start(bf16[2,1024,128]{2,1,0:T(8,128)(2,1)S(1)} %collective-permute-done.30.rest_1_), channel_id=1, source_target_pairs={{8,0},{12,4},{16,8},{20,12},{9,1},{13,5},{17,9},{21,13},{10,2},{14... | collective-permute-start | bytes 1572872 | tf_op jit(solution)/shard_map/ppermute | solution.py:384
  122.1 44.9 %collective-permute-start.21 = (bf16[2,1024,128]{2,1,0:T(8,128)(2,1)S(1)}, bf16[2,1024,128]{2,1,0:T(8,128)(2,1)S(1)}, u32[]{:S(2)}, u32[]{:S(2)}) collective-permute-start(bf16[2,1024,128]{2,1,0:T(8,128)(2,1)S(1)} %collective-permute-done.20.rest_1_), channel_id=1, source_target_pairs={{8,0},{12,4},{16,8},{20,12},{9,1},{13,5},{17,9},{21,13},{10,2},{14... | collective-permute-start | bytes 1572872 | tf_op jit(solution)/shard_map/ppermute | solution.py:384
  133.3 44.9 %collective-permute-start.14 = (bf16[2,1024,128]{2,1,0:T(8,128)(2,1)S(1)}, bf16[2,1024,128]{2,1,0:T(8,128)(2,1)S(1)}, u32[]{:S(2)}, u32[]{:S(2)}) collective-permute-start(bf16[2,1024,128]{2,1,0:T(8,128)(2,1)S(1)} %collective-permute-done.13.rest_1_), channel_id=1, source_target_pairs={{8,0},{12,4},{16,8},{20,12},{9,1},{13,5},{17,9},{21,13},{10,2},{14... | collective-permute-start | bytes 1572872 | tf_op jit(solution)/shard_map/ppermute | solution.py:384
  144.6 40.0 %collective-permute-start.27 = (bf16[2,1024,128]{2,1,0:T(8,128)(2,1)S(1)}, bf16[2,1024,128]{2,1,0:T(8,128)(2,1)S(1)}, u32[]{:S(2)}, u32[]{:S(2)}) collective-permute-start(bf16[2,1024,128]{2,1,0:T(8,128)(2,1)S(1)} %collective-permute-done.26.rest_1_), channel_id=1, source_target_pairs={{8,0},{12,4},{16,8},{20,12},{9,1},{13,5},{17,9},{21,13},{10,2},{14... | collective-permute-start | bytes 1572872 | tf_op jit(solution)/shard_map/ppermute | solution.py:384
  152.3 35.9 %collective-permute-start.36 = (bf16[160,1024]{1,0:T(8,128)(2,1)S(1)}, bf16[160,1024]{1,0:T(8,128)(2,1)S(1)}, u32[]{:S(2)}, u32[]{:S(2)}) collective-permute-start(bf16[160,1024]{1,0:T(8,128)(2,1)S(1)} %get-tuple-element.132), channel_id=1, source_target_pairs={{0,1},{1,0},{2,3},{3,2},{4,5},{5,4},{6,7},{7,6},{8,9},{9,8},{10,11... | collective-permute-start | bytes 983048 | tf_op jit(solution)/shard_map/ppermute | solution.py:370
  155.8 33.4 %collective-permute-start.37 = (bf16[160,1024]{1,0:T(8,128)(2,1)S(1)}, bf16[160,1024]{1,0:T(8,128)(2,1)S(1)}, u32[]{:S(2)}, u32[]{:S(2)}) collective-permute-start(bf16[160,1024]{1,0:T(8,128)(2,1)S(1)} %get-tuple-element.133), channel_id=1, source_target_pairs={{0,2},{1,3},{2,0},{3,1},{4,6},{5,7},{6,4},{7,5},{8,10},{9,11},{10,... | collective-permute-start | bytes 983048 | tf_op jit(solution)/shard_map/ppermute | solution.py:370
  167.0 26.2 %collective-permute-start.38 = (bf16[160,1024]{1,0:T(8,128)(2,1)S(1)}, bf16[160,1024]{1,0:T(8,128)(2,1)S(1)}, u32[]{:S(2)}, u32[]{:S(2)}) collective-permute-start(bf16[160,1024]{1,0:T(8,128)(2,1)S(1)} %get-tuple-element.134), channel_id=1, source_target_pairs={{0,3},{1,2},{2,1},{3,0},{4,7},{5,6},{6,5},{7,4},{8,11},{9,10},{10,... | collective-permute-start | bytes 983048 | tf_op jit(solution)/shard_map/ppermute | solution.py:370
  178.3 58.0 %collective-permute-start.23 = (bf16[1024,512]{1,0:T(8,128)(2,1)S(1)}, bf16[1024,512]{1,0:T(8,128)(2,1)S(1)}, u32[]{:S(2)}, u32[]{:S(2)}) collective-permute-start(bf16[1024,512]{1,0:T(8,128)(2,1)S(1)} %get-tuple-element.99.rest_3_), channel_id=1, source_target_pairs={{0,4},{4,0},{8,12},{12,8},{16,20},{20,16},{24,28},{28,24},{1,5},{5... | collective-permute-start | bytes 3145736 | tf_op jit(solution)/shard_map/ppermute | solution.py:364
  184.6 9.8 %collective-permute-start.33 = (bf16[256,256]{1,0:T(8,128)(2,1)S(1)}, bf16[256,256]{1,0:T(8,128)(2,1)S(1)}, u32[]{:S(2)}, u32[]{:S(2)}) collective-permute-start(bf16[256,256]{1,0:T(8,128)(2,1)S(1)} %get-tuple-element.120), channel_id=1, source_target_pairs={{0,1},{1,0},{2,3},{3,2},{4,5},{5,4},{6,7},{7,6},{8,9},{9,8},{10,11... | collective-permute-start | bytes 393224 | tf_op jit(solution)/shard_map/ppermute | solution.py:370
  188.2 8.8 %collective-permute-start.34 = (bf16[256,256]{1,0:T(8,128)(2,1)S(1)}, bf16[256,256]{1,0:T(8,128)(2,1)S(1)}, u32[]{:S(2)}, u32[]{:S(2)}) collective-permute-start(bf16[256,256]{1,0:T(8,128)(2,1)S(1)} %get-tuple-element.121), channel_id=1, source_target_pairs={{0,2},{1,3},{2,0},{3,1},{4,6},{5,7},{6,4},{7,5},{8,10},{9,11},{10,... | collective-permute-start | bytes 393224 | tf_op jit(solution)/shard_map/ppermute | solution.py:370
  189.2 9.2 %collective-permute-start.35 = (bf16[256,256]{1,0:T(8,128)(2,1)S(1)}, bf16[256,256]{1,0:T(8,128)(2,1)S(1)}, u32[]{:S(2)}, u32[]{:S(2)}) collective-permute-start(bf16[256,256]{1,0:T(8,128)(2,1)S(1)} %get-tuple-element.122), channel_id=1, source_target_pairs={{0,3},{1,2},{2,1},{3,0},{4,7},{5,6},{6,5},{7,4},{8,11},{9,10},{10,... | collective-permute-start | bytes 393224 | tf_op jit(solution)/shard_map/ppermute | solution.py:370
  193.3 8.6 %collective-permute-start.45 = (bf16[256,256]{1,0:T(8,128)(2,1)S(1)}, bf16[256,256]{1,0:T(8,128)(2,1)S(1)}, u32[]{:S(2)}, u32[]{:S(2)}) collective-permute-start(bf16[256,256]{1,0:T(8,128)(2,1)S(1)} %get-tuple-element.141), channel_id=1, source_target_pairs={{0,1},{1,0},{2,3},{3,2},{4,5},{5,4},{6,7},{7,6},{8,9},{9,8},{10,11... | collective-permute-start | bytes 393224 | tf_op jit(solution)/shard_map/ppermute | solution.py:370
  194.4 7.5 %collective-permute-start.46 = (bf16[256,256]{1,0:T(8,128)(2,1)S(1)}, bf16[256,256]{1,0:T(8,128)(2,1)S(1)}, u32[]{:S(2)}, u32[]{:S(2)}) collective-permute-start(bf16[256,256]{1,0:T(8,128)(2,1)S(1)} %get-tuple-element.142), channel_id=1, source_target_pairs={{0,2},{1,3},{2,0},{3,1},{4,6},{5,7},{6,4},{7,5},{8,10},{9,11},{10,... | collective-permute-start | bytes 393224 | tf_op jit(solution)/shard_map/ppermute | solution.py:370
  197.0 7.3 %collective-permute-start.47 = (bf16[256,256]{1,0:T(8,128)(2,1)S(1)}, bf16[256,256]{1,0:T(8,128)(2,1)S(1)}, u32[]{:S(2)}, u32[]{:S(2)}) collective-permute-start(bf16[256,256]{1,0:T(8,128)(2,1)S(1)} %get-tuple-element.143), channel_id=1, source_target_pairs={{0,3},{1,2},{2,1},{3,0},{4,7},{5,6},{6,5},{7,4},{8,11},{9,10},{10,... | collective-permute-start | bytes 393224 | tf_op jit(solution)/shard_map/ppermute | solution.py:370
  199.3 7.3 %collective-permute-start.39 = (bf16[224,256]{1,0:T(8,128)(2,1)S(1)}, bf16[224,256]{1,0:T(8,128)(2,1)S(1)}, u32[]{:S(2)}, u32[]{:S(2)}) collective-permute-start(bf16[224,256]{1,0:T(8,128)(2,1)S(1)} %get-tuple-element.136), channel_id=1, source_target_pairs={{0,8},{4,12},{8,0},{12,4},{16,24},{20,28},{24,16},{28,20},{1,9},{5... | collective-permute-start | bytes 344072 | tf_op jit(solution)/shard_map/ppermute | solution.py:377
  201.9 10.3 %collective-permute-start.40 = (bf16[224,256]{1,0:T(8,128)(2,1)S(1)}, bf16[224,256]{1,0:T(8,128)(2,1)S(1)}, u32[]{:S(2)}, u32[]{:S(2)}) collective-permute-start(bf16[224,256]{1,0:T(8,128)(2,1)S(1)} %get-tuple-element.137), channel_id=1, source_target_pairs={{0,16},{4,20},{8,24},{12,28},{16,0},{20,4},{24,8},{28,12},{1,17},{... | collective-permute-start | bytes 344072 | tf_op jit(solution)/shard_map/ppermute | solution.py:377
  201.9 10.3 %collective-permute-start.41 = (bf16[224,256]{1,0:T(8,128)(2,1)S(1)}, bf16[224,256]{1,0:T(8,128)(2,1)S(1)}, u32[]{:S(2)}, u32[]{:S(2)}) collective-permute-start(bf16[224,256]{1,0:T(8,128)(2,1)S(1)} %get-tuple-element.138), channel_id=1, source_target_pairs={{0,24},{4,28},{8,16},{12,20},{16,8},{20,12},{24,0},{28,4},{1,25},{... | collective-permute-start | bytes 344072 | tf_op jit(solution)/shard_map/ppermute | solution.py:377
  205.0 8.7 %collective-permute-start.48 = (bf16[64,256]{1,0:T(8,128)(2,1)S(1)}, bf16[64,256]{1,0:T(8,128)(2,1)S(1)}, u32[]{:S(2)}, u32[]{:S(2)}) collective-permute-start(bf16[64,256]{1,0:T(8,128)(2,1)S(1)} %get-tuple-element.145), channel_id=1, source_target_pairs={{0,8},{4,12},{8,0},{12,4},{16,24},{20,28},{24,16},{28,20},{1,9},{5... | collective-permute-start | bytes 98312 | tf_op jit(solution)/shard_map/ppermute | solution.py:377
  206.6 30.5 %collective-permute-start.22 = (bf16[1024,256]{1,0:T(8,128)(2,1)S(1)}, bf16[1024,256]{1,0:T(8,128)(2,1)S(1)}, u32[]{:S(2)}, u32[]{:S(2)}) collective-permute-start(bf16[1024,256]{1,0:T(8,128)(2,1)S(1)} %get-tuple-element.98), channel_id=1, source_target_pairs={{0,4},{4,0},{8,12},{12,8},{16,20},{20,16},{24,28},{28,24},{1,5},{5... | collective-permute-start | bytes 1572872 | tf_op jit(solution)/shard_map/ppermute | solution.py:364
  212.2 4.8 %collective-permute-start.49 = (bf16[64,256]{1,0:T(8,128)(2,1)S(1)}, bf16[64,256]{1,0:T(8,128)(2,1)S(1)}, u32[]{:S(2)}, u32[]{:S(2)}) collective-permute-start(bf16[64,256]{1,0:T(8,128)(2,1)S(1)} %get-tuple-element.146), channel_id=1, source_target_pairs={{0,16},{4,20},{8,24},{12,28},{16,0},{20,4},{24,8},{28,12},{1,17},{... | collective-permute-start | bytes 98312 | tf_op jit(solution)/shard_map/ppermute | solution.py:377
  212.2 6.0 %collective-permute-start.50 = (bf16[64,256]{1,0:T(8,128)(2,1)S(1)}, bf16[64,256]{1,0:T(8,128)(2,1)S(1)}, u32[]{:S(2)}, u32[]{:S(2)}) collective-permute-start(bf16[64,256]{1,0:T(8,128)(2,1)S(1)} %get-tuple-element.147), channel_id=1, source_target_pairs={{0,24},{4,28},{8,16},{12,20},{16,8},{20,12},{24,0},{28,4},{1,25},{... | collective-permute-start | bytes 98312 | tf_op jit(solution)/shard_map/ppermute | solution.py:377
  213.8 14.4 %collective-permute-start.42 = (bf16[192,256]{1,0:T(8,128)(2,1)S(1)}, bf16[192,256]{1,0:T(8,128)(2,1)S(1)}, u32[]{:S(2)}, u32[]{:S(2)}) collective-permute-start(bf16[192,256]{1,0:T(8,128)(2,1)S(1)} %get-tuple-element.139.rest_0_), channel_id=1, source_target_pairs={{0,8},{4,12},{8,0},{12,4},{16,24},{20,28},{24,16},{28,20},{1,9},{5... | collective-permute-start | bytes 294920 | tf_op jit(solution)/shard_map/ppermute | solution.py:377
  218.3 4.1 %collective-permute-start.51 = (bf16[64,256]{1,0:T(8,128)(2,1)S(1)}, bf16[64,256]{1,0:T(8,128)(2,1)S(1)}, u32[]{:S(2)}, u32[]{:S(2)}) collective-permute-start(bf16[64,256]{1,0:T(8,128)(2,1)S(1)} %shard_map.127.rest_4_), channel_id=1, source_target_pairs={{0,8},{4,12},{8,0},{12,4},{16,24},{20,28},{24,16},{28,20},{1,9},{5... | collective-permute-start | bytes 98312 | tf_op jit(solution)/shard_map/ppermute | solution.py:377
  219.0 4.8 %collective-permute-start.52 = (bf16[64,256]{1,0:T(8,128)(2,1)S(1)}, bf16[64,256]{1,0:T(8,128)(2,1)S(1)}, u32[]{:S(2)}, u32[]{:S(2)}) collective-permute-start(bf16[64,256]{1,0:T(8,128)(2,1)S(1)} %shard_map.127.rest_4_), channel_id=1, source_target_pairs={{0,16},{4,20},{8,24},{12,28},{16,0},{20,4},{24,8},{28,12},{1,17},{... | collective-permute-start | bytes 98312 | tf_op jit(solution)/shard_map/ppermute | solution.py:377
  222.4 5.7 %collective-permute-start.53 = (bf16[64,256]{1,0:T(8,128)(2,1)S(1)}, bf16[64,256]{1,0:T(8,128)(2,1)S(1)}, u32[]{:S(2)}, u32[]{:S(2)}) collective-permute-start(bf16[64,256]{1,0:T(8,128)(2,1)S(1)} %shard_map.127.rest_4_), channel_id=1, source_target_pairs={{0,24},{4,28},{8,16},{12,20},{16,8},{20,12},{24,0},{28,4},{1,25},{... | collective-permute-start | bytes 98312 | tf_op jit(solution)/shard_map/ppermute | solution.py:377
  223.8 17.9 %collective-permute-start.32 = (bf16[1024,256]{1,0:T(8,128)(2,1)S(1)}, bf16[1024,256]{1,0:T(8,128)(2,1)S(1)}, u32[]{:S(2)}, u32[]{:S(2)}) collective-permute-start(bf16[1024,256]{1,0:T(8,128)(2,1)S(1)} %get-tuple-element.118), channel_id=1, source_target_pairs={{0,4},{4,0},{8,12},{12,8},{16,20},{20,16},{24,28},{28,24},{1,5},{5... | collective-permute-start | bytes 1572872 | tf_op jit(solution)/shard_map/ppermute | solution.py:364
  228.1 7.4 %collective-permute-start.43 = (bf16[192,256]{1,0:T(8,128)(2,1)S(1)}, bf16[192,256]{1,0:T(8,128)(2,1)S(1)}, u32[]{:S(2)}, u32[]{:S(2)}) collective-permute-start(bf16[192,256]{1,0:T(8,128)(2,1)S(1)} %get-tuple-element.139.rest_0_), channel_id=1, source_target_pairs={{0,16},{4,20},{8,24},{12,28},{16,0},{20,4},{24,8},{28,12},{1,17},{... | collective-permute-start | bytes 294920 | tf_op jit(solution)/shard_map/ppermute | solution.py:377
  228.1 7.3 %collective-permute-start.44 = (bf16[192,256]{1,0:T(8,128)(2,1)S(1)}, bf16[192,256]{1,0:T(8,128)(2,1)S(1)}, u32[]{:S(2)}, u32[]{:S(2)}) collective-permute-start(bf16[192,256]{1,0:T(8,128)(2,1)S(1)} %get-tuple-element.139.rest_0_), channel_id=1, source_target_pairs={{0,24},{4,28},{8,16},{12,20},{16,8},{20,12},{24,0},{28,4},{1,25},{... | collective-permute-start | bytes 294920 | tf_op jit(solution)/shard_map/ppermute | solution.py:377
  236.1 9.0 %collective-permute-start.54 = (bf16[4,256,256]{2,1,0:T(8,128)(2,1)S(1)}, bf16[4,256,256]{2,1,0:T(8,128)(2,1)S(1)}, u32[]{:S(2)}, u32[]{:S(2)}) collective-permute-start(bf16[4,256,256]{2,1,0:T(8,128)(2,1)S(1)} %shard_map.128.rest_0_), channel_id=1, source_target_pairs={{0,4},{4,0},{8,12},{12,8},{16,20},{20,16},{24,28},{28,24},{1,5},{5... | collective-permute-start | bytes 1572872 | tf_op jit(solution)/shard_map/ppermute | solution.py:364
  236.1 8.9 %collective-permute-start.55 = (bf16[32,256]{1,0:T(8,128)(2,1)S(1)}, bf16[32,256]{1,0:T(8,128)(2,1)S(1)}, u32[]{:S(2)}, u32[]{:S(2)}) collective-permute-start(bf16[32,256]{1,0:T(8,128)(2,1)S(1)} %get-tuple-element.148.rest_2_), channel_id=1, source_target_pairs={{0,1},{1,0},{2,3},{3,2},{4,5},{5,4},{6,7},{7,6},{8,9},{9,8},{10,11... | collective-permute-start | bytes 49160 | tf_op jit(solution)/shard_map/ppermute | solution.py:370
  236.2 8.8 %collective-permute-start.56 = (bf16[32,256]{1,0:T(8,128)(2,1)S(1)}, bf16[32,256]{1,0:T(8,128)(2,1)S(1)}, u32[]{:S(2)}, u32[]{:S(2)}) collective-permute-start(bf16[32,256]{1,0:T(8,128)(2,1)S(1)} %get-tuple-element.148.rest_2_), channel_id=1, source_target_pairs={{0,2},{1,3},{2,0},{3,1},{4,6},{5,7},{6,4},{7,5},{8,10},{9,11},{10,... | collective-permute-start | bytes 49160 | tf_op jit(solution)/shard_map/ppermute | solution.py:370
  237.1 8.0 %collective-permute-start.57 = (bf16[32,256]{1,0:T(8,128)(2,1)S(1)}, bf16[32,256]{1,0:T(8,128)(2,1)S(1)}, u32[]{:S(2)}, u32[]{:S(2)}) collective-permute-start(bf16[32,256]{1,0:T(8,128)(2,1)S(1)} %get-tuple-element.148.rest_2_), channel_id=1, source_target_pairs={{0,3},{1,2},{2,1},{3,0},{4,7},{5,6},{6,5},{7,4},{8,11},{9,10},{10,... | collective-permute-start | bytes 49160 | tf_op jit(solution)/shard_map/ppermute | solution.py:370
